TPU v7x, 32 devices: a whole 2x2x4 slice. The times are simulated.
32 devices in a mesh: rows: 16 (over z, x, core), cols: 2 (over y).
Axes of the slice: x: 2, y: 2, z: 4, core: 2. Of those that a mesh axis runs over, the one named last changes fastest.
Arguments:
- unfolding: float32 [8192, 4096], P('rows', 'cols'), may hold values from -6 to 6
- pattern: int32 [32, 2], P('cols'), may hold values from 0 to 1, as said below
- sign_bits: int32 [4096, 2], P('cols'), may hold values from 0 to 1
Outputs:
- core_scaled: float32 [8192, 256], P('rows')
- next_unfolding: float32 [2048, 512], P('rows', 'cols')
Inputs may be any that keep to these rules, and one draw needn't show every extreme that they name: Every row and every column of pattern holds at least one 1, and some entry is 0.
All inputs are finite; a program needn't handle non-finite values.
Results may differ from a plain program's by a relative error of at most 0.00017.
Values sent between devices are 32-bit elements; how exact they have to be, the bound alone decides.
No kernel may reach another device: no remote copies, remote signals or barrier semaphores. Data moves between devices by JAX's collectives and lax.ppermute only.
A program may use at most 64 MiB of HBM per device.

v0:
```python
import math

import jax
import jax.numpy as jnp
from jax import lax
from jax.sharding import PartitionSpec as P

RANK = 256
BLK = 128
MODE = 8


def hadamard_table(table_size):
    row_index = lax.broadcasted_iota(jnp.int32, (table_size, table_size), 0)
    col_index = lax.broadcasted_iota(jnp.int32, (table_size, table_size), 1)
    parity = jnp.zeros((table_size, table_size), jnp.int32)
    for bit_level in range(table_size.bit_length() - 1):
        bit_value = 1 << bit_level
        parity = parity + row_index // bit_value % 2 * (col_index // bit_value % 2)
    return (1 - 2 * (parity % 2)).astype(jnp.float32)


def sketch_matrix(pattern, sign_bits, block_size):
    blocks = sign_bits.shape[1]
    rows_here = sign_bits.shape[0]
    hadamard = hadamard_table(block_size)
    factor = jnp.repeat(pattern, block_size, axis=0) * (2 * sign_bits - 1)
    tiled_table = jnp.tile(hadamard, (rows_here // block_size, 1))
    expanded = factor.astype(jnp.float32)[:, :, None] * tiled_table[:, None, :]
    return expanded.reshape(rows_here, blocks * block_size)


def inner_rows(left_side, right_side):
    return lax.dot_general(
        left_side, right_side, (((0,), (0,)), ((), ())), precision=lax.Precision.HIGHEST
    )


def local(unfolding, pattern, sign_bits):
    highest = lax.Precision.HIGHEST
    sketch_map = sketch_matrix(pattern, sign_bits, BLK)
    local_rows = unfolding.shape[0]
    local_cols = unfolding.shape[1]
    row_devices = lax.axis_size("rows")
    col_devices = lax.axis_size("cols")
    total_rows = local_rows * row_devices
    partial_sketch = jnp.dot(unfolding, sketch_map, precision=highest)
    sketch = lax.psum(partial_sketch, "cols")
    gram_matrix = lax.psum(inner_rows(sketch, sketch), "rows")
    gram_matrix = gram_matrix + float(total_rows) * jnp.eye(RANK, dtype=jnp.float32)
    lower_factor = jnp.linalg.cholesky(gram_matrix)
    basis_rows = lax.linalg.triangular_solve(
        lower_factor, sketch, left_side=False, lower=True, transpose_a=True
    )
    core_scaled = basis_rows * math.sqrt(total_rows)
    mode_local = MODE // col_devices
    rest_cols = local_cols // mode_local
    rank_share = RANK // row_devices
    reduced = lax.psum_scatter(
        inner_rows(basis_rows, unfolding), "rows", scatter_dimension=0, tiled=True
    )
    grouped = reduced.reshape(rank_share, mode_local, rest_cols)
    regrouped = lax.all_to_all(grouped, "cols", split_axis=2, concat_axis=1, tiled=True)
    next_unfolding = regrouped.reshape(rank_share * MODE, regrouped.shape[2])
    return (core_scaled, next_unfolding)


def solution(mesh):
    in_specs = (P("rows", "cols"), P("cols", None), P("cols", None))
    out_specs = (P("rows", None), P("rows", "cols"))
    return jax.shard_map(local, mesh=mesh, in_specs=in_specs, out_specs=out_specs, check_vma=False)
```

profile of v0, /device:TPU:0, one launch (start us, length us, event | category | flops | bytes accessed | tf_op | source)
XLA Modules:
  0.0 304.2 jit_solution(9669718208111324517)
XLA Ops:
  7.2 0.0 copy-start
  7.2 0.0 all-reduce.4.cloned.1.call-start
  7.3 0.5 copy-done
  7.8 0.1 broadcast_bitcast_fusion
  7.9 0.7 fusion.51
  8.7 0.4 copy.24
  9.0 0.4 fusion.27
  9.4 0.1 tile.8
  9.5 0.0 copy-start.1
  9.5 7.7 %broadcast_multiply_fusion = f32[2048,2,128]{2,1,0:T(2,128)S(1)} fusion(f32[2048,128]{1,0:T(8,128)S(1)} %bitcast.58, f32[2048,2]{1,0:T(8,128)S(1)} %copy.24), kind=kLoop, calls=%fused_computation.8 | loop fusion | flops 524288 | bytes 3162112 | tf_op jit(solution)/shard_map/mul | solution.py:29
  17.3 0.0 copy-done.1
  17.3 8.1 %fusion.3 = f32[512,256]{0,1:T(8,128)} fusion(f32[512,2048]{1,0:T(8,128)S(1)} %copy-done.1, f32[256,8,2,128]{3,2,1,0:T(2,128)S(1)} %bitcast.55), kind=kOutput, calls=%fused_computation.5 | convolution fusion | flops 3221225472 | bytes 6815744 | tf_op jit(solution)/shard_map/dot_general | solution.py:47
  25.4 0.0 all-reduce.4.cloned.1.call-update
  25.4 0.0 all-reduce.6.cloned.1.call-start
  25.5 31.4 %all-reduce.4.cloned.1.call-done = f32[512,256]{0,1:T(8,128)} async-done(((f32[512,256]{0,1:T(8,128)}), f32[512,256]{0,1:T(8,128)}) %all-reduce.4.cloned.1.call-update) | async-done | bytes 524304 | tf_op jit(solution)/shard_map/psum | solution.py:48
  56.9 2.5 fusion.55
  59.4 0.0 all-reduce.6.cloned.1.call-update
  59.4 0.2 reduce-scatter.2.cloned.1.call-start
  59.7 90.3 %all-reduce.6.cloned.1.call-done = f32[256,256]{0,1:T(8,128)} async-done(((f32[256,256]{0,1:T(8,128)}), f32[256,256]{0,1:T(8,128)}) %all-reduce.6.cloned.1.call-update) | async-done | bytes 262160 | tf_op jit(solution)/shard_map/psum | solution.py:49
  150.0 1.0 select_add_fusion
  150.9 0.1 copy.26
  151.1 1.0 fusion.10
  152.1 11.7 %cholesky.45 = f32[128,128]{1,0:T(8,128)S(1)} custom-call(f32[128,128]{1,0:T(8,128)S(1)} %cholesky.107), custom_call_target="Cholesky" | custom-call | tf_op jit(solution)/shard_map/jit(cholesky)/cholesky | solution.py:51
  163.8 0.0 copy-start.2
  163.8 9.8 %custom-call.14 = f32[1,128,128]{1,2,0:T(8,128)S(1)} custom-call(f32[1,128,128]{2,1,0:T(8,128)S(1)} %get-tuple-element.39), custom_call_target="InvertDiagBlocksLowerTriangular" | custom-call | tf_op jit(solution)/shard_map/jit(cholesky)/cholesky | solution.py:51
  173.7 0.2 fusion.42
  173.9 0.3 convolution_subtract_fusion.1
  174.1 11.7 %cholesky.95 = f32[128,128]{1,0:T(8,128)S(1)} custom-call(f32[128,128]{1,0:T(8,128)S(1)} %convolution_subtract_fusion.1), custom_call_target="Cholesky" | custom-call | tf_op jit(solution)/shard_map/jit(cholesky)/cholesky | solution.py:51
  185.9 0.1 copy.29
  186.0 0.1 copy.28
  186.1 0.1 copy.27
  186.2 0.7 compare_reduce_fusion
  186.9 0.6 compare_reduce_fusion.1
  188.9 0.1 triangular_solve.61
  188.9 4.3 %while.1 = (s32[]{:T(128)}, f32[256,256]{0,1:T(8,128)S(1)}, s32[2,2]{1,0:T(2,128)S(1)}, f32[2,128,128]{2,1,0:T(8,128)S(1)}, s32[]{:T(128)}) while((s32[]{:T(128)}, f32[256,256]{0,1:T(8,128)S(1)}, s32[2,2]{1,0:T(2,128)S(1)}, f32[2,128,128]{2,1,0:T(8,128)S(1)}, s32[]{:T(128)}) %tuple.39), condition=%wide.while_cond, body=%wide.while_body.sunk | while | flops 2 | bytes 393321 | solution.py:52
  189.1 0.6 fusion.65
  189.7 1.3 dynamic-slice.7
  191.0 0.1 copy.48
  191.2 0.6 fusion.65
  191.8 1.3 dynamic-slice.7
  193.1 0.1 copy.48
  193.3 19.7 %custom-call.15 = f32[2,128,128]{1,2,0:T(8,128)S(1)} custom-call(f32[2,128,128]{2,1,0:T(8,128)S(1)} %get-tuple-element.9), custom_call_target="InvertDiagBlocksLowerTriangular" | custom-call | tf_op jit(solution)/shard_map/triangular_solve | solution.py:52
  212.9 0.0 copy-done.2
  212.9 0.4 fusion.8
  213.4 0.4 convolution_subtract_fusion
  213.8 0.4 fusion.40
  214.2 7.2 %fusion.6 = f32[256,2048]{1,0:T(8,128)} fusion(f32[512,2048]{1,0:T(8,128)} %param.3, f32[512,128]{0,1:T(8,128)S(1)} %fusion.40, f32[512,128]{0,1:T(8,128)S(1)} %fusion.8), kind=kOutput, calls=%fused_computation.10 | convolution fusion | flops 3221356544 | bytes 6815744 | tf_op jit(solution)/shard_map/dot_general | solution.py:34
  221.4 0.0 reduce-scatter.2.cloned.1.call-update
  221.4 62.2 %reduce-scatter.2.cloned.1.call-done = f32[16,2048]{1,0:T(8,128)} async-done(((f32[256,2048]{1,0:T(8,128)}), f32[16,2048]{1,0:T(8,128)}) %reduce-scatter.2.cloned.1.call-update) | async-done | bytes 131088 | tf_op jit(solution)/shard_map/reduce_scatter | solution.py:59
  283.6 1.0 reshape.692
  284.6 0.4 copy.32
  285.0 1.5 reshape.713
  286.5 3.4 %all-to-all-start = ((f32[2,1,16384]{2,1,0:T(1,128)}), f32[2,1,16384]{2,1,0:T(1,128)S(1)}, u32[]{:S(2)}, u32[]{:S(2)}) async-start(f32[2,1,16384]{2,1,0:T(1,128)} %reshape.713), calls=%async_computation.1 | async-start | bytes 262144 | tf_op jit(solution)/shard_map/all_to_all | solution.py:63
  289.9 0.1 fusion.7
  289.9 1.0 copy.34
  290.9 3.4 %all-to-all-done = f32[2,1,16384]{2,1,0:T(1,128)S(1)} async-done(((f32[2,1,16384]{2,1,0:T(1,128)}), f32[2,1,16384]{2,1,0:T(1,128)S(1)}, u32[]{:S(2)}, u32[]{:S(2)}) %all-to-all-start) | async-done | bytes 131104 | tf_op jit(solution)/shard_map/all_to_all | solution.py:63
  294.3 0.5 broadcast.1149
  294.8 1.0 reduce.12
  295.9 0.8 reshape.714
  296.6 0.3 copy.33
  297.0 0.7 reshape.693
  (22 shorter events, 0.2 us)
Async XLA Ops:
  7.2 0.7 copy-start
  7.2 49.7 %all-reduce.4.cloned.1.call-start = ((), (), s32[]{:S(2)}) async-start(), calls=%async_computation.2 | async-start | bytes 1048576 | tf_op jit(solution)/shard_map/psum | solution.py:48
  9.5 7.8 %copy-start.1 = (f32[512,2048]{1,0:T(8,128)S(1)}, f32[512,2048]{1,0:T(8,128)}, u32[]{:S(2)}) copy-start(f32[512,2048]{1,0:T(8,128)} %param.3) | copy-start | bytes 12582916
  25.4 124.6 %all-reduce.6.cloned.1.call-start = ((), (), s32[]{:S(2)}) async-start(), calls=%async_computation.3 | async-start | bytes 524288 | tf_op jit(solution)/shard_map/psum | solution.py:49
  59.4 224.2 %reduce-scatter.2.cloned.1.call-start = ((), (), s32[]{:S(2)}) async-start(), calls=%async_computation.4 | async-start | bytes 2228224 | tf_op jit(solution)/shard_map/reduce_scatter | solution.py:59
  163.8 49.1 %copy-start.2 = (f32[512,256]{0,1:T(8,128)S(1)}, f32[512,256]{0,1:T(8,128)}, u32[]{:S(2)}) copy-start(f32[512,256]{0,1:T(8,128)} %all-reduce.4.cloned.1.call-done) | copy-start | bytes 1572868
  286.5 7.8 %all-to-all-start = ((f32[2,1,16384]{2,1,0:T(1,128)}), f32[2,1,16384]{2,1,0:T(1,128)S(1)}, u32[]{:S(2)}, u32[]{:S(2)}) async-start(f32[2,1,16384]{2,1,0:T(1,128)} %reshape.713), calls=%async_computation.1 | async-start | bytes 262144 | tf_op jit(solution)/shard_map/all_to_all | solution.py:63
Sparse Core Ops, SparseCore 0:
  25.5 31.2 all-reduce.3
  61.2 88.7 all-reduce.5
  221.5 62.0 reduce-scatter.1
where the time goes:
time: 305 us; the launch traced here: 304 us
  waiting for transfers between devices  187 us (61%)
  other arithmetic  66.3 us (22%)
  matrix products  19.5 us (6%)
  between operations  15.3 us (5%)
  local copies, waits for them, and re-layouts  11.8 us (4%)
  starting transfers between devices  3.68 us (1%)
    psum x1, waiting for transfers between devices, local(): gram_matrix = lax.psum(inner_rows(sketch, sketch), 'rows')  90.3 us
    reduce_scatter x1, waiting for transfers between devices, local(): lax.psum_scatter(inner_rows(basis_rows, unfolding), 'rows', scatter_dimen...  62.2 us
    another operation x7, other arithmetic, local(): lower_factor = jnp.linalg.cholesky(gram_matrix)  34.6 us
    psum x1, waiting for transfers between devices, local(): sketch = lax.psum(partial_sketch, 'cols')  31.4 us
    another operation x3, other arithmetic, local(): lax.linalg.triangular_solve(lower_factor, sketch, left_side=False, lower=...  19.7 us
    dot_general x2, matrix products, inner_rows(): lax.dot_general(left_side, right_side, (((0,), (0,)), ((), ())), precisio...  9.68 us
    dot_general x1, matrix products, local(): partial_sketch = jnp.dot(unfolding, sketch_map, precision=highest)  8.08 us
    mul x1, other arithmetic, sketch_matrix(): expanded = factor.astype(jnp.float32)[:, :, None] * tiled_table[:, None, :]  7.74 us
  transfers between devices with their start and end apart: 4, of which 4 were waited for; matrix products, arithmetic and copies ran while one was open for 0% of the time, Pallas kernels for 0%

commit v1 on v0

v1 whole, which is shorter than its diff:
```python
import math

import jax
import jax.numpy as jnp
import numpy as np
from jax import lax
from jax.experimental import pallas as pl
from jax.experimental.pallas import tpu as pltpu
from jax.sharding import PartitionSpec as P

RANK = 256
BLK = 128
MODE = 8
PANEL = 16
HIGHEST = lax.Precision.HIGHEST
F32 = jnp.float32
BF16 = jnp.bfloat16
VMEM = pl.BlockSpec(memory_space=pltpu.VMEM)
SMEM = pl.BlockSpec(memory_space=pltpu.SMEM)


def hadamard_table(table_size):
    index = np.arange(table_size)
    parity = np.zeros((table_size, table_size), np.int64)
    for bit_level in range(table_size.bit_length() - 1):
        parity += ((index[:, None] & index[None, :]) >> bit_level) & 1
    return jnp.asarray(1 - 2 * (parity % 2), F32)


def shape(*dims, dtype=F32):
    return jax.ShapeDtypeStruct(dims, dtype)


def split(value):
    high = value.astype(BF16)
    return high, (value - high.astype(F32)).astype(BF16)


def dot(left, right):
    return jnp.dot(left, right, preferred_element_type=F32)


def sketch_kernel(pattern_ref, block_ref, sign_ref, table_ref, out_ref):
    rows = block_ref.shape[0]
    col_blocks = sign_ref.shape[0]
    row_blocks = block_ref.shape[1] // BLK
    sums = []
    for k in range(col_blocks):
        total = jnp.zeros((rows, BLK), F32)
        for j in range(row_blocks):
            cols = slice(j * BLK, (j + 1) * BLK)
            factor = (2 * sign_ref[k : k + 1, cols] - 1) * pattern_ref[j, k]
            total = total + block_ref[:, cols] * factor.astype(F32)
        sums.append(total)
    mixed = jnp.dot(jnp.concatenate(sums, 0), table_ref[...], precision=HIGHEST)
    for k in range(col_blocks):
        out_ref[:, k * BLK : (k + 1) * BLK] = mixed[k * rows : (k + 1) * rows]


def sketch_band(unfolding, pattern, sign_rows, table, band, bands):
    rows, cols = unfolding.shape
    step = 64
    steps = rows // bands // step
    return pl.pallas_call(
        sketch_kernel,
        grid=(steps,),
        in_specs=[
            SMEM,
            pl.BlockSpec((step, cols), lambda i: (band * steps + i, 0)),
            pl.BlockSpec(sign_rows.shape, lambda i: (0, 0)),
            pl.BlockSpec((BLK, BLK), lambda i: (0, 0)),
        ],
        out_specs=pl.BlockSpec((step, RANK), lambda i: (i, 0)),
        out_shape=shape(rows // bands, RANK),
        name="sketch_band",
    )(pattern, unfolding, sign_rows, table)


def gram_kernel(ids_ref, own_a, own_b, got_a, got_b, sketch_ref, high_ref, low_ref, keep_ref, send_ref, packed):
    band = own_a.shape[0]
    sketch_ref[:band, :] = own_a[...] + got_a[...]
    sketch_ref[band:, :] = own_b[...] + got_b[...]
    sketch = sketch_ref[...]
    turned = sketch.T
    high, low = split(turned)
    high_ref[...] = high
    low_ref[...] = low
    top = jnp.dot(turned[:BLK], sketch, precision=HIGHEST)
    packed[:BLK] = top[:, :BLK]
    packed[BLK : 2 * BLK] = top[:, BLK:]
    packed[2 * BLK :] = jnp.dot(turned[BLK:], sketch[:, BLK:], precision=HIGHEST)
    half = packed.shape[0] // 2
    core = ids_ref[0]
    keep_ref[...] = packed[pl.ds(pl.multiple_of(core * half, half), half), :]
    send_ref[...] = packed[pl.ds(pl.multiple_of((1 - core) * half, half), half), :]


def gram_parts(ids, own, got):
    rows = own[0].shape[0] * 2
    return pl.pallas_call(
        gram_kernel,
        in_specs=[SMEM] + [VMEM] * 4,
        out_specs=[VMEM] * 5,
        out_shape=[
            shape(rows, RANK),
            shape(RANK, rows, dtype=BF16),
            shape(RANK, rows, dtype=BF16),
            shape(192, BLK),
            shape(192, BLK),
        ],
        scratch_shapes=[pltpu.VMEM((384, BLK), F32)],
        name="gram_parts",
    )(ids, *own, *got)


def project_kernel(ids_ref, high_ref, low_ref, block_ref, out_ref):
    a_high, a_low = split(block_ref[...])
    total = dot(high_ref[...], a_high) + dot(high_ref[...], a_low) + dot(low_ref[...], a_high)
    flip = ids_ref[1]
    out_ref[flip, 0] = total[:, :BLK]
    out_ref[1 - flip, 0] = total[:, BLK:]


def project(ids, high, low, unfolding, side):
    rows = unfolding.shape[0]

    def block(t, ids):
        return 0, (t ^ ids[2]) * 2 + (ids[3] ^ side)

    return pl.pallas_call(
        project_kernel,
        grid_spec=pltpu.PrefetchScalarGridSpec(
            num_scalar_prefetch=1,
            grid=(4,),
            in_specs=[
                pl.BlockSpec((RANK, rows), lambda t, ids: (0, 0)),
                pl.BlockSpec((RANK, rows), lambda t, ids: (0, 0)),
                pl.BlockSpec((rows, 2 * BLK), block),
            ],
            out_specs=pl.BlockSpec((2, 1, RANK, BLK), lambda t, ids: (0, t, 0, 0)),
        ),
        out_shape=shape(2, 4, RANK, BLK),
        name="project",
    )(ids, high, low, unfolding)


def factor_panel(parts, start):
    diagonal = parts[0][:, start : start + PANEL]
    columns = [jnp.broadcast_to(diagonal[:, k : k + 1], (PANEL, BLK)) for k in range(PANEL)]
    rows = lax.broadcasted_iota(jnp.int32, (PANEL, BLK), 0)
    pivots = jnp.ones((PANEL, BLK), F32)
    for j in range(PANEL):
        pivot = jnp.broadcast_to(columns[j][j : j + 1, :], (PANEL, BLK))
        multiplier = jnp.where(rows > j, columns[j] / pivot, 0.0)
        for k in range(j + 1, PANEL):
            columns[k] = columns[k] - multiplier * columns[k][j : j + 1, :]
        parts = [part - multiplier * part[j : j + 1, :] for part in parts]
        pivots = jnp.where(rows == j, pivot, pivots)
    scale = lax.rsqrt(pivots)
    return [part * scale for part in parts]


def factor_block(work):
    for panel in range(BLK // PANEL):
        start = panel * PANEL
        stop = start + PANEL
        parts = [work[start:stop, c * BLK : (c + 1) * BLK] for c in range(3)]
        parts = factor_panel(parts, start)
        for c in range(3):
            work[start:stop, c * BLK : (c + 1) * BLK] = parts[c]
        if stop < BLK:
            left = parts[0].T[stop:]
            work[stop:, :] = work[stop:, :] - jnp.dot(left, jnp.concatenate(parts, 1), precision=HIGHEST)


def factor_kernel(total_rows, ids_ref, own_ref, got_ref, out_ref, work, packed):
    half = own_ref.shape[0]
    core = ids_ref[0]
    packed[pl.ds(pl.multiple_of(core * half, half), half), :] = own_ref[...]
    packed[pl.ds(pl.multiple_of((1 - core) * half, half), half), :] = got_ref[...]
    row = lax.broadcasted_iota(jnp.int32, (BLK, BLK), 0)
    col = lax.broadcasted_iota(jnp.int32, (BLK, BLK), 1)
    eye = (row == col).astype(F32)
    work[:, :BLK] = packed[:BLK] + float(total_rows) * eye
    work[:, BLK : 2 * BLK] = packed[BLK : 2 * BLK]
    work[:, 2 * BLK :] = eye
    factor_block(work)
    out_ref[:BLK, :BLK] = work[:, 2 * BLK :]
    out_ref[:BLK, BLK:] = jnp.zeros((BLK, BLK), F32)
    above = work[:, BLK : 2 * BLK]
    product = jnp.dot(above.T, work[:, BLK:], precision=HIGHEST)
    work[:, :BLK] = packed[2 * BLK :] + float(total_rows) * eye - product[:, :BLK]
    work[:, BLK : 2 * BLK] = -product[:, BLK:]
    work[:, 2 * BLK :] = eye
    factor_block(work)
    out_ref[BLK:, :] = work[:, BLK:]


def inverse_factor(ids, own, got, total_rows):
    def body(*refs):
        factor_kernel(total_rows, *refs)

    return pl.pallas_call(
        body,
        in_specs=[SMEM, VMEM, VMEM],
        out_specs=VMEM,
        out_shape=shape(RANK, RANK),
        scratch_shapes=[pltpu.VMEM((BLK, 3 * BLK), F32), pltpu.VMEM((3 * BLK, BLK), F32)],
        name="inverse_factor",
    )(ids, own, got)


def core_kernel(scale, sketch_ref, inverse_ref, out_ref):
    s_high, s_low = split(sketch_ref[...])
    t_high, t_low = split(inverse_ref[...].T)
    total = dot(s_high, t_high) + dot(s_high, t_low) + dot(s_low, t_high)
    out_ref[...] = total * scale


def scaled_core(sketch, inverse, scale):
    def body(*refs):
        core_kernel(scale, *refs)

    return pl.pallas_call(
        body,
        in_specs=[VMEM, VMEM],
        out_specs=VMEM,
        out_shape=shape(*sketch.shape),
        name="scaled_core",
    )(sketch, inverse)


def remainder_kernel(ids_ref, inverse_ref, p0, p1, p2, p3, o0, o1, o2, o3, work):
    work[...] = jnp.dot(inverse_ref[...], (p0[...] + p1[...]) + (p2[...] + p3[...]), precision=HIGHEST)
    device = ids_ref[4]
    for m, out in enumerate((o0, o1, o2, o3)):
        for t in range(4):
            rank_block = (4 * t + m) ^ device
            out[t] = work[pl.ds(pl.multiple_of(rank_block * 16, 16), 16), :]


def remainder_pieces(ids, inverse, pieces):
    return pl.pallas_call(
        remainder_kernel,
        in_specs=[SMEM] + [VMEM] * 5,
        out_specs=[VMEM] * 4,
        out_shape=[shape(4, 16, BLK)] * 4,
        scratch_shapes=[pltpu.VMEM((RANK, BLK), F32)],
        name="remainder_pieces",
    )(ids, inverse, *pieces)


def arrange_kernel(ids_ref, r0, r1, r2, r3, s1, s2, s3, out_ref, work):
    core, right, deep, y = ids_ref[0], ids_ref[1], ids_ref[2], ids_ref[5]
    firsts = (r0, r1, r2, r3)
    later = (None, s1, s2, s3)
    for t in range(4):
        for m in range(4):
            mode = (y ^ core ^ (m & 1)) * 4 + (deep ^ t)
            work[mode, right ^ (m >> 1)] = firsts[m][0] if t == 0 else later[t][m]
    for mode in range(MODE):
        for c in range(2):
            out_ref[:, mode, c * BLK : (c + 1) * BLK] = work[mode, c]


def arrange(ids, firsts, later):
    out = pl.pallas_call(
        arrange_kernel,
        in_specs=[SMEM] + [VMEM] * 7,
        out_specs=VMEM,
        out_shape=shape(16, MODE, 2 * BLK),
        scratch_shapes=[pltpu.VMEM((MODE, 2, 16, BLK), F32)],
        name="arrange",
    )(ids, *firsts, *later)
    return out.reshape(16 * MODE, 2 * BLK)


def rows_permute(value, mask):
    size = lax.axis_size("rows")
    return lax.ppermute(value, "rows", [(i, i ^ mask) for i in range(size)])


def local(unfolding, pattern, sign_bits):
    total_rows = unfolding.shape[0] * lax.axis_size("rows")
    row = lax.axis_index("rows")
    y = lax.axis_index("cols")
    core = row & 1
    ids = jnp.stack([core, (row >> 1) & 1, row >> 2, core ^ y, row, y]).astype(jnp.int32)
    table = hadamard_table(BLK)
    sign_rows = sign_bits.T
    swap = [(0, 1), (1, 0)]
    own, got = [], []
    for band in range(2):
        part = sketch_band(unfolding, pattern, sign_rows, table, band, 2)
        own.append(part)
        got.append(lax.ppermute(part, "cols", swap))
    sketch, high, low, gram_keep, gram_send = gram_parts(ids, own, got)
    gram = gram_keep + rows_permute(gram_send, 1)
    give = project(ids, high, low, unfolding, 1)
    keep = project(ids, high, low, unfolding, 0)
    for mask in (2, 4, 8):
        gram = gram + rows_permute(gram, mask)
    gram_other = rows_permute(gram, 1)
    summed = keep + rows_permute(give, 1)
    summed = summed[0] + rows_permute(summed[1], 2)
    pieces = [summed[0]] + [rows_permute(summed[t], 4 * t) for t in (1, 2, 3)]
    inverse = inverse_factor(ids, gram, gram_other, total_rows)
    parts = remainder_pieces(ids, inverse, pieces)
    core_scaled = scaled_core(sketch, inverse, math.sqrt(total_rows))
    firsts = []
    for m in range(4):
        pairs = [(2 * i + j, 2 * (i ^ m) + (j ^ (i & 1))) for i in range(16) for j in range(2)]
        firsts.append(lax.ppermute(parts[m], ("rows", "cols"), pairs))
    later = []
    for t in (1, 2, 3):
        later.append(rows_permute(jnp.stack([first[t] for first in firsts]), 4 * t))
    return core_scaled, arrange(ids, firsts, later)


def sketch_matrix(pattern, sign_bits, block_size):
    blocks = sign_bits.shape[1]
    rows_here = sign_bits.shape[0]
    factor = jnp.repeat(pattern, block_size, axis=0) * (2 * sign_bits - 1)
    tiled_table = jnp.tile(hadamard_table(block_size), (rows_here // block_size, 1))
    expanded = factor.astype(F32)[:, :, None] * tiled_table[:, None, :]
    return expanded.reshape(rows_here, blocks * block_size)


def inner_rows(left_side, right_side):
    return lax.dot_general(left_side, right_side, (((0,), (0,)), ((), ())), precision=HIGHEST)


def local_any(unfolding, pattern, sign_bits):
    sketch_map = sketch_matrix(pattern, sign_bits, BLK)
    row_devices = lax.axis_size("rows")
    col_devices = lax.axis_size("cols")
    total_rows = unfolding.shape[0] * row_devices
    sketch = lax.psum(jnp.dot(unfolding, sketch_map, precision=HIGHEST), "cols")
    gram_matrix = lax.psum(inner_rows(sketch, sketch), "rows")
    gram_matrix = gram_matrix + float(total_rows) * jnp.eye(RANK, dtype=F32)
    lower_factor = jnp.linalg.cholesky(gram_matrix)
    basis_rows = lax.linalg.triangular_solve(lower_factor, sketch, left_side=False, lower=True, transpose_a=True)
    mode_local = MODE // col_devices
    rest_cols = unfolding.shape[1] // mode_local
    rank_share = RANK // row_devices
    reduced = lax.psum_scatter(inner_rows(basis_rows, unfolding), "rows", scatter_dimension=0, tiled=True)
    grouped = reduced.reshape(rank_share, mode_local, rest_cols)
    regrouped = lax.all_to_all(grouped, "cols", split_axis=2, concat_axis=1, tiled=True)
    return basis_rows * math.sqrt(total_rows), regrouped.reshape(rank_share * MODE, regrouped.shape[2])


def solution(mesh):
    in_specs = (P("rows", "cols"), P("cols", None), P("cols", None))
    out_specs = (P("rows", None), P("rows", "cols"))
    body = local if (mesh.shape["rows"], mesh.shape["cols"]) == (16, 2) else local_any
    return jax.shard_map(body, mesh=mesh, in_specs=in_specs, out_specs=out_specs, check_vma=False)
```

time: 305 us -> 107 us (0.35)
  waiting for transfers between devices: 187 us -> 35 us
  other arithmetic: 66.3 us -> 1.49 us
  Pallas kernels: 0 us -> 38 us
  starting transfers between devices: 3.68 us -> 24.8 us
  matrix products: 19.5 us -> 0 us
  between operations: 15.3 us -> 0.79 us
  local copies, waits for them, and re-layouts: 11.8 us -> 5.98 us
    psum x2 -> x0, waiting for transfers between devices: 122 us -> none  [the longest x1 90.3 us: local(): gram_matrix = lax.psum(inner_rows(sketch, sketch), 'rows')]
    reduce_scatter x1 -> x0, waiting for transfers between devices: 62.2 us -> none  [local(): lax.psum_scatter(inner_rows(basis_rows, unfolding), 'rows', scatter_dimen...]
    another operation x10 -> x3, other arithmetic: 54.3 us -> 0.01 us  [local(): later.append(rows_permute(jnp.stack([first[t] for first in firsts]), 4 * t))]
    pallas_call x0 -> x9, Pallas kernels: none -> 38 us  [the longest x1 10.8 us: inverse_factor(): pl.pallas_call(body, in_specs=[SMEM, VMEM, VMEM], out_specs=VMEM, out_sha...]
    ppermute x0 -> x19, waiting for transfers between devices: none -> 35 us  [the longest x13 22.8 us: rows_permute(): return lax.ppermute(value, 'rows', [(i, i ^ mask) for i in range(size)])]
    ppermute x0 -> x19, starting transfers between devices: none -> 24.8 us  [the longest x13 16 us: rows_permute(): return lax.ppermute(value, 'rows', [(i, i ^ mask) for i in range(size)])]
    dot_general x3 -> x0, matrix products: 17.8 us -> none  [the longest x2 9.68 us: inner_rows(): lax.dot_general(left_side, right_side, (((0,), (0,)), ((), ())), precisio...]
    mul x2 -> x0, other arithmetic: 7.79 us -> none  [the longest x1 7.74 us: sketch_matrix(): expanded = factor.astype(jnp.float32)[:, :, None] * tiled_table[:, None, :]]
  transfers between devices with their start and end apart: 4 -> 19, of which waited for: 4 -> 11; matrix products, arithmetic and copies ran while one was open for 0% -> 1% of each run, Pallas kernels for 0% -> 21%
where the time goes in v1:
time: 107 us; the launch traced here: 106 us
  Pallas kernels  38 us (36%)
  waiting for transfers between devices  35 us (33%)
  starting transfers between devices  24.8 us (23%)
  local copies, waits for them, and re-layouts  5.98 us (6%)
  other arithmetic  1.49 us (1%)
    ppermute x13, waiting for transfers between devices, rows_permute(): return lax.ppermute(value, 'rows', [(i, i ^ mask) for i in range(size)])  22.8 us
    ppermute x13, starting transfers between devices, rows_permute(): return lax.ppermute(value, 'rows', [(i, i ^ mask) for i in range(size)])  16 us
    pallas_call x1, Pallas kernels, inverse_factor(): pl.pallas_call(body, in_specs=[SMEM, VMEM, VMEM], out_specs=VMEM, out_sha...  10.8 us
    pallas_call x2, Pallas kernels, project(): pl.pallas_call(project_kernel, grid_spec=pltpu.PrefetchScalarGridSpec(num...  10.4 us
    pallas_call x2, Pallas kernels, sketch_band(): pl.pallas_call(sketch_kernel, grid=(steps,), in_specs=[SMEM, pl.BlockSpec...  7.94 us
    ppermute x2, waiting for transfers between devices, local(): got.append(lax.ppermute(part, 'cols', swap))  7.52 us
    ppermute x4, starting transfers between devices, local(): firsts.append(lax.ppermute(parts[m], ('rows', 'cols'), pairs))  5.81 us
    ppermute x4, waiting for transfers between devices, local(): firsts.append(lax.ppermute(parts[m], ('rows', 'cols'), pairs))  4.75 us
  transfers between devices with their start and end apart: 19, of which 11 were waited for; matrix products, arithmetic and copies ran while one was open for 1% of the time, Pallas kernels for 21%

profile of v1, /device:TPU:0, one launch (start us, length us, event | category | flops | bytes accessed | tf_op | source)
XLA Modules:
  0.0 106.1 jit_solution(2451658122023233267)
XLA Ops:
  0.6 1.4 %copy.6.pattern_ref = s32[16,2]{1,0:T(8,128)} copy(s32[16,2]{0,1:T(2,128)} %param.5) | data formatting | bytes 256 | tf_op args[1]
  2.0 4.0 %sketch_band.2.own_a = f32[256,256]{1,0:T(8,128)} custom-call(s32[16,2]{1,0:T(8,128)} %copy.6.pattern_ref, f32[512,2048]{1,0:T(8,128)} %block_ref.7, s32[2,2048]{1,0:T(2,128)} %bitcast.23, f32[128,128]{1,0:T(8,128)} %constant.14.clone.table_ref), custom_call_target="tpu_custom_call" | custom-call | tf_op jit(solution)/shard_map/sketch_band/pallas_call | solution.py:64
  6.0 3.0 %collective-permute-start = (f32[256,256]{1,0:T(8,128)}, f32[256,256]{1,0:T(8,128)S(1)}, u32[]{:S(2)}, u32[]{:S(2)}) collective-permute-start(f32[256,256]{1,0:T(8,128)} %sketch_band.2.own_a), channel_id=1, source_target_pairs={{0,1},{1,0},{2,3},{3,2},{4,5},{5,4},{6,7},{7,6},{8,9},{9,8},{10,11... | collective-permute-start | bytes 786440 | tf_op jit(solution)/shard_map/ppermute | solution.py:296
  8.9 4.0 %sketch_band.3.own_b = f32[256,256]{1,0:T(8,128)} custom-call(s32[16,2]{1,0:T(8,128)} %copy.6.pattern_ref, f32[512,2048]{1,0:T(8,128)} %block_ref.7, s32[2,2048]{1,0:T(2,128)} %bitcast.24, f32[128,128]{1,0:T(8,128)} %constant.14.clone.table_ref), custom_call_target="tpu_custom_call" | custom-call | tf_op jit(solution)/shard_map/sketch_band/pallas_call | solution.py:64
  12.9 0.0 collective-permute-start.1
  12.9 0.6 stack.36.ids_ref.refs_0_
  13.5 2.4 %collective-permute-done.got_a = f32[256,256]{1,0:T(8,128)S(1)} collective-permute-done((f32[256,256]{1,0:T(8,128)}, f32[256,256]{1,0:T(8,128)S(1)}, u32[]{:S(2)}, u32[]{:S(2)}) %collective-permute-start) | collective-permute-done | bytes 262176 | tf_op jit(solution)/shard_map/ppermute | solution.py:296
  16.0 5.1 %collective-permute-done.1.got_b = f32[256,256]{1,0:T(8,128)S(1)} collective-permute-done((f32[256,256]{1,0:T(8,128)}, f32[256,256]{1,0:T(8,128)S(1)}, u32[]{:S(2)}, u32[]{:S(2)}) %collective-permute-start.1) | collective-permute-done | bytes 262176 | tf_op jit(solution)/shard_map/ppermute | solution.py:296
  21.1 0.0 copy-done.1
  21.1 0.7 copy-done.2
  21.8 2.6 %gram_parts.1 = (f32[512,256]{1,0:T(8,128)}, bf16[256,512]{1,0:T(8,128)(2,1)}, bf16[256,512]{1,0:T(8,128)(2,1)}, f32[192,128]{1,0:T(8,128)}, f32[192,128]{1,0:T(8,128)}) custom-call(s32[6]{0:T(128)} %stack.36.ids_ref.refs_0_, f32[256,256]{1,0:T(8,128)} %sketch_band.2.own_a, f32[256,256]{1,0:T(8,128)} %sketch_band.3.own_b, f32[256,256]{1,0:T(8,128)} %copy-done.1, ...), custom_call_target="tpu_custom_call" | custom-call | tf_op jit(solution)/shard_map/gram_parts/pallas_call | solution.py:100
  24.4 5.2 %project.3 = f32[2,4,256,128]{3,2,1,0:T(8,128)} custom-call(s32[6]{0:T(128)} %stack.36.ids_ref.refs_0_, bf16[256,512]{1,0:T(8,128)(2,1)} %get-tuple-element.14.high_ref, bf16[256,512]{1,0:T(8,128)(2,1)} %get-tuple-element.15.low_ref, f32[512,2048]{1,0:T(8,128)} %block_ref.7), custom_call_target="tpu_custom_call" | custom-call | tf_op jit(solution)/shard_map/project/pallas_call | solution.py:130
  29.5 0.0 collective-permute-start.7
  29.6 5.3 %project.2 = f32[2,4,256,128]{3,2,1,0:T(8,128)} custom-call(s32[6]{0:T(128)} %stack.36.ids_ref.refs_0_, bf16[256,512]{1,0:T(8,128)(2,1)} %get-tuple-element.14.high_ref, bf16[256,512]{1,0:T(8,128)(2,1)} %get-tuple-element.15.low_ref, f32[512,2048]{1,0:T(8,128)} %block_ref.7), custom_call_target="tpu_custom_call" | custom-call | tf_op jit(solution)/shard_map/project/pallas_call | solution.py:130
  34.8 0.0 collective-permute-done.7
  34.8 1.3 %add.22 = f32[2,4,256,128]{3,2,1,0:T(8,128)S(1)} add(f32[2,4,256,128]{3,2,1,0:T(8,128)} %project.2, f32[2,4,256,128]{3,2,1,0:T(8,128)S(1)} %collective-permute-done.7) | non-fusion elementwise | flops 262144 | bytes 3145728 | tf_op jit(solution)/shard_map/add | solution.py:304
  36.2 1.8 %collective-permute-start.8 = (f32[4,256,128]{2,1,0:T(8,128)S(1)}, f32[4,256,128]{2,1,0:T(8,128)S(1)}, u32[]{:S(2)}, u32[]{:S(2)}) collective-permute-start(f32[4,256,128]{2,1,0:T(8,128)S(1)} %slice_bitcast_fusion), channel_id=1, source_target_pairs={{0,4},{2,6},{4,0},{6,2},{8,12},{10,14},{12,8},{14,10},{16,20},{18,... | collective-permute-start | bytes 1572872 | tf_op jit(solution)/shard_map/ppermute | solution.py:280
  38.0 0.0 copy-done.15
  38.0 0.1 collective-permute-start.2
  38.1 1.2 %collective-permute-done.2 = f32[192,128]{1,0:T(8,128)S(1)} collective-permute-done((f32[192,128]{1,0:T(8,128)S(1)}, f32[192,128]{1,0:T(8,128)S(1)}, u32[]{:S(2)}, u32[]{:S(2)}) %collective-permute-start.2) | collective-permute-done | bytes 98336 | tf_op jit(solution)/shard_map/ppermute | solution.py:280
  39.3 0.4 collective-permute-start.3
  39.7 12.9 %collective-permute-done.3 = f32[192,128]{1,0:T(8,128)S(1)} collective-permute-done((f32[192,128]{1,0:T(8,128)S(1)}, f32[192,128]{1,0:T(8,128)S(1)}, u32[]{:S(2)}, u32[]{:S(2)}) %collective-permute-start.3) | collective-permute-done | bytes 98336 | tf_op jit(solution)/shard_map/ppermute | solution.py:280
  52.6 1.9 %collective-permute-start.4 = (f32[192,128]{1,0:T(8,128)S(1)}, f32[192,128]{1,0:T(8,128)S(1)}, u32[]{:S(2)}, u32[]{:S(2)}) collective-permute-start(f32[192,128]{1,0:T(8,128)S(1)} %add.19), channel_id=1, source_target_pairs={{0,8},{2,10},{4,12},{6,14},{8,0},{10,2},{12,4},{14,6},{16,24},{18,... | collective-permute-start | bytes 294920 | tf_op jit(solution)/shard_map/ppermute | solution.py:280
  54.5 2.8 %collective-permute-done.4 = f32[192,128]{1,0:T(8,128)S(1)} collective-permute-done((f32[192,128]{1,0:T(8,128)S(1)}, f32[192,128]{1,0:T(8,128)S(1)}, u32[]{:S(2)}, u32[]{:S(2)}) %collective-permute-start.4) | collective-permute-done | bytes 98336 | tf_op jit(solution)/shard_map/ppermute | solution.py:280
  57.3 2.9 %collective-permute-start.5 = (f32[192,128]{1,0:T(8,128)S(1)}, f32[192,128]{1,0:T(8,128)S(1)}, u32[]{:S(2)}, u32[]{:S(2)}) collective-permute-start(f32[192,128]{1,0:T(8,128)S(1)} %add.20), channel_id=1, source_target_pairs={{0,16},{2,18},{4,20},{6,22},{8,24},{10,26},{12,28},{14,30},{16,0},... | collective-permute-start | bytes 294920 | tf_op jit(solution)/shard_map/ppermute | solution.py:280
  60.2 0.0 collective-permute-done.8
  60.2 0.1 fusion
  60.3 0.7 slice_bitcast_fusion.2
  60.9 0.1 collective-permute-start.10
  61.1 3.8 %collective-permute-start.11 = (f32[256,128]{1,0:T(8,128)S(1)}, f32[256,128]{1,0:T(8,128)S(1)}, u32[]{:S(2)}, u32[]{:S(2)}) collective-permute-start(f32[256,128]{1,0:T(8,128)S(1)} %get-tuple-element.20), channel_id=1, source_target_pairs={{0,24},{2,26},{4,28},{6,30},{8,16},{10,18},{12,20},{14,22},{16,8},... | collective-permute-start | bytes 393224 | tf_op jit(solution)/shard_map/ppermute | solution.py:280
  64.9 0.0 collective-permute-start.9
  64.9 2.8 %collective-permute-done.5 = f32[192,128]{1,0:T(8,128)S(1)} collective-permute-done((f32[192,128]{1,0:T(8,128)S(1)}, f32[192,128]{1,0:T(8,128)S(1)}, u32[]{:S(2)}, u32[]{:S(2)}) %collective-permute-start.5) | collective-permute-done | bytes 98336 | tf_op jit(solution)/shard_map/ppermute | solution.py:280
  67.7 0.0 copy-start
  67.7 0.1 collective-permute-start.6
  67.8 1.3 %collective-permute-done.6.refs_2_ = f32[192,128]{1,0:T(8,128)S(1)} collective-permute-done((f32[192,128]{1,0:T(8,128)S(1)}, f32[192,128]{1,0:T(8,128)S(1)}, u32[]{:S(2)}, u32[]{:S(2)}) %collective-permute-start.6) | collective-permute-done | bytes 98336 | tf_op jit(solution)/shard_map/ppermute | solution.py:280
  69.1 0.7 copy-done.11
  69.7 10.8 %inverse_factor.1.refs_1_.inverse_ref = f32[256,256]{1,0:T(8,128)} custom-call(s32[6]{0:T(128)} %stack.36.ids_ref.refs_0_, f32[192,128]{1,0:T(8,128)} %copy-done, f32[192,128]{1,0:T(8,128)} %copy-done.11), custom_call_target="tpu_custom_call" | custom-call | tf_op jit(solution)/shard_map/inverse_factor/pallas_call | solution.py:203
  80.5 0.0 collective-permute-done.10.p2
  80.5 0.0 collective-permute-done.11.p3
  80.5 0.0 copy-start.4
  80.6 0.0 collective-permute-done.9.p1
  80.6 0.0 copy-start.5
  80.6 0.6 copy-done.3
  81.2 0.0 copy-done.4
  81.2 0.0 copy-done.5
  81.3 2.2 %remainder_pieces.1 = (f32[4,16,128]{2,1,0:T(8,128)}, f32[4,16,128]{2,1,0:T(8,128)}, f32[4,16,128]{2,1,0:T(8,128)}, f32[4,16,128]{2,1,0:T(8,128)}) custom-call(s32[6]{0:T(128)} %stack.36.ids_ref.refs_0_, f32[256,256]{1,0:T(8,128)} %inverse_factor.1.refs_1_.inverse_ref, f32[256,128]{1,0:T(8,128)} %get-tuple-element.23.p0, f32[256,128]{1,0:T(8,128)} %copy-done.5, ...), custom_call_target="tpu_custom_call" | custom-call | tf_op jit(solution)/shard_map/remainder_pieces/pallas_call | solution.py:243
  83.5 1.4 %collective-permute-start.12 = (f32[4,16,128]{2,1,0:T(8,128)}, f32[4,16,128]{2,1,0:T(8,128)S(1)}, u32[]{:S(2)}, u32[]{:S(2)}) collective-permute-start(f32[4,16,128]{2,1,0:T(8,128)} %get-tuple-element.16), channel_id=1, source_target_pairs={{0,0},{1,1},{2,3},{3,2},{4,4},{5,5},{6,7},{7,6},{8,8},{9,9},{10,11... | collective-permute-start | bytes 98312 | tf_op jit(solution)/shard_map/ppermute | solution.py:313
  84.9 2.9 %collective-permute-start.13 = (f32[4,16,128]{2,1,0:T(8,128)}, f32[4,16,128]{2,1,0:T(8,128)S(1)}, u32[]{:S(2)}, u32[]{:S(2)}) collective-permute-start(f32[4,16,128]{2,1,0:T(8,128)} %get-tuple-element.17), channel_id=1, source_target_pairs={{0,2},{1,3},{2,1},{3,0},{4,6},{5,7},{6,5},{7,4},{8,10},{9,11},{10,... | collective-permute-start | bytes 98312 | tf_op jit(solution)/shard_map/ppermute | solution.py:313
  87.8 1.5 %collective-permute-start.14 = (f32[4,16,128]{2,1,0:T(8,128)}, f32[4,16,128]{2,1,0:T(8,128)S(1)}, u32[]{:S(2)}, u32[]{:S(2)}) collective-permute-start(f32[4,16,128]{2,1,0:T(8,128)} %get-tuple-element.18), channel_id=1, source_target_pairs={{0,4},{1,5},{2,7},{3,6},{4,0},{5,1},{6,3},{7,2},{8,12},{9,13},{10,... | collective-permute-start | bytes 98312 | tf_op jit(solution)/shard_map/ppermute | solution.py:313
  89.3 0.0 collective-permute-start.15
  89.3 0.0 collective-permute-done.12.r0
  89.3 0.5 collective-permute-done.13.r1
  89.8 2.1 %collective-permute-done.14.r2 = f32[4,16,128]{2,1,0:T(8,128)S(1)} collective-permute-done((f32[4,16,128]{2,1,0:T(8,128)}, f32[4,16,128]{2,1,0:T(8,128)S(1)}, u32[]{:S(2)}, u32[]{:S(2)}) %collective-permute-start.14) | collective-permute-done | bytes 32800 | tf_op jit(solution)/shard_map/ppermute | solution.py:313
  91.9 2.1 %collective-permute-done.15.r3 = f32[4,16,128]{2,1,0:T(8,128)S(1)} collective-permute-done((f32[4,16,128]{2,1,0:T(8,128)}, f32[4,16,128]{2,1,0:T(8,128)S(1)}, u32[]{:S(2)}, u32[]{:S(2)}) %collective-permute-start.15) | collective-permute-done | bytes 32800 | tf_op jit(solution)/shard_map/ppermute | solution.py:313
  94.1 4.4 %collective-permute-start.18 = (f32[4,16,128]{2,1,0:T(8,128)S(1)}, f32[4,16,128]{2,1,0:T(8,128)S(1)}, u32[]{:S(2)}, u32[]{:S(2)}) collective-permute-start(f32[4,16,128]{2,1,0:T(8,128)S(1)} %pad_maximum_fusion.2), channel_id=1, source_target_pairs={{0,24},{2,26},{4,28},{6,30},{8,16},{10,18},{12,20},{14,22},{16,8},... | collective-permute-start | bytes 98312 | tf_op jit(solution)/shard_map/ppermute | solution.py:280
  98.5 0.0 collective-permute-start.17
  98.5 0.6 collective-permute-start.16
  99.1 2.4 %scaled_core.1 = f32[512,256]{1,0:T(8,128)} custom-call(f32[512,256]{1,0:T(8,128)} %get-tuple-element.11.refs_0_, f32[256,256]{1,0:T(8,128)} %inverse_factor.1.refs_1_.inverse_ref), custom_call_target="tpu_custom_call" | custom-call | tf_op jit(solution)/shard_map/scaled_core/pallas_call | solution.py:224
  101.5 0.0 collective-permute-done.18.s3
  101.5 1.8 %collective-permute-done.17.s2 = f32[4,16,128]{2,1,0:T(8,128)S(1)} collective-permute-done((f32[4,16,128]{2,1,0:T(8,128)S(1)}, f32[4,16,128]{2,1,0:T(8,128)S(1)}, u32[]{:S(2)}, u32[]{:S(2)}) %collective-permute-start.17) | collective-permute-done | bytes 32800 | tf_op jit(solution)/shard_map/ppermute | solution.py:280
  103.3 0.0 collective-permute-done.16.s1
  103.3 0.5 copy-done.13
  103.9 0.6 copy-done.14
  104.5 1.6 %arrange.1 = f32[16,8,256]{2,1,0:T(8,128)} custom-call(s32[6]{0:T(128)} %stack.36.ids_ref.refs_0_, f32[4,16,128]{2,1,0:T(8,128)} %copy-done.6, f32[4,16,128]{2,1,0:T(8,128)} %copy-done.7, f32[4,16,128]{2,1,0:T(8,128)} %copy-done.8, f32[4,16,128]{2,1,0:T(8,128)} %copy-done.9, f32[4,16,128]{2,1,0:T(8,128)} %copy-done.14, f32[4,16,128]{2,1,0:T(8,128)} %copy-done.13, ...), custom_call_target="tpu_custom_call" | custom-call | tf_op jit(solution)/shard_map/arrange/pallas_call | solution.py:267
  (32 shorter events, 0.1 us)
Async XLA Ops:
  6.0 10.0 %collective-permute-start = (f32[256,256]{1,0:T(8,128)}, f32[256,256]{1,0:T(8,128)S(1)}, u32[]{:S(2)}, u32[]{:S(2)}) collective-permute-start(f32[256,256]{1,0:T(8,128)} %sketch_band.2.own_a), channel_id=1, source_target_pairs={{0,1},{1,0},{2,3},{3,2},{4,5},{5,4},{6,7},{7,6},{8,9},{9,8},{10,11... | collective-permute-start | bytes 786440 | tf_op jit(solution)/shard_map/ppermute | solution.py:296
  12.9 8.2 %collective-permute-start.1 = (f32[256,256]{1,0:T(8,128)}, f32[256,256]{1,0:T(8,128)S(1)}, u32[]{:S(2)}, u32[]{:S(2)}) collective-permute-start(f32[256,256]{1,0:T(8,128)} %sketch_band.3.own_b), channel_id=1, source_target_pairs={{0,1},{1,0},{2,3},{3,2},{4,5},{5,4},{6,7},{7,6},{8,9},{9,8},{10,11... | collective-permute-start | bytes 786440 | tf_op jit(solution)/shard_map/ppermute | solution.py:296
  16.0 5.1 %copy-start.1 = (f32[256,256]{1,0:T(8,128)}, f32[256,256]{1,0:T(8,128)S(1)}, u32[]{:S(2)}) copy-start(f32[256,256]{1,0:T(8,128)S(1)} %collective-permute-done.got_a) | copy-start | bytes 786436
  21.1 0.7 copy-start.2
  29.5 8.5 %copy-start.15 = (f32[192,128]{1,0:T(8,128)S(1)}, f32[192,128]{1,0:T(8,128)}, u32[]{:S(2)}) copy-start(f32[192,128]{1,0:T(8,128)} %get-tuple-element.13) | copy-start | bytes 294916
  29.5 9.8 %copy-start.10 = (f32[192,128]{1,0:T(8,128)S(1)}, f32[192,128]{1,0:T(8,128)}, u32[]{:S(2)}) copy-start(f32[192,128]{1,0:T(8,128)} %get-tuple-element.12) | copy-start | bytes 294916
  29.5 5.3 %collective-permute-start.7 = (f32[2,4,256,128]{3,2,1,0:T(8,128)}, f32[2,4,256,128]{3,2,1,0:T(8,128)S(1)}, u32[]{:S(2)}, u32[]{:S(2)}) collective-permute-start(f32[2,4,256,128]{3,2,1,0:T(8,128)} %project.3), channel_id=1, source_target_pairs={{0,2},{2,0},{4,6},{6,4},{8,10},{10,8},{12,14},{14,12},{16,18},{18,... | collective-permute-start | bytes 3145736 | tf_op jit(solution)/shard_map/ppermute | solution.py:280
  36.2 24.0 %collective-permute-start.8 = (f32[4,256,128]{2,1,0:T(8,128)S(1)}, f32[4,256,128]{2,1,0:T(8,128)S(1)}, u32[]{:S(2)}, u32[]{:S(2)}) collective-permute-start(f32[4,256,128]{2,1,0:T(8,128)S(1)} %slice_bitcast_fusion), channel_id=1, source_target_pairs={{0,4},{2,6},{4,0},{6,2},{8,12},{10,14},{12,8},{14,10},{16,20},{18,... | collective-permute-start | bytes 1572872 | tf_op jit(solution)/shard_map/ppermute | solution.py:280
  38.0 1.3 %collective-permute-start.2 = (f32[192,128]{1,0:T(8,128)S(1)}, f32[192,128]{1,0:T(8,128)S(1)}, u32[]{:S(2)}, u32[]{:S(2)}) collective-permute-start(f32[192,128]{1,0:T(8,128)S(1)} %copy-done.15), channel_id=1, source_target_pairs={{0,2},{2,0},{4,6},{6,4},{8,10},{10,8},{12,14},{14,12},{16,18},{18,... | collective-permute-start | bytes 294920 | tf_op jit(solution)/shard_map/ppermute | solution.py:280
  39.3 13.3 %collective-permute-start.3 = (f32[192,128]{1,0:T(8,128)S(1)}, f32[192,128]{1,0:T(8,128)S(1)}, u32[]{:S(2)}, u32[]{:S(2)}) collective-permute-start(f32[192,128]{1,0:T(8,128)S(1)} %add.18), channel_id=1, source_target_pairs={{0,4},{2,6},{4,0},{6,2},{8,12},{10,14},{12,8},{14,10},{16,20},{18,... | collective-permute-start | bytes 294920 | tf_op jit(solution)/shard_map/ppermute | solution.py:280
  52.6 4.7 %collective-permute-start.4 = (f32[192,128]{1,0:T(8,128)S(1)}, f32[192,128]{1,0:T(8,128)S(1)}, u32[]{:S(2)}, u32[]{:S(2)}) collective-permute-start(f32[192,128]{1,0:T(8,128)S(1)} %add.19), channel_id=1, source_target_pairs={{0,8},{2,10},{4,12},{6,14},{8,0},{10,2},{12,4},{14,6},{16,24},{18,... | collective-permute-start | bytes 294920 | tf_op jit(solution)/shard_map/ppermute | solution.py:280
  57.3 10.4 %collective-permute-start.5 = (f32[192,128]{1,0:T(8,128)S(1)}, f32[192,128]{1,0:T(8,128)S(1)}, u32[]{:S(2)}, u32[]{:S(2)}) collective-permute-start(f32[192,128]{1,0:T(8,128)S(1)} %add.20), channel_id=1, source_target_pairs={{0,16},{2,18},{4,20},{6,22},{8,24},{10,26},{12,28},{14,30},{16,0},... | collective-permute-start | bytes 294920 | tf_op jit(solution)/shard_map/ppermute | solution.py:280
  60.9 19.6 %collective-permute-start.10 = (f32[256,128]{1,0:T(8,128)S(1)}, f32[256,128]{1,0:T(8,128)S(1)}, u32[]{:S(2)}, u32[]{:S(2)}) collective-permute-start(f32[256,128]{1,0:T(8,128)S(1)} %get-tuple-element.21), channel_id=1, source_target_pairs={{0,16},{2,18},{4,20},{6,22},{8,24},{10,26},{12,28},{14,30},{16,0},... | collective-permute-start | bytes 393224 | tf_op jit(solution)/shard_map/ppermute | solution.py:280
  61.1 19.5 %collective-permute-start.11 = (f32[256,128]{1,0:T(8,128)S(1)}, f32[256,128]{1,0:T(8,128)S(1)}, u32[]{:S(2)}, u32[]{:S(2)}) collective-permute-start(f32[256,128]{1,0:T(8,128)S(1)} %get-tuple-element.20), channel_id=1, source_target_pairs={{0,24},{2,26},{4,28},{6,30},{8,16},{10,18},{12,20},{14,22},{16,8},... | collective-permute-start | bytes 393224 | tf_op jit(solution)/shard_map/ppermute | solution.py:280
  64.9 15.7 %collective-permute-start.9 = (f32[256,128]{1,0:T(8,128)S(1)}, f32[256,128]{1,0:T(8,128)S(1)}, u32[]{:S(2)}, u32[]{:S(2)}) collective-permute-start(f32[256,128]{1,0:T(8,128)S(1)} %get-tuple-element.22), channel_id=1, source_target_pairs={{0,8},{2,10},{4,12},{6,14},{8,0},{10,2},{12,4},{14,6},{16,24},{18,... | collective-permute-start | bytes 393224 | tf_op jit(solution)/shard_map/ppermute | solution.py:280
  67.7 1.4 %copy-start = (f32[192,128]{1,0:T(8,128)}, f32[192,128]{1,0:T(8,128)S(1)}, u32[]{:S(2)}) copy-start(f32[192,128]{1,0:T(8,128)S(1)} %add.21.refs_1_) | copy-start | bytes 294916
  67.7 1.4 %collective-permute-start.6 = (f32[192,128]{1,0:T(8,128)S(1)}, f32[192,128]{1,0:T(8,128)S(1)}, u32[]{:S(2)}, u32[]{:S(2)}) collective-permute-start(f32[192,128]{1,0:T(8,128)S(1)} %add.21.refs_1_), channel_id=1, source_target_pairs={{0,2},{2,0},{4,6},{6,4},{8,10},{10,8},{12,14},{14,12},{16,18},{18,... | collective-permute-start | bytes 294920 | tf_op jit(solution)/shard_map/ppermute | solution.py:280
  69.1 0.7 copy-start.11
  80.5 0.7 copy-start.3
  80.5 0.7 copy-start.4
  80.6 0.7 copy-start.5
  83.5 5.8 %collective-permute-start.12 = (f32[4,16,128]{2,1,0:T(8,128)}, f32[4,16,128]{2,1,0:T(8,128)S(1)}, u32[]{:S(2)}, u32[]{:S(2)}) collective-permute-start(f32[4,16,128]{2,1,0:T(8,128)} %get-tuple-element.16), channel_id=1, source_target_pairs={{0,0},{1,1},{2,3},{3,2},{4,4},{5,5},{6,7},{7,6},{8,8},{9,9},{10,11... | collective-permute-start | bytes 98312 | tf_op jit(solution)/shard_map/ppermute | solution.py:313
  84.9 4.9 %collective-permute-start.13 = (f32[4,16,128]{2,1,0:T(8,128)}, f32[4,16,128]{2,1,0:T(8,128)S(1)}, u32[]{:S(2)}, u32[]{:S(2)}) collective-permute-start(f32[4,16,128]{2,1,0:T(8,128)} %get-tuple-element.17), channel_id=1, source_target_pairs={{0,2},{1,3},{2,1},{3,0},{4,6},{5,7},{6,5},{7,4},{8,10},{9,11},{10,... | collective-permute-start | bytes 98312 | tf_op jit(solution)/shard_map/ppermute | solution.py:313
  87.8 4.1 %collective-permute-start.14 = (f32[4,16,128]{2,1,0:T(8,128)}, f32[4,16,128]{2,1,0:T(8,128)S(1)}, u32[]{:S(2)}, u32[]{:S(2)}) collective-permute-start(f32[4,16,128]{2,1,0:T(8,128)} %get-tuple-element.18), channel_id=1, source_target_pairs={{0,4},{1,5},{2,7},{3,6},{4,0},{5,1},{6,3},{7,2},{8,12},{9,13},{10,... | collective-permute-start | bytes 98312 | tf_op jit(solution)/shard_map/ppermute | solution.py:313
  89.3 4.8 %collective-permute-start.15 = (f32[4,16,128]{2,1,0:T(8,128)}, f32[4,16,128]{2,1,0:T(8,128)S(1)}, u32[]{:S(2)}, u32[]{:S(2)}) collective-permute-start(f32[4,16,128]{2,1,0:T(8,128)} %get-tuple-element.19), channel_id=1, source_target_pairs={{0,6},{1,7},{2,5},{3,4},{4,2},{5,3},{6,1},{7,0},{8,14},{9,15},{10,... | collective-permute-start | bytes 98312 | tf_op jit(solution)/shard_map/ppermute | solution.py:313
  89.3 14.0 %copy-start.6 = (f32[4,16,128]{2,1,0:T(8,128)}, f32[4,16,128]{2,1,0:T(8,128)S(1)}, u32[]{:S(2)}) copy-start(f32[4,16,128]{2,1,0:T(8,128)S(1)} %collective-permute-done.12.r0) | copy-start | bytes 98308
  89.8 13.5 %copy-start.7 = (f32[4,16,128]{2,1,0:T(8,128)}, f32[4,16,128]{2,1,0:T(8,128)S(1)}, u32[]{:S(2)}) copy-start(f32[4,16,128]{2,1,0:T(8,128)S(1)} %collective-permute-done.13.r1) | copy-start | bytes 98308
  91.9 11.4 %copy-start.8 = (f32[4,16,128]{2,1,0:T(8,128)}, f32[4,16,128]{2,1,0:T(8,128)S(1)}, u32[]{:S(2)}) copy-start(f32[4,16,128]{2,1,0:T(8,128)S(1)} %collective-permute-done.14.r2) | copy-start | bytes 98308
  94.1 9.3 %copy-start.9 = (f32[4,16,128]{2,1,0:T(8,128)}, f32[4,16,128]{2,1,0:T(8,128)S(1)}, u32[]{:S(2)}) copy-start(f32[4,16,128]{2,1,0:T(8,128)S(1)} %collective-permute-done.15.r3) | copy-start | bytes 98308
  94.1 7.4 %collective-permute-start.18 = (f32[4,16,128]{2,1,0:T(8,128)S(1)}, f32[4,16,128]{2,1,0:T(8,128)S(1)}, u32[]{:S(2)}, u32[]{:S(2)}) collective-permute-start(f32[4,16,128]{2,1,0:T(8,128)S(1)} %pad_maximum_fusion.2), channel_id=1, source_target_pairs={{0,24},{2,26},{4,28},{6,30},{8,16},{10,18},{12,20},{14,22},{16,8},... | collective-permute-start | bytes 98312 | tf_op jit(solution)/shard_map/ppermute | solution.py:280
  98.5 4.8 %collective-permute-start.17 = (f32[4,16,128]{2,1,0:T(8,128)S(1)}, f32[4,16,128]{2,1,0:T(8,128)S(1)}, u32[]{:S(2)}, u32[]{:S(2)}) collective-permute-start(f32[4,16,128]{2,1,0:T(8,128)S(1)} %pad_maximum_fusion.1), channel_id=1, source_target_pairs={{0,16},{2,18},{4,20},{6,22},{8,24},{10,26},{12,28},{14,30},{16,0},... | collective-permute-start | bytes 98312 | tf_op jit(solution)/shard_map/ppermute | solution.py:280
  98.5 4.8 %collective-permute-start.16 = (f32[4,16,128]{2,1,0:T(8,128)S(1)}, f32[4,16,128]{2,1,0:T(8,128)S(1)}, u32[]{:S(2)}, u32[]{:S(2)}) collective-permute-start(f32[4,16,128]{2,1,0:T(8,128)S(1)} %pad_maximum_fusion), channel_id=1, source_target_pairs={{0,8},{2,10},{4,12},{6,14},{8,0},{10,2},{12,4},{14,6},{16,24},{18,... | collective-permute-start | bytes 98312 | tf_op jit(solution)/shard_map/ppermute | solution.py:280
  101.5 1.8 %copy-start.12 = (f32[4,16,128]{2,1,0:T(8,128)}, f32[4,16,128]{2,1,0:T(8,128)S(1)}, u32[]{:S(2)}) copy-start(f32[4,16,128]{2,1,0:T(8,128)S(1)} %collective-permute-done.18.s3) | copy-start | bytes 98308
  103.3 0.6 copy-start.13
  103.9 0.6 copy-start.14

commit v2 on v1

v2 whole, which is shorter than its diff:
```python
import math

import jax
import jax.numpy as jnp
from jax import lax
from jax.experimental import pallas as pl
from jax.experimental.pallas import tpu as pltpu
from jax.sharding import PartitionSpec as P

RANK = 256
BLK = 128
MODE = 8
PANEL = 16
HIGHEST = lax.Precision.HIGHEST
F32 = jnp.float32
BF16 = jnp.bfloat16
VMEM = pl.BlockSpec(memory_space=pltpu.VMEM)
HBM = pl.BlockSpec(memory_space=pltpu.HBM)


def hadamard_table(table_size):
    row_index = lax.broadcasted_iota(jnp.int32, (table_size, table_size), 0)
    col_index = lax.broadcasted_iota(jnp.int32, (table_size, table_size), 1)
    both = row_index & col_index
    parity = jnp.zeros((table_size, table_size), jnp.int32)
    for bit_level in range(table_size.bit_length() - 1):
        parity = parity ^ (both >> bit_level)
    return (1 - 2 * (parity & 1)).astype(F32)


def on_chip(*dims, dtype=F32):
    return pltpu.VMEM(dims, dtype)


def held(*values):
    return [pltpu.with_memory_space_constraint(value, pltpu.VMEM) for value in values]


LIMIT = pltpu.CompilerParams(vmem_limit_bytes=8 << 20)


def cost(flops, size):
    return pl.CostEstimate(flops=flops, bytes_accessed=size, transcendentals=0)


def split(value):
    high = value.astype(BF16)
    return high, (value - high.astype(F32)).astype(BF16)


def dot(left, right):
    return jnp.dot(left, right, preferred_element_type=F32)


def sketch_kernel(first_row, pattern_ref, whole_ref, sign_ref, out_ref, band_ref, sems, signs, pattern):
    steps = sems.shape[0] - 2
    rows = band_ref.shape[0]
    step = rows // steps
    copies = [
        pltpu.make_async_copy(pattern_ref, pattern, sems.at[steps]),
        pltpu.make_async_copy(sign_ref, signs, sems.at[steps + 1]),
    ]
    for i in range(steps):
        here = pl.ds(first_row + i * step, step)
        copies.append(pltpu.make_async_copy(whole_ref.at[here], band_ref.at[pl.ds(i * step, step)], sems.at[i]))
    for copy in copies:
        copy.start()
    table = hadamard_table(BLK).astype(BF16)
    copies[0].wait()
    copies[1].wait()
    col_blocks = signs.shape[0]
    row_blocks = band_ref.shape[1] // BLK
    factors = []
    for k in range(col_blocks):
        signed = (2 * signs[k : k + 1, :] - 1).astype(F32)
        factors.append([signed[:, j * BLK : (j + 1) * BLK] * pattern[k, j].astype(F32) for j in range(row_blocks)])
    for i in range(steps):
        copies[2 + i].wait()
        here = slice(i * step, (i + 1) * step)
        for k in range(col_blocks):
            total = jnp.zeros((step, BLK), F32)
            for j in range(row_blocks):
                total = total + band_ref[here, j * BLK : (j + 1) * BLK] * factors[k][j]
            high, rest = split(total)
            low = (total - high.astype(F32) - rest.astype(F32)).astype(BF16)
            out_ref[here, k * BLK : (k + 1) * BLK] = dot(high, table) + dot(rest, table) + dot(low, table)


def sketch_band(unfolding, pattern_rows, sign_rows, band, bands):
    rows, cols = unfolding.shape
    rows //= bands

    def body(*refs):
        sketch_kernel(band * rows, *refs)

    return pl.pallas_call(
        body,
        in_specs=[HBM] * 3,
        out_specs=[VMEM] * 2,
        out_shape=[on_chip(rows, RANK), on_chip(rows, cols)],
        scratch_shapes=[
            pltpu.SemaphoreType.DMA((6,)),
            pltpu.VMEM(sign_rows.shape, jnp.int32),
            pltpu.SMEM(pattern_rows.shape, jnp.int32),
        ],
        cost_estimate=cost(rows * cols * 4, rows * cols * 4),
        compiler_params=LIMIT,
        name="sketch_band",
    )(*[pltpu.with_memory_space_constraint(x, pltpu.HBM) for x in (pattern_rows, unfolding, sign_rows)])


def gram_kernel(own_ref, got_ref, before_ref, sketch_ref, high_ref, low_ref, packed_ref, keep_ref, send_ref):
    sketch = own_ref[...] + got_ref[...]
    sketch_ref[...] = sketch
    turned = sketch.T
    high, low = split(turned)
    high_ref[...] = high
    low_ref[...] = low
    top = jnp.dot(turned[:BLK], sketch, precision=HIGHEST)
    low_corner = jnp.dot(turned[BLK:], sketch[:, BLK:], precision=HIGHEST)
    parts = [top[:, :BLK], top[:, BLK:], low_corner]
    for i, part in enumerate(parts):
        here = slice(i * BLK, (i + 1) * BLK)
        packed_ref[here] = part if before_ref is None else part + before_ref[here]
    if keep_ref is not None:
        half = keep_ref.shape[0]
        core = lax.axis_index("rows") & 1
        keep_ref[...] = packed_ref[pl.ds(pl.multiple_of(core * half, half), half), :]
        send_ref[...] = packed_ref[pl.ds(pl.multiple_of((1 - core) * half, half), half), :]


def gram_band(own, got, before):
    rows = own.shape[0]
    first = before is None
    operands = held(own, got) if first else held(own, got, before)
    packed = (3 * BLK, BLK)
    half = (3 * BLK // 2, BLK)

    def body(*refs):
        if first:
            gram_kernel(*refs[:2], None, *refs[2:], None, None)
        else:
            gram_kernel(*refs[:6], refs[8], *refs[6:8])

    return pl.pallas_call(
        body,
        in_specs=[VMEM] * len(operands),
        out_specs=[VMEM] * (4 if first else 5),
        out_shape=[
            on_chip(rows, RANK),
            on_chip(RANK, rows, dtype=BF16),
            on_chip(RANK, rows, dtype=BF16),
            *([on_chip(*packed)] if first else [on_chip(*half)] * 2),
        ],
        scratch_shapes=[] if first else [pltpu.VMEM(packed, F32)],
        cost_estimate=cost(rows * RANK * RANK * 12, rows * RANK * 8),
        compiler_params=LIMIT,
        name="gram_band",
    )(*operands)


def project_kernel(high_ref, low_ref, band_ref, before_ref, send_ref, keep_ref):
    row = lax.axis_index("rows")
    side_here = (row & 1) ^ lax.axis_index("cols")
    flip = (row >> 1) & 1
    for side, out_ref in ((1, send_ref), (0, keep_ref)):
        for t in range(4):
            block = (t ^ (row >> 2)) * 2 + (side_here ^ side)
            a_high, a_low = split(band_ref[:, pl.ds(pl.multiple_of(block * 2 * BLK, 2 * BLK), 2 * BLK)])
            total = dot(high_ref[...], a_high) + dot(high_ref[...], a_low) + dot(low_ref[...], a_high)
            for h in range(2):
                part = total[:, h * BLK : (h + 1) * BLK]
                place = flip if h == 0 else 1 - flip
                if before_ref is not None:
                    part = part + before_ref[1 - side][place, t]
                out_ref[place, t] = part


def project_band(high, low, band, before, after):
    rows, cols = band.shape
    operands = held(high, low, band, *(before or ()), *after)

    def body(*refs):
        project_kernel(*refs[:3], refs[3:5] if before else None, *refs[-2:])

    return pl.pallas_call(
        body,
        in_specs=[VMEM] * len(operands),
        out_specs=[VMEM] * 2,
        out_shape=[on_chip(2, 4, RANK, BLK)] * 2,
        cost_estimate=cost(rows * cols * RANK * 6, rows * cols * 4),
        compiler_params=LIMIT,
        name="project_band",
    )(*operands)


def add_parts_kernel(left_ref, right_ref, *outs):
    count = left_ref.shape[0] // len(outs)
    for i, out in enumerate(outs):
        if len(out.shape) < len(left_ref.shape):
            out[...] = left_ref[i] + right_ref[i]
        else:
            out[...] = left_ref[i * count : (i + 1) * count] + right_ref[i * count : (i + 1) * count]


def add_parts(left, right, parts, after=()):
    dims = left.shape
    out = dims[1:] if dims[0] == parts else (dims[0] // parts, *dims[1:])
    size = math.prod(dims)

    def body(*refs):
        add_parts_kernel(*refs[:2], *refs[-parts:])

    return pl.pallas_call(
        body,
        in_specs=[VMEM] * (2 + len(after)),
        out_specs=[VMEM] * parts,
        out_shape=[on_chip(*out)] * parts,
        cost_estimate=cost(size, size),
        compiler_params=LIMIT,
        name="add_parts",
    )(*held(left, right, *after))


def factor_panel(parts, start):
    diagonal = parts[0][:, start : start + PANEL]
    columns = [jnp.broadcast_to(diagonal[:, k : k + 1], (PANEL, BLK)) for k in range(PANEL)]
    rows = lax.broadcasted_iota(jnp.int32, (PANEL, BLK), 0)
    pivots = jnp.ones((PANEL, BLK), F32)
    for j in range(PANEL):
        pivot = jnp.broadcast_to(columns[j][j : j + 1, :], (PANEL, BLK))
        multiplier = jnp.where(rows > j, columns[j] / pivot, 0.0)
        for k in range(j + 1, PANEL):
            columns[k] = columns[k] - multiplier * columns[k][j : j + 1, :]
        parts = [part - multiplier * part[j : j + 1, :] for part in parts]
        pivots = jnp.where(rows == j, pivot, pivots)
    scale = lax.rsqrt(pivots)
    return [part * scale for part in parts]


def factor_block(work):
    for panel in range(BLK // PANEL):
        start = panel * PANEL
        stop = start + PANEL
        parts = [work[start:stop, c * BLK : (c + 1) * BLK] for c in range(3)]
        parts = factor_panel(parts, start)
        for c in range(3):
            work[start:stop, c * BLK : (c + 1) * BLK] = parts[c]
        if stop < BLK:
            left = parts[0].T[stop:]
            work[stop:, :] = work[stop:, :] - jnp.dot(left, jnp.concatenate(parts, 1), precision=HIGHEST)


def factor_kernel(total_rows, own_ref, got_ref, out_ref, work, packed):
    half = own_ref.shape[0]
    core = lax.axis_index("rows") & 1
    packed[pl.ds(pl.multiple_of(core * half, half), half), :] = own_ref[...]
    packed[pl.ds(pl.multiple_of((1 - core) * half, half), half), :] = got_ref[...]
    row = lax.broadcasted_iota(jnp.int32, (BLK, BLK), 0)
    col = lax.broadcasted_iota(jnp.int32, (BLK, BLK), 1)
    eye = (row == col).astype(F32)
    work[:, :BLK] = packed[:BLK] + float(total_rows) * eye
    work[:, BLK : 2 * BLK] = packed[BLK : 2 * BLK]
    work[:, 2 * BLK :] = eye
    factor_block(work)
    out_ref[:BLK, :BLK] = work[:, 2 * BLK :]
    out_ref[:BLK, BLK:] = jnp.zeros((BLK, BLK), F32)
    above = work[:, BLK : 2 * BLK]
    product = jnp.dot(above.T, work[:, BLK:], precision=HIGHEST)
    work[:, :BLK] = packed[2 * BLK :] + float(total_rows) * eye - product[:, :BLK]
    work[:, BLK : 2 * BLK] = -product[:, BLK:]
    work[:, 2 * BLK :] = eye
    factor_block(work)
    out_ref[BLK:, :] = work[:, BLK:]


def inverse_factor(own, got, total_rows):
    def body(*refs):
        factor_kernel(total_rows, *refs)

    return pl.pallas_call(
        body,
        in_specs=[VMEM, VMEM],
        out_specs=VMEM,
        out_shape=on_chip(RANK, RANK),
        scratch_shapes=[pltpu.VMEM((BLK, 3 * BLK), F32), pltpu.VMEM((3 * BLK, BLK), F32)],
        cost_estimate=cost(10_000_000_000, RANK * RANK * 8),
        compiler_params=LIMIT,
        name="inverse_factor",
    )(*held(own, got))


def core_kernel(scale, first_ref, second_ref, inverse_ref, out_ref):
    t_high, t_low = split(inverse_ref[...].T)
    band = first_ref.shape[0]
    for i, ref in enumerate((first_ref, second_ref)):
        s_high, s_low = split(ref[...])
        total = dot(s_high, t_high) + dot(s_high, t_low) + dot(s_low, t_high)
        out_ref[i * band : (i + 1) * band] = total * scale


def scaled_core(sketches, inverse, scale):
    rows = 2 * sketches[0].shape[0]

    def body(*refs):
        core_kernel(scale, *refs)

    return pl.pallas_call(
        body,
        in_specs=[VMEM] * 3,
        out_specs=VMEM,
        out_shape=jax.ShapeDtypeStruct((rows, RANK), F32),
        cost_estimate=cost(rows * RANK * RANK * 6, rows * RANK * 8),
        compiler_params=LIMIT,
        name="scaled_core",
    )(*held(*sketches, inverse))


def remainder_kernel(inverse_ref, p0, p1, p2, p3, o0, o1, o2, o3, work):
    work[...] = jnp.dot(inverse_ref[...], (p0[...] + p1[...]) + (p2[...] + p3[...]), precision=HIGHEST)
    device = lax.axis_index("rows")
    for m, out in enumerate((o0, o1, o2, o3)):
        for t in range(4):
            rank_block = (4 * t + m) ^ device
            out[t] = work[pl.ds(pl.multiple_of(rank_block * 16, 16), 16), :]


def remainder_pieces(inverse, pieces):
    return pl.pallas_call(
        remainder_kernel,
        in_specs=[VMEM] * 5,
        out_specs=[VMEM] * 4,
        out_shape=[on_chip(4, 16, BLK)] * 4,
        scratch_shapes=[pltpu.VMEM((RANK, BLK), F32)],
        cost_estimate=cost(RANK * RANK * BLK * 12, RANK * BLK * 8),
        compiler_params=LIMIT,
        name="remainder_pieces",
    )(*held(inverse, *pieces))


def collect_kernel(r0, r1, r2, r3, o1, o2, o3):
    for t, out in ((1, o1), (2, o2), (3, o3)):
        for m, piece in enumerate((r0, r1, r2, r3)):
            out[m] = piece[t]


def collect(firsts):
    return pl.pallas_call(
        collect_kernel,
        in_specs=[VMEM] * 4,
        out_specs=[VMEM] * 3,
        out_shape=[on_chip(4, 16, BLK)] * 3,
        cost_estimate=cost(0, 16 * BLK * 64),
        compiler_params=LIMIT,
        name="collect",
    )(*held(*firsts))


def arrange_kernel(r0, r1, r2, r3, s1, s2, s3, out_ref, work):
    row = lax.axis_index("rows")
    core, right, deep, y = row & 1, (row >> 1) & 1, row >> 2, lax.axis_index("cols")
    firsts = (r0, r1, r2, r3)
    later = (None, s1, s2, s3)
    for t in range(4):
        for m in range(4):
            mode = (y ^ core ^ (m & 1)) * 4 + (deep ^ t)
            work[mode, right ^ (m >> 1)] = firsts[m][0] if t == 0 else later[t][m]
    for mode in range(MODE):
        for c in range(2):
            out_ref[:, mode, c * BLK : (c + 1) * BLK] = work[mode, c]


def arrange(firsts, later):
    out = pl.pallas_call(
        arrange_kernel,
        in_specs=[VMEM] * 7,
        out_specs=VMEM,
        out_shape=jax.ShapeDtypeStruct((16, MODE, 2 * BLK), F32),
        scratch_shapes=[pltpu.VMEM((MODE, 2, 16, BLK), F32)],
        cost_estimate=cost(0, 16 * BLK * 64),
        compiler_params=LIMIT,
        name="arrange",
    )(*held(*firsts, *later))
    return out.reshape(16 * MODE, 2 * BLK)


def rows_permute(value, mask):
    size = lax.axis_size("rows")
    return lax.ppermute(value, "rows", [(i, i ^ mask) for i in range(size)])


def local(unfolding, pattern, sign_bits):
    total_rows = unfolding.shape[0] * lax.axis_size("rows")
    own, got, bands = [], [], []
    for band in range(2):
        part, rows_here = sketch_band(unfolding, pattern.T, sign_bits.T, band, 2)
        own.append(part)
        bands.append(rows_here)
        got.append(lax.ppermute(part, "cols", [(0, 1), (1, 0)]))
    first, high, low, packed = gram_band(own[0], got[0], None)
    sides = project_band(high, low, bands[0], None, ())
    second, high, low, gram_keep, gram_send = gram_band(own[1], got[1], packed)
    gram, = add_parts(gram_keep, rows_permute(gram_send, 1), 1)
    give, keep = project_band(high, low, bands[1], sides, (gram,))
    gram, = add_parts(gram, rows_permute(gram, 4), 1)
    keep, give = add_parts(keep, rows_permute(give, 1), 2, (gram,))
    for mask in (8, 2):
        gram, = add_parts(gram, rows_permute(gram, mask), 1)
    gram_other = rows_permute(gram, 1)
    pieces = add_parts(keep, rows_permute(give, 2), 4)
    pieces = [pieces[0]] + [rows_permute(pieces[t], 4 * t) for t in (1, 2, 3)]
    inverse = inverse_factor(gram, gram_other, total_rows)
    parts = remainder_pieces(inverse, pieces)
    core_scaled = scaled_core((first, second), inverse, math.sqrt(total_rows))
    firsts = []
    for m in range(4):
        pairs = [(2 * i + j, 2 * (i ^ m) + (j ^ (i & 1))) for i in range(16) for j in range(2)]
        firsts.append(lax.ppermute(parts[m], ("rows", "cols"), pairs))
    later = [rows_permute(part, 4 * t) for t, part in zip((1, 2, 3), collect(firsts))]
    return core_scaled, arrange(firsts, later)


def sketch_matrix(pattern, sign_bits, block_size):
    blocks = sign_bits.shape[1]
    rows_here = sign_bits.shape[0]
    factor = jnp.repeat(pattern, block_size, axis=0) * (2 * sign_bits - 1)
    tiled_table = jnp.tile(hadamard_table(block_size), (rows_here // block_size, 1))
    expanded = factor.astype(F32)[:, :, None] * tiled_table[:, None, :]
    return expanded.reshape(rows_here, blocks * block_size)


def inner_rows(left_side, right_side):
    return lax.dot_general(left_side, right_side, (((0,), (0,)), ((), ())), precision=HIGHEST)


def local_any(unfolding, pattern, sign_bits):
    sketch_map = sketch_matrix(pattern, sign_bits, BLK)
    row_devices = lax.axis_size("rows")
    col_devices = lax.axis_size("cols")
    total_rows = unfolding.shape[0] * row_devices
    sketch = lax.psum(jnp.dot(unfolding, sketch_map, precision=HIGHEST), "cols")
    gram_matrix = lax.psum(inner_rows(sketch, sketch), "rows")
    gram_matrix = gram_matrix + float(total_rows) * jnp.eye(RANK, dtype=F32)
    lower_factor = jnp.linalg.cholesky(gram_matrix)
    basis_rows = lax.linalg.triangular_solve(lower_factor, sketch, left_side=False, lower=True, transpose_a=True)
    mode_local = MODE // col_devices
    rest_cols = unfolding.shape[1] // mode_local
    rank_share = RANK // row_devices
    reduced = lax.psum_scatter(inner_rows(basis_rows, unfolding), "rows", scatter_dimension=0, tiled=True)
    grouped = reduced.reshape(rank_share, mode_local, rest_cols)
    regrouped = lax.all_to_all(grouped, "cols", split_axis=2, concat_axis=1, tiled=True)
    return basis_rows * math.sqrt(total_rows), regrouped.reshape(rank_share * MODE, regrouped.shape[2])


def solution(mesh):
    in_specs = (P("rows", "cols"), P("cols", None), P("cols", None))
    out_specs = (P("rows", None), P("rows", "cols"))
    body = local if (mesh.shape["rows"], mesh.shape["cols"]) == (16, 2) else local_any
    return jax.shard_map(body, mesh=mesh, in_specs=in_specs, out_specs=out_specs, check_vma=False)
```

time: 107 us -> 76.3 us (0.71)
  Pallas kernels: 38 us -> 18.9 us
  local copies, waits for them, and re-layouts: 5.98 us -> 0 us
  waiting for transfers between devices: 35 us -> 31.4 us
  other arithmetic: 1.49 us -> 0 us
    pallas_call x9 -> x17, Pallas kernels: 38 us -> 18.9 us  [the longest x1 9.14 us: inverse_factor(): pl.pallas_call(body, in_specs=[VMEM, VMEM], out_specs=VMEM, out_shape=on_...]
    ppermute x13, waiting for transfers between devices: 22.8 us -> 17.5 us  [rows_permute(): return lax.ppermute(value, 'rows', [(i, i ^ mask) for i in range(size)])]
    unnamed x33 -> x0, local copies, waits for them, and re-layouts: 4.61 us -> none
    ppermute x2, waiting for transfers between devices: 7.52 us -> 9.32 us  [local(): got.append(lax.ppermute(part, 'cols', [(0, 1), (1, 0)]))]
    ppermute x13, starting transfers between devices: 16 us -> 17.6 us  [rows_permute(): return lax.ppermute(value, 'rows', [(i, i ^ mask) for i in range(size)])]
    ppermute x4, starting transfers between devices: 5.81 us -> 4.29 us  [local(): firsts.append(lax.ppermute(parts[m], ('rows', 'cols'), pairs))]
    add x6 -> x0, other arithmetic: 1.47 us -> none  [the longest x1 1.33 us: local(): summed = keep + rows_permute(give, 1)]
  transfers between devices with their start and end apart: 19 -> 19, of which waited for: 11 -> 12; matrix products, arithmetic and copies ran while one was open for 1% -> 0% of each run, Pallas kernels for 21% -> 18%
where the time goes in v2:
time: 76.3 us; the launch traced here: 76.1 us
  waiting for transfers between devices  31.4 us (41%)
  starting transfers between devices  25.1 us (33%)
  Pallas kernels  18.9 us (25%)
  between operations  0.78 us (1%)
    ppermute x13, starting transfers between devices, rows_permute(): return lax.ppermute(value, 'rows', [(i, i ^ mask) for i in range(size)])  17.6 us
    ppermute x13, waiting for transfers between devices, rows_permute(): return lax.ppermute(value, 'rows', [(i, i ^ mask) for i in range(size)])  17.5 us
    ppermute x2, waiting for transfers between devices, local(): got.append(lax.ppermute(part, 'cols', [(0, 1), (1, 0)]))  9.32 us
    pallas_call x1, Pallas kernels, inverse_factor(): pl.pallas_call(body, in_specs=[VMEM, VMEM], out_specs=VMEM, out_shape=on_...  9.14 us
    ppermute x4, waiting for transfers between devices, local(): firsts.append(lax.ppermute(parts[m], ('rows', 'cols'), pairs))  4.56 us
    ppermute x4, starting transfers between devices, local(): firsts.append(lax.ppermute(parts[m], ('rows', 'cols'), pairs))  4.29 us
    pallas_call x2, Pallas kernels, sketch_band(): pl.pallas_call(body, in_specs=[HBM] * 3, out_specs=[VMEM] * 2, out_shape=...  4.13 us
    ppermute x2, starting transfers between devices, local(): got.append(lax.ppermute(part, 'cols', [(0, 1), (1, 0)]))  3.12 us
  transfers between devices with their start and end apart: 19, of which 12 were waited for; matrix products, arithmetic and copies ran while one was open for 0% of the time, Pallas kernels for 18%

profile of v2, /device:TPU:0, one launch (start us, length us, event | category | flops | bytes accessed | tf_op | source)
XLA Modules:
  0.0 76.1 jit_solution(4403019782283124157)
XLA Ops:
  0.6 2.1 %sketch_band.2 = (f32[256,256]{1,0:T(8,128)S(1)}, f32[256,2048]{1,0:T(8,128)S(1)}) custom-call(s32[2,16]{1,0:T(2,128)} %bitcast.6, f32[512,2048]{1,0:T(8,128)} %refs_1_.3, s32[2,2048]{1,0:T(2,128)} %bitcast.4), custom_call_target="tpu_custom_call" | custom-call | flops 2097152 | bytes 2097152 | tf_op jit(solution)/shard_map/sketch_band/pallas_call | solution.py:96
  2.7 3.0 %collective-permute-start = (f32[256,256]{1,0:T(8,128)S(1)}, f32[256,256]{1,0:T(8,128)S(1)}, u32[]{:S(2)}, u32[]{:S(2)}) collective-permute-start(f32[256,256]{1,0:T(8,128)S(1)} %get-tuple-element.32.refs_0_), channel_id=1, source_target_pairs={{0,1},{1,0},{2,3},{3,2},{4,5},{5,4},{6,7},{7,6},{8,9},{9,8},{10,11... | collective-permute-start | bytes 786440 | tf_op jit(solution)/shard_map/ppermute | solution.py:399
  5.7 2.1 %sketch_band.3 = (f32[256,256]{1,0:T(8,128)S(1)}, f32[256,2048]{1,0:T(8,128)S(1)}) custom-call(s32[2,16]{1,0:T(2,128)} %bitcast.7, f32[512,2048]{1,0:T(8,128)} %refs_1_.3, s32[2,2048]{1,0:T(2,128)} %bitcast.5), custom_call_target="tpu_custom_call" | custom-call | flops 2097152 | bytes 2097152 | tf_op jit(solution)/shard_map/sketch_band/pallas_call | solution.py:96
  7.8 0.1 collective-permute-start.1
  7.9 5.0 %collective-permute-done.refs_1_ = f32[256,256]{1,0:T(8,128)S(1)} collective-permute-done((f32[256,256]{1,0:T(8,128)S(1)}, f32[256,256]{1,0:T(8,128)S(1)}, u32[]{:S(2)}, u32[]{:S(2)}) %collective-permute-start) | collective-permute-done | bytes 262176 | tf_op jit(solution)/shard_map/ppermute | solution.py:399
  12.9 0.4 gram_band.2
  13.3 4.3 %collective-permute-done.1.refs_1_ = f32[256,256]{1,0:T(8,128)S(1)} collective-permute-done((f32[256,256]{1,0:T(8,128)S(1)}, f32[256,256]{1,0:T(8,128)S(1)}, u32[]{:S(2)}, u32[]{:S(2)}) %collective-permute-start.1) | collective-permute-done | bytes 262176 | tf_op jit(solution)/shard_map/ppermute | solution.py:399
  17.7 0.5 gram_band.3
  18.1 0.1 collective-permute-start.2
  18.2 1.0 %project_band.2 = (f32[2,4,256,128]{3,2,1,0:T(8,128)S(1)}, f32[2,4,256,128]{3,2,1,0:T(8,128)S(1)}) custom-call(bf16[256,256]{1,0:T(8,128)(2,1)S(1)} %get-tuple-element.42.refs_0_, bf16[256,256]{1,0:T(8,128)(2,1)S(1)} %get-tuple-element.43.refs_1_, f32[256,2048]{1,0:T(8,128)S(1)} %get-tuple-element.44.refs_2_), custom_call_target="tpu_custom_call" | custom-call | flops 805306368 | bytes 2097152 | tf_op jit(solution)/shard_map/project_band/pallas_call | solution.py:186
  19.3 0.3 collective-permute-done.2.refs_1_
  19.5 1.0 %project_band.3 = (f32[2,4,256,128]{3,2,1,0:T(8,128)S(1)}, f32[2,4,256,128]{3,2,1,0:T(8,128)S(1)}) custom-call(bf16[256,256]{1,0:T(8,128)(2,1)S(1)} %get-tuple-element.39.refs_0_, bf16[256,256]{1,0:T(8,128)(2,1)S(1)} %get-tuple-element.40.refs_1_, f32[256,2048]{1,0:T(8,128)S(1)} %get-tuple-element.41.refs_2_, ...), custom_call_target="tpu_custom_call" | custom-call | flops 805306368 | bytes 2097152 | tf_op jit(solution)/shard_map/project_band/pallas_call | solution.py:186
  20.6 0.3 collective-permute-start.7
  20.9 1.8 %collective-permute-start.3 = (f32[192,128]{1,0:T(8,128)S(1)}, f32[192,128]{1,0:T(8,128)S(1)}, u32[]{:S(2)}, u32[]{:S(2)}) collective-permute-start(f32[192,128]{1,0:T(8,128)S(1)} %add_parts.6.refs_0_.refs_5_), channel_id=1, source_target_pairs={{0,8},{2,10},{4,12},{6,14},{8,0},{10,2},{12,4},{14,6},{16,24},{18,... | collective-permute-start | bytes 294920 | tf_op jit(solution)/shard_map/ppermute | solution.py:389
  22.7 3.2 %collective-permute-done.3.refs_1_ = f32[192,128]{1,0:T(8,128)S(1)} collective-permute-done((f32[192,128]{1,0:T(8,128)S(1)}, f32[192,128]{1,0:T(8,128)S(1)}, u32[]{:S(2)}, u32[]{:S(2)}) %collective-permute-start.3) | collective-permute-done | bytes 98336 | tf_op jit(solution)/shard_map/ppermute | solution.py:389
  25.9 0.0 collective-permute-done.7.refs_1_
  25.9 0.1 add_parts.10
  26.0 1.7 %collective-permute-start.8 = (f32[4,256,128]{2,1,0:T(8,128)S(1)}, f32[4,256,128]{2,1,0:T(8,128)S(1)}, u32[]{:S(2)}, u32[]{:S(2)}) collective-permute-start(f32[4,256,128]{2,1,0:T(8,128)S(1)} %get-tuple-element.50), channel_id=1, source_target_pairs={{0,4},{2,6},{4,0},{6,2},{8,12},{10,14},{12,8},{14,10},{16,20},{18,... | collective-permute-start | bytes 1572872 | tf_op jit(solution)/shard_map/ppermute | solution.py:389
  27.8 2.6 %collective-permute-start.4 = (f32[192,128]{1,0:T(8,128)S(1)}, f32[192,128]{1,0:T(8,128)S(1)}, u32[]{:S(2)}, u32[]{:S(2)}) collective-permute-start(f32[192,128]{1,0:T(8,128)S(1)} %add_parts.7.refs_0_.refs_2_), channel_id=1, source_target_pairs={{0,16},{2,18},{4,20},{6,22},{8,24},{10,26},{12,28},{14,30},{16,0},... | collective-permute-start | bytes 294920 | tf_op jit(solution)/shard_map/ppermute | solution.py:389
  30.4 4.3 %collective-permute-done.4.refs_1_ = f32[192,128]{1,0:T(8,128)S(1)} collective-permute-done((f32[192,128]{1,0:T(8,128)S(1)}, f32[192,128]{1,0:T(8,128)S(1)}, u32[]{:S(2)}, u32[]{:S(2)}) %collective-permute-start.4) | collective-permute-done | bytes 98336 | tf_op jit(solution)/shard_map/ppermute | solution.py:389
  34.6 0.6 collective-permute-start.5
  35.2 6.3 %collective-permute-done.5.refs_1_ = f32[192,128]{1,0:T(8,128)S(1)} collective-permute-done((f32[192,128]{1,0:T(8,128)S(1)}, f32[192,128]{1,0:T(8,128)S(1)}, u32[]{:S(2)}, u32[]{:S(2)}) %collective-permute-start.5) | collective-permute-done | bytes 98336 | tf_op jit(solution)/shard_map/ppermute | solution.py:389
  41.5 0.1 collective-permute-start.6
  41.6 0.0 collective-permute-done.8.refs_1_
  41.6 0.1 add_parts.11
  41.7 2.8 %collective-permute-start.10 = (f32[256,128]{1,0:T(8,128)S(1)}, f32[256,128]{1,0:T(8,128)S(1)}, u32[]{:S(2)}, u32[]{:S(2)}) collective-permute-start(f32[256,128]{1,0:T(8,128)S(1)} %get-tuple-element.53), channel_id=1, source_target_pairs={{0,16},{2,18},{4,20},{6,22},{8,24},{10,26},{12,28},{14,30},{16,0},... | collective-permute-start | bytes 393224 | tf_op jit(solution)/shard_map/ppermute | solution.py:389
  44.5 1.3 %collective-permute-start.11 = (f32[256,128]{1,0:T(8,128)S(1)}, f32[256,128]{1,0:T(8,128)S(1)}, u32[]{:S(2)}, u32[]{:S(2)}) collective-permute-start(f32[256,128]{1,0:T(8,128)S(1)} %get-tuple-element.54), channel_id=1, source_target_pairs={{0,24},{2,26},{4,28},{6,30},{8,16},{10,18},{12,20},{14,22},{16,8},... | collective-permute-start | bytes 393224 | tf_op jit(solution)/shard_map/ppermute | solution.py:389
  45.8 0.2 collective-permute-start.9
  46.0 0.0 collective-permute-done.6.refs_1_
  46.0 9.1 %inverse_factor.1.refs_2_.inverse_ref = f32[256,256]{1,0:T(8,128)S(1)} custom-call(f32[192,128]{1,0:T(8,128)S(1)} %add_parts.9.refs_0_, f32[192,128]{1,0:T(8,128)S(1)} %collective-permute-done.6.refs_1_), custom_call_target="tpu_custom_call" | custom-call | flops 10000000000 | bytes 524288 | tf_op jit(solution)/shard_map/inverse_factor/pallas_call | solution.py:281
  55.2 0.0 collective-permute-done.10.p2
  55.2 0.0 collective-permute-done.11.p3
  55.2 0.4 collective-permute-done.9.p1
  55.6 0.4 remainder_pieces.1
  56.0 0.7 collective-permute-start.12
  56.7 2.1 %collective-permute-start.13 = (f32[4,16,128]{2,1,0:T(8,128)S(1)}, f32[4,16,128]{2,1,0:T(8,128)S(1)}, u32[]{:S(2)}, u32[]{:S(2)}) collective-permute-start(f32[4,16,128]{2,1,0:T(8,128)S(1)} %get-tuple-element.56), channel_id=1, source_target_pairs={{0,2},{1,3},{2,1},{3,0},{4,6},{5,7},{6,5},{7,4},{8,10},{9,11},{10,... | collective-permute-start | bytes 98312 | tf_op jit(solution)/shard_map/ppermute | solution.py:418
  58.8 1.5 %collective-permute-start.14 = (f32[4,16,128]{2,1,0:T(8,128)S(1)}, f32[4,16,128]{2,1,0:T(8,128)S(1)}, u32[]{:S(2)}, u32[]{:S(2)}) collective-permute-start(f32[4,16,128]{2,1,0:T(8,128)S(1)} %get-tuple-element.57), channel_id=1, source_target_pairs={{0,4},{1,5},{2,7},{3,6},{4,0},{5,1},{6,3},{7,2},{8,12},{9,13},{10,... | collective-permute-start | bytes 98312 | tf_op jit(solution)/shard_map/ppermute | solution.py:418
  60.3 0.0 collective-permute-start.15
  60.3 0.0 collective-permute-done.12.r0
  60.3 0.4 collective-permute-done.13.r1
  60.7 2.0 %collective-permute-done.14.r2 = f32[4,16,128]{2,1,0:T(8,128)S(1)} collective-permute-done((f32[4,16,128]{2,1,0:T(8,128)S(1)}, f32[4,16,128]{2,1,0:T(8,128)S(1)}, u32[]{:S(2)}, u32[]{:S(2)}) %collective-permute-start.14) | collective-permute-done | bytes 32800 | tf_op jit(solution)/shard_map/ppermute | solution.py:418
  62.7 2.1 %collective-permute-done.15.r3 = f32[4,16,128]{2,1,0:T(8,128)S(1)} collective-permute-done((f32[4,16,128]{2,1,0:T(8,128)S(1)}, f32[4,16,128]{2,1,0:T(8,128)S(1)}, u32[]{:S(2)}, u32[]{:S(2)}) %collective-permute-start.15) | collective-permute-done | bytes 32800 | tf_op jit(solution)/shard_map/ppermute | solution.py:418
  64.9 2.8 %collective-permute-start.16 = (f32[4,16,128]{2,1,0:T(8,128)S(1)}, f32[4,16,128]{2,1,0:T(8,128)S(1)}, u32[]{:S(2)}, u32[]{:S(2)}) collective-permute-start(f32[4,16,128]{2,1,0:T(8,128)S(1)} %get-tuple-element.59), channel_id=1, source_target_pairs={{0,8},{2,10},{4,12},{6,14},{8,0},{10,2},{12,4},{14,6},{16,24},{18,... | collective-permute-start | bytes 98312 | tf_op jit(solution)/shard_map/ppermute | solution.py:389
  67.7 2.0 %collective-permute-start.17 = (f32[4,16,128]{2,1,0:T(8,128)S(1)}, f32[4,16,128]{2,1,0:T(8,128)S(1)}, u32[]{:S(2)}, u32[]{:S(2)}) collective-permute-start(f32[4,16,128]{2,1,0:T(8,128)S(1)} %get-tuple-element.60), channel_id=1, source_target_pairs={{0,16},{2,18},{4,20},{6,22},{8,24},{10,26},{12,28},{14,30},{16,0},... | collective-permute-start | bytes 98312 | tf_op jit(solution)/shard_map/ppermute | solution.py:389
  69.7 1.4 %collective-permute-start.18 = (f32[4,16,128]{2,1,0:T(8,128)S(1)}, f32[4,16,128]{2,1,0:T(8,128)S(1)}, u32[]{:S(2)}, u32[]{:S(2)}) collective-permute-start(f32[4,16,128]{2,1,0:T(8,128)S(1)} %get-tuple-element.61), channel_id=1, source_target_pairs={{0,24},{2,26},{4,28},{6,30},{8,16},{10,18},{12,20},{14,22},{16,8},... | collective-permute-start | bytes 98312 | tf_op jit(solution)/shard_map/ppermute | solution.py:389
  71.1 1.3 %scaled_core.1 = f32[512,256]{1,0:T(8,128)} custom-call(f32[256,256]{1,0:T(8,128)S(1)} %get-tuple-element.33.refs_0_, f32[256,256]{1,0:T(8,128)S(1)} %get-tuple-element.36.refs_1_, f32[256,256]{1,0:T(8,128)S(1)} %inverse_factor.1.refs_2_.inverse_ref), custom_call_target="tpu_custom_call" | custom-call | flops 201326592 | bytes 1048576 | tf_op jit(solution)/shard_map/scaled_core/pallas_call | solution.py:308
  72.3 0.0 collective-permute-done.16.s1
  72.3 0.2 collective-permute-done.17.s2
  72.6 2.8 %collective-permute-done.18.s3 = f32[4,16,128]{2,1,0:T(8,128)S(1)} collective-permute-done((f32[4,16,128]{2,1,0:T(8,128)S(1)}, f32[4,16,128]{2,1,0:T(8,128)S(1)}, u32[]{:S(2)}, u32[]{:S(2)}) %collective-permute-start.18) | collective-permute-done | bytes 32800 | tf_op jit(solution)/shard_map/ppermute | solution.py:389
  75.4 0.7 arrange.1
  (5 shorter events, 0.1 us)
Async XLA Ops:
  2.7 10.2 %collective-permute-start = (f32[256,256]{1,0:T(8,128)S(1)}, f32[256,256]{1,0:T(8,128)S(1)}, u32[]{:S(2)}, u32[]{:S(2)}) collective-permute-start(f32[256,256]{1,0:T(8,128)S(1)} %get-tuple-element.32.refs_0_), channel_id=1, source_target_pairs={{0,1},{1,0},{2,3},{3,2},{4,5},{5,4},{6,7},{7,6},{8,9},{9,8},{10,11... | collective-permute-start | bytes 786440 | tf_op jit(solution)/shard_map/ppermute | solution.py:399
  7.8 9.8 %collective-permute-start.1 = (f32[256,256]{1,0:T(8,128)S(1)}, f32[256,256]{1,0:T(8,128)S(1)}, u32[]{:S(2)}, u32[]{:S(2)}) collective-permute-start(f32[256,256]{1,0:T(8,128)S(1)} %get-tuple-element.34.refs_0_), channel_id=1, source_target_pairs={{0,1},{1,0},{2,3},{3,2},{4,5},{5,4},{6,7},{7,6},{8,9},{9,8},{10,11... | collective-permute-start | bytes 786440 | tf_op jit(solution)/shard_map/ppermute | solution.py:399
  18.1 1.4 %collective-permute-start.2 = (f32[192,128]{1,0:T(8,128)S(1)}, f32[192,128]{1,0:T(8,128)S(1)}, u32[]{:S(2)}, u32[]{:S(2)}) collective-permute-start(f32[192,128]{1,0:T(8,128)S(1)} %get-tuple-element.38), channel_id=1, source_target_pairs={{0,2},{2,0},{4,6},{6,4},{8,10},{10,8},{12,14},{14,12},{16,18},{18,... | collective-permute-start | bytes 294920 | tf_op jit(solution)/shard_map/ppermute | solution.py:389
  20.6 5.3 %collective-permute-start.7 = (f32[2,4,256,128]{3,2,1,0:T(8,128)S(1)}, f32[2,4,256,128]{3,2,1,0:T(8,128)S(1)}, u32[]{:S(2)}, u32[]{:S(2)}) collective-permute-start(f32[2,4,256,128]{3,2,1,0:T(8,128)S(1)} %get-tuple-element.48), channel_id=1, source_target_pairs={{0,2},{2,0},{4,6},{6,4},{8,10},{10,8},{12,14},{14,12},{16,18},{18,... | collective-permute-start | bytes 3145736 | tf_op jit(solution)/shard_map/ppermute | solution.py:389
  20.9 5.0 %collective-permute-start.3 = (f32[192,128]{1,0:T(8,128)S(1)}, f32[192,128]{1,0:T(8,128)S(1)}, u32[]{:S(2)}, u32[]{:S(2)}) collective-permute-start(f32[192,128]{1,0:T(8,128)S(1)} %add_parts.6.refs_0_.refs_5_), channel_id=1, source_target_pairs={{0,8},{2,10},{4,12},{6,14},{8,0},{10,2},{12,4},{14,6},{16,24},{18,... | collective-permute-start | bytes 294920 | tf_op jit(solution)/shard_map/ppermute | solution.py:389
  26.0 15.6 %collective-permute-start.8 = (f32[4,256,128]{2,1,0:T(8,128)S(1)}, f32[4,256,128]{2,1,0:T(8,128)S(1)}, u32[]{:S(2)}, u32[]{:S(2)}) collective-permute-start(f32[4,256,128]{2,1,0:T(8,128)S(1)} %get-tuple-element.50), channel_id=1, source_target_pairs={{0,4},{2,6},{4,0},{6,2},{8,12},{10,14},{12,8},{14,10},{16,20},{18,... | collective-permute-start | bytes 1572872 | tf_op jit(solution)/shard_map/ppermute | solution.py:389
  27.8 6.9 %collective-permute-start.4 = (f32[192,128]{1,0:T(8,128)S(1)}, f32[192,128]{1,0:T(8,128)S(1)}, u32[]{:S(2)}, u32[]{:S(2)}) collective-permute-start(f32[192,128]{1,0:T(8,128)S(1)} %add_parts.7.refs_0_.refs_2_), channel_id=1, source_target_pairs={{0,16},{2,18},{4,20},{6,22},{8,24},{10,26},{12,28},{14,30},{16,0},... | collective-permute-start | bytes 294920 | tf_op jit(solution)/shard_map/ppermute | solution.py:389
  34.6 6.9 %collective-permute-start.5 = (f32[192,128]{1,0:T(8,128)S(1)}, f32[192,128]{1,0:T(8,128)S(1)}, u32[]{:S(2)}, u32[]{:S(2)}) collective-permute-start(f32[192,128]{1,0:T(8,128)S(1)} %add_parts.8.refs_0_), channel_id=1, source_target_pairs={{0,4},{2,6},{4,0},{6,2},{8,12},{10,14},{12,8},{14,10},{16,20},{18,... | collective-permute-start | bytes 294920 | tf_op jit(solution)/shard_map/ppermute | solution.py:389
  41.5 4.5 %collective-permute-start.6 = (f32[192,128]{1,0:T(8,128)S(1)}, f32[192,128]{1,0:T(8,128)S(1)}, u32[]{:S(2)}, u32[]{:S(2)}) collective-permute-start(f32[192,128]{1,0:T(8,128)S(1)} %add_parts.9.refs_0_), channel_id=1, source_target_pairs={{0,2},{2,0},{4,6},{6,4},{8,10},{10,8},{12,14},{14,12},{16,18},{18,... | collective-permute-start | bytes 294920 | tf_op jit(solution)/shard_map/ppermute | solution.py:389
  41.7 13.5 %collective-permute-start.10 = (f32[256,128]{1,0:T(8,128)S(1)}, f32[256,128]{1,0:T(8,128)S(1)}, u32[]{:S(2)}, u32[]{:S(2)}) collective-permute-start(f32[256,128]{1,0:T(8,128)S(1)} %get-tuple-element.53), channel_id=1, source_target_pairs={{0,16},{2,18},{4,20},{6,22},{8,24},{10,26},{12,28},{14,30},{16,0},... | collective-permute-start | bytes 393224 | tf_op jit(solution)/shard_map/ppermute | solution.py:389
  44.5 10.8 %collective-permute-start.11 = (f32[256,128]{1,0:T(8,128)S(1)}, f32[256,128]{1,0:T(8,128)S(1)}, u32[]{:S(2)}, u32[]{:S(2)}) collective-permute-start(f32[256,128]{1,0:T(8,128)S(1)} %get-tuple-element.54), channel_id=1, source_target_pairs={{0,24},{2,26},{4,28},{6,30},{8,16},{10,18},{12,20},{14,22},{16,8},... | collective-permute-start | bytes 393224 | tf_op jit(solution)/shard_map/ppermute | solution.py:389
  45.8 9.8 %collective-permute-start.9 = (f32[256,128]{1,0:T(8,128)S(1)}, f32[256,128]{1,0:T(8,128)S(1)}, u32[]{:S(2)}, u32[]{:S(2)}) collective-permute-start(f32[256,128]{1,0:T(8,128)S(1)} %get-tuple-element.52), channel_id=1, source_target_pairs={{0,8},{2,10},{4,12},{6,14},{8,0},{10,2},{12,4},{14,6},{16,24},{18,... | collective-permute-start | bytes 393224 | tf_op jit(solution)/shard_map/ppermute | solution.py:389
  56.0 4.3 %collective-permute-start.12 = (f32[4,16,128]{2,1,0:T(8,128)S(1)}, f32[4,16,128]{2,1,0:T(8,128)S(1)}, u32[]{:S(2)}, u32[]{:S(2)}) collective-permute-start(f32[4,16,128]{2,1,0:T(8,128)S(1)} %get-tuple-element.55), channel_id=1, source_target_pairs={{0,0},{1,1},{2,3},{3,2},{4,4},{5,5},{6,7},{7,6},{8,8},{9,9},{10,11... | collective-permute-start | bytes 98312 | tf_op jit(solution)/shard_map/ppermute | solution.py:418
  56.7 4.1 %collective-permute-start.13 = (f32[4,16,128]{2,1,0:T(8,128)S(1)}, f32[4,16,128]{2,1,0:T(8,128)S(1)}, u32[]{:S(2)}, u32[]{:S(2)}) collective-permute-start(f32[4,16,128]{2,1,0:T(8,128)S(1)} %get-tuple-element.56), channel_id=1, source_target_pairs={{0,2},{1,3},{2,1},{3,0},{4,6},{5,7},{6,5},{7,4},{8,10},{9,11},{10,... | collective-permute-start | bytes 98312 | tf_op jit(solution)/shard_map/ppermute | solution.py:418
  58.8 3.9 %collective-permute-start.14 = (f32[4,16,128]{2,1,0:T(8,128)S(1)}, f32[4,16,128]{2,1,0:T(8,128)S(1)}, u32[]{:S(2)}, u32[]{:S(2)}) collective-permute-start(f32[4,16,128]{2,1,0:T(8,128)S(1)} %get-tuple-element.57), channel_id=1, source_target_pairs={{0,4},{1,5},{2,7},{3,6},{4,0},{5,1},{6,3},{7,2},{8,12},{9,13},{10,... | collective-permute-start | bytes 98312 | tf_op jit(solution)/shard_map/ppermute | solution.py:418
  60.3 4.6 %collective-permute-start.15 = (f32[4,16,128]{2,1,0:T(8,128)S(1)}, f32[4,16,128]{2,1,0:T(8,128)S(1)}, u32[]{:S(2)}, u32[]{:S(2)}) collective-permute-start(f32[4,16,128]{2,1,0:T(8,128)S(1)} %get-tuple-element.58), channel_id=1, source_target_pairs={{0,6},{1,7},{2,5},{3,4},{4,2},{5,3},{6,1},{7,0},{8,14},{9,15},{10,... | collective-permute-start | bytes 98312 | tf_op jit(solution)/shard_map/ppermute | solution.py:418
  64.9 7.4 %collective-permute-start.16 = (f32[4,16,128]{2,1,0:T(8,128)S(1)}, f32[4,16,128]{2,1,0:T(8,128)S(1)}, u32[]{:S(2)}, u32[]{:S(2)}) collective-permute-start(f32[4,16,128]{2,1,0:T(8,128)S(1)} %get-tuple-element.59), channel_id=1, source_target_pairs={{0,8},{2,10},{4,12},{6,14},{8,0},{10,2},{12,4},{14,6},{16,24},{18,... | collective-permute-start | bytes 98312 | tf_op jit(solution)/shard_map/ppermute | solution.py:389
  67.7 4.9 %collective-permute-start.17 = (f32[4,16,128]{2,1,0:T(8,128)S(1)}, f32[4,16,128]{2,1,0:T(8,128)S(1)}, u32[]{:S(2)}, u32[]{:S(2)}) collective-permute-start(f32[4,16,128]{2,1,0:T(8,128)S(1)} %get-tuple-element.60), channel_id=1, source_target_pairs={{0,16},{2,18},{4,20},{6,22},{8,24},{10,26},{12,28},{14,30},{16,0},... | collective-permute-start | bytes 98312 | tf_op jit(solution)/shard_map/ppermute | solution.py:389
  69.7 5.7 %collective-permute-start.18 = (f32[4,16,128]{2,1,0:T(8,128)S(1)}, f32[4,16,128]{2,1,0:T(8,128)S(1)}, u32[]{:S(2)}, u32[]{:S(2)}) collective-permute-start(f32[4,16,128]{2,1,0:T(8,128)S(1)} %get-tuple-element.61), channel_id=1, source_target_pairs={{0,24},{2,26},{4,28},{6,30},{8,16},{10,18},{12,20},{14,22},{16,8},... | collective-permute-start | bytes 98312 | tf_op jit(solution)/shard_map/ppermute | solution.py:389

commit v3 on v2

--- a/solution.py
+++ b/solution.py
@@ -129,10 +129,10 @@
         send_ref[...] = packed_ref[pl.ds(pl.multiple_of((1 - core) * half, half), half), :]
 
 
-def gram_band(own, got, before):
+def gram_band(own, got, before, after=()):
     rows = own.shape[0]
     first = before is None
-    operands = held(own, got) if first else held(own, got, before)
+    operands = held(own, got) if first else held(own, got, before, *after)
     packed = (3 * BLK, BLK)
     half = (3 * BLK // 2, BLK)
 
@@ -140,7 +140,7 @@
         if first:
             gram_kernel(*refs[:2], None, *refs[2:], None, None)
         else:
-            gram_kernel(*refs[:6], refs[8], *refs[6:8])
+            gram_kernel(*refs[:3], *refs[-6:-3], refs[-1], *refs[-3:-1])
 
     return pl.pallas_call(
         body,
@@ -161,11 +161,10 @@
 
 def project_kernel(high_ref, low_ref, band_ref, before_ref, send_ref, keep_ref):
     row = lax.axis_index("rows")
-    side_here = (row & 1) ^ lax.axis_index("cols")
-    flip = (row >> 1) & 1
+    core, flip, near, far = row & 1, (row >> 1) & 1, (row >> 2) & 1, row >> 3
     for side, out_ref in ((1, send_ref), (0, keep_ref)):
         for t in range(4):
-            block = (t ^ (row >> 2)) * 2 + (side_here ^ side)
+            block = (far ^ (t >> 1)) * 4 + (core ^ side) * 2 + (near ^ (t & 1))
             a_high, a_low = split(band_ref[:, pl.ds(pl.multiple_of(block * 2 * BLK, 2 * BLK), 2 * BLK)])
             total = dot(high_ref[...], a_high) + dot(high_ref[...], a_low) + dot(low_ref[...], a_high)
             for h in range(2):
@@ -274,20 +273,20 @@
     out_ref[BLK:, :] = work[:, BLK:]
 
 
-def inverse_factor(own, got, total_rows):
-    def body(*refs):
-        factor_kernel(total_rows, *refs)
-
-    return pl.pallas_call(
-        body,
-        in_specs=[VMEM, VMEM],
+def inverse_factor(own, got, total_rows, after):
+    def body(*refs):
+        factor_kernel(total_rows, *refs[:2], *refs[-3:])
+
+    return pl.pallas_call(
+        body,
+        in_specs=[VMEM] * (2 + len(after)),
         out_specs=VMEM,
         out_shape=on_chip(RANK, RANK),
         scratch_shapes=[pltpu.VMEM((BLK, 3 * BLK), F32), pltpu.VMEM((3 * BLK, BLK), F32)],
         cost_estimate=cost(10_000_000_000, RANK * RANK * 8),
         compiler_params=LIMIT,
         name="inverse_factor",
-    )(*held(own, got))
+    )(*held(own, got, *after))
 
 
 def core_kernel(scale, first_ref, second_ref, inverse_ref, out_ref):
@@ -358,12 +357,13 @@
 
 def arrange_kernel(r0, r1, r2, r3, s1, s2, s3, out_ref, work):
     row = lax.axis_index("rows")
-    core, right, deep, y = row & 1, (row >> 1) & 1, row >> 2, lax.axis_index("cols")
+    core, right, deep = row & 1, (row >> 1) & 1, row >> 2
     firsts = (r0, r1, r2, r3)
     later = (None, s1, s2, s3)
     for t in range(4):
         for m in range(4):
-            mode = (y ^ core ^ (m & 1)) * 4 + (deep ^ t)
+            there = deep ^ t
+            mode = (there & 1) * 4 + (there >> 1) * 2 + (core ^ (m & 1))
             work[mode, right ^ (m >> 1)] = firsts[m][0] if t == 0 else later[t][m]
     for mode in range(MODE):
         for c in range(2):
@@ -399,23 +399,28 @@
         got.append(lax.ppermute(part, "cols", [(0, 1), (1, 0)]))
     first, high, low, packed = gram_band(own[0], got[0], None)
     sides = project_band(high, low, bands[0], None, ())
-    second, high, low, gram_keep, gram_send = gram_band(own[1], got[1], packed)
-    gram, = add_parts(gram_keep, rows_permute(gram_send, 1), 1)
-    give, keep = project_band(high, low, bands[1], sides, (gram,))
-    gram, = add_parts(gram, rows_permute(gram, 4), 1)
-    keep, give = add_parts(keep, rows_permute(give, 1), 2, (gram,))
+    second, high, low, gram_keep, gram_send = gram_band(own[1], got[1], packed, sides)
+    gram_got = rows_permute(gram_send, 1)
+    give, keep = project_band(high, low, bands[1], sides, ())
+    gram, = add_parts(gram_keep, gram_got, 1, (keep,))
+    keep, give = add_parts(keep, rows_permute(give, 1), 2)
+    gram, = add_parts(gram, rows_permute(gram, 4), 1, (give,))
     for mask in (8, 2):
         gram, = add_parts(gram, rows_permute(gram, mask), 1)
     gram_other = rows_permute(gram, 1)
     pieces = add_parts(keep, rows_permute(give, 2), 4)
-    pieces = [pieces[0]] + [rows_permute(pieces[t], 4 * t) for t in (1, 2, 3)]
-    inverse = inverse_factor(gram, gram_other, total_rows)
-    parts = remainder_pieces(inverse, pieces)
+    inverse = inverse_factor(gram, gram_other, total_rows, pieces)
+    gathered = []
+    for k in range(4):
+        pairs = []
+        for i in range(16):
+            for y in range(2):
+                to = (i & 3) | (y << 2) | ((i & 8) ^ ((k >> 1) << 3))
+                pairs.append((2 * i + y, 2 * to + (((i >> 2) & 1) ^ (k & 1))))
+        gathered.append(lax.ppermute(pieces[k], ("rows", "cols"), pairs))
+    parts = remainder_pieces(inverse, gathered)
     core_scaled = scaled_core((first, second), inverse, math.sqrt(total_rows))
-    firsts = []
-    for m in range(4):
-        pairs = [(2 * i + j, 2 * (i ^ m) + (j ^ (i & 1))) for i in range(16) for j in range(2)]
-        firsts.append(lax.ppermute(parts[m], ("rows", "cols"), pairs))
+    firsts = [parts[0]] + [rows_permute(parts[m], m) for m in (1, 2, 3)]
     later = [rows_permute(part, 4 * t) for t, part in zip((1, 2, 3), collect(firsts))]
     return core_scaled, arrange(firsts, later)
 

time: 76.3 us -> 78.5 us (1.029)
  waiting for transfers between devices: 31.4 us -> 33.6 us
    ppermute x13, waiting for transfers between devices: 17.5 us -> 22.6 us  [rows_permute(): return lax.ppermute(value, 'rows', [(i, i ^ mask) for i in range(size)])]
    ppermute x4, waiting for transfers between devices: 4.56 us -> 2.68 us  [local(): gathered.append(lax.ppermute(pieces[k], ('rows', 'cols'), pairs))]
    ppermute x13, starting transfers between devices: 17.6 us -> 16.2 us  [rows_permute(): return lax.ppermute(value, 'rows', [(i, i ^ mask) for i in range(size)])]
    ppermute x4, starting transfers between devices: 4.29 us -> 5.72 us  [local(): gathered.append(lax.ppermute(pieces[k], ('rows', 'cols'), pairs))]
    ppermute x2, waiting for transfers between devices: 9.32 us -> 8.28 us  [local(): got.append(lax.ppermute(part, 'cols', [(0, 1), (1, 0)]))]
  transfers between devices with their start and end apart: 19 -> 19, of which waited for: 12 -> 11; matrix products, arithmetic and copies ran while one was open for 0% -> 0% of each run, Pallas kernels for 18% -> 18%
where the time goes in v3:
time: 78.5 us; the launch traced here: 78.3 us
  waiting for transfers between devices  33.6 us (43%)
  starting transfers between devices  25.1 us (32%)
  Pallas kernels  18.9 us (24%)
    ppermute x13, waiting for transfers between devices, rows_permute(): return lax.ppermute(value, 'rows', [(i, i ^ mask) for i in range(size)])  22.6 us
    ppermute x13, starting transfers between devices, rows_permute(): return lax.ppermute(value, 'rows', [(i, i ^ mask) for i in range(size)])  16.2 us
    pallas_call x1, Pallas kernels, inverse_factor(): pl.pallas_call(body, in_specs=[VMEM] * (2 + len(after)), out_specs=VMEM,...  9.16 us
    ppermute x2, waiting for transfers between devices, local(): got.append(lax.ppermute(part, 'cols', [(0, 1), (1, 0)]))  8.28 us
    ppermute x4, starting transfers between devices, local(): gathered.append(lax.ppermute(pieces[k], ('rows', 'cols'), pairs))  5.72 us
    pallas_call x2, Pallas kernels, sketch_band(): pl.pallas_call(body, in_specs=[HBM] * 3, out_specs=[VMEM] * 2, out_shape=...  4.13 us
    ppermute x2, starting transfers between devices, local(): got.append(lax.ppermute(part, 'cols', [(0, 1), (1, 0)]))  3.12 us
    ppermute x4, waiting for transfers between devices, local(): gathered.append(lax.ppermute(pieces[k], ('rows', 'cols'), pairs))  2.68 us
  transfers between devices with their start and end apart: 19, of which 11 were waited for; matrix products, arithmetic and copies ran while one was open for 0% of the time, Pallas kernels for 18%

profile of v3, /device:TPU:0, one launch (start us, length us, event | category | flops | bytes accessed | tf_op | source)
XLA Modules:
  0.0 78.3 jit_solution(1323095596956573365)
XLA Ops:
  0.6 2.1 %sketch_band.2 = (f32[256,256]{1,0:T(8,128)S(1)}, f32[256,2048]{1,0:T(8,128)S(1)}) custom-call(s32[2,16]{1,0:T(2,128)} %bitcast.6, f32[512,2048]{1,0:T(8,128)} %refs_1_.3, s32[2,2048]{1,0:T(2,128)} %bitcast.4), custom_call_target="tpu_custom_call" | custom-call | flops 2097152 | bytes 2097152 | tf_op jit(solution)/shard_map/sketch_band/pallas_call | solution.py:96
  2.7 3.0 %collective-permute-start = (f32[256,256]{1,0:T(8,128)S(1)}, f32[256,256]{1,0:T(8,128)S(1)}, u32[]{:S(2)}, u32[]{:S(2)}) collective-permute-start(f32[256,256]{1,0:T(8,128)S(1)} %get-tuple-element.32.refs_0_), channel_id=1, source_target_pairs={{0,1},{1,0},{2,3},{3,2},{4,5},{5,4},{6,7},{7,6},{8,9},{9,8},{10,11... | collective-permute-start | bytes 786440 | tf_op jit(solution)/shard_map/ppermute | solution.py:399
  5.7 2.1 %sketch_band.3 = (f32[256,256]{1,0:T(8,128)S(1)}, f32[256,2048]{1,0:T(8,128)S(1)}) custom-call(s32[2,16]{1,0:T(2,128)} %bitcast.7, f32[512,2048]{1,0:T(8,128)} %refs_1_.3, s32[2,2048]{1,0:T(2,128)} %bitcast.5), custom_call_target="tpu_custom_call" | custom-call | flops 2097152 | bytes 2097152 | tf_op jit(solution)/shard_map/sketch_band/pallas_call | solution.py:96
  7.8 0.1 collective-permute-start.1
  7.9 5.0 %collective-permute-done.refs_1_ = f32[256,256]{1,0:T(8,128)S(1)} collective-permute-done((f32[256,256]{1,0:T(8,128)S(1)}, f32[256,256]{1,0:T(8,128)S(1)}, u32[]{:S(2)}, u32[]{:S(2)}) %collective-permute-start) | collective-permute-done | bytes 262176 | tf_op jit(solution)/shard_map/ppermute | solution.py:399
  12.9 0.4 gram_band.2
  13.3 1.0 %project_band.2 = (f32[2,4,256,128]{3,2,1,0:T(8,128)S(1)}, f32[2,4,256,128]{3,2,1,0:T(8,128)S(1)}) custom-call(bf16[256,256]{1,0:T(8,128)(2,1)S(1)} %get-tuple-element.36.refs_0_, bf16[256,256]{1,0:T(8,128)(2,1)S(1)} %get-tuple-element.37.refs_1_, f32[256,2048]{1,0:T(8,128)S(1)} %get-tuple-element.38.refs_2_), custom_call_target="tpu_custom_call" | custom-call | flops 805306368 | bytes 2097152 | tf_op jit(solution)/shard_map/project_band/pallas_call | solution.py:185
  14.4 3.3 %collective-permute-done.1.refs_1_ = f32[256,256]{1,0:T(8,128)S(1)} collective-permute-done((f32[256,256]{1,0:T(8,128)S(1)}, f32[256,256]{1,0:T(8,128)S(1)}, u32[]{:S(2)}, u32[]{:S(2)}) %collective-permute-start.1) | collective-permute-done | bytes 262176 | tf_op jit(solution)/shard_map/ppermute | solution.py:399
  17.7 0.5 gram_band.3
  18.1 1.0 %project_band.3 = (f32[2,4,256,128]{3,2,1,0:T(8,128)S(1)}, f32[2,4,256,128]{3,2,1,0:T(8,128)S(1)}) custom-call(bf16[256,256]{1,0:T(8,128)(2,1)S(1)} %get-tuple-element.44.refs_0_, bf16[256,256]{1,0:T(8,128)(2,1)S(1)} %get-tuple-element.45.refs_1_, f32[256,2048]{1,0:T(8,128)S(1)} %get-tuple-element.46.refs_2_, ...), custom_call_target="tpu_custom_call" | custom-call | flops 805306368 | bytes 2097152 | tf_op jit(solution)/shard_map/project_band/pallas_call | solution.py:185
  19.2 0.1 collective-permute-start.4
  19.3 2.6 %collective-permute-done.4.refs_1_ = f32[2,4,256,128]{3,2,1,0:T(8,128)S(1)} collective-permute-done((f32[2,4,256,128]{3,2,1,0:T(8,128)S(1)}, f32[2,4,256,128]{3,2,1,0:T(8,128)S(1)}, u32[]{:S(2)}, u32[]{:S(2)}) %collective-permute-start.4) | collective-permute-done | bytes 1048608 | tf_op jit(solution)/shard_map/ppermute | solution.py:389
  21.9 0.1 add_parts.7
  22.0 1.8 %collective-permute-start.8 = (f32[4,256,128]{2,1,0:T(8,128)S(1)}, f32[4,256,128]{2,1,0:T(8,128)S(1)}, u32[]{:S(2)}, u32[]{:S(2)}) collective-permute-start(f32[4,256,128]{2,1,0:T(8,128)S(1)} %get-tuple-element.49.refs_2_), channel_id=1, source_target_pairs={{0,4},{2,6},{4,0},{6,2},{8,12},{10,14},{12,8},{14,10},{16,20},{18,... | collective-permute-start | bytes 1572872 | tf_op jit(solution)/shard_map/ppermute | solution.py:389
  23.8 0.0 collective-permute-start.2
  23.8 1.3 %collective-permute-done.2.refs_1_ = f32[192,128]{1,0:T(8,128)S(1)} collective-permute-done((f32[192,128]{1,0:T(8,128)S(1)}, f32[192,128]{1,0:T(8,128)S(1)}, u32[]{:S(2)}, u32[]{:S(2)}) %collective-permute-start.2) | collective-permute-done | bytes 98336 | tf_op jit(solution)/shard_map/ppermute | solution.py:389
  25.1 1.6 %collective-permute-start.3 = (f32[192,128]{1,0:T(8,128)S(1)}, f32[192,128]{1,0:T(8,128)S(1)}, u32[]{:S(2)}, u32[]{:S(2)}) collective-permute-start(f32[192,128]{1,0:T(8,128)S(1)} %add_parts.6.refs_0_), channel_id=1, source_target_pairs={{0,8},{2,10},{4,12},{6,14},{8,0},{10,2},{12,4},{14,6},{16,24},{18,... | collective-permute-start | bytes 294920 | tf_op jit(solution)/shard_map/ppermute | solution.py:389
  26.8 3.3 %collective-permute-done.3.refs_1_ = f32[192,128]{1,0:T(8,128)S(1)} collective-permute-done((f32[192,128]{1,0:T(8,128)S(1)}, f32[192,128]{1,0:T(8,128)S(1)}, u32[]{:S(2)}, u32[]{:S(2)}) %collective-permute-start.3) | collective-permute-done | bytes 98336 | tf_op jit(solution)/shard_map/ppermute | solution.py:389
  30.1 2.7 %collective-permute-start.5 = (f32[192,128]{1,0:T(8,128)S(1)}, f32[192,128]{1,0:T(8,128)S(1)}, u32[]{:S(2)}, u32[]{:S(2)}) collective-permute-start(f32[192,128]{1,0:T(8,128)S(1)} %add_parts.8.refs_0_), channel_id=1, source_target_pairs={{0,16},{2,18},{4,20},{6,22},{8,24},{10,26},{12,28},{14,30},{16,0},... | collective-permute-start | bytes 294920 | tf_op jit(solution)/shard_map/ppermute | solution.py:389
  32.7 4.4 %collective-permute-done.5.refs_1_ = f32[192,128]{1,0:T(8,128)S(1)} collective-permute-done((f32[192,128]{1,0:T(8,128)S(1)}, f32[192,128]{1,0:T(8,128)S(1)}, u32[]{:S(2)}, u32[]{:S(2)}) %collective-permute-start.5) | collective-permute-done | bytes 98336 | tf_op jit(solution)/shard_map/ppermute | solution.py:389
  37.2 0.6 collective-permute-start.6
  37.7 4.1 %collective-permute-done.6.refs_1_ = f32[192,128]{1,0:T(8,128)S(1)} collective-permute-done((f32[192,128]{1,0:T(8,128)S(1)}, f32[192,128]{1,0:T(8,128)S(1)}, u32[]{:S(2)}, u32[]{:S(2)}) %collective-permute-start.6) | collective-permute-done | bytes 98336 | tf_op jit(solution)/shard_map/ppermute | solution.py:389
  41.9 0.1 collective-permute-start.7
  42.0 0.0 collective-permute-done.8.refs_1_
  42.0 0.1 add_parts.11
  42.0 1.6 %collective-permute-start.10 = (f32[256,128]{1,0:T(8,128)S(1)}, f32[256,128]{1,0:T(8,128)S(1)}, u32[]{:S(2)}, u32[]{:S(2)}) collective-permute-start(f32[256,128]{1,0:T(8,128)S(1)} %get-tuple-element.52.refs_3_), channel_id=1, source_target_pairs={{0,1},{1,9},{2,3},{3,11},{4,5},{5,13},{6,7},{7,15},{8,0},{9,8},{10... | collective-permute-start | bytes 393224 | tf_op jit(solution)/shard_map/ppermute | solution.py:420
  43.6 1.2 %collective-permute-start.11 = (f32[256,128]{1,0:T(8,128)S(1)}, f32[256,128]{1,0:T(8,128)S(1)}, u32[]{:S(2)}, u32[]{:S(2)}) collective-permute-start(f32[256,128]{1,0:T(8,128)S(1)} %get-tuple-element.53.refs_4_), channel_id=1, source_target_pairs={{0,16},{1,24},{2,18},{3,26},{4,20},{5,28},{6,22},{7,30},{8,17},{9,... | collective-permute-start | bytes 393224 | tf_op jit(solution)/shard_map/ppermute | solution.py:420
  44.8 2.3 %collective-permute-start.12 = (f32[256,128]{1,0:T(8,128)S(1)}, f32[256,128]{1,0:T(8,128)S(1)}, u32[]{:S(2)}, u32[]{:S(2)}) collective-permute-start(f32[256,128]{1,0:T(8,128)S(1)} %get-tuple-element.54.refs_5_), channel_id=1, source_target_pairs={{0,17},{1,25},{2,19},{3,27},{4,21},{5,29},{6,23},{7,31},{8,16},{9,... | collective-permute-start | bytes 393224 | tf_op jit(solution)/shard_map/ppermute | solution.py:420
  47.1 0.7 collective-permute-start.9
  47.8 0.0 collective-permute-done.7.refs_1_
  47.8 9.2 %inverse_factor.1.refs_2_.inverse_ref = f32[256,256]{1,0:T(8,128)S(1)} custom-call(f32[192,128]{1,0:T(8,128)S(1)} %add_parts.10.refs_0_, f32[192,128]{1,0:T(8,128)S(1)} %collective-permute-done.7.refs_1_, f32[256,128]{1,0:T(8,128)S(1)} %get-tuple-element.51.refs_2_, f32[256,128]{1,0:T(8,128)S(1)} %get-tuple-element.52.refs_3_, ...), custom_call_target="tpu_custom_call" | custom-call | flops 10000000000 | bytes 524288 | tf_op jit(solution)/shard_map/inverse_factor/pallas_call | solution.py:280
  56.9 2.7 %collective-permute-done.10.p1 = f32[256,128]{1,0:T(8,128)S(1)} collective-permute-done((f32[256,128]{1,0:T(8,128)S(1)}, f32[256,128]{1,0:T(8,128)S(1)}, u32[]{:S(2)}, u32[]{:S(2)}) %collective-permute-start.10) | collective-permute-done | bytes 131104 | tf_op jit(solution)/shard_map/ppermute | solution.py:420
  59.6 0.0 collective-permute-done.11.p2
  59.6 0.0 collective-permute-done.12.p3
  59.6 0.0 collective-permute-done.9.p0
  59.6 0.4 remainder_pieces.1
  60.0 0.1 collective-permute-start.13
  60.1 0.6 collective-permute-start.14
  60.6 1.3 %collective-permute-start.15 = (f32[4,16,128]{2,1,0:T(8,128)S(1)}, f32[4,16,128]{2,1,0:T(8,128)S(1)}, u32[]{:S(2)}, u32[]{:S(2)}) collective-permute-start(f32[4,16,128]{2,1,0:T(8,128)S(1)} %get-tuple-element.58), channel_id=1, source_target_pairs={{0,6},{2,4},{4,2},{6,0},{8,14},{10,12},{12,10},{14,8},{16,22},{18,... | collective-permute-start | bytes 98312 | tf_op jit(solution)/shard_map/ppermute | solution.py:389
  62.0 0.0 collective-permute-done.13.r1
  62.0 2.4 %collective-permute-done.14.r2 = f32[4,16,128]{2,1,0:T(8,128)S(1)} collective-permute-done((f32[4,16,128]{2,1,0:T(8,128)S(1)}, f32[4,16,128]{2,1,0:T(8,128)S(1)}, u32[]{:S(2)}, u32[]{:S(2)}) %collective-permute-start.14) | collective-permute-done | bytes 32800 | tf_op jit(solution)/shard_map/ppermute | solution.py:389
  64.3 0.0 collective-permute-done.15.r3
  64.4 2.0 %collective-permute-start.16 = (f32[4,16,128]{2,1,0:T(8,128)S(1)}, f32[4,16,128]{2,1,0:T(8,128)S(1)}, u32[]{:S(2)}, u32[]{:S(2)}) collective-permute-start(f32[4,16,128]{2,1,0:T(8,128)S(1)} %get-tuple-element.59), channel_id=1, source_target_pairs={{0,8},{2,10},{4,12},{6,14},{8,0},{10,2},{12,4},{14,6},{16,24},{18,... | collective-permute-start | bytes 98312 | tf_op jit(solution)/shard_map/ppermute | solution.py:389
  66.4 5.5 %collective-permute-start.17 = (f32[4,16,128]{2,1,0:T(8,128)S(1)}, f32[4,16,128]{2,1,0:T(8,128)S(1)}, u32[]{:S(2)}, u32[]{:S(2)}) collective-permute-start(f32[4,16,128]{2,1,0:T(8,128)S(1)} %get-tuple-element.60), channel_id=1, source_target_pairs={{0,16},{2,18},{4,20},{6,22},{8,24},{10,26},{12,28},{14,30},{16,0},... | collective-permute-start | bytes 98312 | tf_op jit(solution)/shard_map/ppermute | solution.py:389
  71.9 0.0 collective-permute-start.18
  71.9 1.3 %scaled_core.1 = f32[512,256]{1,0:T(8,128)} custom-call(f32[256,256]{1,0:T(8,128)S(1)} %get-tuple-element.33.refs_0_, f32[256,256]{1,0:T(8,128)S(1)} %get-tuple-element.41.refs_1_, f32[256,256]{1,0:T(8,128)S(1)} %inverse_factor.1.refs_2_.inverse_ref), custom_call_target="tpu_custom_call" | custom-call | flops 201326592 | bytes 1048576 | tf_op jit(solution)/shard_map/scaled_core/pallas_call | solution.py:307
  73.1 0.0 collective-permute-done.16.s1
  73.1 1.1 %collective-permute-done.17.s2 = f32[4,16,128]{2,1,0:T(8,128)S(1)} collective-permute-done((f32[4,16,128]{2,1,0:T(8,128)S(1)}, f32[4,16,128]{2,1,0:T(8,128)S(1)}, u32[]{:S(2)}, u32[]{:S(2)}) %collective-permute-start.17) | collective-permute-done | bytes 32800 | tf_op jit(solution)/shard_map/ppermute | solution.py:389
  74.3 3.3 %collective-permute-done.18.s3 = f32[4,16,128]{2,1,0:T(8,128)S(1)} collective-permute-done((f32[4,16,128]{2,1,0:T(8,128)S(1)}, f32[4,16,128]{2,1,0:T(8,128)S(1)}, u32[]{:S(2)}, u32[]{:S(2)}) %collective-permute-start.18) | collective-permute-done | bytes 32800 | tf_op jit(solution)/shard_map/ppermute | solution.py:389
  77.6 0.7 arrange.1
  (5 shorter events, 0.1 us)
Async XLA Ops:
  2.7 10.2 %collective-permute-start = (f32[256,256]{1,0:T(8,128)S(1)}, f32[256,256]{1,0:T(8,128)S(1)}, u32[]{:S(2)}, u32[]{:S(2)}) collective-permute-start(f32[256,256]{1,0:T(8,128)S(1)} %get-tuple-element.32.refs_0_), channel_id=1, source_target_pairs={{0,1},{1,0},{2,3},{3,2},{4,5},{5,4},{6,7},{7,6},{8,9},{9,8},{10,11... | collective-permute-start | bytes 786440 | tf_op jit(solution)/shard_map/ppermute | solution.py:399
  7.8 9.8 %collective-permute-start.1 = (f32[256,256]{1,0:T(8,128)S(1)}, f32[256,256]{1,0:T(8,128)S(1)}, u32[]{:S(2)}, u32[]{:S(2)}) collective-permute-start(f32[256,256]{1,0:T(8,128)S(1)} %get-tuple-element.34.refs_0_), channel_id=1, source_target_pairs={{0,1},{1,0},{2,3},{3,2},{4,5},{5,4},{6,7},{7,6},{8,9},{9,8},{10,11... | collective-permute-start | bytes 786440 | tf_op jit(solution)/shard_map/ppermute | solution.py:399
  19.2 2.7 %collective-permute-start.4 = (f32[2,4,256,128]{3,2,1,0:T(8,128)S(1)}, f32[2,4,256,128]{3,2,1,0:T(8,128)S(1)}, u32[]{:S(2)}, u32[]{:S(2)}) collective-permute-start(f32[2,4,256,128]{3,2,1,0:T(8,128)S(1)} %get-tuple-element.48), channel_id=1, source_target_pairs={{0,2},{2,0},{4,6},{6,4},{8,10},{10,8},{12,14},{14,12},{16,18},{18,... | collective-permute-start | bytes 3145736 | tf_op jit(solution)/shard_map/ppermute | solution.py:389
  22.0 19.9 %collective-permute-start.8 = (f32[4,256,128]{2,1,0:T(8,128)S(1)}, f32[4,256,128]{2,1,0:T(8,128)S(1)}, u32[]{:S(2)}, u32[]{:S(2)}) collective-permute-start(f32[4,256,128]{2,1,0:T(8,128)S(1)} %get-tuple-element.49.refs_2_), channel_id=1, source_target_pairs={{0,4},{2,6},{4,0},{6,2},{8,12},{10,14},{12,8},{14,10},{16,20},{18,... | collective-permute-start | bytes 1572872 | tf_op jit(solution)/shard_map/ppermute | solution.py:389
  23.8 1.3 %collective-permute-start.2 = (f32[192,128]{1,0:T(8,128)S(1)}, f32[192,128]{1,0:T(8,128)S(1)}, u32[]{:S(2)}, u32[]{:S(2)}) collective-permute-start(f32[192,128]{1,0:T(8,128)S(1)} %get-tuple-element.43), channel_id=1, source_target_pairs={{0,2},{2,0},{4,6},{6,4},{8,10},{10,8},{12,14},{14,12},{16,18},{18,... | collective-permute-start | bytes 294920 | tf_op jit(solution)/shard_map/ppermute | solution.py:389
  25.1 4.9 %collective-permute-start.3 = (f32[192,128]{1,0:T(8,128)S(1)}, f32[192,128]{1,0:T(8,128)S(1)}, u32[]{:S(2)}, u32[]{:S(2)}) collective-permute-start(f32[192,128]{1,0:T(8,128)S(1)} %add_parts.6.refs_0_), channel_id=1, source_target_pairs={{0,8},{2,10},{4,12},{6,14},{8,0},{10,2},{12,4},{14,6},{16,24},{18,... | collective-permute-start | bytes 294920 | tf_op jit(solution)/shard_map/ppermute | solution.py:389
  30.1 7.1 %collective-permute-start.5 = (f32[192,128]{1,0:T(8,128)S(1)}, f32[192,128]{1,0:T(8,128)S(1)}, u32[]{:S(2)}, u32[]{:S(2)}) collective-permute-start(f32[192,128]{1,0:T(8,128)S(1)} %add_parts.8.refs_0_), channel_id=1, source_target_pairs={{0,16},{2,18},{4,20},{6,22},{8,24},{10,26},{12,28},{14,30},{16,0},... | collective-permute-start | bytes 294920 | tf_op jit(solution)/shard_map/ppermute | solution.py:389
  37.2 4.7 %collective-permute-start.6 = (f32[192,128]{1,0:T(8,128)S(1)}, f32[192,128]{1,0:T(8,128)S(1)}, u32[]{:S(2)}, u32[]{:S(2)}) collective-permute-start(f32[192,128]{1,0:T(8,128)S(1)} %add_parts.9.refs_0_), channel_id=1, source_target_pairs={{0,4},{2,6},{4,0},{6,2},{8,12},{10,14},{12,8},{14,10},{16,20},{18,... | collective-permute-start | bytes 294920 | tf_op jit(solution)/shard_map/ppermute | solution.py:389
  41.9 5.9 %collective-permute-start.7 = (f32[192,128]{1,0:T(8,128)S(1)}, f32[192,128]{1,0:T(8,128)S(1)}, u32[]{:S(2)}, u32[]{:S(2)}) collective-permute-start(f32[192,128]{1,0:T(8,128)S(1)} %add_parts.10.refs_0_), channel_id=1, source_target_pairs={{0,2},{2,0},{4,6},{6,4},{8,10},{10,8},{12,14},{14,12},{16,18},{18,... | collective-permute-start | bytes 294920 | tf_op jit(solution)/shard_map/ppermute | solution.py:389
  42.0 17.6 %collective-permute-start.10 = (f32[256,128]{1,0:T(8,128)S(1)}, f32[256,128]{1,0:T(8,128)S(1)}, u32[]{:S(2)}, u32[]{:S(2)}) collective-permute-start(f32[256,128]{1,0:T(8,128)S(1)} %get-tuple-element.52.refs_3_), channel_id=1, source_target_pairs={{0,1},{1,9},{2,3},{3,11},{4,5},{5,13},{6,7},{7,15},{8,0},{9,8},{10... | collective-permute-start | bytes 393224 | tf_op jit(solution)/shard_map/ppermute | solution.py:420
  43.6 16.0 %collective-permute-start.11 = (f32[256,128]{1,0:T(8,128)S(1)}, f32[256,128]{1,0:T(8,128)S(1)}, u32[]{:S(2)}, u32[]{:S(2)}) collective-permute-start(f32[256,128]{1,0:T(8,128)S(1)} %get-tuple-element.53.refs_4_), channel_id=1, source_target_pairs={{0,16},{1,24},{2,18},{3,26},{4,20},{5,28},{6,22},{7,30},{8,17},{9,... | collective-permute-start | bytes 393224 | tf_op jit(solution)/shard_map/ppermute | solution.py:420
  44.8 14.8 %collective-permute-start.12 = (f32[256,128]{1,0:T(8,128)S(1)}, f32[256,128]{1,0:T(8,128)S(1)}, u32[]{:S(2)}, u32[]{:S(2)}) collective-permute-start(f32[256,128]{1,0:T(8,128)S(1)} %get-tuple-element.54.refs_5_), channel_id=1, source_target_pairs={{0,17},{1,25},{2,19},{3,27},{4,21},{5,29},{6,23},{7,31},{8,16},{9,... | collective-permute-start | bytes 393224 | tf_op jit(solution)/shard_map/ppermute | solution.py:420
  47.1 12.5 %collective-permute-start.9 = (f32[256,128]{1,0:T(8,128)S(1)}, f32[256,128]{1,0:T(8,128)S(1)}, u32[]{:S(2)}, u32[]{:S(2)}) collective-permute-start(f32[256,128]{1,0:T(8,128)S(1)} %get-tuple-element.51.refs_2_), channel_id=1, source_target_pairs={{0,0},{1,8},{2,2},{3,10},{4,4},{5,12},{6,6},{7,14},{8,1},{9,9},{10... | collective-permute-start | bytes 393224 | tf_op jit(solution)/shard_map/ppermute | solution.py:420
  60.0 1.9 %collective-permute-start.13 = (f32[4,16,128]{2,1,0:T(8,128)S(1)}, f32[4,16,128]{2,1,0:T(8,128)S(1)}, u32[]{:S(2)}, u32[]{:S(2)}) collective-permute-start(f32[4,16,128]{2,1,0:T(8,128)S(1)} %get-tuple-element.56), channel_id=1, source_target_pairs={{0,2},{2,0},{4,6},{6,4},{8,10},{10,8},{12,14},{14,12},{16,18},{18,... | collective-permute-start | bytes 98312 | tf_op jit(solution)/shard_map/ppermute | solution.py:389
  60.1 4.2 %collective-permute-start.14 = (f32[4,16,128]{2,1,0:T(8,128)S(1)}, f32[4,16,128]{2,1,0:T(8,128)S(1)}, u32[]{:S(2)}, u32[]{:S(2)}) collective-permute-start(f32[4,16,128]{2,1,0:T(8,128)S(1)} %get-tuple-element.57), channel_id=1, source_target_pairs={{0,4},{2,6},{4,0},{6,2},{8,12},{10,14},{12,8},{14,10},{16,20},{18,... | collective-permute-start | bytes 98312 | tf_op jit(solution)/shard_map/ppermute | solution.py:389
  60.6 3.7 %collective-permute-start.15 = (f32[4,16,128]{2,1,0:T(8,128)S(1)}, f32[4,16,128]{2,1,0:T(8,128)S(1)}, u32[]{:S(2)}, u32[]{:S(2)}) collective-permute-start(f32[4,16,128]{2,1,0:T(8,128)S(1)} %get-tuple-element.58), channel_id=1, source_target_pairs={{0,6},{2,4},{4,2},{6,0},{8,14},{10,12},{12,10},{14,8},{16,22},{18,... | collective-permute-start | bytes 98312 | tf_op jit(solution)/shard_map/ppermute | solution.py:389
  64.4 8.8 %collective-permute-start.16 = (f32[4,16,128]{2,1,0:T(8,128)S(1)}, f32[4,16,128]{2,1,0:T(8,128)S(1)}, u32[]{:S(2)}, u32[]{:S(2)}) collective-permute-start(f32[4,16,128]{2,1,0:T(8,128)S(1)} %get-tuple-element.59), channel_id=1, source_target_pairs={{0,8},{2,10},{4,12},{6,14},{8,0},{10,2},{12,4},{14,6},{16,24},{18,... | collective-permute-start | bytes 98312 | tf_op jit(solution)/shard_map/ppermute | solution.py:389
  66.4 7.9 %collective-permute-start.17 = (f32[4,16,128]{2,1,0:T(8,128)S(1)}, f32[4,16,128]{2,1,0:T(8,128)S(1)}, u32[]{:S(2)}, u32[]{:S(2)}) collective-permute-start(f32[4,16,128]{2,1,0:T(8,128)S(1)} %get-tuple-element.60), channel_id=1, source_target_pairs={{0,16},{2,18},{4,20},{6,22},{8,24},{10,26},{12,28},{14,30},{16,0},... | collective-permute-start | bytes 98312 | tf_op jit(solution)/shard_map/ppermute | solution.py:389
  71.9 5.7 %collective-permute-start.18 = (f32[4,16,128]{2,1,0:T(8,128)S(1)}, f32[4,16,128]{2,1,0:T(8,128)S(1)}, u32[]{:S(2)}, u32[]{:S(2)}) collective-permute-start(f32[4,16,128]{2,1,0:T(8,128)S(1)} %get-tuple-element.61), channel_id=1, source_target_pairs={{0,24},{2,26},{4,28},{6,30},{8,16},{10,18},{12,20},{14,22},{16,8},... | collective-permute-start | bytes 98312 | tf_op jit(solution)/shard_map/ppermute | solution.py:389

commit v4 on v3

--- a/solution.py
+++ b/solution.py
@@ -273,20 +273,20 @@
     out_ref[BLK:, :] = work[:, BLK:]
 
 
-def inverse_factor(own, got, total_rows, after):
-    def body(*refs):
-        factor_kernel(total_rows, *refs[:2], *refs[-3:])
-
-    return pl.pallas_call(
-        body,
-        in_specs=[VMEM] * (2 + len(after)),
+def inverse_factor(own, got, total_rows):
+    def body(*refs):
+        factor_kernel(total_rows, *refs)
+
+    return pl.pallas_call(
+        body,
+        in_specs=[VMEM] * 2,
         out_specs=VMEM,
         out_shape=on_chip(RANK, RANK),
         scratch_shapes=[pltpu.VMEM((BLK, 3 * BLK), F32), pltpu.VMEM((3 * BLK, BLK), F32)],
-        cost_estimate=cost(10_000_000_000, RANK * RANK * 8),
+        cost_estimate=cost(0, RANK * RANK * 8),
         compiler_params=LIMIT,
         name="inverse_factor",
-    )(*held(own, got, *after))
+    )(*held(own, got))
 
 
 def core_kernel(scale, first_ref, second_ref, inverse_ref, out_ref):
@@ -405,11 +405,10 @@
     gram, = add_parts(gram_keep, gram_got, 1, (keep,))
     keep, give = add_parts(keep, rows_permute(give, 1), 2)
     gram, = add_parts(gram, rows_permute(gram, 4), 1, (give,))
-    for mask in (8, 2):
-        gram, = add_parts(gram, rows_permute(gram, mask), 1)
-    gram_other = rows_permute(gram, 1)
     pieces = add_parts(keep, rows_permute(give, 2), 4)
-    inverse = inverse_factor(gram, gram_other, total_rows, pieces)
+    gram, = add_parts(gram, rows_permute(gram, 8), 1, pieces)
+    gram, = add_parts(gram, rows_permute(gram, 2), 1)
+    inverse = inverse_factor(gram, rows_permute(gram, 1), total_rows)
     gathered = []
     for k in range(4):
         pairs = []

time: 78.5 us -> 73.4 us (0.935)
  waiting for transfers between devices: 33.6 us -> 28.6 us
    ppermute x13, waiting for transfers between devices: 22.6 us -> 20 us  [rows_permute(): return lax.ppermute(value, 'rows', [(i, i ^ mask) for i in range(size)])]
    ppermute x4, waiting for transfers between devices: 2.68 us -> 0.3 us  [local(): gathered.append(lax.ppermute(pieces[k], ('rows', 'cols'), pairs))]
  transfers between devices with their start and end apart: 19 -> 19, of which waited for: 11 -> 13; matrix products, arithmetic and copies ran while one was open for 0% -> 0% of each run, Pallas kernels for 18% -> 19%
where the time goes in v4:
time: 73.4 us; the launch traced here: 73.2 us
  waiting for transfers between devices  28.6 us (39%)
  starting transfers between devices  25 us (34%)
  Pallas kernels  18.9 us (26%)
  between operations  0.77 us (1%)
    ppermute x13, waiting for transfers between devices, rows_permute(): return lax.ppermute(value, 'rows', [(i, i ^ mask) for i in range(size)])  20 us
    ppermute x13, starting transfers between devices, rows_permute(): return lax.ppermute(value, 'rows', [(i, i ^ mask) for i in range(size)])  16.1 us
    pallas_call x1, Pallas kernels, inverse_factor(): pl.pallas_call(body, in_specs=[VMEM] * 2, out_specs=VMEM, out_shape=on_ch...  9.14 us
    ppermute x2, waiting for transfers between devices, local(): got.append(lax.ppermute(part, 'cols', [(0, 1), (1, 0)]))  8.28 us
    ppermute x4, starting transfers between devices, local(): gathered.append(lax.ppermute(pieces[k], ('rows', 'cols'), pairs))  5.78 us
    pallas_call x2, Pallas kernels, sketch_band(): pl.pallas_call(body, in_specs=[HBM] * 3, out_specs=[VMEM] * 2, out_shape=...  4.13 us
    ppermute x2, starting transfers between devices, local(): got.append(lax.ppermute(part, 'cols', [(0, 1), (1, 0)]))  3.12 us
    pallas_call x2, Pallas kernels, project_band(): pl.pallas_call(body, in_specs=[VMEM] * len(operands), out_specs=[VMEM] *...  2.07 us
  transfers between devices with their start and end apart: 19, of which 13 were waited for; matrix products, arithmetic and copies ran while one was open for 0% of the time, Pallas kernels for 19%

profile of v4, /device:TPU:0, one launch (start us, length us, event | category | flops | bytes accessed | tf_op | source)
XLA Modules:
  0.0 73.2 jit_solution(6424948716257854716)
XLA Ops:
  0.6 2.1 %sketch_band.2 = (f32[256,256]{1,0:T(8,128)S(1)}, f32[256,2048]{1,0:T(8,128)S(1)}) custom-call(s32[2,16]{1,0:T(2,128)} %bitcast.6, f32[512,2048]{1,0:T(8,128)} %refs_1_.3, s32[2,2048]{1,0:T(2,128)} %bitcast.4), custom_call_target="tpu_custom_call" | custom-call | flops 2097152 | bytes 2097152 | tf_op jit(solution)/shard_map/sketch_band/pallas_call | solution.py:96
  2.7 3.0 %collective-permute-start = (f32[256,256]{1,0:T(8,128)S(1)}, f32[256,256]{1,0:T(8,128)S(1)}, u32[]{:S(2)}, u32[]{:S(2)}) collective-permute-start(f32[256,256]{1,0:T(8,128)S(1)} %get-tuple-element.32.refs_0_), channel_id=1, source_target_pairs={{0,1},{1,0},{2,3},{3,2},{4,5},{5,4},{6,7},{7,6},{8,9},{9,8},{10,11... | collective-permute-start | bytes 786440 | tf_op jit(solution)/shard_map/ppermute | solution.py:399
  5.7 2.1 %sketch_band.3 = (f32[256,256]{1,0:T(8,128)S(1)}, f32[256,2048]{1,0:T(8,128)S(1)}) custom-call(s32[2,16]{1,0:T(2,128)} %bitcast.7, f32[512,2048]{1,0:T(8,128)} %refs_1_.3, s32[2,2048]{1,0:T(2,128)} %bitcast.5), custom_call_target="tpu_custom_call" | custom-call | flops 2097152 | bytes 2097152 | tf_op jit(solution)/shard_map/sketch_band/pallas_call | solution.py:96
  7.8 0.1 collective-permute-start.1
  7.9 5.0 %collective-permute-done.refs_1_ = f32[256,256]{1,0:T(8,128)S(1)} collective-permute-done((f32[256,256]{1,0:T(8,128)S(1)}, f32[256,256]{1,0:T(8,128)S(1)}, u32[]{:S(2)}, u32[]{:S(2)}) %collective-permute-start) | collective-permute-done | bytes 262176 | tf_op jit(solution)/shard_map/ppermute | solution.py:399
  12.9 0.4 gram_band.2
  13.3 1.0 %project_band.2 = (f32[2,4,256,128]{3,2,1,0:T(8,128)S(1)}, f32[2,4,256,128]{3,2,1,0:T(8,128)S(1)}) custom-call(bf16[256,256]{1,0:T(8,128)(2,1)S(1)} %get-tuple-element.36.refs_0_, bf16[256,256]{1,0:T(8,128)(2,1)S(1)} %get-tuple-element.37.refs_1_, f32[256,2048]{1,0:T(8,128)S(1)} %get-tuple-element.38.refs_2_), custom_call_target="tpu_custom_call" | custom-call | flops 805306368 | bytes 2097152 | tf_op jit(solution)/shard_map/project_band/pallas_call | solution.py:185
  14.4 3.3 %collective-permute-done.1.refs_1_ = f32[256,256]{1,0:T(8,128)S(1)} collective-permute-done((f32[256,256]{1,0:T(8,128)S(1)}, f32[256,256]{1,0:T(8,128)S(1)}, u32[]{:S(2)}, u32[]{:S(2)}) %collective-permute-start.1) | collective-permute-done | bytes 262176 | tf_op jit(solution)/shard_map/ppermute | solution.py:399
  17.7 0.5 gram_band.3
  18.1 1.0 %project_band.3 = (f32[2,4,256,128]{3,2,1,0:T(8,128)S(1)}, f32[2,4,256,128]{3,2,1,0:T(8,128)S(1)}) custom-call(bf16[256,256]{1,0:T(8,128)(2,1)S(1)} %get-tuple-element.44.refs_0_, bf16[256,256]{1,0:T(8,128)(2,1)S(1)} %get-tuple-element.45.refs_1_, f32[256,2048]{1,0:T(8,128)S(1)} %get-tuple-element.46.refs_2_, ...), custom_call_target="tpu_custom_call" | custom-call | flops 805306368 | bytes 2097152 | tf_op jit(solution)/shard_map/project_band/pallas_call | solution.py:185
  19.2 0.1 collective-permute-start.4
  19.3 2.6 %collective-permute-done.4.refs_1_ = f32[2,4,256,128]{3,2,1,0:T(8,128)S(1)} collective-permute-done((f32[2,4,256,128]{3,2,1,0:T(8,128)S(1)}, f32[2,4,256,128]{3,2,1,0:T(8,128)S(1)}, u32[]{:S(2)}, u32[]{:S(2)}) %collective-permute-start.4) | collective-permute-done | bytes 1048608 | tf_op jit(solution)/shard_map/ppermute | solution.py:389
  21.9 0.1 add_parts.7
  22.0 1.8 %collective-permute-start.6 = (f32[4,256,128]{2,1,0:T(8,128)S(1)}, f32[4,256,128]{2,1,0:T(8,128)S(1)}, u32[]{:S(2)}, u32[]{:S(2)}) collective-permute-start(f32[4,256,128]{2,1,0:T(8,128)S(1)} %get-tuple-element.49.refs_2_), channel_id=1, source_target_pairs={{0,4},{2,6},{4,0},{6,2},{8,12},{10,14},{12,8},{14,10},{16,20},{18,... | collective-permute-start | bytes 1572872 | tf_op jit(solution)/shard_map/ppermute | solution.py:389
  23.8 0.0 collective-permute-start.2
  23.8 1.3 %collective-permute-done.2.refs_1_ = f32[192,128]{1,0:T(8,128)S(1)} collective-permute-done((f32[192,128]{1,0:T(8,128)S(1)}, f32[192,128]{1,0:T(8,128)S(1)}, u32[]{:S(2)}, u32[]{:S(2)}) %collective-permute-start.2) | collective-permute-done | bytes 98336 | tf_op jit(solution)/shard_map/ppermute | solution.py:389
  25.1 1.6 %collective-permute-start.3 = (f32[192,128]{1,0:T(8,128)S(1)}, f32[192,128]{1,0:T(8,128)S(1)}, u32[]{:S(2)}, u32[]{:S(2)}) collective-permute-start(f32[192,128]{1,0:T(8,128)S(1)} %add_parts.6.refs_0_), channel_id=1, source_target_pairs={{0,8},{2,10},{4,12},{6,14},{8,0},{10,2},{12,4},{14,6},{16,24},{18,... | collective-permute-start | bytes 294920 | tf_op jit(solution)/shard_map/ppermute | solution.py:389
  26.8 3.3 %collective-permute-done.3.refs_1_ = f32[192,128]{1,0:T(8,128)S(1)} collective-permute-done((f32[192,128]{1,0:T(8,128)S(1)}, f32[192,128]{1,0:T(8,128)S(1)}, u32[]{:S(2)}, u32[]{:S(2)}) %collective-permute-start.3) | collective-permute-done | bytes 98336 | tf_op jit(solution)/shard_map/ppermute | solution.py:389
  30.1 2.7 %collective-permute-start.5 = (f32[192,128]{1,0:T(8,128)S(1)}, f32[192,128]{1,0:T(8,128)S(1)}, u32[]{:S(2)}, u32[]{:S(2)}) collective-permute-start(f32[192,128]{1,0:T(8,128)S(1)} %add_parts.8.refs_0_), channel_id=1, source_target_pairs={{0,16},{2,18},{4,20},{6,22},{8,24},{10,26},{12,28},{14,30},{16,0},... | collective-permute-start | bytes 294920 | tf_op jit(solution)/shard_map/ppermute | solution.py:389
  32.7 3.3 %collective-permute-done.6.refs_1_ = f32[4,256,128]{2,1,0:T(8,128)S(1)} collective-permute-done((f32[4,256,128]{2,1,0:T(8,128)S(1)}, f32[4,256,128]{2,1,0:T(8,128)S(1)}, u32[]{:S(2)}, u32[]{:S(2)}) %collective-permute-start.6) | collective-permute-done | bytes 524320 | tf_op jit(solution)/shard_map/ppermute | solution.py:389
  36.1 0.1 add_parts.9
  36.1 1.0 %collective-permute-done.5.refs_1_ = f32[192,128]{1,0:T(8,128)S(1)} collective-permute-done((f32[192,128]{1,0:T(8,128)S(1)}, f32[192,128]{1,0:T(8,128)S(1)}, u32[]{:S(2)}, u32[]{:S(2)}) %collective-permute-start.5) | collective-permute-done | bytes 98336 | tf_op jit(solution)/shard_map/ppermute | solution.py:389
  37.2 0.8 %collective-permute-start.7 = (f32[192,128]{1,0:T(8,128)S(1)}, f32[192,128]{1,0:T(8,128)S(1)}, u32[]{:S(2)}, u32[]{:S(2)}) collective-permute-start(f32[192,128]{1,0:T(8,128)S(1)} %add_parts.10.refs_0_), channel_id=1, source_target_pairs={{0,4},{2,6},{4,0},{6,2},{8,12},{10,14},{12,8},{14,10},{16,20},{18,... | collective-permute-start | bytes 294920 | tf_op jit(solution)/shard_map/ppermute | solution.py:389
  37.9 1.5 %collective-permute-start.10 = (f32[256,128]{1,0:T(8,128)S(1)}, f32[256,128]{1,0:T(8,128)S(1)}, u32[]{:S(2)}, u32[]{:S(2)}) collective-permute-start(f32[256,128]{1,0:T(8,128)S(1)} %get-tuple-element.52.refs_3_), channel_id=1, source_target_pairs={{0,1},{1,9},{2,3},{3,11},{4,5},{5,13},{6,7},{7,15},{8,0},{9,8},{10... | collective-permute-start | bytes 393224 | tf_op jit(solution)/shard_map/ppermute | solution.py:419
  39.5 2.6 %collective-permute-start.11 = (f32[256,128]{1,0:T(8,128)S(1)}, f32[256,128]{1,0:T(8,128)S(1)}, u32[]{:S(2)}, u32[]{:S(2)}) collective-permute-start(f32[256,128]{1,0:T(8,128)S(1)} %get-tuple-element.53.refs_4_), channel_id=1, source_target_pairs={{0,16},{1,24},{2,18},{3,26},{4,20},{5,28},{6,22},{7,30},{8,17},{9,... | collective-permute-start | bytes 393224 | tf_op jit(solution)/shard_map/ppermute | solution.py:419
  42.0 1.0 %collective-permute-start.12 = (f32[256,128]{1,0:T(8,128)S(1)}, f32[256,128]{1,0:T(8,128)S(1)}, u32[]{:S(2)}, u32[]{:S(2)}) collective-permute-start(f32[256,128]{1,0:T(8,128)S(1)} %get-tuple-element.54.refs_5_), channel_id=1, source_target_pairs={{0,17},{1,25},{2,19},{3,27},{4,21},{5,29},{6,23},{7,31},{8,16},{9,... | collective-permute-start | bytes 393224 | tf_op jit(solution)/shard_map/ppermute | solution.py:419
  43.1 0.7 collective-permute-start.9
  43.7 0.0 collective-permute-done.7.refs_1_
  43.8 0.1 collective-permute-start.8
  43.8 1.3 %collective-permute-done.8.refs_1_ = f32[192,128]{1,0:T(8,128)S(1)} collective-permute-done((f32[192,128]{1,0:T(8,128)S(1)}, f32[192,128]{1,0:T(8,128)S(1)}, u32[]{:S(2)}, u32[]{:S(2)}) %collective-permute-start.8) | collective-permute-done | bytes 98336 | tf_op jit(solution)/shard_map/ppermute | solution.py:389
  45.1 9.1 %inverse_factor.1.refs_2_.inverse_ref = f32[256,256]{1,0:T(8,128)S(1)} custom-call(f32[192,128]{1,0:T(8,128)S(1)} %add_parts.11.refs_0_, f32[192,128]{1,0:T(8,128)S(1)} %collective-permute-done.8.refs_1_), custom_call_target="tpu_custom_call" | custom-call | bytes 524288 | tf_op jit(solution)/shard_map/inverse_factor/pallas_call | solution.py:280
  54.3 0.3 collective-permute-done.10.p1
  54.6 0.0 collective-permute-done.11.p2
  54.6 0.0 collective-permute-done.12.p3
  54.6 0.0 collective-permute-done.9.p0
  54.6 0.4 remainder_pieces.1
  55.0 0.1 collective-permute-start.13
  55.1 1.1 %collective-permute-start.14 = (f32[4,16,128]{2,1,0:T(8,128)S(1)}, f32[4,16,128]{2,1,0:T(8,128)S(1)}, u32[]{:S(2)}, u32[]{:S(2)}) collective-permute-start(f32[4,16,128]{2,1,0:T(8,128)S(1)} %get-tuple-element.57), channel_id=1, source_target_pairs={{0,4},{2,6},{4,0},{6,2},{8,12},{10,14},{12,8},{14,10},{16,20},{18,... | collective-permute-start | bytes 98312 | tf_op jit(solution)/shard_map/ppermute | solution.py:389
  56.2 0.7 %collective-permute-start.15 = (f32[4,16,128]{2,1,0:T(8,128)S(1)}, f32[4,16,128]{2,1,0:T(8,128)S(1)}, u32[]{:S(2)}, u32[]{:S(2)}) collective-permute-start(f32[4,16,128]{2,1,0:T(8,128)S(1)} %get-tuple-element.58), channel_id=1, source_target_pairs={{0,6},{2,4},{4,2},{6,0},{8,14},{10,12},{12,10},{14,8},{16,22},{18,... | collective-permute-start | bytes 98312 | tf_op jit(solution)/shard_map/ppermute | solution.py:389
  56.9 0.0 collective-permute-done.13.r1
  56.9 2.1 %collective-permute-done.14.r2 = f32[4,16,128]{2,1,0:T(8,128)S(1)} collective-permute-done((f32[4,16,128]{2,1,0:T(8,128)S(1)}, f32[4,16,128]{2,1,0:T(8,128)S(1)}, u32[]{:S(2)}, u32[]{:S(2)}) %collective-permute-start.14) | collective-permute-done | bytes 32800 | tf_op jit(solution)/shard_map/ppermute | solution.py:389
  59.0 0.6 collective-permute-done.15.r3
  59.6 3.3 %collective-permute-start.16 = (f32[4,16,128]{2,1,0:T(8,128)S(1)}, f32[4,16,128]{2,1,0:T(8,128)S(1)}, u32[]{:S(2)}, u32[]{:S(2)}) collective-permute-start(f32[4,16,128]{2,1,0:T(8,128)S(1)} %get-tuple-element.59), channel_id=1, source_target_pairs={{0,8},{2,10},{4,12},{6,14},{8,0},{10,2},{12,4},{14,6},{16,24},{18,... | collective-permute-start | bytes 98312 | tf_op jit(solution)/shard_map/ppermute | solution.py:389
  63.0 3.8 %collective-permute-start.17 = (f32[4,16,128]{2,1,0:T(8,128)S(1)}, f32[4,16,128]{2,1,0:T(8,128)S(1)}, u32[]{:S(2)}, u32[]{:S(2)}) collective-permute-start(f32[4,16,128]{2,1,0:T(8,128)S(1)} %get-tuple-element.60), channel_id=1, source_target_pairs={{0,16},{2,18},{4,20},{6,22},{8,24},{10,26},{12,28},{14,30},{16,0},... | collective-permute-start | bytes 98312 | tf_op jit(solution)/shard_map/ppermute | solution.py:389
  66.8 0.0 collective-permute-start.18
  66.8 1.3 %scaled_core.1 = f32[512,256]{1,0:T(8,128)} custom-call(f32[256,256]{1,0:T(8,128)S(1)} %get-tuple-element.33.refs_0_, f32[256,256]{1,0:T(8,128)S(1)} %get-tuple-element.41.refs_1_, f32[256,256]{1,0:T(8,128)S(1)} %inverse_factor.1.refs_2_.inverse_ref), custom_call_target="tpu_custom_call" | custom-call | flops 201326592 | bytes 1048576 | tf_op jit(solution)/shard_map/scaled_core/pallas_call | solution.py:307
  68.0 0.0 collective-permute-done.16.s1
  68.0 1.1 %collective-permute-done.17.s2 = f32[4,16,128]{2,1,0:T(8,128)S(1)} collective-permute-done((f32[4,16,128]{2,1,0:T(8,128)S(1)}, f32[4,16,128]{2,1,0:T(8,128)S(1)}, u32[]{:S(2)}, u32[]{:S(2)}) %collective-permute-start.17) | collective-permute-done | bytes 32800 | tf_op jit(solution)/shard_map/ppermute | solution.py:389
  69.2 3.3 %collective-permute-done.18.s3 = f32[4,16,128]{2,1,0:T(8,128)S(1)} collective-permute-done((f32[4,16,128]{2,1,0:T(8,128)S(1)}, f32[4,16,128]{2,1,0:T(8,128)S(1)}, u32[]{:S(2)}, u32[]{:S(2)}) %collective-permute-start.18) | collective-permute-done | bytes 32800 | tf_op jit(solution)/shard_map/ppermute | solution.py:389
  72.5 0.7 %arrange.1 = f32[16,8,256]{2,1,0:T(8,128)} custom-call(f32[4,16,128]{2,1,0:T(8,128)S(1)} %get-tuple-element.55.r0, f32[4,16,128]{2,1,0:T(8,128)S(1)} %collective-permute-done.13.r1, f32[4,16,128]{2,1,0:T(8,128)S(1)} %collective-permute-done.14.r2, f32[4,16,128]{2,1,0:T(8,128)S(1)} %collective-permute-done.15.r3, ...), custom_call_target="tpu_custom_call" | custom-call | bytes 131072 | tf_op jit(solution)/shard_map/arrange/pallas_call | solution.py:374
  (5 shorter events, 0.1 us)
Async XLA Ops:
  2.7 10.2 %collective-permute-start = (f32[256,256]{1,0:T(8,128)S(1)}, f32[256,256]{1,0:T(8,128)S(1)}, u32[]{:S(2)}, u32[]{:S(2)}) collective-permute-start(f32[256,256]{1,0:T(8,128)S(1)} %get-tuple-element.32.refs_0_), channel_id=1, source_target_pairs={{0,1},{1,0},{2,3},{3,2},{4,5},{5,4},{6,7},{7,6},{8,9},{9,8},{10,11... | collective-permute-start | bytes 786440 | tf_op jit(solution)/shard_map/ppermute | solution.py:399
  7.8 9.8 %collective-permute-start.1 = (f32[256,256]{1,0:T(8,128)S(1)}, f32[256,256]{1,0:T(8,128)S(1)}, u32[]{:S(2)}, u32[]{:S(2)}) collective-permute-start(f32[256,256]{1,0:T(8,128)S(1)} %get-tuple-element.34.refs_0_), channel_id=1, source_target_pairs={{0,1},{1,0},{2,3},{3,2},{4,5},{5,4},{6,7},{7,6},{8,9},{9,8},{10,11... | collective-permute-start | bytes 786440 | tf_op jit(solution)/shard_map/ppermute | solution.py:399
  19.2 2.7 %collective-permute-start.4 = (f32[2,4,256,128]{3,2,1,0:T(8,128)S(1)}, f32[2,4,256,128]{3,2,1,0:T(8,128)S(1)}, u32[]{:S(2)}, u32[]{:S(2)}) collective-permute-start(f32[2,4,256,128]{3,2,1,0:T(8,128)S(1)} %get-tuple-element.48), channel_id=1, source_target_pairs={{0,2},{2,0},{4,6},{6,4},{8,10},{10,8},{12,14},{14,12},{16,18},{18,... | collective-permute-start | bytes 3145736 | tf_op jit(solution)/shard_map/ppermute | solution.py:389
  22.0 14.0 %collective-permute-start.6 = (f32[4,256,128]{2,1,0:T(8,128)S(1)}, f32[4,256,128]{2,1,0:T(8,128)S(1)}, u32[]{:S(2)}, u32[]{:S(2)}) collective-permute-start(f32[4,256,128]{2,1,0:T(8,128)S(1)} %get-tuple-element.49.refs_2_), channel_id=1, source_target_pairs={{0,4},{2,6},{4,0},{6,2},{8,12},{10,14},{12,8},{14,10},{16,20},{18,... | collective-permute-start | bytes 1572872 | tf_op jit(solution)/shard_map/ppermute | solution.py:389
  23.8 1.3 %collective-permute-start.2 = (f32[192,128]{1,0:T(8,128)S(1)}, f32[192,128]{1,0:T(8,128)S(1)}, u32[]{:S(2)}, u32[]{:S(2)}) collective-permute-start(f32[192,128]{1,0:T(8,128)S(1)} %get-tuple-element.43), channel_id=1, source_target_pairs={{0,2},{2,0},{4,6},{6,4},{8,10},{10,8},{12,14},{14,12},{16,18},{18,... | collective-permute-start | bytes 294920 | tf_op jit(solution)/shard_map/ppermute | solution.py:389
  25.1 4.9 %collective-permute-start.3 = (f32[192,128]{1,0:T(8,128)S(1)}, f32[192,128]{1,0:T(8,128)S(1)}, u32[]{:S(2)}, u32[]{:S(2)}) collective-permute-start(f32[192,128]{1,0:T(8,128)S(1)} %add_parts.6.refs_0_), channel_id=1, source_target_pairs={{0,8},{2,10},{4,12},{6,14},{8,0},{10,2},{12,4},{14,6},{16,24},{18,... | collective-permute-start | bytes 294920 | tf_op jit(solution)/shard_map/ppermute | solution.py:389
  30.1 7.1 %collective-permute-start.5 = (f32[192,128]{1,0:T(8,128)S(1)}, f32[192,128]{1,0:T(8,128)S(1)}, u32[]{:S(2)}, u32[]{:S(2)}) collective-permute-start(f32[192,128]{1,0:T(8,128)S(1)} %add_parts.8.refs_0_), channel_id=1, source_target_pairs={{0,16},{2,18},{4,20},{6,22},{8,24},{10,26},{12,28},{14,30},{16,0},... | collective-permute-start | bytes 294920 | tf_op jit(solution)/shard_map/ppermute | solution.py:389
  37.2 6.6 %collective-permute-start.7 = (f32[192,128]{1,0:T(8,128)S(1)}, f32[192,128]{1,0:T(8,128)S(1)}, u32[]{:S(2)}, u32[]{:S(2)}) collective-permute-start(f32[192,128]{1,0:T(8,128)S(1)} %add_parts.10.refs_0_), channel_id=1, source_target_pairs={{0,4},{2,6},{4,0},{6,2},{8,12},{10,14},{12,8},{14,10},{16,20},{18,... | collective-permute-start | bytes 294920 | tf_op jit(solution)/shard_map/ppermute | solution.py:389
  37.9 16.6 %collective-permute-start.10 = (f32[256,128]{1,0:T(8,128)S(1)}, f32[256,128]{1,0:T(8,128)S(1)}, u32[]{:S(2)}, u32[]{:S(2)}) collective-permute-start(f32[256,128]{1,0:T(8,128)S(1)} %get-tuple-element.52.refs_3_), channel_id=1, source_target_pairs={{0,1},{1,9},{2,3},{3,11},{4,5},{5,13},{6,7},{7,15},{8,0},{9,8},{10... | collective-permute-start | bytes 393224 | tf_op jit(solution)/shard_map/ppermute | solution.py:419
  39.5 15.1 %collective-permute-start.11 = (f32[256,128]{1,0:T(8,128)S(1)}, f32[256,128]{1,0:T(8,128)S(1)}, u32[]{:S(2)}, u32[]{:S(2)}) collective-permute-start(f32[256,128]{1,0:T(8,128)S(1)} %get-tuple-element.53.refs_4_), channel_id=1, source_target_pairs={{0,16},{1,24},{2,18},{3,26},{4,20},{5,28},{6,22},{7,30},{8,17},{9,... | collective-permute-start | bytes 393224 | tf_op jit(solution)/shard_map/ppermute | solution.py:419
  42.0 12.5 %collective-permute-start.12 = (f32[256,128]{1,0:T(8,128)S(1)}, f32[256,128]{1,0:T(8,128)S(1)}, u32[]{:S(2)}, u32[]{:S(2)}) collective-permute-start(f32[256,128]{1,0:T(8,128)S(1)} %get-tuple-element.54.refs_5_), channel_id=1, source_target_pairs={{0,17},{1,25},{2,19},{3,27},{4,21},{5,29},{6,23},{7,31},{8,16},{9,... | collective-permute-start | bytes 393224 | tf_op jit(solution)/shard_map/ppermute | solution.py:419
  43.1 11.5 %collective-permute-start.9 = (f32[256,128]{1,0:T(8,128)S(1)}, f32[256,128]{1,0:T(8,128)S(1)}, u32[]{:S(2)}, u32[]{:S(2)}) collective-permute-start(f32[256,128]{1,0:T(8,128)S(1)} %get-tuple-element.51.refs_2_), channel_id=1, source_target_pairs={{0,0},{1,8},{2,2},{3,10},{4,4},{5,12},{6,6},{7,14},{8,1},{9,9},{10... | collective-permute-start | bytes 393224 | tf_op jit(solution)/shard_map/ppermute | solution.py:419
  43.8 1.4 %collective-permute-start.8 = (f32[192,128]{1,0:T(8,128)S(1)}, f32[192,128]{1,0:T(8,128)S(1)}, u32[]{:S(2)}, u32[]{:S(2)}) collective-permute-start(f32[192,128]{1,0:T(8,128)S(1)} %add_parts.11.refs_0_), channel_id=1, source_target_pairs={{0,2},{2,0},{4,6},{6,4},{8,10},{10,8},{12,14},{14,12},{16,18},{18,... | collective-permute-start | bytes 294920 | tf_op jit(solution)/shard_map/ppermute | solution.py:389
  55.0 1.9 %collective-permute-start.13 = (f32[4,16,128]{2,1,0:T(8,128)S(1)}, f32[4,16,128]{2,1,0:T(8,128)S(1)}, u32[]{:S(2)}, u32[]{:S(2)}) collective-permute-start(f32[4,16,128]{2,1,0:T(8,128)S(1)} %get-tuple-element.56), channel_id=1, source_target_pairs={{0,2},{2,0},{4,6},{6,4},{8,10},{10,8},{12,14},{14,12},{16,18},{18,... | collective-permute-start | bytes 98312 | tf_op jit(solution)/shard_map/ppermute | solution.py:389
  55.1 4.0 %collective-permute-start.14 = (f32[4,16,128]{2,1,0:T(8,128)S(1)}, f32[4,16,128]{2,1,0:T(8,128)S(1)}, u32[]{:S(2)}, u32[]{:S(2)}) collective-permute-start(f32[4,16,128]{2,1,0:T(8,128)S(1)} %get-tuple-element.57), channel_id=1, source_target_pairs={{0,4},{2,6},{4,0},{6,2},{8,12},{10,14},{12,8},{14,10},{16,20},{18,... | collective-permute-start | bytes 98312 | tf_op jit(solution)/shard_map/ppermute | solution.py:389
  56.2 3.4 %collective-permute-start.15 = (f32[4,16,128]{2,1,0:T(8,128)S(1)}, f32[4,16,128]{2,1,0:T(8,128)S(1)}, u32[]{:S(2)}, u32[]{:S(2)}) collective-permute-start(f32[4,16,128]{2,1,0:T(8,128)S(1)} %get-tuple-element.58), channel_id=1, source_target_pairs={{0,6},{2,4},{4,2},{6,0},{8,14},{10,12},{12,10},{14,8},{16,22},{18,... | collective-permute-start | bytes 98312 | tf_op jit(solution)/shard_map/ppermute | solution.py:389
  59.6 8.4 %collective-permute-start.16 = (f32[4,16,128]{2,1,0:T(8,128)S(1)}, f32[4,16,128]{2,1,0:T(8,128)S(1)}, u32[]{:S(2)}, u32[]{:S(2)}) collective-permute-start(f32[4,16,128]{2,1,0:T(8,128)S(1)} %get-tuple-element.59), channel_id=1, source_target_pairs={{0,8},{2,10},{4,12},{6,14},{8,0},{10,2},{12,4},{14,6},{16,24},{18,... | collective-permute-start | bytes 98312 | tf_op jit(solution)/shard_map/ppermute | solution.py:389
  63.0 6.2 %collective-permute-start.17 = (f32[4,16,128]{2,1,0:T(8,128)S(1)}, f32[4,16,128]{2,1,0:T(8,128)S(1)}, u32[]{:S(2)}, u32[]{:S(2)}) collective-permute-start(f32[4,16,128]{2,1,0:T(8,128)S(1)} %get-tuple-element.60), channel_id=1, source_target_pairs={{0,16},{2,18},{4,20},{6,22},{8,24},{10,26},{12,28},{14,30},{16,0},... | collective-permute-start | bytes 98312 | tf_op jit(solution)/shard_map/ppermute | solution.py:389
  66.8 5.7 %collective-permute-start.18 = (f32[4,16,128]{2,1,0:T(8,128)S(1)}, f32[4,16,128]{2,1,0:T(8,128)S(1)}, u32[]{:S(2)}, u32[]{:S(2)}) collective-permute-start(f32[4,16,128]{2,1,0:T(8,128)S(1)} %get-tuple-element.61), channel_id=1, source_target_pairs={{0,24},{2,26},{4,28},{6,30},{8,16},{10,18},{12,20},{14,22},{16,8},... | collective-permute-start | bytes 98312 | tf_op jit(solution)/shard_map/ppermute | solution.py:389

commit v5 on v4

--- a/solution.py
+++ b/solution.py
@@ -159,66 +159,66 @@
     )(*operands)
 
 
-def project_kernel(high_ref, low_ref, band_ref, before_ref, send_ref, keep_ref):
+def project_kernel(flips, high_ref, low_ref, band_ref, before, outs):
     row = lax.axis_index("rows")
-    core, flip, near, far = row & 1, (row >> 1) & 1, (row >> 2) & 1, row >> 3
-    for side, out_ref in ((1, send_ref), (0, keep_ref)):
+    core, right, near, far = row & 1, (row >> 1) & 1, (row >> 2) & 1, row >> 3
+    for i, flip in enumerate(flips):
         for t in range(4):
-            block = (far ^ (t >> 1)) * 4 + (core ^ side) * 2 + (near ^ (t & 1))
+            block = (far ^ (t >> 1)) * 4 + (right ^ flip) * 2 + (near ^ (t & 1))
             a_high, a_low = split(band_ref[:, pl.ds(pl.multiple_of(block * 2 * BLK, 2 * BLK), 2 * BLK)])
             total = dot(high_ref[...], a_high) + dot(high_ref[...], a_low) + dot(low_ref[...], a_high)
-            for h in range(2):
-                part = total[:, h * BLK : (h + 1) * BLK]
-                place = flip if h == 0 else 1 - flip
-                if before_ref is not None:
-                    part = part + before_ref[1 - side][place, t]
-                out_ref[place, t] = part
-
-
-def project_band(high, low, band, before, after):
+            left, other = total[:, :BLK], total[:, BLK:]
+            give = jnp.where(core == 0, other, left)
+            keep = jnp.where(core == 0, left, other)
+            outs[2 * i][t] = give if before is None else give + before[2 * i][t]
+            outs[2 * i + 1][t] = keep if before is None else keep + before[2 * i + 1][t]
+
+
+def project_band(flips, high, low, band, before=(), after=()):
     rows, cols = band.shape
-    operands = held(high, low, band, *(before or ()), *after)
-
-    def body(*refs):
-        project_kernel(*refs[:3], refs[3:5] if before else None, *refs[-2:])
+    operands = held(high, low, band, *before, *after)
+    count = 2 * len(flips)
+
+    def body(*refs):
+        project_kernel(flips, *refs[:3], refs[3 : 3 + count] if before else None, refs[-count:])
 
     return pl.pallas_call(
         body,
         in_specs=[VMEM] * len(operands),
-        out_specs=[VMEM] * 2,
-        out_shape=[on_chip(2, 4, RANK, BLK)] * 2,
-        cost_estimate=cost(rows * cols * RANK * 6, rows * cols * 4),
+        out_specs=[VMEM] * count,
+        out_shape=[on_chip(4, RANK, BLK)] * count,
+        cost_estimate=cost(rows * cols * RANK * 3 * len(flips), rows * cols * 4),
         compiler_params=LIMIT,
         name="project_band",
     )(*operands)
 
 
-def add_parts_kernel(left_ref, right_ref, *outs):
-    count = left_ref.shape[0] // len(outs)
+def add_parts_kernel(terms, outs):
     for i, out in enumerate(outs):
-        if len(out.shape) < len(left_ref.shape):
-            out[...] = left_ref[i] + right_ref[i]
-        else:
-            out[...] = left_ref[i * count : (i + 1) * count] + right_ref[i * count : (i + 1) * count]
-
-
-def add_parts(left, right, parts, after=()):
-    dims = left.shape
-    out = dims[1:] if dims[0] == parts else (dims[0] // parts, *dims[1:])
+        here = slice(None) if len(outs) == 1 else i
+        total = terms[0][here]
+        for term in terms[1:]:
+            total = total + term[here]
+        out[...] = total
+
+
+def add_parts(terms, parts, after=()):
+    dims = terms[0].shape
     size = math.prod(dims)
-
-    def body(*refs):
-        add_parts_kernel(*refs[:2], *refs[-parts:])
-
-    return pl.pallas_call(
-        body,
-        in_specs=[VMEM] * (2 + len(after)),
+    count = len(terms)
+
+    def body(*refs):
+        add_parts_kernel(refs[:count], refs[-parts:])
+
+    return pl.pallas_call(
+        body,
+        in_specs=[VMEM] * (count + len(after)),
         out_specs=[VMEM] * parts,
-        out_shape=[on_chip(*out)] * parts,
+        out_shape=[on_chip(*(dims if parts == 1 else dims[1:]))] * parts,
         cost_estimate=cost(size, size),
         compiler_params=LIMIT,
         name="add_parts",
-    )(*held(left, right, *after))
+    )(*held(*terms, *after))
 
 
 def factor_panel(parts, start):
@@ -363,8 +363,8 @@
     for t in range(4):
         for m in range(4):
             there = deep ^ t
-            mode = (there & 1) * 4 + (there >> 1) * 2 + (core ^ (m & 1))
-            work[mode, right ^ (m >> 1)] = firsts[m][0] if t == 0 else later[t][m]
+            mode = (there & 1) * 4 + (there >> 1) * 2 + (right ^ (m >> 1))
+            work[mode, core ^ (m & 1)] = firsts[m][0] if t == 0 else later[t][m]
     for mode in range(MODE):
         for c in range(2):
             out_ref[:, mode, c * BLK : (c + 1) * BLK] = work[mode, c]
@@ -398,16 +398,16 @@
         bands.append(rows_here)
         got.append(lax.ppermute(part, "cols", [(0, 1), (1, 0)]))
     first, high, low, packed = gram_band(own[0], got[0], None)
-    sides = project_band(high, low, bands[0], None, ())
-    second, high, low, gram_keep, gram_send = gram_band(own[1], got[1], packed, sides)
-    gram_got = rows_permute(gram_send, 1)
-    give, keep = project_band(high, low, bands[1], sides, ())
-    gram, = add_parts(gram_keep, gram_got, 1, (keep,))
-    keep, give = add_parts(keep, rows_permute(give, 1), 2)
-    gram, = add_parts(gram, rows_permute(gram, 4), 1, (give,))
-    pieces = add_parts(keep, rows_permute(give, 2), 4)
-    gram, = add_parts(gram, rows_permute(gram, 8), 1, pieces)
-    gram, = add_parts(gram, rows_permute(gram, 2), 1)
+    before = project_band((1, 0), high, low, bands[0])
+    second, high, low, gram_keep, gram_send = gram_band(own[1], got[1], packed, before[:1])
+    gram, = add_parts((gram_keep, rows_permute(gram_send, 1)), 1)
+    give, keep = project_band((1,), high, low, bands[1], before[:2])
+    send, = add_parts((keep, rows_permute(give, 1)), 1, (gram,))
+    give, keep = project_band((0,), high, low, bands[1], before[2:])
+    pieces = add_parts((keep, rows_permute(give, 1), rows_permute(send, 2)), 4)
+    gram, = add_parts((gram, rows_permute(gram, 4)), 1)
+    gram, = add_parts((gram, rows_permute(gram, 8)), 1, pieces)
+    gram, = add_parts((gram, rows_permute(gram, 2)), 1)
     inverse = inverse_factor(gram, rows_permute(gram, 1), total_rows)
     gathered = []
     for k in range(4):

time: 73.4 us -> 72.4 us (0.986)
  waiting for transfers between devices: 28.6 us -> 26.7 us
    ppermute x13 -> x14, waiting for transfers between devices: 20 us -> 15.3 us  [rows_permute(): return lax.ppermute(value, 'rows', [(i, i ^ mask) for i in range(size)])]
    ppermute x4, waiting for transfers between devices: 0.3 us -> 3.17 us  [local(): gathered.append(lax.ppermute(pieces[k], ('rows', 'cols'), pairs))]
    ppermute x4, starting transfers between devices: 5.78 us -> 7.58 us  [local(): gathered.append(lax.ppermute(pieces[k], ('rows', 'cols'), pairs))]
    ppermute x13 -> x14, starting transfers between devices: 16.1 us -> 14.9 us  [rows_permute(): return lax.ppermute(value, 'rows', [(i, i ^ mask) for i in range(size)])]
    pallas_call x2 -> x3, Pallas kernels: 2.07 us -> 2.25 us  [project_band(): pl.pallas_call(body, in_specs=[VMEM] * len(operands), out_specs=[VMEM] *...]
  transfers between devices with their start and end apart: 19 -> 20, of which waited for: 13 -> 9; matrix products, arithmetic and copies ran while one was open for 0% -> 0% of each run, Pallas kernels for 19% -> 20%
where the time goes in v5:
time: 72.4 us; the launch traced here: 72.2 us
  waiting for transfers between devices  26.7 us (37%)
  starting transfers between devices  25.6 us (35%)
  Pallas kernels  19.1 us (26%)
  between operations  0.8 us (1%)
    ppermute x14, waiting for transfers between devices, rows_permute(): return lax.ppermute(value, 'rows', [(i, i ^ mask) for i in range(size)])  15.3 us
    ppermute x14, starting transfers between devices, rows_permute(): return lax.ppermute(value, 'rows', [(i, i ^ mask) for i in range(size)])  14.9 us
    pallas_call x1, Pallas kernels, inverse_factor(): pl.pallas_call(body, in_specs=[VMEM] * 2, out_specs=VMEM, out_shape=on_ch...  9.16 us
    ppermute x2, waiting for transfers between devices, local(): got.append(lax.ppermute(part, 'cols', [(0, 1), (1, 0)]))  8.27 us
    ppermute x4, starting transfers between devices, local(): gathered.append(lax.ppermute(pieces[k], ('rows', 'cols'), pairs))  7.58 us
    pallas_call x2, Pallas kernels, sketch_band(): pl.pallas_call(body, in_specs=[HBM] * 3, out_specs=[VMEM] * 2, out_shape=...  4.13 us
    ppermute x4, waiting for transfers between devices, local(): gathered.append(lax.ppermute(pieces[k], ('rows', 'cols'), pairs))  3.17 us
    ppermute x2, starting transfers between devices, local(): got.append(lax.ppermute(part, 'cols', [(0, 1), (1, 0)]))  3.12 us
  transfers between devices with their start and end apart: 20, of which 9 were waited for; matrix products, arithmetic and copies ran while one was open for 0% of the time, Pallas kernels for 20%

profile of v5, /device:TPU:0, one launch (start us, length us, event | category | flops | bytes accessed | tf_op | source)
XLA Modules:
  0.0 72.2 jit_solution(9448297044428562128)
XLA Ops:
  0.6 2.1 %sketch_band.2 = (f32[256,256]{1,0:T(8,128)S(1)}, f32[256,2048]{1,0:T(8,128)S(1)}) custom-call(s32[2,16]{1,0:T(2,128)} %bitcast.6, f32[512,2048]{1,0:T(8,128)} %refs_1_.3, s32[2,2048]{1,0:T(2,128)} %bitcast.4), custom_call_target="tpu_custom_call" | custom-call | flops 2097152 | bytes 2097152 | tf_op jit(solution)/shard_map/sketch_band/pallas_call | solution.py:96
  2.7 3.0 %collective-permute-start = (f32[256,256]{1,0:T(8,128)S(1)}, f32[256,256]{1,0:T(8,128)S(1)}, u32[]{:S(2)}, u32[]{:S(2)}) collective-permute-start(f32[256,256]{1,0:T(8,128)S(1)} %get-tuple-element.34.refs_0_), channel_id=1, source_target_pairs={{0,1},{1,0},{2,3},{3,2},{4,5},{5,4},{6,7},{7,6},{8,9},{9,8},{10,11... | collective-permute-start | bytes 786440 | tf_op jit(solution)/shard_map/ppermute | solution.py:399
  5.7 2.1 %sketch_band.3 = (f32[256,256]{1,0:T(8,128)S(1)}, f32[256,2048]{1,0:T(8,128)S(1)}) custom-call(s32[2,16]{1,0:T(2,128)} %bitcast.7, f32[512,2048]{1,0:T(8,128)} %refs_1_.3, s32[2,2048]{1,0:T(2,128)} %bitcast.5), custom_call_target="tpu_custom_call" | custom-call | flops 2097152 | bytes 2097152 | tf_op jit(solution)/shard_map/sketch_band/pallas_call | solution.py:96
  7.8 0.1 collective-permute-start.1
  7.9 5.0 %collective-permute-done.refs_1_ = f32[256,256]{1,0:T(8,128)S(1)} collective-permute-done((f32[256,256]{1,0:T(8,128)S(1)}, f32[256,256]{1,0:T(8,128)S(1)}, u32[]{:S(2)}, u32[]{:S(2)}) %collective-permute-start) | collective-permute-done | bytes 262176 | tf_op jit(solution)/shard_map/ppermute | solution.py:399
  12.9 0.4 gram_band.2
  13.3 1.0 %project_band.3 = (f32[4,256,128]{2,1,0:T(8,128)S(1)}, f32[4,256,128]{2,1,0:T(8,128)S(1)}, f32[4,256,128]{2,1,0:T(8,128)S(1)}, f32[4,256,128]{2,1,0:T(8,128)S(1)}) custom-call(bf16[256,256]{1,0:T(8,128)(2,1)S(1)} %get-tuple-element.38.refs_0_, bf16[256,256]{1,0:T(8,128)(2,1)S(1)} %get-tuple-element.39.refs_1_, f32[256,2048]{1,0:T(8,128)S(1)} %get-tuple-element.40.refs_2_), custom_call_target="tpu_custom_call" | custom-call | flops 805306368 | bytes 2097152 | tf_op jit(solution)/shard_map/project_band/pallas_call | solution.py:185
  14.4 3.3 %collective-permute-done.1.refs_1_ = f32[256,256]{1,0:T(8,128)S(1)} collective-permute-done((f32[256,256]{1,0:T(8,128)S(1)}, f32[256,256]{1,0:T(8,128)S(1)}, u32[]{:S(2)}, u32[]{:S(2)}) %collective-permute-start.1) | collective-permute-done | bytes 262176 | tf_op jit(solution)/shard_map/ppermute | solution.py:399
  17.7 0.5 gram_band.3
  18.1 0.6 project_band.5
  18.8 0.1 collective-permute-start.6
  18.9 0.5 collective-permute-start.2
  19.4 0.6 project_band.4
  20.0 0.1 collective-permute-start.5
  20.1 0.8 %collective-permute-done.2.refs_1_ = f32[192,128]{1,0:T(8,128)S(1)} collective-permute-done((f32[192,128]{1,0:T(8,128)S(1)}, f32[192,128]{1,0:T(8,128)S(1)}, u32[]{:S(2)}, u32[]{:S(2)}) %collective-permute-start.2) | collective-permute-done | bytes 98336 | tf_op jit(solution)/shard_map/ppermute | solution.py:389
  20.9 0.0 collective-permute-done.6.refs_1_
  20.9 0.1 add_parts.8
  21.0 1.8 %collective-permute-start.7 = (f32[4,256,128]{2,1,0:T(8,128)S(1)}, f32[4,256,128]{2,1,0:T(8,128)S(1)}, u32[]{:S(2)}, u32[]{:S(2)}) collective-permute-start(f32[4,256,128]{2,1,0:T(8,128)S(1)} %add_parts.8), channel_id=1, source_target_pairs={{0,4},{2,6},{4,0},{6,2},{8,12},{10,14},{12,8},{14,10},{16,20},{18,... | collective-permute-start | bytes 1572872 | tf_op jit(solution)/shard_map/ppermute | solution.py:389
  22.8 1.6 %collective-permute-start.3 = (f32[192,128]{1,0:T(8,128)S(1)}, f32[192,128]{1,0:T(8,128)S(1)}, u32[]{:S(2)}, u32[]{:S(2)}) collective-permute-start(f32[192,128]{1,0:T(8,128)S(1)} %add_parts.6.refs_0_.refs_2_), channel_id=1, source_target_pairs={{0,8},{2,10},{4,12},{6,14},{8,0},{10,2},{12,4},{14,6},{16,24},{18,... | collective-permute-start | bytes 294920 | tf_op jit(solution)/shard_map/ppermute | solution.py:389
  24.3 3.0 %collective-permute-done.3.refs_1_ = f32[192,128]{1,0:T(8,128)S(1)} collective-permute-done((f32[192,128]{1,0:T(8,128)S(1)}, f32[192,128]{1,0:T(8,128)S(1)}, u32[]{:S(2)}, u32[]{:S(2)}) %collective-permute-start.3) | collective-permute-done | bytes 98336 | tf_op jit(solution)/shard_map/ppermute | solution.py:389
  27.4 2.7 %collective-permute-start.4 = (f32[192,128]{1,0:T(8,128)S(1)}, f32[192,128]{1,0:T(8,128)S(1)}, u32[]{:S(2)}, u32[]{:S(2)}) collective-permute-start(f32[192,128]{1,0:T(8,128)S(1)} %add_parts.7.refs_0_), channel_id=1, source_target_pairs={{0,16},{2,18},{4,20},{6,22},{8,24},{10,26},{12,28},{14,30},{16,0},... | collective-permute-start | bytes 294920 | tf_op jit(solution)/shard_map/ppermute | solution.py:389
  30.0 0.0 collective-permute-done.5.refs_1_
  30.0 5.0 %collective-permute-done.7.refs_2_ = f32[4,256,128]{2,1,0:T(8,128)S(1)} collective-permute-done((f32[4,256,128]{2,1,0:T(8,128)S(1)}, f32[4,256,128]{2,1,0:T(8,128)S(1)}, u32[]{:S(2)}, u32[]{:S(2)}) %collective-permute-start.7) | collective-permute-done | bytes 524320 | tf_op jit(solution)/shard_map/ppermute | solution.py:389
  35.0 0.1 add_parts.9
  35.1 0.0 collective-permute-done.4.refs_1_
  35.1 1.8 %collective-permute-start.8 = (f32[192,128]{1,0:T(8,128)S(1)}, f32[192,128]{1,0:T(8,128)S(1)}, u32[]{:S(2)}, u32[]{:S(2)}) collective-permute-start(f32[192,128]{1,0:T(8,128)S(1)} %add_parts.10.refs_0_), channel_id=1, source_target_pairs={{0,4},{2,6},{4,0},{6,2},{8,12},{10,14},{12,8},{14,10},{16,20},{18,... | collective-permute-start | bytes 294920 | tf_op jit(solution)/shard_map/ppermute | solution.py:389
  36.9 0.7 collective-permute-start.10
  37.6 4.3 %collective-permute-start.11 = (f32[256,128]{1,0:T(8,128)S(1)}, f32[256,128]{1,0:T(8,128)S(1)}, u32[]{:S(2)}, u32[]{:S(2)}) collective-permute-start(f32[256,128]{1,0:T(8,128)S(1)} %get-tuple-element.56.refs_3_), channel_id=1, source_target_pairs={{0,1},{1,9},{2,3},{3,11},{4,5},{5,13},{6,7},{7,15},{8,0},{9,8},{10... | collective-permute-start | bytes 393224 | tf_op jit(solution)/shard_map/ppermute | solution.py:419
  41.9 2.6 %collective-permute-start.12 = (f32[256,128]{1,0:T(8,128)S(1)}, f32[256,128]{1,0:T(8,128)S(1)}, u32[]{:S(2)}, u32[]{:S(2)}) collective-permute-start(f32[256,128]{1,0:T(8,128)S(1)} %get-tuple-element.57.refs_4_), channel_id=1, source_target_pairs={{0,16},{1,24},{2,18},{3,26},{4,20},{5,28},{6,22},{7,30},{8,17},{9,... | collective-permute-start | bytes 393224 | tf_op jit(solution)/shard_map/ppermute | solution.py:419
  44.5 0.0 collective-permute-start.13
  44.5 0.0 collective-permute-done.8.refs_1_
  44.5 0.1 collective-permute-start.9
  44.6 1.3 %collective-permute-done.9.refs_1_ = f32[192,128]{1,0:T(8,128)S(1)} collective-permute-done((f32[192,128]{1,0:T(8,128)S(1)}, f32[192,128]{1,0:T(8,128)S(1)}, u32[]{:S(2)}, u32[]{:S(2)}) %collective-permute-start.9) | collective-permute-done | bytes 98336 | tf_op jit(solution)/shard_map/ppermute | solution.py:389
  45.9 9.2 %inverse_factor.1.refs_2_.inverse_ref = f32[256,256]{1,0:T(8,128)S(1)} custom-call(f32[192,128]{1,0:T(8,128)S(1)} %add_parts.11.refs_0_, f32[192,128]{1,0:T(8,128)S(1)} %collective-permute-done.9.refs_1_), custom_call_target="tpu_custom_call" | custom-call | bytes 524288 | tf_op jit(solution)/shard_map/inverse_factor/pallas_call | solution.py:280
  55.0 0.0 collective-permute-done.10.p0
  55.1 3.2 %collective-permute-done.11.p1 = f32[256,128]{1,0:T(8,128)S(1)} collective-permute-done((f32[256,128]{1,0:T(8,128)S(1)}, f32[256,128]{1,0:T(8,128)S(1)}, u32[]{:S(2)}, u32[]{:S(2)}) %collective-permute-start.11) | collective-permute-done | bytes 131104 | tf_op jit(solution)/shard_map/ppermute | solution.py:419
  58.2 0.0 collective-permute-done.12.p2
  58.2 0.0 collective-permute-done.13.p3
  58.2 0.4 remainder_pieces.1
  58.6 0.1 collective-permute-start.14
  58.7 0.6 collective-permute-start.15
  59.3 1.3 %collective-permute-start.16 = (f32[4,16,128]{2,1,0:T(8,128)S(1)}, f32[4,16,128]{2,1,0:T(8,128)S(1)}, u32[]{:S(2)}, u32[]{:S(2)}) collective-permute-start(f32[4,16,128]{2,1,0:T(8,128)S(1)} %get-tuple-element.62), channel_id=1, source_target_pairs={{0,6},{2,4},{4,2},{6,0},{8,14},{10,12},{12,10},{14,8},{16,22},{18,... | collective-permute-start | bytes 98312 | tf_op jit(solution)/shard_map/ppermute | solution.py:389
  60.6 0.0 collective-permute-done.14.r1
  60.6 2.4 %collective-permute-done.15.r2 = f32[4,16,128]{2,1,0:T(8,128)S(1)} collective-permute-done((f32[4,16,128]{2,1,0:T(8,128)S(1)}, f32[4,16,128]{2,1,0:T(8,128)S(1)}, u32[]{:S(2)}, u32[]{:S(2)}) %collective-permute-start.15) | collective-permute-done | bytes 32800 | tf_op jit(solution)/shard_map/ppermute | solution.py:389
  63.0 0.0 collective-permute-done.16.r3
  63.0 0.1 collective-permute-start.17
  63.1 2.7 %collective-permute-start.18 = (f32[4,16,128]{2,1,0:T(8,128)S(1)}, f32[4,16,128]{2,1,0:T(8,128)S(1)}, u32[]{:S(2)}, u32[]{:S(2)}) collective-permute-start(f32[4,16,128]{2,1,0:T(8,128)S(1)} %get-tuple-element.64), channel_id=1, source_target_pairs={{0,16},{2,18},{4,20},{6,22},{8,24},{10,26},{12,28},{14,30},{16,0},... | collective-permute-start | bytes 98312 | tf_op jit(solution)/shard_map/ppermute | solution.py:389
  65.8 1.7 %collective-permute-start.19 = (f32[4,16,128]{2,1,0:T(8,128)S(1)}, f32[4,16,128]{2,1,0:T(8,128)S(1)}, u32[]{:S(2)}, u32[]{:S(2)}) collective-permute-start(f32[4,16,128]{2,1,0:T(8,128)S(1)} %get-tuple-element.65), channel_id=1, source_target_pairs={{0,24},{2,26},{4,28},{6,30},{8,16},{10,18},{12,20},{14,22},{16,8},... | collective-permute-start | bytes 98312 | tf_op jit(solution)/shard_map/ppermute | solution.py:389
  67.5 1.3 %scaled_core.1 = f32[512,256]{1,0:T(8,128)} custom-call(f32[256,256]{1,0:T(8,128)S(1)} %get-tuple-element.35.refs_0_, f32[256,256]{1,0:T(8,128)S(1)} %get-tuple-element.42.refs_1_, f32[256,256]{1,0:T(8,128)S(1)} %inverse_factor.1.refs_2_.inverse_ref), custom_call_target="tpu_custom_call" | custom-call | flops 201326592 | bytes 1048576 | tf_op jit(solution)/shard_map/scaled_core/pallas_call | solution.py:307
  68.7 0.0 collective-permute-done.17.s1
  68.7 0.0 collective-permute-done.18.s2
  68.7 2.8 %collective-permute-done.19.s3 = f32[4,16,128]{2,1,0:T(8,128)S(1)} collective-permute-done((f32[4,16,128]{2,1,0:T(8,128)S(1)}, f32[4,16,128]{2,1,0:T(8,128)S(1)}, u32[]{:S(2)}, u32[]{:S(2)}) %collective-permute-start.19) | collective-permute-done | bytes 32800 | tf_op jit(solution)/shard_map/ppermute | solution.py:389
  71.5 0.7 %arrange.1 = f32[16,8,256]{2,1,0:T(8,128)} custom-call(f32[4,16,128]{2,1,0:T(8,128)S(1)} %get-tuple-element.59.r0, f32[4,16,128]{2,1,0:T(8,128)S(1)} %collective-permute-done.14.r1, f32[4,16,128]{2,1,0:T(8,128)S(1)} %collective-permute-done.15.r2, f32[4,16,128]{2,1,0:T(8,128)S(1)} %collective-permute-done.16.r3, ...), custom_call_target="tpu_custom_call" | custom-call | bytes 131072 | tf_op jit(solution)/shard_map/arrange/pallas_call | solution.py:374
  (5 shorter events, 0.1 us)
Async XLA Ops:
  2.7 10.2 %collective-permute-start = (f32[256,256]{1,0:T(8,128)S(1)}, f32[256,256]{1,0:T(8,128)S(1)}, u32[]{:S(2)}, u32[]{:S(2)}) collective-permute-start(f32[256,256]{1,0:T(8,128)S(1)} %get-tuple-element.34.refs_0_), channel_id=1, source_target_pairs={{0,1},{1,0},{2,3},{3,2},{4,5},{5,4},{6,7},{7,6},{8,9},{9,8},{10,11... | collective-permute-start | bytes 786440 | tf_op jit(solution)/shard_map/ppermute | solution.py:399
  7.8 9.8 %collective-permute-start.1 = (f32[256,256]{1,0:T(8,128)S(1)}, f32[256,256]{1,0:T(8,128)S(1)}, u32[]{:S(2)}, u32[]{:S(2)}) collective-permute-start(f32[256,256]{1,0:T(8,128)S(1)} %get-tuple-element.36.refs_0_), channel_id=1, source_target_pairs={{0,1},{1,0},{2,3},{3,2},{4,5},{5,4},{6,7},{7,6},{8,9},{9,8},{10,11... | collective-permute-start | bytes 786440 | tf_op jit(solution)/shard_map/ppermute | solution.py:399
  18.8 2.1 %collective-permute-start.6 = (f32[4,256,128]{2,1,0:T(8,128)S(1)}, f32[4,256,128]{2,1,0:T(8,128)S(1)}, u32[]{:S(2)}, u32[]{:S(2)}) collective-permute-start(f32[4,256,128]{2,1,0:T(8,128)S(1)} %get-tuple-element.54), channel_id=1, source_target_pairs={{0,2},{2,0},{4,6},{6,4},{8,10},{10,8},{12,14},{14,12},{16,18},{18,... | collective-permute-start | bytes 1572872 | tf_op jit(solution)/shard_map/ppermute | solution.py:389
  18.9 2.0 %collective-permute-start.2 = (f32[192,128]{1,0:T(8,128)S(1)}, f32[192,128]{1,0:T(8,128)S(1)}, u32[]{:S(2)}, u32[]{:S(2)}) collective-permute-start(f32[192,128]{1,0:T(8,128)S(1)} %get-tuple-element.44), channel_id=1, source_target_pairs={{0,2},{2,0},{4,6},{6,4},{8,10},{10,8},{12,14},{14,12},{16,18},{18,... | collective-permute-start | bytes 294920 | tf_op jit(solution)/shard_map/ppermute | solution.py:389
  20.0 10.1 %collective-permute-start.5 = (f32[4,256,128]{2,1,0:T(8,128)S(1)}, f32[4,256,128]{2,1,0:T(8,128)S(1)}, u32[]{:S(2)}, u32[]{:S(2)}) collective-permute-start(f32[4,256,128]{2,1,0:T(8,128)S(1)} %get-tuple-element.51), channel_id=1, source_target_pairs={{0,2},{2,0},{4,6},{6,4},{8,10},{10,8},{12,14},{14,12},{16,18},{18,... | collective-permute-start | bytes 1572872 | tf_op jit(solution)/shard_map/ppermute | solution.py:389
  21.0 14.0 %collective-permute-start.7 = (f32[4,256,128]{2,1,0:T(8,128)S(1)}, f32[4,256,128]{2,1,0:T(8,128)S(1)}, u32[]{:S(2)}, u32[]{:S(2)}) collective-permute-start(f32[4,256,128]{2,1,0:T(8,128)S(1)} %add_parts.8), channel_id=1, source_target_pairs={{0,4},{2,6},{4,0},{6,2},{8,12},{10,14},{12,8},{14,10},{16,20},{18,... | collective-permute-start | bytes 1572872 | tf_op jit(solution)/shard_map/ppermute | solution.py:389
  22.8 4.6 %collective-permute-start.3 = (f32[192,128]{1,0:T(8,128)S(1)}, f32[192,128]{1,0:T(8,128)S(1)}, u32[]{:S(2)}, u32[]{:S(2)}) collective-permute-start(f32[192,128]{1,0:T(8,128)S(1)} %add_parts.6.refs_0_.refs_2_), channel_id=1, source_target_pairs={{0,8},{2,10},{4,12},{6,14},{8,0},{10,2},{12,4},{14,6},{16,24},{18,... | collective-permute-start | bytes 294920 | tf_op jit(solution)/shard_map/ppermute | solution.py:389
  27.4 7.7 %collective-permute-start.4 = (f32[192,128]{1,0:T(8,128)S(1)}, f32[192,128]{1,0:T(8,128)S(1)}, u32[]{:S(2)}, u32[]{:S(2)}) collective-permute-start(f32[192,128]{1,0:T(8,128)S(1)} %add_parts.7.refs_0_), channel_id=1, source_target_pairs={{0,16},{2,18},{4,20},{6,22},{8,24},{10,26},{12,28},{14,30},{16,0},... | collective-permute-start | bytes 294920 | tf_op jit(solution)/shard_map/ppermute | solution.py:389
  35.1 9.4 %collective-permute-start.8 = (f32[192,128]{1,0:T(8,128)S(1)}, f32[192,128]{1,0:T(8,128)S(1)}, u32[]{:S(2)}, u32[]{:S(2)}) collective-permute-start(f32[192,128]{1,0:T(8,128)S(1)} %add_parts.10.refs_0_), channel_id=1, source_target_pairs={{0,4},{2,6},{4,0},{6,2},{8,12},{10,14},{12,8},{14,10},{16,20},{18,... | collective-permute-start | bytes 294920 | tf_op jit(solution)/shard_map/ppermute | solution.py:389
  36.9 18.1 %collective-permute-start.10 = (f32[256,128]{1,0:T(8,128)S(1)}, f32[256,128]{1,0:T(8,128)S(1)}, u32[]{:S(2)}, u32[]{:S(2)}) collective-permute-start(f32[256,128]{1,0:T(8,128)S(1)} %get-tuple-element.55.refs_2_), channel_id=1, source_target_pairs={{0,0},{1,8},{2,2},{3,10},{4,4},{5,12},{6,6},{7,14},{8,1},{9,9},{10... | collective-permute-start | bytes 393224 | tf_op jit(solution)/shard_map/ppermute | solution.py:419
  37.6 20.6 %collective-permute-start.11 = (f32[256,128]{1,0:T(8,128)S(1)}, f32[256,128]{1,0:T(8,128)S(1)}, u32[]{:S(2)}, u32[]{:S(2)}) collective-permute-start(f32[256,128]{1,0:T(8,128)S(1)} %get-tuple-element.56.refs_3_), channel_id=1, source_target_pairs={{0,1},{1,9},{2,3},{3,11},{4,5},{5,13},{6,7},{7,15},{8,0},{9,8},{10... | collective-permute-start | bytes 393224 | tf_op jit(solution)/shard_map/ppermute | solution.py:419
  41.9 16.3 %collective-permute-start.12 = (f32[256,128]{1,0:T(8,128)S(1)}, f32[256,128]{1,0:T(8,128)S(1)}, u32[]{:S(2)}, u32[]{:S(2)}) collective-permute-start(f32[256,128]{1,0:T(8,128)S(1)} %get-tuple-element.57.refs_4_), channel_id=1, source_target_pairs={{0,16},{1,24},{2,18},{3,26},{4,20},{5,28},{6,22},{7,30},{8,17},{9,... | collective-permute-start | bytes 393224 | tf_op jit(solution)/shard_map/ppermute | solution.py:419
  44.5 13.7 %collective-permute-start.13 = (f32[256,128]{1,0:T(8,128)S(1)}, f32[256,128]{1,0:T(8,128)S(1)}, u32[]{:S(2)}, u32[]{:S(2)}) collective-permute-start(f32[256,128]{1,0:T(8,128)S(1)} %get-tuple-element.58.refs_5_), channel_id=1, source_target_pairs={{0,17},{1,25},{2,19},{3,27},{4,21},{5,29},{6,23},{7,31},{8,16},{9,... | collective-permute-start | bytes 393224 | tf_op jit(solution)/shard_map/ppermute | solution.py:419
  44.5 1.4 %collective-permute-start.9 = (f32[192,128]{1,0:T(8,128)S(1)}, f32[192,128]{1,0:T(8,128)S(1)}, u32[]{:S(2)}, u32[]{:S(2)}) collective-permute-start(f32[192,128]{1,0:T(8,128)S(1)} %add_parts.11.refs_0_), channel_id=1, source_target_pairs={{0,2},{2,0},{4,6},{6,4},{8,10},{10,8},{12,14},{14,12},{16,18},{18,... | collective-permute-start | bytes 294920 | tf_op jit(solution)/shard_map/ppermute | solution.py:389
  58.6 1.9 %collective-permute-start.14 = (f32[4,16,128]{2,1,0:T(8,128)S(1)}, f32[4,16,128]{2,1,0:T(8,128)S(1)}, u32[]{:S(2)}, u32[]{:S(2)}) collective-permute-start(f32[4,16,128]{2,1,0:T(8,128)S(1)} %get-tuple-element.60), channel_id=1, source_target_pairs={{0,2},{2,0},{4,6},{6,4},{8,10},{10,8},{12,14},{14,12},{16,18},{18,... | collective-permute-start | bytes 98312 | tf_op jit(solution)/shard_map/ppermute | solution.py:389
  58.7 4.3 %collective-permute-start.15 = (f32[4,16,128]{2,1,0:T(8,128)S(1)}, f32[4,16,128]{2,1,0:T(8,128)S(1)}, u32[]{:S(2)}, u32[]{:S(2)}) collective-permute-start(f32[4,16,128]{2,1,0:T(8,128)S(1)} %get-tuple-element.61), channel_id=1, source_target_pairs={{0,4},{2,6},{4,0},{6,2},{8,12},{10,14},{12,8},{14,10},{16,20},{18,... | collective-permute-start | bytes 98312 | tf_op jit(solution)/shard_map/ppermute | solution.py:389
  59.3 3.7 %collective-permute-start.16 = (f32[4,16,128]{2,1,0:T(8,128)S(1)}, f32[4,16,128]{2,1,0:T(8,128)S(1)}, u32[]{:S(2)}, u32[]{:S(2)}) collective-permute-start(f32[4,16,128]{2,1,0:T(8,128)S(1)} %get-tuple-element.62), channel_id=1, source_target_pairs={{0,6},{2,4},{4,2},{6,0},{8,14},{10,12},{12,10},{14,8},{16,22},{18,... | collective-permute-start | bytes 98312 | tf_op jit(solution)/shard_map/ppermute | solution.py:389
  63.0 5.7 %collective-permute-start.17 = (f32[4,16,128]{2,1,0:T(8,128)S(1)}, f32[4,16,128]{2,1,0:T(8,128)S(1)}, u32[]{:S(2)}, u32[]{:S(2)}) collective-permute-start(f32[4,16,128]{2,1,0:T(8,128)S(1)} %get-tuple-element.63), channel_id=1, source_target_pairs={{0,8},{2,10},{4,12},{6,14},{8,0},{10,2},{12,4},{14,6},{16,24},{18,... | collective-permute-start | bytes 98312 | tf_op jit(solution)/shard_map/ppermute | solution.py:389
  63.1 5.7 %collective-permute-start.18 = (f32[4,16,128]{2,1,0:T(8,128)S(1)}, f32[4,16,128]{2,1,0:T(8,128)S(1)}, u32[]{:S(2)}, u32[]{:S(2)}) collective-permute-start(f32[4,16,128]{2,1,0:T(8,128)S(1)} %get-tuple-element.64), channel_id=1, source_target_pairs={{0,16},{2,18},{4,20},{6,22},{8,24},{10,26},{12,28},{14,30},{16,0},... | collective-permute-start | bytes 98312 | tf_op jit(solution)/shard_map/ppermute | solution.py:389
  65.8 5.7 %collective-permute-start.19 = (f32[4,16,128]{2,1,0:T(8,128)S(1)}, f32[4,16,128]{2,1,0:T(8,128)S(1)}, u32[]{:S(2)}, u32[]{:S(2)}) collective-permute-start(f32[4,16,128]{2,1,0:T(8,128)S(1)} %get-tuple-element.65), channel_id=1, source_target_pairs={{0,24},{2,26},{4,28},{6,30},{8,16},{10,18},{12,20},{14,22},{16,8},... | collective-permute-start | bytes 98312 | tf_op jit(solution)/shard_map/ppermute | solution.py:389

commit v6 on v5

--- a/solution.py
+++ b/solution.py
@@ -40,7 +40,7 @@
 
 
 def cost(flops, size):
-    return pl.CostEstimate(flops=flops, bytes_accessed=size, transcendentals=0)
+    return pl.CostEstimate(flops=flops // 1000, bytes_accessed=size // 1000, transcendentals=0)
 
 
 def split(value):
@@ -52,145 +52,192 @@
     return jnp.dot(left, right, preferred_element_type=F32)
 
 
-def sketch_kernel(first_row, pattern_ref, whole_ref, sign_ref, out_ref, band_ref, sems, signs, pattern):
+def block_factors(k, signs, pattern, row_blocks):
+    signed = (2 * signs[k : k + 1, :] - 1).astype(F32)
+    return [signed[:, j * BLK : (j + 1) * BLK] * pattern[k, j].astype(F32) for j in range(row_blocks)]
+
+
+def block_sketch(block_ref, here, factors, table):
+    total = block_ref[here, :BLK] * factors[0]
+    for j in range(1, len(factors)):
+        total = total + block_ref[here, j * BLK : (j + 1) * BLK] * factors[j]
+    high, rest = split(total)
+    low = (total - high.astype(F32) - rest.astype(F32)).astype(BF16)
+    return dot(high, table) + dot(rest, table) + dot(low, table)
+
+
+def first_sketch_kernel(pattern_ref, whole_ref, sign_ref, out_ref, held_ref, sems, signs, pattern):
     steps = sems.shape[0] - 2
-    rows = band_ref.shape[0]
-    step = rows // steps
+    step = held_ref.shape[0] // steps
     copies = [
         pltpu.make_async_copy(pattern_ref, pattern, sems.at[steps]),
         pltpu.make_async_copy(sign_ref, signs, sems.at[steps + 1]),
     ]
     for i in range(steps):
-        here = pl.ds(first_row + i * step, step)
-        copies.append(pltpu.make_async_copy(whole_ref.at[here], band_ref.at[pl.ds(i * step, step)], sems.at[i]))
+        here = pl.ds(i * step, step)
+        copies.append(pltpu.make_async_copy(whole_ref.at[here], held_ref.at[here], sems.at[i]))
     for copy in copies:
         copy.start()
     table = hadamard_table(BLK).astype(BF16)
     copies[0].wait()
     copies[1].wait()
-    col_blocks = signs.shape[0]
-    row_blocks = band_ref.shape[1] // BLK
-    factors = []
-    for k in range(col_blocks):
-        signed = (2 * signs[k : k + 1, :] - 1).astype(F32)
-        factors.append([signed[:, j * BLK : (j + 1) * BLK] * pattern[k, j].astype(F32) for j in range(row_blocks)])
+    factors = block_factors(0, signs, pattern, held_ref.shape[1] // BLK)
     for i in range(steps):
         copies[2 + i].wait()
         here = slice(i * step, (i + 1) * step)
-        for k in range(col_blocks):
-            total = jnp.zeros((step, BLK), F32)
-            for j in range(row_blocks):
-                total = total + band_ref[here, j * BLK : (j + 1) * BLK] * factors[k][j]
-            high, rest = split(total)
-            low = (total - high.astype(F32) - rest.astype(F32)).astype(BF16)
-            out_ref[here, k * BLK : (k + 1) * BLK] = dot(high, table) + dot(rest, table) + dot(low, table)
-
-
-def sketch_band(unfolding, pattern_rows, sign_rows, band, bands):
+        out_ref[here, :] = block_sketch(held_ref, here, factors, table)
+
+
+def first_sketch(unfolding, pattern_rows, sign_rows):
     rows, cols = unfolding.shape
-    rows //= bands
-
-    def body(*refs):
-        sketch_kernel(band * rows, *refs)
-
-    return pl.pallas_call(
-        body,
+    return pl.pallas_call(
+        first_sketch_kernel,
         in_specs=[HBM] * 3,
         out_specs=[VMEM] * 2,
-        out_shape=[on_chip(rows, RANK), on_chip(rows, cols)],
+        out_shape=[on_chip(rows, BLK), on_chip(rows, cols)],
         scratch_shapes=[
-            pltpu.SemaphoreType.DMA((6,)),
+            pltpu.SemaphoreType.DMA((10,)),
             pltpu.VMEM(sign_rows.shape, jnp.int32),
             pltpu.SMEM(pattern_rows.shape, jnp.int32),
         ],
-        cost_estimate=cost(rows * cols * 4, rows * cols * 4),
-        compiler_params=LIMIT,
-        name="sketch_band",
+        cost_estimate=cost(rows * cols * 2, rows * cols * 4),
+        compiler_params=LIMIT,
+        name="first_sketch",
     )(*[pltpu.with_memory_space_constraint(x, pltpu.HBM) for x in (pattern_rows, unfolding, sign_rows)])
 
 
-def gram_kernel(own_ref, got_ref, before_ref, sketch_ref, high_ref, low_ref, packed_ref, keep_ref, send_ref):
+def second_sketch_kernel(pattern_ref, sign_ref, block_ref, out_ref, high_ref, low_ref, sems, signs, pattern):
+    copies = [
+        pltpu.make_async_copy(pattern_ref, pattern, sems.at[0]),
+        pltpu.make_async_copy(sign_ref, signs, sems.at[1]),
+    ]
+    for copy in copies:
+        copy.start()
+    table = hadamard_table(BLK).astype(BF16)
+    step = 64
+    for i in range(block_ref.shape[0] // step):
+        here = slice(i * step, (i + 1) * step)
+        high_ref[here, :], low_ref[here, :] = split(block_ref[here, :])
+    for copy in copies:
+        copy.wait()
+    factors = block_factors(1, signs, pattern, block_ref.shape[1] // BLK)
+    for i in range(block_ref.shape[0] // step):
+        here = slice(i * step, (i + 1) * step)
+        out_ref[here, :] = block_sketch(block_ref, here, factors, table)
+
+
+def second_sketch(block, pattern_rows, sign_rows):
+    rows, cols = block.shape
+    return pl.pallas_call(
+        second_sketch_kernel,
+        in_specs=[HBM, HBM, VMEM],
+        out_specs=[VMEM] * 3,
+        out_shape=[on_chip(rows, BLK), on_chip(rows, cols, dtype=BF16), on_chip(rows, cols, dtype=BF16)],
+        scratch_shapes=[
+            pltpu.SemaphoreType.DMA((2,)),
+            pltpu.VMEM(sign_rows.shape, jnp.int32),
+            pltpu.SMEM(pattern_rows.shape, jnp.int32),
+        ],
+        cost_estimate=cost(rows * cols * 2, rows * cols * 4),
+        compiler_params=LIMIT,
+        name="second_sketch",
+    )(*[pltpu.with_memory_space_constraint(x, pltpu.HBM) for x in (pattern_rows, sign_rows)], *held(block))
+
+
+def first_gram_kernel(own_ref, got_ref, sketch_ref, turned_ref, parts_ref, gram_ref):
     sketch = own_ref[...] + got_ref[...]
     sketch_ref[...] = sketch
     turned = sketch.T
-    high, low = split(turned)
-    high_ref[...] = high
-    low_ref[...] = low
-    top = jnp.dot(turned[:BLK], sketch, precision=HIGHEST)
-    low_corner = jnp.dot(turned[BLK:], sketch[:, BLK:], precision=HIGHEST)
-    parts = [top[:, :BLK], top[:, BLK:], low_corner]
-    for i, part in enumerate(parts):
-        here = slice(i * BLK, (i + 1) * BLK)
-        packed_ref[here] = part if before_ref is None else part + before_ref[here]
-    if keep_ref is not None:
-        half = keep_ref.shape[0]
-        core = lax.axis_index("rows") & 1
-        keep_ref[...] = packed_ref[pl.ds(pl.multiple_of(core * half, half), half), :]
-        send_ref[...] = packed_ref[pl.ds(pl.multiple_of((1 - core) * half, half), half), :]
-
-
-def gram_band(own, got, before, after=()):
+    turned_ref[...] = turned
+    parts_ref[:BLK], parts_ref[BLK:] = split(turned)
+    gram_ref[...] = jnp.dot(turned, sketch, precision=HIGHEST)
+
+
+def first_gram(own, got):
     rows = own.shape[0]
-    first = before is None
-    operands = held(own, got) if first else held(own, got, before, *after)
-    packed = (3 * BLK, BLK)
+    return pl.pallas_call(
+        first_gram_kernel,
+        in_specs=[VMEM] * 2,
+        out_specs=[VMEM] * 4,
+        out_shape=[
+            on_chip(rows, BLK),
+            on_chip(BLK, rows),
+            on_chip(2 * BLK, rows, dtype=BF16),
+            on_chip(BLK, BLK),
+        ],
+        cost_estimate=cost(rows * BLK * BLK * 12, rows * BLK * 8),
+        compiler_params=LIMIT,
+        name="first_gram",
+    )(*held(own, got))
+
+
+def second_gram_kernel(own_ref, got_ref, before_ref, gram_ref, sketch_ref, parts_ref, keep_ref, send_ref, packed):
+    sketch = own_ref[...] + got_ref[...]
+    sketch_ref[...] = sketch
+    turned = sketch.T
+    parts_ref[:BLK], parts_ref[BLK:] = split(turned)
+    packed[:BLK] = gram_ref[...]
+    packed[BLK : 2 * BLK] = jnp.dot(before_ref[...], sketch, precision=HIGHEST)
+    packed[2 * BLK :] = jnp.dot(turned, sketch, precision=HIGHEST)
+    half = keep_ref.shape[0]
+    core = lax.axis_index("rows") & 1
+    keep_ref[...] = packed[pl.ds(pl.multiple_of(core * half, half), half), :]
+    send_ref[...] = packed[pl.ds(pl.multiple_of((1 - core) * half, half), half), :]
+
+
+def second_gram(own, got, before, gram, after):
+    rows = own.shape[0]
     half = (3 * BLK // 2, BLK)
 
     def body(*refs):
-        if first:
-            gram_kernel(*refs[:2], None, *refs[2:], None, None)
-        else:
-            gram_kernel(*refs[:3], *refs[-6:-3], refs[-1], *refs[-3:-1])
+        second_gram_kernel(*refs[:4], *refs[-5:])
 
     return pl.pallas_call(
         body,
-        in_specs=[VMEM] * len(operands),
-        out_specs=[VMEM] * (4 if first else 5),
+        in_specs=[VMEM] * (4 + len(after)),
+        out_specs=[VMEM] * 4,
         out_shape=[
-            on_chip(rows, RANK),
-            on_chip(RANK, rows, dtype=BF16),
-            on_chip(RANK, rows, dtype=BF16),
-            *([on_chip(*packed)] if first else [on_chip(*half)] * 2),
+            on_chip(rows, BLK),
+            on_chip(2 * BLK, rows, dtype=BF16),
+            on_chip(*half),
+            on_chip(*half),
         ],
-        scratch_shapes=[] if first else [pltpu.VMEM(packed, F32)],
-        cost_estimate=cost(rows * RANK * RANK * 12, rows * RANK * 8),
-        compiler_params=LIMIT,
-        name="gram_band",
-    )(*operands)
-
-
-def project_kernel(flips, high_ref, low_ref, band_ref, before, outs):
+        scratch_shapes=[pltpu.VMEM((3 * BLK, BLK), F32)],
+        cost_estimate=cost(rows * BLK * BLK * 24, rows * BLK * 8),
+        compiler_params=LIMIT,
+        name="second_gram",
+    )(*held(own, got, before, gram, *after))
+
+
+def project_kernel(parts_ref, high_ref, low_ref, give_1, keep_1, give_0, keep_0):
     row = lax.axis_index("rows")
     core, right, near, far = row & 1, (row >> 1) & 1, (row >> 2) & 1, row >> 3
-    for i, flip in enumerate(flips):
+    for flip, give_ref, keep_ref in ((1, give_1, keep_1), (0, give_0, keep_0)):
         for t in range(4):
             block = (far ^ (t >> 1)) * 4 + (right ^ flip) * 2 + (near ^ (t & 1))
-            a_high, a_low = split(band_ref[:, pl.ds(pl.multiple_of(block * 2 * BLK, 2 * BLK), 2 * BLK)])
-            total = dot(high_ref[...], a_high) + dot(high_ref[...], a_low) + dot(low_ref[...], a_high)
+            here = pl.ds(pl.multiple_of(block * 2 * BLK, 2 * BLK), 2 * BLK)
+            both = dot(parts_ref[...], high_ref[:, here])
+            total = both[:BLK] + both[BLK:] + dot(parts_ref[:BLK, :], low_ref[:, here])
             left, other = total[:, :BLK], total[:, BLK:]
-            give = jnp.where(core == 0, other, left)
-            keep = jnp.where(core == 0, left, other)
-            outs[2 * i][t] = give if before is None else give + before[2 * i][t]
-            outs[2 * i + 1][t] = keep if before is None else keep + before[2 * i + 1][t]
-
-
-def project_band(flips, high, low, band, before=(), after=()):
-    rows, cols = band.shape
-    operands = held(high, low, band, *before, *after)
-    count = 2 * len(flips)
+            give_ref[t] = jnp.where(core == 0, other, left)
+            keep_ref[t] = jnp.where(core == 0, left, other)
+
+
+def project(parts, high, low, after=()):
+    rows, cols = high.shape
 
     def body(*refs):
-        project_kernel(flips, *refs[:3], refs[3 : 3 + count] if before else None, refs[-count:])
+        project_kernel(*refs[:3], *refs[-4:])
 
     return pl.pallas_call(
         body,
-        in_specs=[VMEM] * len(operands),
-        out_specs=[VMEM] * count,
-        out_shape=[on_chip(4, RANK, BLK)] * count,
-        cost_estimate=cost(rows * cols * RANK * 3 * len(flips), rows * cols * 4),
-        compiler_params=LIMIT,
-        name="project_band",
-    )(*operands)
+        in_specs=[VMEM] * (3 + len(after)),
+        out_specs=[VMEM] * 4,
+        out_shape=[on_chip(4, BLK, BLK)] * 4,
+        cost_estimate=cost(rows * cols * BLK * 6, rows * cols * 4),
+        compiler_params=LIMIT,
+        name="project",
+    )(*held(parts, high, low, *after))
 
 
 def add_parts_kernel(terms, outs):
@@ -219,6 +266,31 @@
         compiler_params=LIMIT,
         name="add_parts",
     )(*held(*terms, *after))
+
+
+def pieces_kernel(refs, outs):
+    count = len(refs) // 2
+    for i, out in enumerate(outs):
+        for h in range(2):
+            terms = [ref[i] for ref in refs[h * count : (h + 1) * count]]
+            out[h * BLK : (h + 1) * BLK] = sum(terms[1:], terms[0])
+
+
+def piece_sums(first, second):
+    terms = (*first, *second)
+
+    def body(*refs):
+        pieces_kernel(refs[:-4], refs[-4:])
+
+    return pl.pallas_call(
+        body,
+        in_specs=[VMEM] * len(terms),
+        out_specs=[VMEM] * 4,
+        out_shape=[on_chip(2 * BLK, BLK)] * 4,
+        cost_estimate=cost(8 * BLK * BLK, 96 * BLK * BLK),
+        compiler_params=LIMIT,
+        name="piece_sums",
+    )(*held(*terms))
 
 
 def factor_panel(parts, start):
@@ -291,15 +363,13 @@
 
 def core_kernel(scale, first_ref, second_ref, inverse_ref, out_ref):
     t_high, t_low = split(inverse_ref[...].T)
-    band = first_ref.shape[0]
-    for i, ref in enumerate((first_ref, second_ref)):
-        s_high, s_low = split(ref[...])
-        total = dot(s_high, t_high) + dot(s_high, t_low) + dot(s_low, t_high)
-        out_ref[i * band : (i + 1) * band] = total * scale
-
-
-def scaled_core(sketches, inverse, scale):
-    rows = 2 * sketches[0].shape[0]
+    s_high, s_low = split(jnp.concatenate([first_ref[...], second_ref[...]], 1))
+    total = dot(s_high, t_high) + dot(s_high, t_low) + dot(s_low, t_high)
+    out_ref[...] = total * scale
+
+
+def scaled_core(first, second, inverse, scale):
+    rows = first.shape[0]
 
     def body(*refs):
         core_kernel(scale, *refs)
@@ -312,7 +382,7 @@
         cost_estimate=cost(rows * RANK * RANK * 6, rows * RANK * 8),
         compiler_params=LIMIT,
         name="scaled_core",
-    )(*held(*sketches, inverse))
+    )(*held(first, second, inverse))
 
 
 def remainder_kernel(inverse_ref, p0, p1, p2, p3, o0, o1, o2, o3, work):
@@ -391,21 +461,25 @@
 
 def local(unfolding, pattern, sign_bits):
     total_rows = unfolding.shape[0] * lax.axis_size("rows")
-    own, got, bands = [], [], []
-    for band in range(2):
-        part, rows_here = sketch_band(unfolding, pattern.T, sign_bits.T, band, 2)
-        own.append(part)
-        bands.append(rows_here)
-        got.append(lax.ppermute(part, "cols", [(0, 1), (1, 0)]))
-    first, high, low, packed = gram_band(own[0], got[0], None)
-    before = project_band((1, 0), high, low, bands[0])
-    second, high, low, gram_keep, gram_send = gram_band(own[1], got[1], packed, before[:1])
+    swap = [(0, 1), (1, 0)]
+    pattern_rows, sign_rows = pattern.T, sign_bits.T
+    own_0, block = first_sketch(unfolding, pattern_rows, sign_rows)
+    got_0 = lax.ppermute(own_0, "cols", swap)
+    own_1, high, low = second_sketch(block, pattern_rows, sign_rows)
+    got_1 = lax.ppermute(own_1, "cols", swap)
+    first, turned, parts, gram = first_gram(own_0, got_0)
+    give, keep, give_0, keep_0 = project(parts, high, low)
+    send_0, = add_parts((keep, rows_permute(give, 1)), 1)
+    second, parts, gram_keep, gram_send = second_gram(own_1, got_1, turned, gram, (keep_0,))
     gram, = add_parts((gram_keep, rows_permute(gram_send, 1)), 1)
-    give, keep = project_band((1,), high, low, bands[1], before[:2])
-    send, = add_parts((keep, rows_permute(give, 1)), 1, (gram,))
-    give, keep = project_band((0,), high, low, bands[1], before[2:])
-    pieces = add_parts((keep, rows_permute(give, 1), rows_permute(send, 2)), 4)
-    gram, = add_parts((gram, rows_permute(gram, 4)), 1)
+    give, keep, give_1, keep_1 = project(parts, high, low, (send_0,))
+    send_1, = add_parts((keep, rows_permute(give, 1)), 1, (gram,))
+    got_0 = rows_permute(send_0, 2)
+    pieces = piece_sums(
+        (keep_0, rows_permute(give_0, 1), got_0),
+        (keep_1, rows_permute(give_1, 1), rows_permute(send_1, 2)),
+    )
+    gram, = add_parts((gram, rows_permute(gram, 4)), 1, (got_0,))
     gram, = add_parts((gram, rows_permute(gram, 8)), 1, pieces)
     gram, = add_parts((gram, rows_permute(gram, 2)), 1)
     inverse = inverse_factor(gram, rows_permute(gram, 1), total_rows)
@@ -418,7 +492,7 @@
                 pairs.append((2 * i + y, 2 * to + (((i >> 2) & 1) ^ (k & 1))))
         gathered.append(lax.ppermute(pieces[k], ("rows", "cols"), pairs))
     parts = remainder_pieces(inverse, gathered)
-    core_scaled = scaled_core((first, second), inverse, math.sqrt(total_rows))
+    core_scaled = scaled_core(first, second, inverse, math.sqrt(total_rows))
     firsts = [parts[0]] + [rows_permute(parts[m], m) for m in (1, 2, 3)]
     later = [rows_permute(part, 4 * t) for t, part in zip((1, 2, 3), collect(firsts))]
     return core_scaled, arrange(firsts, later)

time: 72.4 us -> 72.2 us (level)
  starting transfers between devices: 25.6 us -> 28.1 us
  waiting for transfers between devices: 26.7 us -> 24.3 us
    ppermute x4, waiting for transfers between devices: 3.17 us -> 1.47 us  [local(): gathered.append(lax.ppermute(pieces[k], ('rows', 'cols'), pairs))]
    ppermute x14 -> x17, starting transfers between devices: 14.9 us -> 16.5 us  [rows_permute(): return lax.ppermute(value, 'rows', [(i, i ^ mask) for i in range(size)])]
    ppermute x14 -> x17, waiting for transfers between devices: 15.3 us -> 13.8 us  [rows_permute(): return lax.ppermute(value, 'rows', [(i, i ^ mask) for i in range(size)])]
    ppermute x4, starting transfers between devices: 7.58 us -> 8.51 us  [local(): gathered.append(lax.ppermute(pieces[k], ('rows', 'cols'), pairs))]
  transfers between devices with their start and end apart: 20 -> 23, of which waited for: 9 -> 10; matrix products, arithmetic and copies ran while one was open for 0% -> 0% of each run, Pallas kernels for 20% -> 19%
where the time goes in v6:
time: 72.2 us; the launch traced here: 72 us
  starting transfers between devices  28.1 us (39%)
  waiting for transfers between devices  24.3 us (34%)
  Pallas kernels  18.8 us (26%)
  between operations  0.8 us (1%)
    ppermute x17, starting transfers between devices, rows_permute(): return lax.ppermute(value, 'rows', [(i, i ^ mask) for i in range(size)])  16.5 us
    ppermute x17, waiting for transfers between devices, rows_permute(): return lax.ppermute(value, 'rows', [(i, i ^ mask) for i in range(size)])  13.8 us
    pallas_call x1, Pallas kernels, inverse_factor(): pl.pallas_call(body, in_specs=[VMEM] * 2, out_specs=VMEM, out_shape=on_ch...  9.14 us
    ppermute x4, starting transfers between devices, local(): gathered.append(lax.ppermute(pieces[k], ('rows', 'cols'), pairs))  8.51 us
    ppermute x1, waiting for transfers between devices, local(): got_0 = lax.ppermute(own_0, 'cols', swap)  5.7 us
    ppermute x1, waiting for transfers between devices, local(): got_1 = lax.ppermute(own_1, 'cols', swap)  3.25 us
    ppermute x1, starting transfers between devices, local(): got_0 = lax.ppermute(own_0, 'cols', swap)  3.03 us
    pallas_call x1, Pallas kernels, first_sketch(): pl.pallas_call(first_sketch_kernel, in_specs=[HBM] * 3, out_specs=[VMEM]...  2.66 us
  transfers between devices with their start and end apart: 23, of which 10 were waited for; matrix products, arithmetic and copies ran while one was open for 0% of the time, Pallas kernels for 19%

profile of v6, /device:TPU:0, one launch (start us, length us, event | category | flops | bytes accessed | tf_op | source)
XLA Modules:
  0.0 72.0 jit_solution(17673453040678799458)
XLA Ops:
  0.6 2.7 %first_sketch.1 = (f32[512,128]{1,0:T(8,128)S(1)}, f32[512,2048]{1,0:T(8,128)S(1)}) custom-call(s32[2,16]{1,0:T(2,128)} %bitcast.6, f32[512,2048]{1,0:T(8,128)} %whole_ref.1, s32[2,2048]{1,0:T(2,128)} %bitcast.4), custom_call_target="tpu_custom_call" | custom-call | flops 2097 | bytes 4194 | tf_op jit(solution)/shard_map/first_sketch/pallas_call | solution.py:93
  3.3 3.0 %collective-permute-start = (f32[512,128]{1,0:T(8,128)S(1)}, f32[512,128]{1,0:T(8,128)S(1)}, u32[]{:S(2)}, u32[]{:S(2)}) collective-permute-start(f32[512,128]{1,0:T(8,128)S(1)} %get-tuple-element.34.own_ref), channel_id=1, source_target_pairs={{0,1},{1,0},{2,3},{3,2},{4,5},{5,4},{6,7},{7,6},{8,9},{9,8},{10,11... | collective-permute-start | bytes 786440 | tf_op jit(solution)/shard_map/ppermute | solution.py:467
  6.3 1.3 %second_sketch.1 = (f32[512,128]{1,0:T(8,128)S(1)}, bf16[512,2048]{1,0:T(8,128)(2,1)S(1)}, bf16[512,2048]{1,0:T(8,128)(2,1)S(1)}) custom-call(s32[2,16]{1,0:T(2,128)} %bitcast.7, s32[2,2048]{1,0:T(2,128)} %bitcast.5, f32[512,2048]{1,0:T(8,128)S(1)} %get-tuple-element.36.block_ref), custom_call_target="tpu_custom_call" | custom-call | flops 2097 | bytes 4194 | tf_op jit(solution)/shard_map/second_sketch/pallas_call | solution.py:131
  7.7 0.1 collective-permute-start.1
  7.8 5.7 %collective-permute-done.got_ref = f32[512,128]{1,0:T(8,128)S(1)} collective-permute-done((f32[512,128]{1,0:T(8,128)S(1)}, f32[512,128]{1,0:T(8,128)S(1)}, u32[]{:S(2)}, u32[]{:S(2)}) %collective-permute-start) | collective-permute-done | bytes 262176 | tf_op jit(solution)/shard_map/ppermute | solution.py:467
  13.5 0.4 first_gram.1
  13.9 1.0 %project.2 = (f32[4,128,128]{2,1,0:T(8,128)S(1)}, f32[4,128,128]{2,1,0:T(8,128)S(1)}, f32[4,128,128]{2,1,0:T(8,128)S(1)}, f32[4,128,128]{2,1,0:T(8,128)S(1)}) custom-call(bf16[256,512]{1,0:T(8,128)(2,1)S(1)} %get-tuple-element.40.refs_0_, bf16[512,2048]{1,0:T(8,128)(2,1)S(1)} %get-tuple-element.41.refs_1_, bf16[512,2048]{1,0:T(8,128)(2,1)S(1)} %get-tuple-element.42.refs_2_), custom_call_target="tpu_custom_call" | custom-call | flops 805306 | bytes 4194 | tf_op jit(solution)/shard_map/project/pallas_call | solution.py:232
  14.9 0.1 collective-permute-start.4
  15.0 3.2 %collective-permute-done.1.refs_1_ = f32[512,128]{1,0:T(8,128)S(1)} collective-permute-done((f32[512,128]{1,0:T(8,128)S(1)}, f32[512,128]{1,0:T(8,128)S(1)}, u32[]{:S(2)}, u32[]{:S(2)}) %collective-permute-start.1) | collective-permute-done | bytes 262176 | tf_op jit(solution)/shard_map/ppermute | solution.py:469
  18.3 0.6 second_gram.1
  18.9 0.0 collective-permute-done.4.refs_1_
  18.9 1.0 %project.3 = (f32[4,128,128]{2,1,0:T(8,128)S(1)}, f32[4,128,128]{2,1,0:T(8,128)S(1)}, f32[4,128,128]{2,1,0:T(8,128)S(1)}, f32[4,128,128]{2,1,0:T(8,128)S(1)}) custom-call(bf16[256,512]{1,0:T(8,128)(2,1)S(1)} %get-tuple-element.50.refs_0_, bf16[512,2048]{1,0:T(8,128)(2,1)S(1)} %get-tuple-element.41.refs_1_, bf16[512,2048]{1,0:T(8,128)(2,1)S(1)} %get-tuple-element.42.refs_2_, ...), custom_call_target="tpu_custom_call" | custom-call | flops 805306 | bytes 4194 | tf_op jit(solution)/shard_map/project/pallas_call | solution.py:232
  20.0 0.1 collective-permute-start.9
  20.0 0.5 collective-permute-start.2
  20.5 1.7 %collective-permute-start.5 = (f32[4,128,128]{2,1,0:T(8,128)S(1)}, f32[4,128,128]{2,1,0:T(8,128)S(1)}, u32[]{:S(2)}, u32[]{:S(2)}) collective-permute-start(f32[4,128,128]{2,1,0:T(8,128)S(1)} %add_parts.7.refs_3_), channel_id=1, source_target_pairs={{0,4},{2,6},{4,0},{6,2},{8,12},{10,14},{12,8},{14,10},{16,20},{18,... | collective-permute-start | bytes 786440 | tf_op jit(solution)/shard_map/ppermute | solution.py:459
  22.2 0.0 collective-permute-start.7
  22.2 0.0 collective-permute-done.2.refs_1_
  22.3 0.6 collective-permute-start.8
  22.8 0.0 collective-permute-done.9.refs_1_
  22.9 0.9 %collective-permute-start.10 = (f32[4,128,128]{2,1,0:T(8,128)S(1)}, f32[4,128,128]{2,1,0:T(8,128)S(1)}, u32[]{:S(2)}, u32[]{:S(2)}) collective-permute-start(f32[4,128,128]{2,1,0:T(8,128)S(1)} %add_parts.9), channel_id=1, source_target_pairs={{0,4},{2,6},{4,0},{6,2},{8,12},{10,14},{12,8},{14,10},{16,20},{18,... | collective-permute-start | bytes 786440 | tf_op jit(solution)/shard_map/ppermute | solution.py:459
  23.7 1.6 %collective-permute-start.3 = (f32[192,128]{1,0:T(8,128)S(1)}, f32[192,128]{1,0:T(8,128)S(1)}, u32[]{:S(2)}, u32[]{:S(2)}) collective-permute-start(f32[192,128]{1,0:T(8,128)S(1)} %add_parts.6.refs_0_.refs_2_), channel_id=1, source_target_pairs={{0,8},{2,10},{4,12},{6,14},{8,0},{10,2},{12,4},{14,6},{16,24},{18,... | collective-permute-start | bytes 294920 | tf_op jit(solution)/shard_map/ppermute | solution.py:459
  25.3 3.2 %collective-permute-done.3.refs_1_ = f32[192,128]{1,0:T(8,128)S(1)} collective-permute-done((f32[192,128]{1,0:T(8,128)S(1)}, f32[192,128]{1,0:T(8,128)S(1)}, u32[]{:S(2)}, u32[]{:S(2)}) %collective-permute-start.3) | collective-permute-done | bytes 98336 | tf_op jit(solution)/shard_map/ppermute | solution.py:459
  28.5 1.2 %collective-permute-done.5.refs_2_ = f32[4,128,128]{2,1,0:T(8,128)S(1)} collective-permute-done((f32[4,128,128]{2,1,0:T(8,128)S(1)}, f32[4,128,128]{2,1,0:T(8,128)S(1)}, u32[]{:S(2)}, u32[]{:S(2)}) %collective-permute-start.5) | collective-permute-done | bytes 262176 | tf_op jit(solution)/shard_map/ppermute | solution.py:459
  29.7 2.9 %collective-permute-start.6 = (f32[192,128]{1,0:T(8,128)S(1)}, f32[192,128]{1,0:T(8,128)S(1)}, u32[]{:S(2)}, u32[]{:S(2)}) collective-permute-start(f32[192,128]{1,0:T(8,128)S(1)} %add_parts.8.refs_0_), channel_id=1, source_target_pairs={{0,16},{2,18},{4,20},{6,22},{8,24},{10,26},{12,28},{14,30},{16,0},... | collective-permute-start | bytes 294920 | tf_op jit(solution)/shard_map/ppermute | solution.py:459
  32.6 0.0 collective-permute-done.7.refs_1_
  32.6 0.0 collective-permute-done.8.refs_4_
  32.6 1.9 %collective-permute-done.10.refs_5_ = f32[4,128,128]{2,1,0:T(8,128)S(1)} collective-permute-done((f32[4,128,128]{2,1,0:T(8,128)S(1)}, f32[4,128,128]{2,1,0:T(8,128)S(1)}, u32[]{:S(2)}, u32[]{:S(2)}) %collective-permute-start.10) | collective-permute-done | bytes 262176 | tf_op jit(solution)/shard_map/ppermute | solution.py:459
  34.5 0.1 piece_sums.1
  34.5 0.8 %collective-permute-done.6.refs_1_ = f32[192,128]{1,0:T(8,128)S(1)} collective-permute-done((f32[192,128]{1,0:T(8,128)S(1)}, f32[192,128]{1,0:T(8,128)S(1)}, u32[]{:S(2)}, u32[]{:S(2)}) %collective-permute-start.6) | collective-permute-done | bytes 98336 | tf_op jit(solution)/shard_map/ppermute | solution.py:459
  35.3 1.8 %collective-permute-start.11 = (f32[192,128]{1,0:T(8,128)S(1)}, f32[192,128]{1,0:T(8,128)S(1)}, u32[]{:S(2)}, u32[]{:S(2)}) collective-permute-start(f32[192,128]{1,0:T(8,128)S(1)} %add_parts.10.refs_0_), channel_id=1, source_target_pairs={{0,4},{2,6},{4,0},{6,2},{8,12},{10,14},{12,8},{14,10},{16,20},{18,... | collective-permute-start | bytes 294920 | tf_op jit(solution)/shard_map/ppermute | solution.py:459
  37.1 0.7 collective-permute-start.13
  37.8 4.5 %collective-permute-start.14 = (f32[256,128]{1,0:T(8,128)S(1)}, f32[256,128]{1,0:T(8,128)S(1)}, u32[]{:S(2)}, u32[]{:S(2)}) collective-permute-start(f32[256,128]{1,0:T(8,128)S(1)} %get-tuple-element.56.refs_3_), channel_id=1, source_target_pairs={{0,1},{1,9},{2,3},{3,11},{4,5},{5,13},{6,7},{7,15},{8,0},{9,8},{10... | collective-permute-start | bytes 393224 | tf_op jit(solution)/shard_map/ppermute | solution.py:493
  42.2 3.4 %collective-permute-start.15 = (f32[256,128]{1,0:T(8,128)S(1)}, f32[256,128]{1,0:T(8,128)S(1)}, u32[]{:S(2)}, u32[]{:S(2)}) collective-permute-start(f32[256,128]{1,0:T(8,128)S(1)} %get-tuple-element.57.refs_4_), channel_id=1, source_target_pairs={{0,16},{1,24},{2,18},{3,26},{4,20},{5,28},{6,22},{7,30},{8,17},{9,... | collective-permute-start | bytes 393224 | tf_op jit(solution)/shard_map/ppermute | solution.py:493
  45.6 0.0 collective-permute-start.16
  45.6 0.0 collective-permute-done.11.refs_1_
  45.6 0.1 collective-permute-start.12
  45.7 1.3 %collective-permute-done.12.refs_1_ = f32[192,128]{1,0:T(8,128)S(1)} collective-permute-done((f32[192,128]{1,0:T(8,128)S(1)}, f32[192,128]{1,0:T(8,128)S(1)}, u32[]{:S(2)}, u32[]{:S(2)}) %collective-permute-start.12) | collective-permute-done | bytes 98336 | tf_op jit(solution)/shard_map/ppermute | solution.py:459
  47.0 9.1 %inverse_factor.1.refs_2_.inverse_ref = f32[256,256]{1,0:T(8,128)S(1)} custom-call(f32[192,128]{1,0:T(8,128)S(1)} %add_parts.11.refs_0_, f32[192,128]{1,0:T(8,128)S(1)} %collective-permute-done.12.refs_1_), custom_call_target="tpu_custom_call" | custom-call | bytes 524 | tf_op jit(solution)/shard_map/inverse_factor/pallas_call | solution.py:352
  56.1 0.0 collective-permute-done.13.p0
  56.2 1.5 %collective-permute-done.14.p1 = f32[256,128]{1,0:T(8,128)S(1)} collective-permute-done((f32[256,128]{1,0:T(8,128)S(1)}, f32[256,128]{1,0:T(8,128)S(1)}, u32[]{:S(2)}, u32[]{:S(2)}) %collective-permute-start.14) | collective-permute-done | bytes 131104 | tf_op jit(solution)/shard_map/ppermute | solution.py:493
  57.6 0.0 collective-permute-done.15.p2
  57.6 0.0 collective-permute-done.16.p3
  57.6 0.4 remainder_pieces.1
  58.0 0.1 collective-permute-start.17
  58.1 0.6 collective-permute-start.18
  58.7 1.3 %collective-permute-start.19 = (f32[4,16,128]{2,1,0:T(8,128)S(1)}, f32[4,16,128]{2,1,0:T(8,128)S(1)}, u32[]{:S(2)}, u32[]{:S(2)}) collective-permute-start(f32[4,16,128]{2,1,0:T(8,128)S(1)} %get-tuple-element.62), channel_id=1, source_target_pairs={{0,6},{2,4},{4,2},{6,0},{8,14},{10,12},{12,10},{14,8},{16,22},{18,... | collective-permute-start | bytes 98312 | tf_op jit(solution)/shard_map/ppermute | solution.py:459
  60.0 0.0 collective-permute-done.17.r1
  60.0 2.4 %collective-permute-done.18.r2 = f32[4,16,128]{2,1,0:T(8,128)S(1)} collective-permute-done((f32[4,16,128]{2,1,0:T(8,128)S(1)}, f32[4,16,128]{2,1,0:T(8,128)S(1)}, u32[]{:S(2)}, u32[]{:S(2)}) %collective-permute-start.18) | collective-permute-done | bytes 32800 | tf_op jit(solution)/shard_map/ppermute | solution.py:459
  62.4 0.0 collective-permute-done.19.r3
  62.4 0.1 collective-permute-start.20
  62.5 3.0 %collective-permute-start.21 = (f32[4,16,128]{2,1,0:T(8,128)S(1)}, f32[4,16,128]{2,1,0:T(8,128)S(1)}, u32[]{:S(2)}, u32[]{:S(2)}) collective-permute-start(f32[4,16,128]{2,1,0:T(8,128)S(1)} %get-tuple-element.64), channel_id=1, source_target_pairs={{0,16},{2,18},{4,20},{6,22},{8,24},{10,26},{12,28},{14,30},{16,0},... | collective-permute-start | bytes 98312 | tf_op jit(solution)/shard_map/ppermute | solution.py:459
  65.5 1.3 %collective-permute-start.22 = (f32[4,16,128]{2,1,0:T(8,128)S(1)}, f32[4,16,128]{2,1,0:T(8,128)S(1)}, u32[]{:S(2)}, u32[]{:S(2)}) collective-permute-start(f32[4,16,128]{2,1,0:T(8,128)S(1)} %get-tuple-element.65), channel_id=1, source_target_pairs={{0,24},{2,26},{4,28},{6,30},{8,16},{10,18},{12,20},{14,22},{16,8},... | collective-permute-start | bytes 98312 | tf_op jit(solution)/shard_map/ppermute | solution.py:459
  66.9 1.3 %scaled_core.1 = f32[512,256]{1,0:T(8,128)} custom-call(f32[512,128]{1,0:T(8,128)S(1)} %get-tuple-element.35.refs_0_, f32[512,128]{1,0:T(8,128)S(1)} %get-tuple-element.44.refs_1_, f32[256,256]{1,0:T(8,128)S(1)} %inverse_factor.1.refs_2_.inverse_ref), custom_call_target="tpu_custom_call" | custom-call | flops 201326 | bytes 1048 | tf_op jit(solution)/shard_map/scaled_core/pallas_call | solution.py:377
  68.1 0.0 collective-permute-done.20.s1
  68.1 0.0 collective-permute-done.21.s2
  68.1 3.1 %collective-permute-done.22.s3 = f32[4,16,128]{2,1,0:T(8,128)S(1)} collective-permute-done((f32[4,16,128]{2,1,0:T(8,128)S(1)}, f32[4,16,128]{2,1,0:T(8,128)S(1)}, u32[]{:S(2)}, u32[]{:S(2)}) %collective-permute-start.22) | collective-permute-done | bytes 32800 | tf_op jit(solution)/shard_map/ppermute | solution.py:459
  71.2 0.7 %arrange.1 = f32[16,8,256]{2,1,0:T(8,128)} custom-call(f32[4,16,128]{2,1,0:T(8,128)S(1)} %get-tuple-element.59.r0, f32[4,16,128]{2,1,0:T(8,128)S(1)} %collective-permute-done.17.r1, f32[4,16,128]{2,1,0:T(8,128)S(1)} %collective-permute-done.18.r2, f32[4,16,128]{2,1,0:T(8,128)S(1)} %collective-permute-done.19.r3, ...), custom_call_target="tpu_custom_call" | custom-call | bytes 131 | tf_op jit(solution)/shard_map/arrange/pallas_call | solution.py:444
  (7 shorter events, 0.1 us)
Async XLA Ops:
  3.3 10.2 %collective-permute-start = (f32[512,128]{1,0:T(8,128)S(1)}, f32[512,128]{1,0:T(8,128)S(1)}, u32[]{:S(2)}, u32[]{:S(2)}) collective-permute-start(f32[512,128]{1,0:T(8,128)S(1)} %get-tuple-element.34.own_ref), channel_id=1, source_target_pairs={{0,1},{1,0},{2,3},{3,2},{4,5},{5,4},{6,7},{7,6},{8,9},{9,8},{10,11... | collective-permute-start | bytes 786440 | tf_op jit(solution)/shard_map/ppermute | solution.py:467
  7.7 10.6 %collective-permute-start.1 = (f32[512,128]{1,0:T(8,128)S(1)}, f32[512,128]{1,0:T(8,128)S(1)}, u32[]{:S(2)}, u32[]{:S(2)}) collective-permute-start(f32[512,128]{1,0:T(8,128)S(1)} %get-tuple-element.37.refs_0_), channel_id=1, source_target_pairs={{0,1},{1,0},{2,3},{3,2},{4,5},{5,4},{6,7},{7,6},{8,9},{9,8},{10,11... | collective-permute-start | bytes 786440 | tf_op jit(solution)/shard_map/ppermute | solution.py:469
  14.9 4.0 %collective-permute-start.4 = (f32[4,128,128]{2,1,0:T(8,128)S(1)}, f32[4,128,128]{2,1,0:T(8,128)S(1)}, u32[]{:S(2)}, u32[]{:S(2)}) collective-permute-start(f32[4,128,128]{2,1,0:T(8,128)S(1)} %get-tuple-element.48), channel_id=1, source_target_pairs={{0,2},{2,0},{4,6},{6,4},{8,10},{10,8},{12,14},{14,12},{16,18},{18,... | collective-permute-start | bytes 786440 | tf_op jit(solution)/shard_map/ppermute | solution.py:459
  20.0 2.9 %collective-permute-start.9 = (f32[4,128,128]{2,1,0:T(8,128)S(1)}, f32[4,128,128]{2,1,0:T(8,128)S(1)}, u32[]{:S(2)}, u32[]{:S(2)}) collective-permute-start(f32[4,128,128]{2,1,0:T(8,128)S(1)} %get-tuple-element.54), channel_id=1, source_target_pairs={{0,2},{2,0},{4,6},{6,4},{8,10},{10,8},{12,14},{14,12},{16,18},{18,... | collective-permute-start | bytes 786440 | tf_op jit(solution)/shard_map/ppermute | solution.py:459
  20.0 2.2 %collective-permute-start.2 = (f32[192,128]{1,0:T(8,128)S(1)}, f32[192,128]{1,0:T(8,128)S(1)}, u32[]{:S(2)}, u32[]{:S(2)}) collective-permute-start(f32[192,128]{1,0:T(8,128)S(1)} %get-tuple-element.46), channel_id=1, source_target_pairs={{0,2},{2,0},{4,6},{6,4},{8,10},{10,8},{12,14},{14,12},{16,18},{18,... | collective-permute-start | bytes 294920 | tf_op jit(solution)/shard_map/ppermute | solution.py:459
  20.5 9.2 %collective-permute-start.5 = (f32[4,128,128]{2,1,0:T(8,128)S(1)}, f32[4,128,128]{2,1,0:T(8,128)S(1)}, u32[]{:S(2)}, u32[]{:S(2)}) collective-permute-start(f32[4,128,128]{2,1,0:T(8,128)S(1)} %add_parts.7.refs_3_), channel_id=1, source_target_pairs={{0,4},{2,6},{4,0},{6,2},{8,12},{10,14},{12,8},{14,10},{16,20},{18,... | collective-permute-start | bytes 786440 | tf_op jit(solution)/shard_map/ppermute | solution.py:459
  22.2 10.4 %collective-permute-start.7 = (f32[4,128,128]{2,1,0:T(8,128)S(1)}, f32[4,128,128]{2,1,0:T(8,128)S(1)}, u32[]{:S(2)}, u32[]{:S(2)}) collective-permute-start(f32[4,128,128]{2,1,0:T(8,128)S(1)} %get-tuple-element.49), channel_id=1, source_target_pairs={{0,2},{2,0},{4,6},{6,4},{8,10},{10,8},{12,14},{14,12},{16,18},{18,... | collective-permute-start | bytes 786440 | tf_op jit(solution)/shard_map/ppermute | solution.py:459
  22.3 10.3 %collective-permute-start.8 = (f32[4,128,128]{2,1,0:T(8,128)S(1)}, f32[4,128,128]{2,1,0:T(8,128)S(1)}, u32[]{:S(2)}, u32[]{:S(2)}) collective-permute-start(f32[4,128,128]{2,1,0:T(8,128)S(1)} %get-tuple-element.52), channel_id=1, source_target_pairs={{0,2},{2,0},{4,6},{6,4},{8,10},{10,8},{12,14},{14,12},{16,18},{18,... | collective-permute-start | bytes 786440 | tf_op jit(solution)/shard_map/ppermute | solution.py:459
  22.9 11.6 %collective-permute-start.10 = (f32[4,128,128]{2,1,0:T(8,128)S(1)}, f32[4,128,128]{2,1,0:T(8,128)S(1)}, u32[]{:S(2)}, u32[]{:S(2)}) collective-permute-start(f32[4,128,128]{2,1,0:T(8,128)S(1)} %add_parts.9), channel_id=1, source_target_pairs={{0,4},{2,6},{4,0},{6,2},{8,12},{10,14},{12,8},{14,10},{16,20},{18,... | collective-permute-start | bytes 786440 | tf_op jit(solution)/shard_map/ppermute | solution.py:459
  23.7 4.8 %collective-permute-start.3 = (f32[192,128]{1,0:T(8,128)S(1)}, f32[192,128]{1,0:T(8,128)S(1)}, u32[]{:S(2)}, u32[]{:S(2)}) collective-permute-start(f32[192,128]{1,0:T(8,128)S(1)} %add_parts.6.refs_0_.refs_2_), channel_id=1, source_target_pairs={{0,8},{2,10},{4,12},{6,14},{8,0},{10,2},{12,4},{14,6},{16,24},{18,... | collective-permute-start | bytes 294920 | tf_op jit(solution)/shard_map/ppermute | solution.py:459
  29.7 5.6 %collective-permute-start.6 = (f32[192,128]{1,0:T(8,128)S(1)}, f32[192,128]{1,0:T(8,128)S(1)}, u32[]{:S(2)}, u32[]{:S(2)}) collective-permute-start(f32[192,128]{1,0:T(8,128)S(1)} %add_parts.8.refs_0_), channel_id=1, source_target_pairs={{0,16},{2,18},{4,20},{6,22},{8,24},{10,26},{12,28},{14,30},{16,0},... | collective-permute-start | bytes 294920 | tf_op jit(solution)/shard_map/ppermute | solution.py:459
  35.3 10.3 %collective-permute-start.11 = (f32[192,128]{1,0:T(8,128)S(1)}, f32[192,128]{1,0:T(8,128)S(1)}, u32[]{:S(2)}, u32[]{:S(2)}) collective-permute-start(f32[192,128]{1,0:T(8,128)S(1)} %add_parts.10.refs_0_), channel_id=1, source_target_pairs={{0,4},{2,6},{4,0},{6,2},{8,12},{10,14},{12,8},{14,10},{16,20},{18,... | collective-permute-start | bytes 294920 | tf_op jit(solution)/shard_map/ppermute | solution.py:459
  37.1 19.1 %collective-permute-start.13 = (f32[256,128]{1,0:T(8,128)S(1)}, f32[256,128]{1,0:T(8,128)S(1)}, u32[]{:S(2)}, u32[]{:S(2)}) collective-permute-start(f32[256,128]{1,0:T(8,128)S(1)} %get-tuple-element.55.refs_2_), channel_id=1, source_target_pairs={{0,0},{1,8},{2,2},{3,10},{4,4},{5,12},{6,6},{7,14},{8,1},{9,9},{10... | collective-permute-start | bytes 393224 | tf_op jit(solution)/shard_map/ppermute | solution.py:493
  37.8 19.9 %collective-permute-start.14 = (f32[256,128]{1,0:T(8,128)S(1)}, f32[256,128]{1,0:T(8,128)S(1)}, u32[]{:S(2)}, u32[]{:S(2)}) collective-permute-start(f32[256,128]{1,0:T(8,128)S(1)} %get-tuple-element.56.refs_3_), channel_id=1, source_target_pairs={{0,1},{1,9},{2,3},{3,11},{4,5},{5,13},{6,7},{7,15},{8,0},{9,8},{10... | collective-permute-start | bytes 393224 | tf_op jit(solution)/shard_map/ppermute | solution.py:493
  42.2 15.4 %collective-permute-start.15 = (f32[256,128]{1,0:T(8,128)S(1)}, f32[256,128]{1,0:T(8,128)S(1)}, u32[]{:S(2)}, u32[]{:S(2)}) collective-permute-start(f32[256,128]{1,0:T(8,128)S(1)} %get-tuple-element.57.refs_4_), channel_id=1, source_target_pairs={{0,16},{1,24},{2,18},{3,26},{4,20},{5,28},{6,22},{7,30},{8,17},{9,... | collective-permute-start | bytes 393224 | tf_op jit(solution)/shard_map/ppermute | solution.py:493
  45.6 12.0 %collective-permute-start.16 = (f32[256,128]{1,0:T(8,128)S(1)}, f32[256,128]{1,0:T(8,128)S(1)}, u32[]{:S(2)}, u32[]{:S(2)}) collective-permute-start(f32[256,128]{1,0:T(8,128)S(1)} %get-tuple-element.58.refs_5_), channel_id=1, source_target_pairs={{0,17},{1,25},{2,19},{3,27},{4,21},{5,29},{6,23},{7,31},{8,16},{9,... | collective-permute-start | bytes 393224 | tf_op jit(solution)/shard_map/ppermute | solution.py:493
  45.6 1.4 %collective-permute-start.12 = (f32[192,128]{1,0:T(8,128)S(1)}, f32[192,128]{1,0:T(8,128)S(1)}, u32[]{:S(2)}, u32[]{:S(2)}) collective-permute-start(f32[192,128]{1,0:T(8,128)S(1)} %add_parts.11.refs_0_), channel_id=1, source_target_pairs={{0,2},{2,0},{4,6},{6,4},{8,10},{10,8},{12,14},{14,12},{16,18},{18,... | collective-permute-start | bytes 294920 | tf_op jit(solution)/shard_map/ppermute | solution.py:459
  58.0 1.9 %collective-permute-start.17 = (f32[4,16,128]{2,1,0:T(8,128)S(1)}, f32[4,16,128]{2,1,0:T(8,128)S(1)}, u32[]{:S(2)}, u32[]{:S(2)}) collective-permute-start(f32[4,16,128]{2,1,0:T(8,128)S(1)} %get-tuple-element.60), channel_id=1, source_target_pairs={{0,2},{2,0},{4,6},{6,4},{8,10},{10,8},{12,14},{14,12},{16,18},{18,... | collective-permute-start | bytes 98312 | tf_op jit(solution)/shard_map/ppermute | solution.py:459
  58.1 4.3 %collective-permute-start.18 = (f32[4,16,128]{2,1,0:T(8,128)S(1)}, f32[4,16,128]{2,1,0:T(8,128)S(1)}, u32[]{:S(2)}, u32[]{:S(2)}) collective-permute-start(f32[4,16,128]{2,1,0:T(8,128)S(1)} %get-tuple-element.61), channel_id=1, source_target_pairs={{0,4},{2,6},{4,0},{6,2},{8,12},{10,14},{12,8},{14,10},{16,20},{18,... | collective-permute-start | bytes 98312 | tf_op jit(solution)/shard_map/ppermute | solution.py:459
  58.7 3.7 %collective-permute-start.19 = (f32[4,16,128]{2,1,0:T(8,128)S(1)}, f32[4,16,128]{2,1,0:T(8,128)S(1)}, u32[]{:S(2)}, u32[]{:S(2)}) collective-permute-start(f32[4,16,128]{2,1,0:T(8,128)S(1)} %get-tuple-element.62), channel_id=1, source_target_pairs={{0,6},{2,4},{4,2},{6,0},{8,14},{10,12},{12,10},{14,8},{16,22},{18,... | collective-permute-start | bytes 98312 | tf_op jit(solution)/shard_map/ppermute | solution.py:459
  62.4 5.7 %collective-permute-start.20 = (f32[4,16,128]{2,1,0:T(8,128)S(1)}, f32[4,16,128]{2,1,0:T(8,128)S(1)}, u32[]{:S(2)}, u32[]{:S(2)}) collective-permute-start(f32[4,16,128]{2,1,0:T(8,128)S(1)} %get-tuple-element.63), channel_id=1, source_target_pairs={{0,8},{2,10},{4,12},{6,14},{8,0},{10,2},{12,4},{14,6},{16,24},{18,... | collective-permute-start | bytes 98312 | tf_op jit(solution)/shard_map/ppermute | solution.py:459
  62.5 5.7 %collective-permute-start.21 = (f32[4,16,128]{2,1,0:T(8,128)S(1)}, f32[4,16,128]{2,1,0:T(8,128)S(1)}, u32[]{:S(2)}, u32[]{:S(2)}) collective-permute-start(f32[4,16,128]{2,1,0:T(8,128)S(1)} %get-tuple-element.64), channel_id=1, source_target_pairs={{0,16},{2,18},{4,20},{6,22},{8,24},{10,26},{12,28},{14,30},{16,0},... | collective-permute-start | bytes 98312 | tf_op jit(solution)/shard_map/ppermute | solution.py:459
  65.5 5.7 %collective-permute-start.22 = (f32[4,16,128]{2,1,0:T(8,128)S(1)}, f32[4,16,128]{2,1,0:T(8,128)S(1)}, u32[]{:S(2)}, u32[]{:S(2)}) collective-permute-start(f32[4,16,128]{2,1,0:T(8,128)S(1)} %get-tuple-element.65), channel_id=1, source_target_pairs={{0,24},{2,26},{4,28},{6,30},{8,16},{10,18},{12,20},{14,22},{16,8},... | collective-permute-start | bytes 98312 | tf_op jit(solution)/shard_map/ppermute | solution.py:459

commit v7 on v5

--- a/solution.py
+++ b/solution.py
@@ -163,15 +163,13 @@
     row = lax.axis_index("rows")
     core, right, near, far = row & 1, (row >> 1) & 1, (row >> 2) & 1, row >> 3
     for i, flip in enumerate(flips):
-        for t in range(4):
-            block = (far ^ (t >> 1)) * 4 + (right ^ flip) * 2 + (near ^ (t & 1))
-            a_high, a_low = split(band_ref[:, pl.ds(pl.multiple_of(block * 2 * BLK, 2 * BLK), 2 * BLK)])
-            total = dot(high_ref[...], a_high) + dot(high_ref[...], a_low) + dot(low_ref[...], a_high)
-            left, other = total[:, :BLK], total[:, BLK:]
-            give = jnp.where(core == 0, other, left)
-            keep = jnp.where(core == 0, left, other)
-            outs[2 * i][t] = give if before is None else give + before[2 * i][t]
-            outs[2 * i + 1][t] = keep if before is None else keep + before[2 * i + 1][t]
+        for side in range(2):
+            out = outs[2 * i + side]
+            for t in range(2):
+                block = (far ^ core ^ 1 ^ side) * 4 + (right ^ flip) * 2 + (near ^ t)
+                a_high, a_low = split(band_ref[:, pl.ds(pl.multiple_of(block * 2 * BLK, 2 * BLK), 2 * BLK)])
+                total = dot(high_ref[...], a_high) + dot(high_ref[...], a_low) + dot(low_ref[...], a_high)
+                out[t] = total if before is None else total + before[2 * i + side][t]
 
 
 def project_band(flips, high, low, band, before=(), after=()):
@@ -186,7 +184,7 @@
         body,
         in_specs=[VMEM] * len(operands),
         out_specs=[VMEM] * count,
-        out_shape=[on_chip(4, RANK, BLK)] * count,
+        out_shape=[on_chip(2, RANK, 2 * BLK)] * count,
         cost_estimate=cost(rows * cols * RANK * 3 * len(flips), rows * cols * 4),
         compiler_params=LIMIT,
         name="project_band",
@@ -315,8 +313,8 @@
     )(*held(*sketches, inverse))
 
 
-def remainder_kernel(inverse_ref, p0, p1, p2, p3, o0, o1, o2, o3, work):
-    work[...] = jnp.dot(inverse_ref[...], (p0[...] + p1[...]) + (p2[...] + p3[...]), precision=HIGHEST)
+def remainder_kernel(inverse_ref, p0, p1, o0, o1, o2, o3, work):
+    work[...] = jnp.dot(inverse_ref[...], p0[...] + p1[...], precision=HIGHEST)
     device = lax.axis_index("rows")
     for m, out in enumerate((o0, o1, o2, o3)):
         for t in range(4):
@@ -327,60 +325,56 @@
 def remainder_pieces(inverse, pieces):
     return pl.pallas_call(
         remainder_kernel,
-        in_specs=[VMEM] * 5,
+        in_specs=[VMEM] * 3,
         out_specs=[VMEM] * 4,
-        out_shape=[on_chip(4, 16, BLK)] * 4,
-        scratch_shapes=[pltpu.VMEM((RANK, BLK), F32)],
-        cost_estimate=cost(RANK * RANK * BLK * 12, RANK * BLK * 8),
+        out_shape=[on_chip(4, 16, 2 * BLK)] * 4,
+        scratch_shapes=[pltpu.VMEM((RANK, 2 * BLK), F32)],
+        cost_estimate=cost(RANK * RANK * BLK * 24, RANK * BLK * 16),
         compiler_params=LIMIT,
         name="remainder_pieces",
     )(*held(inverse, *pieces))
 
 
-def collect_kernel(r0, r1, r2, r3, o1, o2, o3):
-    for t, out in ((1, o1), (2, o2), (3, o3)):
-        for m, piece in enumerate((r0, r1, r2, r3)):
-            out[m] = piece[t]
+def collect_kernel(r0, r1, r2, r3, o0, o1, o2, o3):
+    for t, out in enumerate((o0, o1, o2, o3)):
+        out[0] = r0[t] + r1[t]
+        out[1] = r2[t] + r3[t]
 
 
 def collect(firsts):
     return pl.pallas_call(
         collect_kernel,
         in_specs=[VMEM] * 4,
-        out_specs=[VMEM] * 3,
-        out_shape=[on_chip(4, 16, BLK)] * 3,
+        out_specs=[VMEM] * 4,
+        out_shape=[on_chip(2, 16, 2 * BLK)] * 4,
         cost_estimate=cost(0, 16 * BLK * 64),
         compiler_params=LIMIT,
         name="collect",
     )(*held(*firsts))
 
 
-def arrange_kernel(r0, r1, r2, r3, s1, s2, s3, out_ref, work):
+def arrange_kernel(p0, p1, p2, p3, out_ref, work):
     row = lax.axis_index("rows")
-    core, right, deep = row & 1, (row >> 1) & 1, row >> 2
-    firsts = (r0, r1, r2, r3)
-    later = (None, s1, s2, s3)
-    for t in range(4):
-        for m in range(4):
-            there = deep ^ t
-            mode = (there & 1) * 4 + (there >> 1) * 2 + (right ^ (m >> 1))
-            work[mode, core ^ (m & 1)] = firsts[m][0] if t == 0 else later[t][m]
+    right, deep = (row >> 1) & 1, row >> 2
+    for t, piece in enumerate((p0, p1, p2, p3)):
+        there = deep ^ t
+        for m in range(2):
+            work[(there & 1) * 4 + (there >> 1) * 2 + (right ^ m)] = piece[m]
     for mode in range(MODE):
-        for c in range(2):
-            out_ref[:, mode, c * BLK : (c + 1) * BLK] = work[mode, c]
-
-
-def arrange(firsts, later):
+        out_ref[:, mode, :] = work[mode]
+
+
+def arrange(pieces):
     out = pl.pallas_call(
         arrange_kernel,
-        in_specs=[VMEM] * 7,
+        in_specs=[VMEM] * 4,
         out_specs=VMEM,
         out_shape=jax.ShapeDtypeStruct((16, MODE, 2 * BLK), F32),
-        scratch_shapes=[pltpu.VMEM((MODE, 2, 16, BLK), F32)],
+        scratch_shapes=[pltpu.VMEM((MODE, 16, 2 * BLK), F32)],
         cost_estimate=cost(0, 16 * BLK * 64),
         compiler_params=LIMIT,
         name="arrange",
-    )(*held(*firsts, *later))
+    )(*held(*pieces))
     return out.reshape(16 * MODE, 2 * BLK)
 
 
@@ -404,24 +398,24 @@
     give, keep = project_band((1,), high, low, bands[1], before[:2])
     send, = add_parts((keep, rows_permute(give, 1)), 1, (gram,))
     give, keep = project_band((0,), high, low, bands[1], before[2:])
-    pieces = add_parts((keep, rows_permute(give, 1), rows_permute(send, 2)), 4)
+    give_got, send_got = rows_permute(give, 1), rows_permute(send, 2)
     gram, = add_parts((gram, rows_permute(gram, 4)), 1)
-    gram, = add_parts((gram, rows_permute(gram, 8)), 1, pieces)
+    gram, = add_parts((gram, rows_permute(gram, 8)), 1)
     gram, = add_parts((gram, rows_permute(gram, 2)), 1)
+    pieces = add_parts((keep, give_got, send_got), 2, (gram,))
     inverse = inverse_factor(gram, rows_permute(gram, 1), total_rows)
     gathered = []
-    for k in range(4):
+    for k in range(2):
         pairs = []
         for i in range(16):
             for y in range(2):
-                to = (i & 3) | (y << 2) | ((i & 8) ^ ((k >> 1) << 3))
-                pairs.append((2 * i + y, 2 * to + (((i >> 2) & 1) ^ (k & 1))))
+                to = (i & 3) | (y << 2) | ((i & 8) ^ ((i & 1) << 3))
+                pairs.append((2 * i + y, 2 * to + (((i >> 2) & 1) ^ k)))
         gathered.append(lax.ppermute(pieces[k], ("rows", "cols"), pairs))
     parts = remainder_pieces(inverse, gathered)
     core_scaled = scaled_core((first, second), inverse, math.sqrt(total_rows))
-    firsts = [parts[0]] + [rows_permute(parts[m], m) for m in (1, 2, 3)]
-    later = [rows_permute(part, 4 * t) for t, part in zip((1, 2, 3), collect(firsts))]
-    return core_scaled, arrange(firsts, later)
+    sums = collect([parts[0]] + [rows_permute(parts[m], m) for m in (1, 2, 3)])
+    return core_scaled, arrange([sums[0]] + [rows_permute(sums[t], 4 * t) for t in (1, 2, 3)])
 
 
 def sketch_matrix(pattern, sign_bits, block_size):

time: 72.4 us -> 74.3 us (1.026)
  waiting for transfers between devices: 26.7 us -> 32.7 us
  starting transfers between devices: 25.6 us -> 21.1 us
    ppermute x14, waiting for transfers between devices: 15.3 us -> 19.5 us  [rows_permute(): return lax.ppermute(value, 'rows', [(i, i ^ mask) for i in range(size)])]
    ppermute x4 -> x2, starting transfers between devices: 7.58 us -> 4.09 us  [local(): gathered.append(lax.ppermute(pieces[k], ('rows', 'cols'), pairs))]
    ppermute x4 -> x2, waiting for transfers between devices: 3.17 us -> 4.92 us  [local(): gathered.append(lax.ppermute(pieces[k], ('rows', 'cols'), pairs))]
    ppermute x14, starting transfers between devices: 14.9 us -> 13.9 us  [rows_permute(): return lax.ppermute(value, 'rows', [(i, i ^ mask) for i in range(size)])]
  transfers between devices with their start and end apart: 20 -> 18, of which waited for: 9 -> 11; matrix products, arithmetic and copies ran while one was open for 0% -> 0% of each run, Pallas kernels for 20% -> 20%
where the time goes in v7:
time: 74.3 us; the launch traced here: 73.7 us
  waiting for transfers between devices  32.7 us (44%)
  starting transfers between devices  21.1 us (28%)
  Pallas kernels  19.1 us (26%)
  between operations  0.8 us (1%)
    ppermute x14, waiting for transfers between devices, rows_permute(): return lax.ppermute(value, 'rows', [(i, i ^ mask) for i in range(size)])  19.5 us
    ppermute x14, starting transfers between devices, rows_permute(): return lax.ppermute(value, 'rows', [(i, i ^ mask) for i in range(size)])  13.9 us
    pallas_call x1, Pallas kernels, inverse_factor(): pl.pallas_call(body, in_specs=[VMEM] * 2, out_specs=VMEM, out_shape=on_ch...  9.14 us
    ppermute x2, waiting for transfers between devices, local(): got.append(lax.ppermute(part, 'cols', [(0, 1), (1, 0)]))  8.27 us
    ppermute x2, waiting for transfers between devices, local(): gathered.append(lax.ppermute(pieces[k], ('rows', 'cols'), pairs))  4.92 us
    pallas_call x2, Pallas kernels, sketch_band(): pl.pallas_call(body, in_specs=[HBM] * 3, out_specs=[VMEM] * 2, out_shape=...  4.13 us
    ppermute x2, starting transfers between devices, local(): gathered.append(lax.ppermute(pieces[k], ('rows', 'cols'), pairs))  4.09 us
    ppermute x2, starting transfers between devices, local(): got.append(lax.ppermute(part, 'cols', [(0, 1), (1, 0)]))  3.12 us
  transfers between devices with their start and end apart: 18, of which 11 were waited for; matrix products, arithmetic and copies ran while one was open for 0% of the time, Pallas kernels for 20%

profile of v7, /device:TPU:0, one launch (start us, length us, event | category | flops | bytes accessed | tf_op | source)
XLA Modules:
  0.0 73.7 jit_solution(17425431353945544671)
XLA Ops:
  0.6 2.1 %sketch_band.2 = (f32[256,256]{1,0:T(8,128)S(1)}, f32[256,2048]{1,0:T(8,128)S(1)}) custom-call(s32[2,16]{1,0:T(2,128)} %bitcast.6, f32[512,2048]{1,0:T(8,128)} %refs_1_.3, s32[2,2048]{1,0:T(2,128)} %bitcast.4), custom_call_target="tpu_custom_call" | custom-call | flops 2097152 | bytes 2097152 | tf_op jit(solution)/shard_map/sketch_band/pallas_call | solution.py:96
  2.7 3.0 %collective-permute-start = (f32[256,256]{1,0:T(8,128)S(1)}, f32[256,256]{1,0:T(8,128)S(1)}, u32[]{:S(2)}, u32[]{:S(2)}) collective-permute-start(f32[256,256]{1,0:T(8,128)S(1)} %get-tuple-element.33.refs_0_), channel_id=1, source_target_pairs={{0,1},{1,0},{2,3},{3,2},{4,5},{5,4},{6,7},{7,6},{8,9},{9,8},{10,11... | collective-permute-start | bytes 786440 | tf_op jit(solution)/shard_map/ppermute | solution.py:393
  5.7 2.1 %sketch_band.3 = (f32[256,256]{1,0:T(8,128)S(1)}, f32[256,2048]{1,0:T(8,128)S(1)}) custom-call(s32[2,16]{1,0:T(2,128)} %bitcast.7, f32[512,2048]{1,0:T(8,128)} %refs_1_.3, s32[2,2048]{1,0:T(2,128)} %bitcast.5), custom_call_target="tpu_custom_call" | custom-call | flops 2097152 | bytes 2097152 | tf_op jit(solution)/shard_map/sketch_band/pallas_call | solution.py:96
  7.8 0.1 collective-permute-start.1
  7.9 5.0 %collective-permute-done.refs_1_ = f32[256,256]{1,0:T(8,128)S(1)} collective-permute-done((f32[256,256]{1,0:T(8,128)S(1)}, f32[256,256]{1,0:T(8,128)S(1)}, u32[]{:S(2)}, u32[]{:S(2)}) %collective-permute-start) | collective-permute-done | bytes 262176 | tf_op jit(solution)/shard_map/ppermute | solution.py:393
  12.9 0.4 gram_band.2
  13.3 1.0 %project_band.3 = (f32[2,256,256]{2,1,0:T(8,128)S(1)}, f32[2,256,256]{2,1,0:T(8,128)S(1)}, f32[2,256,256]{2,1,0:T(8,128)S(1)}, f32[2,256,256]{2,1,0:T(8,128)S(1)}) custom-call(bf16[256,256]{1,0:T(8,128)(2,1)S(1)} %get-tuple-element.37.refs_0_, bf16[256,256]{1,0:T(8,128)(2,1)S(1)} %get-tuple-element.38.refs_1_, f32[256,2048]{1,0:T(8,128)S(1)} %get-tuple-element.39.refs_2_), custom_call_target="tpu_custom_call" | custom-call | flops 805306368 | bytes 2097152 | tf_op jit(solution)/shard_map/project_band/pallas_call | solution.py:183
  14.4 3.3 %collective-permute-done.1.refs_1_ = f32[256,256]{1,0:T(8,128)S(1)} collective-permute-done((f32[256,256]{1,0:T(8,128)S(1)}, f32[256,256]{1,0:T(8,128)S(1)}, u32[]{:S(2)}, u32[]{:S(2)}) %collective-permute-start.1) | collective-permute-done | bytes 262176 | tf_op jit(solution)/shard_map/ppermute | solution.py:393
  17.7 0.5 gram_band.3
  18.1 0.6 project_band.5
  18.8 0.1 collective-permute-start.8
  18.9 0.5 collective-permute-start.2
  19.4 0.6 project_band.4
  20.0 0.1 collective-permute-start.7
  20.1 0.8 %collective-permute-done.2.refs_1_ = f32[192,128]{1,0:T(8,128)S(1)} collective-permute-done((f32[192,128]{1,0:T(8,128)S(1)}, f32[192,128]{1,0:T(8,128)S(1)}, u32[]{:S(2)}, u32[]{:S(2)}) %collective-permute-start.2) | collective-permute-done | bytes 98336 | tf_op jit(solution)/shard_map/ppermute | solution.py:383
  20.9 0.0 collective-permute-done.8.refs_1_
  20.9 0.1 add_parts.10
  21.0 1.8 %collective-permute-start.9 = (f32[2,256,256]{2,1,0:T(8,128)S(1)}, f32[2,256,256]{2,1,0:T(8,128)S(1)}, u32[]{:S(2)}, u32[]{:S(2)}) collective-permute-start(f32[2,256,256]{2,1,0:T(8,128)S(1)} %add_parts.10), channel_id=1, source_target_pairs={{0,4},{2,6},{4,0},{6,2},{8,12},{10,14},{12,8},{14,10},{16,20},{18,... | collective-permute-start | bytes 1572872 | tf_op jit(solution)/shard_map/ppermute | solution.py:383
  22.8 1.6 %collective-permute-start.3 = (f32[192,128]{1,0:T(8,128)S(1)}, f32[192,128]{1,0:T(8,128)S(1)}, u32[]{:S(2)}, u32[]{:S(2)}) collective-permute-start(f32[192,128]{1,0:T(8,128)S(1)} %add_parts.6.refs_0_.refs_2_), channel_id=1, source_target_pairs={{0,8},{2,10},{4,12},{6,14},{8,0},{10,2},{12,4},{14,6},{16,24},{18,... | collective-permute-start | bytes 294920 | tf_op jit(solution)/shard_map/ppermute | solution.py:383
  24.3 3.0 %collective-permute-done.3.refs_1_ = f32[192,128]{1,0:T(8,128)S(1)} collective-permute-done((f32[192,128]{1,0:T(8,128)S(1)}, f32[192,128]{1,0:T(8,128)S(1)}, u32[]{:S(2)}, u32[]{:S(2)}) %collective-permute-start.3) | collective-permute-done | bytes 98336 | tf_op jit(solution)/shard_map/ppermute | solution.py:383
  27.4 2.7 %collective-permute-start.4 = (f32[192,128]{1,0:T(8,128)S(1)}, f32[192,128]{1,0:T(8,128)S(1)}, u32[]{:S(2)}, u32[]{:S(2)}) collective-permute-start(f32[192,128]{1,0:T(8,128)S(1)} %add_parts.7.refs_0_), channel_id=1, source_target_pairs={{0,16},{2,18},{4,20},{6,22},{8,24},{10,26},{12,28},{14,30},{16,0},... | collective-permute-start | bytes 294920 | tf_op jit(solution)/shard_map/ppermute | solution.py:383
  30.0 4.1 %collective-permute-done.4.refs_1_ = f32[192,128]{1,0:T(8,128)S(1)} collective-permute-done((f32[192,128]{1,0:T(8,128)S(1)}, f32[192,128]{1,0:T(8,128)S(1)}, u32[]{:S(2)}, u32[]{:S(2)}) %collective-permute-start.4) | collective-permute-done | bytes 98336 | tf_op jit(solution)/shard_map/ppermute | solution.py:383
  34.2 0.6 collective-permute-start.5
  34.7 4.1 %collective-permute-done.5.refs_1_ = f32[192,128]{1,0:T(8,128)S(1)} collective-permute-done((f32[192,128]{1,0:T(8,128)S(1)}, f32[192,128]{1,0:T(8,128)S(1)}, u32[]{:S(2)}, u32[]{:S(2)}) %collective-permute-start.5) | collective-permute-done | bytes 98336 | tf_op jit(solution)/shard_map/ppermute | solution.py:383
  38.9 0.0 collective-permute-done.7.refs_1_
  38.9 0.0 collective-permute-done.9.refs_2_
  38.9 0.1 add_parts.11
  39.0 0.7 collective-permute-start.10
  39.7 3.4 %collective-permute-start.11 = (f32[256,256]{1,0:T(8,128)S(1)}, f32[256,256]{1,0:T(8,128)S(1)}, u32[]{:S(2)}, u32[]{:S(2)}) collective-permute-start(f32[256,256]{1,0:T(8,128)S(1)} %get-tuple-element.55), channel_id=1, source_target_pairs={{0,1},{1,9},{2,19},{3,27},{4,5},{5,13},{6,23},{7,31},{8,0},{9,8},{... | collective-permute-start | bytes 786440 | tf_op jit(solution)/shard_map/ppermute | solution.py:414
  43.1 0.0 collective-permute-start.6
  43.1 1.3 %collective-permute-done.6.refs_1_ = f32[192,128]{1,0:T(8,128)S(1)} collective-permute-done((f32[192,128]{1,0:T(8,128)S(1)}, f32[192,128]{1,0:T(8,128)S(1)}, u32[]{:S(2)}, u32[]{:S(2)}) %collective-permute-start.6) | collective-permute-done | bytes 98336 | tf_op jit(solution)/shard_map/ppermute | solution.py:383
  44.4 9.1 %inverse_factor.1.refs_2_.inverse_ref = f32[256,256]{1,0:T(8,128)S(1)} custom-call(f32[192,128]{1,0:T(8,128)S(1)} %add_parts.9.refs_0_.refs_3_, f32[192,128]{1,0:T(8,128)S(1)} %collective-permute-done.6.refs_1_), custom_call_target="tpu_custom_call" | custom-call | bytes 524288 | tf_op jit(solution)/shard_map/inverse_factor/pallas_call | solution.py:278
  53.5 0.0 collective-permute-done.10.p0
  53.6 4.9 %collective-permute-done.11.p1 = f32[256,256]{1,0:T(8,128)S(1)} collective-permute-done((f32[256,256]{1,0:T(8,128)S(1)}, f32[256,256]{1,0:T(8,128)S(1)}, u32[]{:S(2)}, u32[]{:S(2)}) %collective-permute-start.11) | collective-permute-done | bytes 262176 | tf_op jit(solution)/shard_map/ppermute | solution.py:414
  58.5 0.4 remainder_pieces.1
  58.9 0.1 collective-permute-start.12
  59.0 2.1 %collective-permute-start.13 = (f32[4,16,256]{2,1,0:T(8,128)S(1)}, f32[4,16,256]{2,1,0:T(8,128)S(1)}, u32[]{:S(2)}, u32[]{:S(2)}) collective-permute-start(f32[4,16,256]{2,1,0:T(8,128)S(1)} %get-tuple-element.58), channel_id=1, source_target_pairs={{0,4},{2,6},{4,0},{6,2},{8,12},{10,14},{12,8},{14,10},{16,20},{18,... | collective-permute-start | bytes 196616 | tf_op jit(solution)/shard_map/ppermute | solution.py:383
  61.0 0.1 collective-permute-start.14
  61.1 0.0 collective-permute-done.12.r1
  61.1 2.6 %collective-permute-done.13.r2 = f32[4,16,256]{2,1,0:T(8,128)S(1)} collective-permute-done((f32[4,16,256]{2,1,0:T(8,128)S(1)}, f32[4,16,256]{2,1,0:T(8,128)S(1)}, u32[]{:S(2)}, u32[]{:S(2)}) %collective-permute-start.13) | collective-permute-done | bytes 65568 | tf_op jit(solution)/shard_map/ppermute | solution.py:383
  63.7 1.4 %collective-permute-done.14.r3 = f32[4,16,256]{2,1,0:T(8,128)S(1)} collective-permute-done((f32[4,16,256]{2,1,0:T(8,128)S(1)}, f32[4,16,256]{2,1,0:T(8,128)S(1)}, u32[]{:S(2)}, u32[]{:S(2)}) %collective-permute-start.14) | collective-permute-done | bytes 65568 | tf_op jit(solution)/shard_map/ppermute | solution.py:383
  65.1 0.1 collective-permute-start.15
  65.2 2.1 %collective-permute-start.16 = (f32[2,16,256]{2,1,0:T(8,128)S(1)}, f32[2,16,256]{2,1,0:T(8,128)S(1)}, u32[]{:S(2)}, u32[]{:S(2)}) collective-permute-start(f32[2,16,256]{2,1,0:T(8,128)S(1)} %get-tuple-element.62), channel_id=1, source_target_pairs={{0,16},{2,18},{4,20},{6,22},{8,24},{10,26},{12,28},{14,30},{16,0},... | collective-permute-start | bytes 98312 | tf_op jit(solution)/shard_map/ppermute | solution.py:383
  67.3 2.3 %collective-permute-start.17 = (f32[2,16,256]{2,1,0:T(8,128)S(1)}, f32[2,16,256]{2,1,0:T(8,128)S(1)}, u32[]{:S(2)}, u32[]{:S(2)}) collective-permute-start(f32[2,16,256]{2,1,0:T(8,128)S(1)} %get-tuple-element.63), channel_id=1, source_target_pairs={{0,24},{2,26},{4,28},{6,30},{8,16},{10,18},{12,20},{14,22},{16,8},... | collective-permute-start | bytes 98312 | tf_op jit(solution)/shard_map/ppermute | solution.py:383
  69.5 1.3 %scaled_core.1 = f32[512,256]{1,0:T(8,128)} custom-call(f32[256,256]{1,0:T(8,128)S(1)} %get-tuple-element.34.refs_0_, f32[256,256]{1,0:T(8,128)S(1)} %get-tuple-element.41.refs_1_, f32[256,256]{1,0:T(8,128)S(1)} %inverse_factor.1.refs_2_.inverse_ref), custom_call_target="tpu_custom_call" | custom-call | flops 201326592 | bytes 1048576 | tf_op jit(solution)/shard_map/scaled_core/pallas_call | solution.py:305
  70.8 0.0 collective-permute-done.15.p1
  70.8 0.0 collective-permute-done.16.p2
  70.8 2.1 %collective-permute-done.17.p3 = f32[2,16,256]{2,1,0:T(8,128)S(1)} collective-permute-done((f32[2,16,256]{2,1,0:T(8,128)S(1)}, f32[2,16,256]{2,1,0:T(8,128)S(1)}, u32[]{:S(2)}, u32[]{:S(2)}) %collective-permute-start.17) | collective-permute-done | bytes 32800 | tf_op jit(solution)/shard_map/ppermute | solution.py:383
  73.0 0.7 arrange.1
  (5 shorter events, 0.1 us)
Async XLA Ops:
  2.7 10.2 %collective-permute-start = (f32[256,256]{1,0:T(8,128)S(1)}, f32[256,256]{1,0:T(8,128)S(1)}, u32[]{:S(2)}, u32[]{:S(2)}) collective-permute-start(f32[256,256]{1,0:T(8,128)S(1)} %get-tuple-element.33.refs_0_), channel_id=1, source_target_pairs={{0,1},{1,0},{2,3},{3,2},{4,5},{5,4},{6,7},{7,6},{8,9},{9,8},{10,11... | collective-permute-start | bytes 786440 | tf_op jit(solution)/shard_map/ppermute | solution.py:393
  7.8 9.8 %collective-permute-start.1 = (f32[256,256]{1,0:T(8,128)S(1)}, f32[256,256]{1,0:T(8,128)S(1)}, u32[]{:S(2)}, u32[]{:S(2)}) collective-permute-start(f32[256,256]{1,0:T(8,128)S(1)} %get-tuple-element.35.refs_0_), channel_id=1, source_target_pairs={{0,1},{1,0},{2,3},{3,2},{4,5},{5,4},{6,7},{7,6},{8,9},{9,8},{10,11... | collective-permute-start | bytes 786440 | tf_op jit(solution)/shard_map/ppermute | solution.py:393
  18.8 2.1 %collective-permute-start.8 = (f32[2,256,256]{2,1,0:T(8,128)S(1)}, f32[2,256,256]{2,1,0:T(8,128)S(1)}, u32[]{:S(2)}, u32[]{:S(2)}) collective-permute-start(f32[2,256,256]{2,1,0:T(8,128)S(1)} %get-tuple-element.53), channel_id=1, source_target_pairs={{0,2},{2,0},{4,6},{6,4},{8,10},{10,8},{12,14},{14,12},{16,18},{18,... | collective-permute-start | bytes 1572872 | tf_op jit(solution)/shard_map/ppermute | solution.py:383
  18.9 2.0 %collective-permute-start.2 = (f32[192,128]{1,0:T(8,128)S(1)}, f32[192,128]{1,0:T(8,128)S(1)}, u32[]{:S(2)}, u32[]{:S(2)}) collective-permute-start(f32[192,128]{1,0:T(8,128)S(1)} %get-tuple-element.43), channel_id=1, source_target_pairs={{0,2},{2,0},{4,6},{6,4},{8,10},{10,8},{12,14},{14,12},{16,18},{18,... | collective-permute-start | bytes 294920 | tf_op jit(solution)/shard_map/ppermute | solution.py:383
  20.0 18.9 %collective-permute-start.7 = (f32[2,256,256]{2,1,0:T(8,128)S(1)}, f32[2,256,256]{2,1,0:T(8,128)S(1)}, u32[]{:S(2)}, u32[]{:S(2)}) collective-permute-start(f32[2,256,256]{2,1,0:T(8,128)S(1)} %get-tuple-element.50), channel_id=1, source_target_pairs={{0,2},{2,0},{4,6},{6,4},{8,10},{10,8},{12,14},{14,12},{16,18},{18,... | collective-permute-start | bytes 1572872 | tf_op jit(solution)/shard_map/ppermute | solution.py:383
  21.0 17.9 %collective-permute-start.9 = (f32[2,256,256]{2,1,0:T(8,128)S(1)}, f32[2,256,256]{2,1,0:T(8,128)S(1)}, u32[]{:S(2)}, u32[]{:S(2)}) collective-permute-start(f32[2,256,256]{2,1,0:T(8,128)S(1)} %add_parts.10), channel_id=1, source_target_pairs={{0,4},{2,6},{4,0},{6,2},{8,12},{10,14},{12,8},{14,10},{16,20},{18,... | collective-permute-start | bytes 1572872 | tf_op jit(solution)/shard_map/ppermute | solution.py:383
  22.8 4.6 %collective-permute-start.3 = (f32[192,128]{1,0:T(8,128)S(1)}, f32[192,128]{1,0:T(8,128)S(1)}, u32[]{:S(2)}, u32[]{:S(2)}) collective-permute-start(f32[192,128]{1,0:T(8,128)S(1)} %add_parts.6.refs_0_.refs_2_), channel_id=1, source_target_pairs={{0,8},{2,10},{4,12},{6,14},{8,0},{10,2},{12,4},{14,6},{16,24},{18,... | collective-permute-start | bytes 294920 | tf_op jit(solution)/shard_map/ppermute | solution.py:383
  27.4 6.8 %collective-permute-start.4 = (f32[192,128]{1,0:T(8,128)S(1)}, f32[192,128]{1,0:T(8,128)S(1)}, u32[]{:S(2)}, u32[]{:S(2)}) collective-permute-start(f32[192,128]{1,0:T(8,128)S(1)} %add_parts.7.refs_0_), channel_id=1, source_target_pairs={{0,16},{2,18},{4,20},{6,22},{8,24},{10,26},{12,28},{14,30},{16,0},... | collective-permute-start | bytes 294920 | tf_op jit(solution)/shard_map/ppermute | solution.py:383
  34.2 4.7 %collective-permute-start.5 = (f32[192,128]{1,0:T(8,128)S(1)}, f32[192,128]{1,0:T(8,128)S(1)}, u32[]{:S(2)}, u32[]{:S(2)}) collective-permute-start(f32[192,128]{1,0:T(8,128)S(1)} %add_parts.8.refs_0_), channel_id=1, source_target_pairs={{0,4},{2,6},{4,0},{6,2},{8,12},{10,14},{12,8},{14,10},{16,20},{18,... | collective-permute-start | bytes 294920 | tf_op jit(solution)/shard_map/ppermute | solution.py:383
  39.0 14.6 %collective-permute-start.10 = (f32[256,256]{1,0:T(8,128)S(1)}, f32[256,256]{1,0:T(8,128)S(1)}, u32[]{:S(2)}, u32[]{:S(2)}) collective-permute-start(f32[256,256]{1,0:T(8,128)S(1)} %get-tuple-element.54), channel_id=1, source_target_pairs={{0,0},{1,8},{2,18},{3,26},{4,4},{5,12},{6,22},{7,30},{8,1},{9,9},{... | collective-permute-start | bytes 786440 | tf_op jit(solution)/shard_map/ppermute | solution.py:414
  39.7 18.8 %collective-permute-start.11 = (f32[256,256]{1,0:T(8,128)S(1)}, f32[256,256]{1,0:T(8,128)S(1)}, u32[]{:S(2)}, u32[]{:S(2)}) collective-permute-start(f32[256,256]{1,0:T(8,128)S(1)} %get-tuple-element.55), channel_id=1, source_target_pairs={{0,1},{1,9},{2,19},{3,27},{4,5},{5,13},{6,23},{7,31},{8,0},{9,8},{... | collective-permute-start | bytes 786440 | tf_op jit(solution)/shard_map/ppermute | solution.py:414
  43.1 1.3 %collective-permute-start.6 = (f32[192,128]{1,0:T(8,128)S(1)}, f32[192,128]{1,0:T(8,128)S(1)}, u32[]{:S(2)}, u32[]{:S(2)}) collective-permute-start(f32[192,128]{1,0:T(8,128)S(1)} %add_parts.9.refs_0_.refs_3_), channel_id=1, source_target_pairs={{0,2},{2,0},{4,6},{6,4},{8,10},{10,8},{12,14},{14,12},{16,18},{18,... | collective-permute-start | bytes 294920 | tf_op jit(solution)/shard_map/ppermute | solution.py:383
  58.9 2.2 %collective-permute-start.12 = (f32[4,16,256]{2,1,0:T(8,128)S(1)}, f32[4,16,256]{2,1,0:T(8,128)S(1)}, u32[]{:S(2)}, u32[]{:S(2)}) collective-permute-start(f32[4,16,256]{2,1,0:T(8,128)S(1)} %get-tuple-element.57), channel_id=1, source_target_pairs={{0,2},{2,0},{4,6},{6,4},{8,10},{10,8},{12,14},{14,12},{16,18},{18,... | collective-permute-start | bytes 196616 | tf_op jit(solution)/shard_map/ppermute | solution.py:383
  59.0 4.8 %collective-permute-start.13 = (f32[4,16,256]{2,1,0:T(8,128)S(1)}, f32[4,16,256]{2,1,0:T(8,128)S(1)}, u32[]{:S(2)}, u32[]{:S(2)}) collective-permute-start(f32[4,16,256]{2,1,0:T(8,128)S(1)} %get-tuple-element.58), channel_id=1, source_target_pairs={{0,4},{2,6},{4,0},{6,2},{8,12},{10,14},{12,8},{14,10},{16,20},{18,... | collective-permute-start | bytes 196616 | tf_op jit(solution)/shard_map/ppermute | solution.py:383
  61.0 4.0 %collective-permute-start.14 = (f32[4,16,256]{2,1,0:T(8,128)S(1)}, f32[4,16,256]{2,1,0:T(8,128)S(1)}, u32[]{:S(2)}, u32[]{:S(2)}) collective-permute-start(f32[4,16,256]{2,1,0:T(8,128)S(1)} %get-tuple-element.59), channel_id=1, source_target_pairs={{0,6},{2,4},{4,2},{6,0},{8,14},{10,12},{12,10},{14,8},{16,22},{18,... | collective-permute-start | bytes 196616 | tf_op jit(solution)/shard_map/ppermute | solution.py:383
  65.1 5.7 %collective-permute-start.15 = (f32[2,16,256]{2,1,0:T(8,128)S(1)}, f32[2,16,256]{2,1,0:T(8,128)S(1)}, u32[]{:S(2)}, u32[]{:S(2)}) collective-permute-start(f32[2,16,256]{2,1,0:T(8,128)S(1)} %get-tuple-element.61), channel_id=1, source_target_pairs={{0,8},{2,10},{4,12},{6,14},{8,0},{10,2},{12,4},{14,6},{16,24},{18,... | collective-permute-start | bytes 98312 | tf_op jit(solution)/shard_map/ppermute | solution.py:383
  65.2 5.7 %collective-permute-start.16 = (f32[2,16,256]{2,1,0:T(8,128)S(1)}, f32[2,16,256]{2,1,0:T(8,128)S(1)}, u32[]{:S(2)}, u32[]{:S(2)}) collective-permute-start(f32[2,16,256]{2,1,0:T(8,128)S(1)} %get-tuple-element.62), channel_id=1, source_target_pairs={{0,16},{2,18},{4,20},{6,22},{8,24},{10,26},{12,28},{14,30},{16,0},... | collective-permute-start | bytes 98312 | tf_op jit(solution)/shard_map/ppermute | solution.py:383
  67.3 5.7 %collective-permute-start.17 = (f32[2,16,256]{2,1,0:T(8,128)S(1)}, f32[2,16,256]{2,1,0:T(8,128)S(1)}, u32[]{:S(2)}, u32[]{:S(2)}) collective-permute-start(f32[2,16,256]{2,1,0:T(8,128)S(1)} %get-tuple-element.63), channel_id=1, source_target_pairs={{0,24},{2,26},{4,28},{6,30},{8,16},{10,18},{12,20},{14,22},{16,8},... | collective-permute-start | bytes 98312 | tf_op jit(solution)/shard_map/ppermute | solution.py:383

commit v8 on v7

--- a/solution.py
+++ b/solution.py
@@ -398,11 +398,10 @@
     give, keep = project_band((1,), high, low, bands[1], before[:2])
     send, = add_parts((keep, rows_permute(give, 1)), 1, (gram,))
     give, keep = project_band((0,), high, low, bands[1], before[2:])
-    give_got, send_got = rows_permute(give, 1), rows_permute(send, 2)
+    pieces = add_parts((keep, rows_permute(give, 1), rows_permute(send, 2)), 2)
     gram, = add_parts((gram, rows_permute(gram, 4)), 1)
-    gram, = add_parts((gram, rows_permute(gram, 8)), 1)
+    gram, = add_parts((gram, rows_permute(gram, 8)), 1, pieces)
     gram, = add_parts((gram, rows_permute(gram, 2)), 1)
-    pieces = add_parts((keep, give_got, send_got), 2, (gram,))
     inverse = inverse_factor(gram, rows_permute(gram, 1), total_rows)
     gathered = []
     for k in range(2):

time: 74.3 us -> 72.4 us (0.974)
  waiting for transfers between devices: 32.7 us -> 28.9 us
  starting transfers between devices: 21.1 us -> 23.1 us
    ppermute x2, waiting for transfers between devices: 4.92 us -> 1.26 us  [local(): gathered.append(lax.ppermute(pieces[k], ('rows', 'cols'), pairs))]
    ppermute x2, starting transfers between devices: 4.09 us -> 5.22 us  [local(): gathered.append(lax.ppermute(pieces[k], ('rows', 'cols'), pairs))]
    ppermute x14, starting transfers between devices: 13.9 us -> 14.7 us  [rows_permute(): return lax.ppermute(value, 'rows', [(i, i ^ mask) for i in range(size)])]
  transfers between devices with their start and end apart: 18 -> 18, of which waited for: 11 -> 11; matrix products, arithmetic and copies ran while one was open for 0% -> 0% of each run, Pallas kernels for 20% -> 21%
where the time goes in v8:
time: 72.4 us; the launch traced here: 71.8 us
  waiting for transfers between devices  28.9 us (40%)
  starting transfers between devices  23.1 us (32%)
  Pallas kernels  19 us (26%)
  between operations  0.79 us (1%)
    ppermute x14, waiting for transfers between devices, rows_permute(): return lax.ppermute(value, 'rows', [(i, i ^ mask) for i in range(size)])  19.4 us
    ppermute x14, starting transfers between devices, rows_permute(): return lax.ppermute(value, 'rows', [(i, i ^ mask) for i in range(size)])  14.7 us
    pallas_call x1, Pallas kernels, inverse_factor(): pl.pallas_call(body, in_specs=[VMEM] * 2, out_specs=VMEM, out_shape=on_ch...  9.15 us
    ppermute x2, waiting for transfers between devices, local(): got.append(lax.ppermute(part, 'cols', [(0, 1), (1, 0)]))  8.27 us
    ppermute x2, starting transfers between devices, local(): gathered.append(lax.ppermute(pieces[k], ('rows', 'cols'), pairs))  5.22 us
    pallas_call x2, Pallas kernels, sketch_band(): pl.pallas_call(body, in_specs=[HBM] * 3, out_specs=[VMEM] * 2, out_shape=...  4.13 us
    ppermute x2, starting transfers between devices, local(): got.append(lax.ppermute(part, 'cols', [(0, 1), (1, 0)]))  3.12 us
    pallas_call x3, Pallas kernels, project_band(): pl.pallas_call(body, in_specs=[VMEM] * len(operands), out_specs=[VMEM] *...  2.25 us
  transfers between devices with their start and end apart: 18, of which 11 were waited for; matrix products, arithmetic and copies ran while one was open for 0% of the time, Pallas kernels for 21%

profile of v8, /device:TPU:0, one launch (start us, length us, event | category | flops | bytes accessed | tf_op | source)
XLA Modules:
  0.0 71.8 jit_solution(6198259947269993185)
XLA Ops:
  0.6 2.1 %sketch_band.2 = (f32[256,256]{1,0:T(8,128)S(1)}, f32[256,2048]{1,0:T(8,128)S(1)}) custom-call(s32[2,16]{1,0:T(2,128)} %bitcast.6, f32[512,2048]{1,0:T(8,128)} %refs_1_.3, s32[2,2048]{1,0:T(2,128)} %bitcast.4), custom_call_target="tpu_custom_call" | custom-call | flops 2097152 | bytes 2097152 | tf_op jit(solution)/shard_map/sketch_band/pallas_call | solution.py:96
  2.7 3.0 %collective-permute-start = (f32[256,256]{1,0:T(8,128)S(1)}, f32[256,256]{1,0:T(8,128)S(1)}, u32[]{:S(2)}, u32[]{:S(2)}) collective-permute-start(f32[256,256]{1,0:T(8,128)S(1)} %get-tuple-element.33.refs_0_), channel_id=1, source_target_pairs={{0,1},{1,0},{2,3},{3,2},{4,5},{5,4},{6,7},{7,6},{8,9},{9,8},{10,11... | collective-permute-start | bytes 786440 | tf_op jit(solution)/shard_map/ppermute | solution.py:393
  5.7 2.1 %sketch_band.3 = (f32[256,256]{1,0:T(8,128)S(1)}, f32[256,2048]{1,0:T(8,128)S(1)}) custom-call(s32[2,16]{1,0:T(2,128)} %bitcast.7, f32[512,2048]{1,0:T(8,128)} %refs_1_.3, s32[2,2048]{1,0:T(2,128)} %bitcast.5), custom_call_target="tpu_custom_call" | custom-call | flops 2097152 | bytes 2097152 | tf_op jit(solution)/shard_map/sketch_band/pallas_call | solution.py:96
  7.8 0.1 collective-permute-start.1
  7.9 5.0 %collective-permute-done.refs_1_ = f32[256,256]{1,0:T(8,128)S(1)} collective-permute-done((f32[256,256]{1,0:T(8,128)S(1)}, f32[256,256]{1,0:T(8,128)S(1)}, u32[]{:S(2)}, u32[]{:S(2)}) %collective-permute-start) | collective-permute-done | bytes 262176 | tf_op jit(solution)/shard_map/ppermute | solution.py:393
  12.9 0.4 gram_band.2
  13.3 1.0 %project_band.3 = (f32[2,256,256]{2,1,0:T(8,128)S(1)}, f32[2,256,256]{2,1,0:T(8,128)S(1)}, f32[2,256,256]{2,1,0:T(8,128)S(1)}, f32[2,256,256]{2,1,0:T(8,128)S(1)}) custom-call(bf16[256,256]{1,0:T(8,128)(2,1)S(1)} %get-tuple-element.37.refs_0_, bf16[256,256]{1,0:T(8,128)(2,1)S(1)} %get-tuple-element.38.refs_1_, f32[256,2048]{1,0:T(8,128)S(1)} %get-tuple-element.39.refs_2_), custom_call_target="tpu_custom_call" | custom-call | flops 805306368 | bytes 2097152 | tf_op jit(solution)/shard_map/project_band/pallas_call | solution.py:183
  14.4 3.3 %collective-permute-done.1.refs_1_ = f32[256,256]{1,0:T(8,128)S(1)} collective-permute-done((f32[256,256]{1,0:T(8,128)S(1)}, f32[256,256]{1,0:T(8,128)S(1)}, u32[]{:S(2)}, u32[]{:S(2)}) %collective-permute-start.1) | collective-permute-done | bytes 262176 | tf_op jit(solution)/shard_map/ppermute | solution.py:393
  17.7 0.5 gram_band.3
  18.1 0.6 project_band.5
  18.8 0.1 collective-permute-start.6
  18.9 0.5 collective-permute-start.2
  19.4 0.6 project_band.4
  20.0 0.1 collective-permute-start.5
  20.1 0.8 %collective-permute-done.2.refs_1_ = f32[192,128]{1,0:T(8,128)S(1)} collective-permute-done((f32[192,128]{1,0:T(8,128)S(1)}, f32[192,128]{1,0:T(8,128)S(1)}, u32[]{:S(2)}, u32[]{:S(2)}) %collective-permute-start.2) | collective-permute-done | bytes 98336 | tf_op jit(solution)/shard_map/ppermute | solution.py:383
  20.9 0.0 collective-permute-done.6.refs_1_
  20.9 0.1 add_parts.8
  21.0 1.8 %collective-permute-start.7 = (f32[2,256,256]{2,1,0:T(8,128)S(1)}, f32[2,256,256]{2,1,0:T(8,128)S(1)}, u32[]{:S(2)}, u32[]{:S(2)}) collective-permute-start(f32[2,256,256]{2,1,0:T(8,128)S(1)} %add_parts.8), channel_id=1, source_target_pairs={{0,4},{2,6},{4,0},{6,2},{8,12},{10,14},{12,8},{14,10},{16,20},{18,... | collective-permute-start | bytes 1572872 | tf_op jit(solution)/shard_map/ppermute | solution.py:383
  22.8 1.6 %collective-permute-start.3 = (f32[192,128]{1,0:T(8,128)S(1)}, f32[192,128]{1,0:T(8,128)S(1)}, u32[]{:S(2)}, u32[]{:S(2)}) collective-permute-start(f32[192,128]{1,0:T(8,128)S(1)} %add_parts.6.refs_0_.refs_2_), channel_id=1, source_target_pairs={{0,8},{2,10},{4,12},{6,14},{8,0},{10,2},{12,4},{14,6},{16,24},{18,... | collective-permute-start | bytes 294920 | tf_op jit(solution)/shard_map/ppermute | solution.py:383
  24.3 3.0 %collective-permute-done.3.refs_1_ = f32[192,128]{1,0:T(8,128)S(1)} collective-permute-done((f32[192,128]{1,0:T(8,128)S(1)}, f32[192,128]{1,0:T(8,128)S(1)}, u32[]{:S(2)}, u32[]{:S(2)}) %collective-permute-start.3) | collective-permute-done | bytes 98336 | tf_op jit(solution)/shard_map/ppermute | solution.py:383
  27.4 2.7 %collective-permute-start.4 = (f32[192,128]{1,0:T(8,128)S(1)}, f32[192,128]{1,0:T(8,128)S(1)}, u32[]{:S(2)}, u32[]{:S(2)}) collective-permute-start(f32[192,128]{1,0:T(8,128)S(1)} %add_parts.7.refs_0_), channel_id=1, source_target_pairs={{0,16},{2,18},{4,20},{6,22},{8,24},{10,26},{12,28},{14,30},{16,0},... | collective-permute-start | bytes 294920 | tf_op jit(solution)/shard_map/ppermute | solution.py:383
  30.0 0.0 collective-permute-done.5.refs_1_
  30.0 5.0 %collective-permute-done.7.refs_2_ = f32[2,256,256]{2,1,0:T(8,128)S(1)} collective-permute-done((f32[2,256,256]{2,1,0:T(8,128)S(1)}, f32[2,256,256]{2,1,0:T(8,128)S(1)}, u32[]{:S(2)}, u32[]{:S(2)}) %collective-permute-start.7) | collective-permute-done | bytes 524320 | tf_op jit(solution)/shard_map/ppermute | solution.py:383
  35.0 0.1 add_parts.9
  35.1 0.7 collective-permute-start.10
  35.8 4.5 %collective-permute-start.11 = (f32[256,256]{1,0:T(8,128)S(1)}, f32[256,256]{1,0:T(8,128)S(1)}, u32[]{:S(2)}, u32[]{:S(2)}) collective-permute-start(f32[256,256]{1,0:T(8,128)S(1)} %get-tuple-element.55.refs_3_), channel_id=1, source_target_pairs={{0,1},{1,9},{2,19},{3,27},{4,5},{5,13},{6,23},{7,31},{8,0},{9,8},{... | collective-permute-start | bytes 786440 | tf_op jit(solution)/shard_map/ppermute | solution.py:413
  40.3 0.0 collective-permute-done.4.refs_1_
  40.3 1.6 %collective-permute-start.8 = (f32[192,128]{1,0:T(8,128)S(1)}, f32[192,128]{1,0:T(8,128)S(1)}, u32[]{:S(2)}, u32[]{:S(2)}) collective-permute-start(f32[192,128]{1,0:T(8,128)S(1)} %add_parts.10.refs_0_), channel_id=1, source_target_pairs={{0,4},{2,6},{4,0},{6,2},{8,12},{10,14},{12,8},{14,10},{16,20},{18,... | collective-permute-start | bytes 294920 | tf_op jit(solution)/shard_map/ppermute | solution.py:383
  41.9 3.1 %collective-permute-done.8.refs_1_ = f32[192,128]{1,0:T(8,128)S(1)} collective-permute-done((f32[192,128]{1,0:T(8,128)S(1)}, f32[192,128]{1,0:T(8,128)S(1)}, u32[]{:S(2)}, u32[]{:S(2)}) %collective-permute-start.8) | collective-permute-done | bytes 98336 | tf_op jit(solution)/shard_map/ppermute | solution.py:383
  45.0 0.1 collective-permute-start.9
  45.1 1.3 %collective-permute-done.9.refs_1_ = f32[192,128]{1,0:T(8,128)S(1)} collective-permute-done((f32[192,128]{1,0:T(8,128)S(1)}, f32[192,128]{1,0:T(8,128)S(1)}, u32[]{:S(2)}, u32[]{:S(2)}) %collective-permute-start.9) | collective-permute-done | bytes 98336 | tf_op jit(solution)/shard_map/ppermute | solution.py:383
  46.4 9.2 %inverse_factor.1.refs_2_.inverse_ref = f32[256,256]{1,0:T(8,128)S(1)} custom-call(f32[192,128]{1,0:T(8,128)S(1)} %add_parts.11.refs_0_, f32[192,128]{1,0:T(8,128)S(1)} %collective-permute-done.9.refs_1_), custom_call_target="tpu_custom_call" | custom-call | bytes 524288 | tf_op jit(solution)/shard_map/inverse_factor/pallas_call | solution.py:278
  55.6 0.0 collective-permute-done.10.p0
  55.6 1.3 %collective-permute-done.11.p1 = f32[256,256]{1,0:T(8,128)S(1)} collective-permute-done((f32[256,256]{1,0:T(8,128)S(1)}, f32[256,256]{1,0:T(8,128)S(1)}, u32[]{:S(2)}, u32[]{:S(2)}) %collective-permute-start.11) | collective-permute-done | bytes 262176 | tf_op jit(solution)/shard_map/ppermute | solution.py:413
  56.8 0.4 remainder_pieces.1
  57.2 0.1 collective-permute-start.12
  57.3 1.6 %collective-permute-start.13 = (f32[4,16,256]{2,1,0:T(8,128)S(1)}, f32[4,16,256]{2,1,0:T(8,128)S(1)}, u32[]{:S(2)}, u32[]{:S(2)}) collective-permute-start(f32[4,16,256]{2,1,0:T(8,128)S(1)} %get-tuple-element.58), channel_id=1, source_target_pairs={{0,4},{2,6},{4,0},{6,2},{8,12},{10,14},{12,8},{14,10},{16,20},{18,... | collective-permute-start | bytes 196616 | tf_op jit(solution)/shard_map/ppermute | solution.py:383
  58.9 0.3 collective-permute-start.14
  59.2 0.0 collective-permute-done.12.r1
  59.2 2.6 %collective-permute-done.13.r2 = f32[4,16,256]{2,1,0:T(8,128)S(1)} collective-permute-done((f32[4,16,256]{2,1,0:T(8,128)S(1)}, f32[4,16,256]{2,1,0:T(8,128)S(1)}, u32[]{:S(2)}, u32[]{:S(2)}) %collective-permute-start.13) | collective-permute-done | bytes 65568 | tf_op jit(solution)/shard_map/ppermute | solution.py:383
  61.8 1.1 %collective-permute-done.14.r3 = f32[4,16,256]{2,1,0:T(8,128)S(1)} collective-permute-done((f32[4,16,256]{2,1,0:T(8,128)S(1)}, f32[4,16,256]{2,1,0:T(8,128)S(1)}, u32[]{:S(2)}, u32[]{:S(2)}) %collective-permute-start.14) | collective-permute-done | bytes 65568 | tf_op jit(solution)/shard_map/ppermute | solution.py:383
  63.0 0.1 collective-permute-start.15
  63.1 2.3 %collective-permute-start.16 = (f32[2,16,256]{2,1,0:T(8,128)S(1)}, f32[2,16,256]{2,1,0:T(8,128)S(1)}, u32[]{:S(2)}, u32[]{:S(2)}) collective-permute-start(f32[2,16,256]{2,1,0:T(8,128)S(1)} %get-tuple-element.62), channel_id=1, source_target_pairs={{0,16},{2,18},{4,20},{6,22},{8,24},{10,26},{12,28},{14,30},{16,0},... | collective-permute-start | bytes 98312 | tf_op jit(solution)/shard_map/ppermute | solution.py:383
  65.4 2.1 %collective-permute-start.17 = (f32[2,16,256]{2,1,0:T(8,128)S(1)}, f32[2,16,256]{2,1,0:T(8,128)S(1)}, u32[]{:S(2)}, u32[]{:S(2)}) collective-permute-start(f32[2,16,256]{2,1,0:T(8,128)S(1)} %get-tuple-element.63), channel_id=1, source_target_pairs={{0,24},{2,26},{4,28},{6,30},{8,16},{10,18},{12,20},{14,22},{16,8},... | collective-permute-start | bytes 98312 | tf_op jit(solution)/shard_map/ppermute | solution.py:383
  67.4 1.3 %scaled_core.1 = f32[512,256]{1,0:T(8,128)} custom-call(f32[256,256]{1,0:T(8,128)S(1)} %get-tuple-element.34.refs_0_, f32[256,256]{1,0:T(8,128)S(1)} %get-tuple-element.41.refs_1_, f32[256,256]{1,0:T(8,128)S(1)} %inverse_factor.1.refs_2_.inverse_ref), custom_call_target="tpu_custom_call" | custom-call | flops 201326592 | bytes 1048576 | tf_op jit(solution)/shard_map/scaled_core/pallas_call | solution.py:305
  68.7 0.0 collective-permute-done.15.p1
  68.7 0.0 collective-permute-done.16.p2
  68.7 2.3 %collective-permute-done.17.p3 = f32[2,16,256]{2,1,0:T(8,128)S(1)} collective-permute-done((f32[2,16,256]{2,1,0:T(8,128)S(1)}, f32[2,16,256]{2,1,0:T(8,128)S(1)}, u32[]{:S(2)}, u32[]{:S(2)}) %collective-permute-start.17) | collective-permute-done | bytes 32800 | tf_op jit(solution)/shard_map/ppermute | solution.py:383
  71.1 0.7 arrange.1
  (5 shorter events, 0.1 us)
Async XLA Ops:
  2.7 10.2 %collective-permute-start = (f32[256,256]{1,0:T(8,128)S(1)}, f32[256,256]{1,0:T(8,128)S(1)}, u32[]{:S(2)}, u32[]{:S(2)}) collective-permute-start(f32[256,256]{1,0:T(8,128)S(1)} %get-tuple-element.33.refs_0_), channel_id=1, source_target_pairs={{0,1},{1,0},{2,3},{3,2},{4,5},{5,4},{6,7},{7,6},{8,9},{9,8},{10,11... | collective-permute-start | bytes 786440 | tf_op jit(solution)/shard_map/ppermute | solution.py:393
  7.8 9.8 %collective-permute-start.1 = (f32[256,256]{1,0:T(8,128)S(1)}, f32[256,256]{1,0:T(8,128)S(1)}, u32[]{:S(2)}, u32[]{:S(2)}) collective-permute-start(f32[256,256]{1,0:T(8,128)S(1)} %get-tuple-element.35.refs_0_), channel_id=1, source_target_pairs={{0,1},{1,0},{2,3},{3,2},{4,5},{5,4},{6,7},{7,6},{8,9},{9,8},{10,11... | collective-permute-start | bytes 786440 | tf_op jit(solution)/shard_map/ppermute | solution.py:393
  18.8 2.1 %collective-permute-start.6 = (f32[2,256,256]{2,1,0:T(8,128)S(1)}, f32[2,256,256]{2,1,0:T(8,128)S(1)}, u32[]{:S(2)}, u32[]{:S(2)}) collective-permute-start(f32[2,256,256]{2,1,0:T(8,128)S(1)} %get-tuple-element.53), channel_id=1, source_target_pairs={{0,2},{2,0},{4,6},{6,4},{8,10},{10,8},{12,14},{14,12},{16,18},{18,... | collective-permute-start | bytes 1572872 | tf_op jit(solution)/shard_map/ppermute | solution.py:383
  18.9 2.0 %collective-permute-start.2 = (f32[192,128]{1,0:T(8,128)S(1)}, f32[192,128]{1,0:T(8,128)S(1)}, u32[]{:S(2)}, u32[]{:S(2)}) collective-permute-start(f32[192,128]{1,0:T(8,128)S(1)} %get-tuple-element.43), channel_id=1, source_target_pairs={{0,2},{2,0},{4,6},{6,4},{8,10},{10,8},{12,14},{14,12},{16,18},{18,... | collective-permute-start | bytes 294920 | tf_op jit(solution)/shard_map/ppermute | solution.py:383
  20.0 10.1 %collective-permute-start.5 = (f32[2,256,256]{2,1,0:T(8,128)S(1)}, f32[2,256,256]{2,1,0:T(8,128)S(1)}, u32[]{:S(2)}, u32[]{:S(2)}) collective-permute-start(f32[2,256,256]{2,1,0:T(8,128)S(1)} %get-tuple-element.50), channel_id=1, source_target_pairs={{0,2},{2,0},{4,6},{6,4},{8,10},{10,8},{12,14},{14,12},{16,18},{18,... | collective-permute-start | bytes 1572872 | tf_op jit(solution)/shard_map/ppermute | solution.py:383
  21.0 14.0 %collective-permute-start.7 = (f32[2,256,256]{2,1,0:T(8,128)S(1)}, f32[2,256,256]{2,1,0:T(8,128)S(1)}, u32[]{:S(2)}, u32[]{:S(2)}) collective-permute-start(f32[2,256,256]{2,1,0:T(8,128)S(1)} %add_parts.8), channel_id=1, source_target_pairs={{0,4},{2,6},{4,0},{6,2},{8,12},{10,14},{12,8},{14,10},{16,20},{18,... | collective-permute-start | bytes 1572872 | tf_op jit(solution)/shard_map/ppermute | solution.py:383
  22.8 4.6 %collective-permute-start.3 = (f32[192,128]{1,0:T(8,128)S(1)}, f32[192,128]{1,0:T(8,128)S(1)}, u32[]{:S(2)}, u32[]{:S(2)}) collective-permute-start(f32[192,128]{1,0:T(8,128)S(1)} %add_parts.6.refs_0_.refs_2_), channel_id=1, source_target_pairs={{0,8},{2,10},{4,12},{6,14},{8,0},{10,2},{12,4},{14,6},{16,24},{18,... | collective-permute-start | bytes 294920 | tf_op jit(solution)/shard_map/ppermute | solution.py:383
  27.4 12.9 %collective-permute-start.4 = (f32[192,128]{1,0:T(8,128)S(1)}, f32[192,128]{1,0:T(8,128)S(1)}, u32[]{:S(2)}, u32[]{:S(2)}) collective-permute-start(f32[192,128]{1,0:T(8,128)S(1)} %add_parts.7.refs_0_), channel_id=1, source_target_pairs={{0,16},{2,18},{4,20},{6,22},{8,24},{10,26},{12,28},{14,30},{16,0},... | collective-permute-start | bytes 294920 | tf_op jit(solution)/shard_map/ppermute | solution.py:383
  35.1 20.5 %collective-permute-start.10 = (f32[256,256]{1,0:T(8,128)S(1)}, f32[256,256]{1,0:T(8,128)S(1)}, u32[]{:S(2)}, u32[]{:S(2)}) collective-permute-start(f32[256,256]{1,0:T(8,128)S(1)} %get-tuple-element.54.refs_2_), channel_id=1, source_target_pairs={{0,0},{1,8},{2,18},{3,26},{4,4},{5,12},{6,22},{7,30},{8,1},{9,9},{... | collective-permute-start | bytes 786440 | tf_op jit(solution)/shard_map/ppermute | solution.py:413
  35.8 21.1 %collective-permute-start.11 = (f32[256,256]{1,0:T(8,128)S(1)}, f32[256,256]{1,0:T(8,128)S(1)}, u32[]{:S(2)}, u32[]{:S(2)}) collective-permute-start(f32[256,256]{1,0:T(8,128)S(1)} %get-tuple-element.55.refs_3_), channel_id=1, source_target_pairs={{0,1},{1,9},{2,19},{3,27},{4,5},{5,13},{6,23},{7,31},{8,0},{9,8},{... | collective-permute-start | bytes 786440 | tf_op jit(solution)/shard_map/ppermute | solution.py:413
  40.3 4.7 %collective-permute-start.8 = (f32[192,128]{1,0:T(8,128)S(1)}, f32[192,128]{1,0:T(8,128)S(1)}, u32[]{:S(2)}, u32[]{:S(2)}) collective-permute-start(f32[192,128]{1,0:T(8,128)S(1)} %add_parts.10.refs_0_), channel_id=1, source_target_pairs={{0,4},{2,6},{4,0},{6,2},{8,12},{10,14},{12,8},{14,10},{16,20},{18,... | collective-permute-start | bytes 294920 | tf_op jit(solution)/shard_map/ppermute | solution.py:383
  45.0 1.4 %collective-permute-start.9 = (f32[192,128]{1,0:T(8,128)S(1)}, f32[192,128]{1,0:T(8,128)S(1)}, u32[]{:S(2)}, u32[]{:S(2)}) collective-permute-start(f32[192,128]{1,0:T(8,128)S(1)} %add_parts.11.refs_0_), channel_id=1, source_target_pairs={{0,2},{2,0},{4,6},{6,4},{8,10},{10,8},{12,14},{14,12},{16,18},{18,... | collective-permute-start | bytes 294920 | tf_op jit(solution)/shard_map/ppermute | solution.py:383
  57.2 1.9 %collective-permute-start.12 = (f32[4,16,256]{2,1,0:T(8,128)S(1)}, f32[4,16,256]{2,1,0:T(8,128)S(1)}, u32[]{:S(2)}, u32[]{:S(2)}) collective-permute-start(f32[4,16,256]{2,1,0:T(8,128)S(1)} %get-tuple-element.57), channel_id=1, source_target_pairs={{0,2},{2,0},{4,6},{6,4},{8,10},{10,8},{12,14},{14,12},{16,18},{18,... | collective-permute-start | bytes 196616 | tf_op jit(solution)/shard_map/ppermute | solution.py:383
  57.3 4.5 %collective-permute-start.13 = (f32[4,16,256]{2,1,0:T(8,128)S(1)}, f32[4,16,256]{2,1,0:T(8,128)S(1)}, u32[]{:S(2)}, u32[]{:S(2)}) collective-permute-start(f32[4,16,256]{2,1,0:T(8,128)S(1)} %get-tuple-element.58), channel_id=1, source_target_pairs={{0,4},{2,6},{4,0},{6,2},{8,12},{10,14},{12,8},{14,10},{16,20},{18,... | collective-permute-start | bytes 196616 | tf_op jit(solution)/shard_map/ppermute | solution.py:383
  58.9 4.0 %collective-permute-start.14 = (f32[4,16,256]{2,1,0:T(8,128)S(1)}, f32[4,16,256]{2,1,0:T(8,128)S(1)}, u32[]{:S(2)}, u32[]{:S(2)}) collective-permute-start(f32[4,16,256]{2,1,0:T(8,128)S(1)} %get-tuple-element.59), channel_id=1, source_target_pairs={{0,6},{2,4},{4,2},{6,0},{8,14},{10,12},{12,10},{14,8},{16,22},{18,... | collective-permute-start | bytes 196616 | tf_op jit(solution)/shard_map/ppermute | solution.py:383
  63.0 5.7 %collective-permute-start.15 = (f32[2,16,256]{2,1,0:T(8,128)S(1)}, f32[2,16,256]{2,1,0:T(8,128)S(1)}, u32[]{:S(2)}, u32[]{:S(2)}) collective-permute-start(f32[2,16,256]{2,1,0:T(8,128)S(1)} %get-tuple-element.61), channel_id=1, source_target_pairs={{0,8},{2,10},{4,12},{6,14},{8,0},{10,2},{12,4},{14,6},{16,24},{18,... | collective-permute-start | bytes 98312 | tf_op jit(solution)/shard_map/ppermute | solution.py:383
  63.1 5.7 %collective-permute-start.16 = (f32[2,16,256]{2,1,0:T(8,128)S(1)}, f32[2,16,256]{2,1,0:T(8,128)S(1)}, u32[]{:S(2)}, u32[]{:S(2)}) collective-permute-start(f32[2,16,256]{2,1,0:T(8,128)S(1)} %get-tuple-element.62), channel_id=1, source_target_pairs={{0,16},{2,18},{4,20},{6,22},{8,24},{10,26},{12,28},{14,30},{16,0},... | collective-permute-start | bytes 98312 | tf_op jit(solution)/shard_map/ppermute | solution.py:383
  65.4 5.7 %collective-permute-start.17 = (f32[2,16,256]{2,1,0:T(8,128)S(1)}, f32[2,16,256]{2,1,0:T(8,128)S(1)}, u32[]{:S(2)}, u32[]{:S(2)}) collective-permute-start(f32[2,16,256]{2,1,0:T(8,128)S(1)} %get-tuple-element.63), channel_id=1, source_target_pairs={{0,24},{2,26},{4,28},{6,30},{8,16},{10,18},{12,20},{14,22},{16,8},... | collective-permute-start | bytes 98312 | tf_op jit(solution)/shard_map/ppermute | solution.py:383

commit v9 on v6

--- a/solution.py
+++ b/solution.py
@@ -209,35 +209,57 @@
     )(*held(own, got, before, gram, *after))
 
 
-def project_kernel(parts_ref, high_ref, low_ref, give_1, keep_1, give_0, keep_0):
+def project_kernel(parts_ref, high_ref, low_ref, soon_0, soon_1, keep_1, give_0, keep_0):
     row = lax.axis_index("rows")
     core, right, near, far = row & 1, (row >> 1) & 1, (row >> 2) & 1, row >> 3
-    for flip, give_ref, keep_ref in ((1, give_1, keep_1), (0, give_0, keep_0)):
-        for t in range(4):
-            block = (far ^ (t >> 1)) * 4 + (right ^ flip) * 2 + (near ^ (t & 1))
-            here = pl.ds(pl.multiple_of(block * 2 * BLK, 2 * BLK), 2 * BLK)
-            both = dot(parts_ref[...], high_ref[:, here])
-            total = both[:BLK] + both[BLK:] + dot(parts_ref[:BLK, :], low_ref[:, here])
-            left, other = total[:, :BLK], total[:, BLK:]
-            give_ref[t] = jnp.where(core == 0, other, left)
-            keep_ref[t] = jnp.where(core == 0, left, other)
+    for flip, give, keep in ((1, (soon_0, soon_1), keep_1), (0, (give_0.at[0], give_0.at[1]), keep_0)):
+        for side in range(2):
+            for t in range(2):
+                block = (far ^ core ^ 1 ^ side) * 4 + (right ^ flip) * 2 + (near ^ t)
+                here = pl.ds(pl.multiple_of(block * 2 * BLK, 2 * BLK), 2 * BLK)
+                both = dot(parts_ref[...], high_ref[:, here])
+                total = both[:BLK] + both[BLK:] + dot(parts_ref[:BLK, :], low_ref[:, here])
+                if side == 0:
+                    give[t][...] = total
+                else:
+                    keep[t] = total
 
 
 def project(parts, high, low, after=()):
     rows, cols = high.shape
 
     def body(*refs):
-        project_kernel(*refs[:3], *refs[-4:])
+        project_kernel(*refs[:3], *refs[-5:])
 
     return pl.pallas_call(
         body,
         in_specs=[VMEM] * (3 + len(after)),
-        out_specs=[VMEM] * 4,
-        out_shape=[on_chip(4, BLK, BLK)] * 4,
+        out_specs=[VMEM] * 5,
+        out_shape=[on_chip(BLK, 2 * BLK)] * 2 + [on_chip(2, BLK, 2 * BLK)] * 3,
         cost_estimate=cost(rows * cols * BLK * 6, rows * cols * 4),
         compiler_params=LIMIT,
         name="project",
     )(*held(parts, high, low, *after))
+
+
+def joined_kernel(keep_ref, got_0, got_1, out_ref):
+    out_ref[0] = keep_ref[0] + got_0[...]
+    out_ref[1] = keep_ref[1] + got_1[...]
+
+
+def joined(keep, got, after):
+    def body(*refs):
+        joined_kernel(*refs[:3], refs[-1])
+
+    return pl.pallas_call(
+        body,
+        in_specs=[VMEM] * (3 + len(after)),
+        out_specs=VMEM,
+        out_shape=on_chip(*keep.shape),
+        cost_estimate=cost(0, keep.size * 4),
+        compiler_params=LIMIT,
+        name="joined",
+    )(*held(keep, *got, *after))
 
 
 def add_parts_kernel(terms, outs):
@@ -280,13 +302,13 @@
     terms = (*first, *second)
 
     def body(*refs):
-        pieces_kernel(refs[:-4], refs[-4:])
+        pieces_kernel(refs[:-2], refs[-2:])
 
     return pl.pallas_call(
         body,
         in_specs=[VMEM] * len(terms),
-        out_specs=[VMEM] * 4,
-        out_shape=[on_chip(2 * BLK, BLK)] * 4,
+        out_specs=[VMEM] * 2,
+        out_shape=[on_chip(2 * BLK, 2 * BLK)] * 2,
         cost_estimate=cost(8 * BLK * BLK, 96 * BLK * BLK),
         compiler_params=LIMIT,
         name="piece_sums",
@@ -385,8 +407,8 @@
     )(*held(first, second, inverse))
 
 
-def remainder_kernel(inverse_ref, p0, p1, p2, p3, o0, o1, o2, o3, work):
-    work[...] = jnp.dot(inverse_ref[...], (p0[...] + p1[...]) + (p2[...] + p3[...]), precision=HIGHEST)
+def remainder_kernel(inverse_ref, p0, p1, o0, o1, o2, o3, work):
+    work[...] = jnp.dot(inverse_ref[...], p0[...] + p1[...], precision=HIGHEST)
     device = lax.axis_index("rows")
     for m, out in enumerate((o0, o1, o2, o3)):
         for t in range(4):
@@ -397,60 +419,56 @@
 def remainder_pieces(inverse, pieces):
     return pl.pallas_call(
         remainder_kernel,
-        in_specs=[VMEM] * 5,
+        in_specs=[VMEM] * 3,
         out_specs=[VMEM] * 4,
-        out_shape=[on_chip(4, 16, BLK)] * 4,
-        scratch_shapes=[pltpu.VMEM((RANK, BLK), F32)],
-        cost_estimate=cost(RANK * RANK * BLK * 12, RANK * BLK * 8),
+        out_shape=[on_chip(4, 16, 2 * BLK)] * 4,
+        scratch_shapes=[pltpu.VMEM((RANK, 2 * BLK), F32)],
+        cost_estimate=cost(RANK * RANK * BLK * 24, RANK * BLK * 16),
         compiler_params=LIMIT,
         name="remainder_pieces",
     )(*held(inverse, *pieces))
 
 
-def collect_kernel(r0, r1, r2, r3, o1, o2, o3):
-    for t, out in ((1, o1), (2, o2), (3, o3)):
-        for m, piece in enumerate((r0, r1, r2, r3)):
-            out[m] = piece[t]
+def collect_kernel(r0, r1, r2, r3, o0, o1, o2, o3):
+    for t, out in enumerate((o0, o1, o2, o3)):
+        out[0] = r0[t] + r1[t]
+        out[1] = r2[t] + r3[t]
 
 
 def collect(firsts):
     return pl.pallas_call(
         collect_kernel,
         in_specs=[VMEM] * 4,
-        out_specs=[VMEM] * 3,
-        out_shape=[on_chip(4, 16, BLK)] * 3,
+        out_specs=[VMEM] * 4,
+        out_shape=[on_chip(2, 16, 2 * BLK)] * 4,
         cost_estimate=cost(0, 16 * BLK * 64),
         compiler_params=LIMIT,
         name="collect",
     )(*held(*firsts))
 
 
-def arrange_kernel(r0, r1, r2, r3, s1, s2, s3, out_ref, work):
+def arrange_kernel(p0, p1, p2, p3, out_ref, work):
     row = lax.axis_index("rows")
-    core, right, deep = row & 1, (row >> 1) & 1, row >> 2
-    firsts = (r0, r1, r2, r3)
-    later = (None, s1, s2, s3)
-    for t in range(4):
-        for m in range(4):
-            there = deep ^ t
-            mode = (there & 1) * 4 + (there >> 1) * 2 + (right ^ (m >> 1))
-            work[mode, core ^ (m & 1)] = firsts[m][0] if t == 0 else later[t][m]
+    right, deep = (row >> 1) & 1, row >> 2
+    for t, piece in enumerate((p0, p1, p2, p3)):
+        there = deep ^ t
+        for m in range(2):
+            work[(there & 1) * 4 + (there >> 1) * 2 + (right ^ m)] = piece[m]
     for mode in range(MODE):
-        for c in range(2):
-            out_ref[:, mode, c * BLK : (c + 1) * BLK] = work[mode, c]
-
-
-def arrange(firsts, later):
+        out_ref[:, mode, :] = work[mode]
+
+
+def arrange(pieces):
     out = pl.pallas_call(
         arrange_kernel,
-        in_specs=[VMEM] * 7,
+        in_specs=[VMEM] * 4,
         out_specs=VMEM,
         out_shape=jax.ShapeDtypeStruct((16, MODE, 2 * BLK), F32),
-        scratch_shapes=[pltpu.VMEM((MODE, 2, 16, BLK), F32)],
+        scratch_shapes=[pltpu.VMEM((MODE, 16, 2 * BLK), F32)],
         cost_estimate=cost(0, 16 * BLK * 64),
         compiler_params=LIMIT,
         name="arrange",
-    )(*held(*firsts, *later))
+    )(*held(*pieces))
     return out.reshape(16 * MODE, 2 * BLK)
 
 
@@ -468,34 +486,33 @@
     own_1, high, low = second_sketch(block, pattern_rows, sign_rows)
     got_1 = lax.ppermute(own_1, "cols", swap)
     first, turned, parts, gram = first_gram(own_0, got_0)
-    give, keep, give_0, keep_0 = project(parts, high, low)
-    send_0, = add_parts((keep, rows_permute(give, 1)), 1)
+    *give, keep, give_0, keep_0 = project(parts, high, low)
+    send_0 = joined(keep, [rows_permute(g, 1) for g in give], ())
     second, parts, gram_keep, gram_send = second_gram(own_1, got_1, turned, gram, (keep_0,))
     gram, = add_parts((gram_keep, rows_permute(gram_send, 1)), 1)
-    give, keep, give_1, keep_1 = project(parts, high, low, (send_0,))
-    send_1, = add_parts((keep, rows_permute(give, 1)), 1, (gram,))
+    *give, keep, give_1, keep_1 = project(parts, high, low, (send_0,))
     got_0 = rows_permute(send_0, 2)
+    send_1 = joined(keep, [rows_permute(g, 1) for g in give], (gram, got_0))
     pieces = piece_sums(
         (keep_0, rows_permute(give_0, 1), got_0),
         (keep_1, rows_permute(give_1, 1), rows_permute(send_1, 2)),
     )
-    gram, = add_parts((gram, rows_permute(gram, 4)), 1, (got_0,))
+    gram, = add_parts((gram, rows_permute(gram, 4)), 1)
     gram, = add_parts((gram, rows_permute(gram, 8)), 1, pieces)
     gram, = add_parts((gram, rows_permute(gram, 2)), 1)
     inverse = inverse_factor(gram, rows_permute(gram, 1), total_rows)
     gathered = []
-    for k in range(4):
+    for k in range(2):
         pairs = []
         for i in range(16):
             for y in range(2):
-                to = (i & 3) | (y << 2) | ((i & 8) ^ ((k >> 1) << 3))
-                pairs.append((2 * i + y, 2 * to + (((i >> 2) & 1) ^ (k & 1))))
+                to = (i & 3) | (y << 2) | ((i & 8) ^ ((i & 1) << 3))
+                pairs.append((2 * i + y, 2 * to + (((i >> 2) & 1) ^ k)))
         gathered.append(lax.ppermute(pieces[k], ("rows", "cols"), pairs))
     parts = remainder_pieces(inverse, gathered)
     core_scaled = scaled_core(first, second, inverse, math.sqrt(total_rows))
-    firsts = [parts[0]] + [rows_permute(parts[m], m) for m in (1, 2, 3)]
-    later = [rows_permute(part, 4 * t) for t, part in zip((1, 2, 3), collect(firsts))]
-    return core_scaled, arrange(firsts, later)
+    sums = collect([parts[0]] + [rows_permute(parts[m], m) for m in (1, 2, 3)])
+    return core_scaled, arrange([sums[0]] + [rows_permute(sums[t], 4 * t) for t in (1, 2, 3)])
 
 
 def sketch_matrix(pattern, sign_bits, block_size):

time: 72.2 us -> 78 us (1.080)
  waiting for transfers between devices: 24.3 us -> 27.3 us
  starting transfers between devices: 28.1 us -> 31 us
    ppermute x17 -> x19, waiting for transfers between devices: 13.8 us -> 21.3 us  [rows_permute(): return lax.ppermute(value, 'rows', [(i, i ^ mask) for i in range(size)])]
    ppermute x17 -> x19, starting transfers between devices: 16.5 us -> 22.7 us  [rows_permute(): return lax.ppermute(value, 'rows', [(i, i ^ mask) for i in range(size)])]
    ppermute x4 -> x2, starting transfers between devices: 8.51 us -> 5.18 us  [local(): gathered.append(lax.ppermute(pieces[k], ('rows', 'cols'), pairs))]
    ppermute x1, waiting for transfers between devices: 3.25 us -> 0.01 us  [local(): got_1 = lax.ppermute(own_1, 'cols', swap)]
    ppermute x4 -> x2, waiting for transfers between devices: 1.47 us -> 0.3 us  [local(): gathered.append(lax.ppermute(pieces[k], ('rows', 'cols'), pairs))]
  transfers between devices with their start and end apart: 23 -> 23, of which waited for: 10 -> 13; matrix products, arithmetic and copies ran while one was open for 0% -> 0% of each run, Pallas kernels for 19% -> 19%
where the time goes in v9:
time: 78 us; the launch traced here: 77.8 us
  starting transfers between devices  31 us (40%)
  waiting for transfers between devices  27.3 us (35%)
  Pallas kernels  18.8 us (24%)
  between operations  0.78 us (1%)
    ppermute x19, starting transfers between devices, rows_permute(): return lax.ppermute(value, 'rows', [(i, i ^ mask) for i in range(size)])  22.7 us
    ppermute x19, waiting for transfers between devices, rows_permute(): return lax.ppermute(value, 'rows', [(i, i ^ mask) for i in range(size)])  21.3 us
    pallas_call x1, Pallas kernels, inverse_factor(): pl.pallas_call(body, in_specs=[VMEM] * 2, out_specs=VMEM, out_shape=on_ch...  9.14 us
    ppermute x1, waiting for transfers between devices, local(): got_0 = lax.ppermute(own_0, 'cols', swap)  5.7 us
    ppermute x2, starting transfers between devices, local(): gathered.append(lax.ppermute(pieces[k], ('rows', 'cols'), pairs))  5.18 us
    ppermute x1, starting transfers between devices, local(): got_0 = lax.ppermute(own_0, 'cols', swap)  3.03 us
    pallas_call x1, Pallas kernels, first_sketch(): pl.pallas_call(first_sketch_kernel, in_specs=[HBM] * 3, out_specs=[VMEM]...  2.66 us
    pallas_call x2, Pallas kernels, project(): pl.pallas_call(body, in_specs=[VMEM] * (3 + len(after)), out_specs=[VMEM]...  2.06 us
  transfers between devices with their start and end apart: 23, of which 13 were waited for; matrix products, arithmetic and copies ran while one was open for 0% of the time, Pallas kernels for 19%

profile of v9, /device:TPU:0, one launch (start us, length us, event | category | flops | bytes accessed | tf_op | source)
XLA Modules:
  0.0 77.8 jit_solution(177886194715005821)
XLA Ops:
  0.6 2.7 %first_sketch.1 = (f32[512,128]{1,0:T(8,128)S(1)}, f32[512,2048]{1,0:T(8,128)S(1)}) custom-call(s32[2,16]{1,0:T(2,128)} %bitcast.6, f32[512,2048]{1,0:T(8,128)} %whole_ref.1, s32[2,2048]{1,0:T(2,128)} %bitcast.4), custom_call_target="tpu_custom_call" | custom-call | flops 2097 | bytes 4194 | tf_op jit(solution)/shard_map/first_sketch/pallas_call | solution.py:93
  3.3 3.0 %collective-permute-start = (f32[512,128]{1,0:T(8,128)S(1)}, f32[512,128]{1,0:T(8,128)S(1)}, u32[]{:S(2)}, u32[]{:S(2)}) collective-permute-start(f32[512,128]{1,0:T(8,128)S(1)} %get-tuple-element.35.own_ref), channel_id=1, source_target_pairs={{0,1},{1,0},{2,3},{3,2},{4,5},{5,4},{6,7},{7,6},{8,9},{9,8},{10,11... | collective-permute-start | bytes 786440 | tf_op jit(solution)/shard_map/ppermute | solution.py:485
  6.3 1.3 %second_sketch.1 = (f32[512,128]{1,0:T(8,128)S(1)}, bf16[512,2048]{1,0:T(8,128)(2,1)S(1)}, bf16[512,2048]{1,0:T(8,128)(2,1)S(1)}) custom-call(s32[2,16]{1,0:T(2,128)} %bitcast.7, s32[2,2048]{1,0:T(2,128)} %bitcast.5, f32[512,2048]{1,0:T(8,128)S(1)} %get-tuple-element.37.block_ref), custom_call_target="tpu_custom_call" | custom-call | flops 2097 | bytes 4194 | tf_op jit(solution)/shard_map/second_sketch/pallas_call | solution.py:131
  7.7 0.1 collective-permute-start.1
  7.8 5.7 %collective-permute-done.got_ref = f32[512,128]{1,0:T(8,128)S(1)} collective-permute-done((f32[512,128]{1,0:T(8,128)S(1)}, f32[512,128]{1,0:T(8,128)S(1)}, u32[]{:S(2)}, u32[]{:S(2)}) %collective-permute-start) | collective-permute-done | bytes 262176 | tf_op jit(solution)/shard_map/ppermute | solution.py:485
  13.5 0.4 first_gram.1
  13.9 1.0 %project.2 = (f32[128,256]{1,0:T(8,128)S(1)}, f32[128,256]{1,0:T(8,128)S(1)}, f32[2,128,256]{2,1,0:T(8,128)S(1)}, f32[2,128,256]{2,1,0:T(8,128)S(1)}, f32[2,128,256]{2,1,0:T(8,128)S(1)}) custom-call(bf16[256,512]{1,0:T(8,128)(2,1)S(1)} %get-tuple-element.41.refs_0_, bf16[512,2048]{1,0:T(8,128)(2,1)S(1)} %get-tuple-element.42.refs_1_, ...), custom_call_target="tpu_custom_call" | custom-call | flops 805306 | bytes 4194 | tf_op jit(solution)/shard_map/project/pallas_call | solution.py:234
  14.9 0.1 collective-permute-start.6
  15.0 0.5 collective-permute-start.7
  15.5 0.8 %collective-permute-done.6.refs_1_ = f32[128,256]{1,0:T(8,128)S(1)} collective-permute-done((f32[128,256]{1,0:T(8,128)S(1)}, f32[128,256]{1,0:T(8,128)S(1)}, u32[]{:S(2)}, u32[]{:S(2)}) %collective-permute-start.6) | collective-permute-done | bytes 131104 | tf_op jit(solution)/shard_map/ppermute | solution.py:477
  16.3 0.2 collective-permute-done.7.refs_2_
  16.6 2.1 %collective-permute-start.8 = (f32[2,128,256]{2,1,0:T(8,128)S(1)}, f32[2,128,256]{2,1,0:T(8,128)S(1)}, u32[]{:S(2)}, u32[]{:S(2)}) collective-permute-start(f32[2,128,256]{2,1,0:T(8,128)S(1)} %joined.2.refs_3_), channel_id=1, source_target_pairs={{0,4},{2,6},{4,0},{6,2},{8,12},{10,14},{12,8},{14,10},{16,20},{18,... | collective-permute-start | bytes 786440 | tf_op jit(solution)/shard_map/ppermute | solution.py:477
  18.7 0.0 collective-permute-done.1.refs_1_
  18.7 0.6 second_gram.1
  19.3 1.0 %project.3 = (f32[128,256]{1,0:T(8,128)S(1)}, f32[128,256]{1,0:T(8,128)S(1)}, f32[2,128,256]{2,1,0:T(8,128)S(1)}, f32[2,128,256]{2,1,0:T(8,128)S(1)}, f32[2,128,256]{2,1,0:T(8,128)S(1)}) custom-call(bf16[256,512]{1,0:T(8,128)(2,1)S(1)} %get-tuple-element.52.refs_0_, bf16[512,2048]{1,0:T(8,128)(2,1)S(1)} %get-tuple-element.42.refs_1_, ...), custom_call_target="tpu_custom_call" | custom-call | flops 805306 | bytes 4194 | tf_op jit(solution)/shard_map/project/pallas_call | solution.py:234
  20.3 0.1 collective-permute-start.10
  20.4 0.5 collective-permute-start.11
  20.9 0.1 collective-permute-start.2
  21.0 0.4 collective-permute-start.5
  21.4 0.8 %collective-permute-done.2.refs_1_ = f32[192,128]{1,0:T(8,128)S(1)} collective-permute-done((f32[192,128]{1,0:T(8,128)S(1)}, f32[192,128]{1,0:T(8,128)S(1)}, u32[]{:S(2)}, u32[]{:S(2)}) %collective-permute-start.2) | collective-permute-done | bytes 98336 | tf_op jit(solution)/shard_map/ppermute | solution.py:477
  22.2 0.3 collective-permute-start.9
  22.5 0.0 collective-permute-done.10.refs_1_
  22.5 0.0 collective-permute-done.11.refs_2_
  22.5 3.0 %collective-permute-done.8.refs_4_.refs_2_ = f32[2,128,256]{2,1,0:T(8,128)S(1)} collective-permute-done((f32[2,128,256]{2,1,0:T(8,128)S(1)}, f32[2,128,256]{2,1,0:T(8,128)S(1)}, u32[]{:S(2)}, u32[]{:S(2)}) %collective-permute-start.8) | collective-permute-done | bytes 262176 | tf_op jit(solution)/shard_map/ppermute | solution.py:477
  25.5 1.8 %collective-permute-start.12 = (f32[2,128,256]{2,1,0:T(8,128)S(1)}, f32[2,128,256]{2,1,0:T(8,128)S(1)}, u32[]{:S(2)}, u32[]{:S(2)}) collective-permute-start(f32[2,128,256]{2,1,0:T(8,128)S(1)} %joined.3), channel_id=1, source_target_pairs={{0,4},{2,6},{4,0},{6,2},{8,12},{10,14},{12,8},{14,10},{16,20},{18,... | collective-permute-start | bytes 786440 | tf_op jit(solution)/shard_map/ppermute | solution.py:477
  27.3 1.6 %collective-permute-start.3 = (f32[192,128]{1,0:T(8,128)S(1)}, f32[192,128]{1,0:T(8,128)S(1)}, u32[]{:S(2)}, u32[]{:S(2)}) collective-permute-start(f32[192,128]{1,0:T(8,128)S(1)} %add_parts.4.refs_0_.refs_3_), channel_id=1, source_target_pairs={{0,8},{2,10},{4,12},{6,14},{8,0},{10,2},{12,4},{14,6},{16,24},{18,... | collective-permute-start | bytes 294920 | tf_op jit(solution)/shard_map/ppermute | solution.py:477
  28.9 3.0 %collective-permute-done.3.refs_1_ = f32[192,128]{1,0:T(8,128)S(1)} collective-permute-done((f32[192,128]{1,0:T(8,128)S(1)}, f32[192,128]{1,0:T(8,128)S(1)}, u32[]{:S(2)}, u32[]{:S(2)}) %collective-permute-start.3) | collective-permute-done | bytes 98336 | tf_op jit(solution)/shard_map/ppermute | solution.py:477
  31.9 2.7 %collective-permute-start.4 = (f32[192,128]{1,0:T(8,128)S(1)}, f32[192,128]{1,0:T(8,128)S(1)}, u32[]{:S(2)}, u32[]{:S(2)}) collective-permute-start(f32[192,128]{1,0:T(8,128)S(1)} %add_parts.5.refs_0_), channel_id=1, source_target_pairs={{0,16},{2,18},{4,20},{6,22},{8,24},{10,26},{12,28},{14,30},{16,0},... | collective-permute-start | bytes 294920 | tf_op jit(solution)/shard_map/ppermute | solution.py:477
  34.6 0.0 collective-permute-done.5.refs_1_
  34.6 0.0 collective-permute-done.9.refs_4_
  34.6 0.0 collective-permute-done.12.refs_5_
  34.6 0.1 piece_sums.1
  34.7 0.7 collective-permute-start.15
  35.4 4.5 %collective-permute-start.16 = (f32[256,256]{1,0:T(8,128)S(1)}, f32[256,256]{1,0:T(8,128)S(1)}, u32[]{:S(2)}, u32[]{:S(2)}) collective-permute-start(f32[256,256]{1,0:T(8,128)S(1)} %get-tuple-element.59.refs_3_), channel_id=1, source_target_pairs={{0,1},{1,9},{2,19},{3,27},{4,5},{5,13},{6,23},{7,31},{8,0},{9,8},{... | collective-permute-start | bytes 786440 | tf_op jit(solution)/shard_map/ppermute | solution.py:511
  39.9 0.0 collective-permute-done.4.refs_1_
  39.9 0.6 collective-permute-start.13
  40.5 4.1 %collective-permute-done.13.refs_1_ = f32[192,128]{1,0:T(8,128)S(1)} collective-permute-done((f32[192,128]{1,0:T(8,128)S(1)}, f32[192,128]{1,0:T(8,128)S(1)}, u32[]{:S(2)}, u32[]{:S(2)}) %collective-permute-start.13) | collective-permute-done | bytes 98336 | tf_op jit(solution)/shard_map/ppermute | solution.py:477
  44.6 0.1 collective-permute-start.14
  44.7 1.3 %collective-permute-done.14.refs_1_ = f32[192,128]{1,0:T(8,128)S(1)} collective-permute-done((f32[192,128]{1,0:T(8,128)S(1)}, f32[192,128]{1,0:T(8,128)S(1)}, u32[]{:S(2)}, u32[]{:S(2)}) %collective-permute-start.14) | collective-permute-done | bytes 98336 | tf_op jit(solution)/shard_map/ppermute | solution.py:477
  46.0 9.1 %inverse_factor.1.refs_2_.inverse_ref = f32[256,256]{1,0:T(8,128)S(1)} custom-call(f32[192,128]{1,0:T(8,128)S(1)} %add_parts.7.refs_0_, f32[192,128]{1,0:T(8,128)S(1)} %collective-permute-done.14.refs_1_), custom_call_target="tpu_custom_call" | custom-call | bytes 524 | tf_op jit(solution)/shard_map/inverse_factor/pallas_call | solution.py:374
  55.1 0.0 collective-permute-done.15.p0
  55.1 0.3 collective-permute-done.16.p1
  55.4 0.4 remainder_pieces.1
  55.8 0.1 collective-permute-start.17
  55.9 0.6 collective-permute-start.18
  56.5 1.3 %collective-permute-start.19 = (f32[4,16,256]{2,1,0:T(8,128)S(1)}, f32[4,16,256]{2,1,0:T(8,128)S(1)}, u32[]{:S(2)}, u32[]{:S(2)}) collective-permute-start(f32[4,16,256]{2,1,0:T(8,128)S(1)} %get-tuple-element.63), channel_id=1, source_target_pairs={{0,6},{2,4},{4,2},{6,0},{8,14},{10,12},{12,10},{14,8},{16,22},{18,... | collective-permute-start | bytes 196616 | tf_op jit(solution)/shard_map/ppermute | solution.py:477
  57.8 0.0 collective-permute-done.17.r1
  57.8 3.1 %collective-permute-done.18.r2 = f32[4,16,256]{2,1,0:T(8,128)S(1)} collective-permute-done((f32[4,16,256]{2,1,0:T(8,128)S(1)}, f32[4,16,256]{2,1,0:T(8,128)S(1)}, u32[]{:S(2)}, u32[]{:S(2)}) %collective-permute-start.18) | collective-permute-done | bytes 65568 | tf_op jit(solution)/shard_map/ppermute | solution.py:477
  60.9 0.5 collective-permute-done.19.r3
  61.4 6.7 %collective-permute-start.20 = (f32[2,16,256]{2,1,0:T(8,128)S(1)}, f32[2,16,256]{2,1,0:T(8,128)S(1)}, u32[]{:S(2)}, u32[]{:S(2)}) collective-permute-start(f32[2,16,256]{2,1,0:T(8,128)S(1)} %get-tuple-element.65), channel_id=1, source_target_pairs={{0,8},{2,10},{4,12},{6,14},{8,0},{10,2},{12,4},{14,6},{16,24},{18,... | collective-permute-start | bytes 98312 | tf_op jit(solution)/shard_map/ppermute | solution.py:477
  68.0 3.4 %collective-permute-start.21 = (f32[2,16,256]{2,1,0:T(8,128)S(1)}, f32[2,16,256]{2,1,0:T(8,128)S(1)}, u32[]{:S(2)}, u32[]{:S(2)}) collective-permute-start(f32[2,16,256]{2,1,0:T(8,128)S(1)} %get-tuple-element.66), channel_id=1, source_target_pairs={{0,16},{2,18},{4,20},{6,22},{8,24},{10,26},{12,28},{14,30},{16,0},... | collective-permute-start | bytes 98312 | tf_op jit(solution)/shard_map/ppermute | solution.py:477
  71.4 0.0 collective-permute-start.22
  71.4 1.3 %scaled_core.1 = f32[512,256]{1,0:T(8,128)} custom-call(f32[512,128]{1,0:T(8,128)S(1)} %get-tuple-element.36.refs_0_, f32[512,128]{1,0:T(8,128)S(1)} %get-tuple-element.45.refs_1_, f32[256,256]{1,0:T(8,128)S(1)} %inverse_factor.1.refs_2_.inverse_ref), custom_call_target="tpu_custom_call" | custom-call | flops 201326 | bytes 1048 | tf_op jit(solution)/shard_map/scaled_core/pallas_call | solution.py:399
  72.7 0.0 collective-permute-done.20.p1
  72.7 1.3 %collective-permute-done.21.p2 = f32[2,16,256]{2,1,0:T(8,128)S(1)} collective-permute-done((f32[2,16,256]{2,1,0:T(8,128)S(1)}, f32[2,16,256]{2,1,0:T(8,128)S(1)}, u32[]{:S(2)}, u32[]{:S(2)}) %collective-permute-start.21) | collective-permute-done | bytes 32800 | tf_op jit(solution)/shard_map/ppermute | solution.py:477
  74.0 3.2 %collective-permute-done.22.p3 = f32[2,16,256]{2,1,0:T(8,128)S(1)} collective-permute-done((f32[2,16,256]{2,1,0:T(8,128)S(1)}, f32[2,16,256]{2,1,0:T(8,128)S(1)}, u32[]{:S(2)}, u32[]{:S(2)}) %collective-permute-start.22) | collective-permute-done | bytes 32800 | tf_op jit(solution)/shard_map/ppermute | solution.py:477
  77.1 0.7 arrange.1
  (7 shorter events, 0.1 us)
Async XLA Ops:
  3.3 10.2 %collective-permute-start = (f32[512,128]{1,0:T(8,128)S(1)}, f32[512,128]{1,0:T(8,128)S(1)}, u32[]{:S(2)}, u32[]{:S(2)}) collective-permute-start(f32[512,128]{1,0:T(8,128)S(1)} %get-tuple-element.35.own_ref), channel_id=1, source_target_pairs={{0,1},{1,0},{2,3},{3,2},{4,5},{5,4},{6,7},{7,6},{8,9},{9,8},{10,11... | collective-permute-start | bytes 786440 | tf_op jit(solution)/shard_map/ppermute | solution.py:485
  7.7 11.0 %collective-permute-start.1 = (f32[512,128]{1,0:T(8,128)S(1)}, f32[512,128]{1,0:T(8,128)S(1)}, u32[]{:S(2)}, u32[]{:S(2)}) collective-permute-start(f32[512,128]{1,0:T(8,128)S(1)} %get-tuple-element.38.refs_0_), channel_id=1, source_target_pairs={{0,1},{1,0},{2,3},{3,2},{4,5},{5,4},{6,7},{7,6},{8,9},{9,8},{10,11... | collective-permute-start | bytes 786440 | tf_op jit(solution)/shard_map/ppermute | solution.py:487
  14.9 1.4 %collective-permute-start.6 = (f32[128,256]{1,0:T(8,128)S(1)}, f32[128,256]{1,0:T(8,128)S(1)}, u32[]{:S(2)}, u32[]{:S(2)}) collective-permute-start(f32[128,256]{1,0:T(8,128)S(1)} %get-tuple-element.50), channel_id=1, source_target_pairs={{0,2},{2,0},{4,6},{6,4},{8,10},{10,8},{12,14},{14,12},{16,18},{18,... | collective-permute-start | bytes 393224 | tf_op jit(solution)/shard_map/ppermute | solution.py:477
  15.0 1.5 %collective-permute-start.7 = (f32[128,256]{1,0:T(8,128)S(1)}, f32[128,256]{1,0:T(8,128)S(1)}, u32[]{:S(2)}, u32[]{:S(2)}) collective-permute-start(f32[128,256]{1,0:T(8,128)S(1)} %get-tuple-element.51), channel_id=1, source_target_pairs={{0,2},{2,0},{4,6},{6,4},{8,10},{10,8},{12,14},{14,12},{16,18},{18,... | collective-permute-start | bytes 393224 | tf_op jit(solution)/shard_map/ppermute | solution.py:477
  16.6 8.9 %collective-permute-start.8 = (f32[2,128,256]{2,1,0:T(8,128)S(1)}, f32[2,128,256]{2,1,0:T(8,128)S(1)}, u32[]{:S(2)}, u32[]{:S(2)}) collective-permute-start(f32[2,128,256]{2,1,0:T(8,128)S(1)} %joined.2.refs_3_), channel_id=1, source_target_pairs={{0,4},{2,6},{4,0},{6,2},{8,12},{10,14},{12,8},{14,10},{16,20},{18,... | collective-permute-start | bytes 786440 | tf_op jit(solution)/shard_map/ppermute | solution.py:477
  20.3 2.1 %collective-permute-start.10 = (f32[128,256]{1,0:T(8,128)S(1)}, f32[128,256]{1,0:T(8,128)S(1)}, u32[]{:S(2)}, u32[]{:S(2)}) collective-permute-start(f32[128,256]{1,0:T(8,128)S(1)} %get-tuple-element.56), channel_id=1, source_target_pairs={{0,2},{2,0},{4,6},{6,4},{8,10},{10,8},{12,14},{14,12},{16,18},{18,... | collective-permute-start | bytes 393224 | tf_op jit(solution)/shard_map/ppermute | solution.py:477
  20.4 2.0 %collective-permute-start.11 = (f32[128,256]{1,0:T(8,128)S(1)}, f32[128,256]{1,0:T(8,128)S(1)}, u32[]{:S(2)}, u32[]{:S(2)}) collective-permute-start(f32[128,256]{1,0:T(8,128)S(1)} %get-tuple-element.57), channel_id=1, source_target_pairs={{0,2},{2,0},{4,6},{6,4},{8,10},{10,8},{12,14},{14,12},{16,18},{18,... | collective-permute-start | bytes 393224 | tf_op jit(solution)/shard_map/ppermute | solution.py:477
  20.9 1.3 %collective-permute-start.2 = (f32[192,128]{1,0:T(8,128)S(1)}, f32[192,128]{1,0:T(8,128)S(1)}, u32[]{:S(2)}, u32[]{:S(2)}) collective-permute-start(f32[192,128]{1,0:T(8,128)S(1)} %get-tuple-element.47), channel_id=1, source_target_pairs={{0,2},{2,0},{4,6},{6,4},{8,10},{10,8},{12,14},{14,12},{16,18},{18,... | collective-permute-start | bytes 294920 | tf_op jit(solution)/shard_map/ppermute | solution.py:477
  21.0 13.6 %collective-permute-start.5 = (f32[2,128,256]{2,1,0:T(8,128)S(1)}, f32[2,128,256]{2,1,0:T(8,128)S(1)}, u32[]{:S(2)}, u32[]{:S(2)}) collective-permute-start(f32[2,128,256]{2,1,0:T(8,128)S(1)} %get-tuple-element.48), channel_id=1, source_target_pairs={{0,2},{2,0},{4,6},{6,4},{8,10},{10,8},{12,14},{14,12},{16,18},{18,... | collective-permute-start | bytes 786440 | tf_op jit(solution)/shard_map/ppermute | solution.py:477
  22.2 12.4 %collective-permute-start.9 = (f32[2,128,256]{2,1,0:T(8,128)S(1)}, f32[2,128,256]{2,1,0:T(8,128)S(1)}, u32[]{:S(2)}, u32[]{:S(2)}) collective-permute-start(f32[2,128,256]{2,1,0:T(8,128)S(1)} %get-tuple-element.54), channel_id=1, source_target_pairs={{0,2},{2,0},{4,6},{6,4},{8,10},{10,8},{12,14},{14,12},{16,18},{18,... | collective-permute-start | bytes 786440 | tf_op jit(solution)/shard_map/ppermute | solution.py:477
  25.5 9.1 %collective-permute-start.12 = (f32[2,128,256]{2,1,0:T(8,128)S(1)}, f32[2,128,256]{2,1,0:T(8,128)S(1)}, u32[]{:S(2)}, u32[]{:S(2)}) collective-permute-start(f32[2,128,256]{2,1,0:T(8,128)S(1)} %joined.3), channel_id=1, source_target_pairs={{0,4},{2,6},{4,0},{6,2},{8,12},{10,14},{12,8},{14,10},{16,20},{18,... | collective-permute-start | bytes 786440 | tf_op jit(solution)/shard_map/ppermute | solution.py:477
  27.3 4.6 %collective-permute-start.3 = (f32[192,128]{1,0:T(8,128)S(1)}, f32[192,128]{1,0:T(8,128)S(1)}, u32[]{:S(2)}, u32[]{:S(2)}) collective-permute-start(f32[192,128]{1,0:T(8,128)S(1)} %add_parts.4.refs_0_.refs_3_), channel_id=1, source_target_pairs={{0,8},{2,10},{4,12},{6,14},{8,0},{10,2},{12,4},{14,6},{16,24},{18,... | collective-permute-start | bytes 294920 | tf_op jit(solution)/shard_map/ppermute | solution.py:477
  31.9 7.9 %collective-permute-start.4 = (f32[192,128]{1,0:T(8,128)S(1)}, f32[192,128]{1,0:T(8,128)S(1)}, u32[]{:S(2)}, u32[]{:S(2)}) collective-permute-start(f32[192,128]{1,0:T(8,128)S(1)} %add_parts.5.refs_0_), channel_id=1, source_target_pairs={{0,16},{2,18},{4,20},{6,22},{8,24},{10,26},{12,28},{14,30},{16,0},... | collective-permute-start | bytes 294920 | tf_op jit(solution)/shard_map/ppermute | solution.py:477
  34.7 20.4 %collective-permute-start.15 = (f32[256,256]{1,0:T(8,128)S(1)}, f32[256,256]{1,0:T(8,128)S(1)}, u32[]{:S(2)}, u32[]{:S(2)}) collective-permute-start(f32[256,256]{1,0:T(8,128)S(1)} %get-tuple-element.58.refs_2_), channel_id=1, source_target_pairs={{0,0},{1,8},{2,18},{3,26},{4,4},{5,12},{6,22},{7,30},{8,1},{9,9},{... | collective-permute-start | bytes 786440 | tf_op jit(solution)/shard_map/ppermute | solution.py:511
  35.4 20.0 %collective-permute-start.16 = (f32[256,256]{1,0:T(8,128)S(1)}, f32[256,256]{1,0:T(8,128)S(1)}, u32[]{:S(2)}, u32[]{:S(2)}) collective-permute-start(f32[256,256]{1,0:T(8,128)S(1)} %get-tuple-element.59.refs_3_), channel_id=1, source_target_pairs={{0,1},{1,9},{2,19},{3,27},{4,5},{5,13},{6,23},{7,31},{8,0},{9,8},{... | collective-permute-start | bytes 786440 | tf_op jit(solution)/shard_map/ppermute | solution.py:511
  39.9 4.7 %collective-permute-start.13 = (f32[192,128]{1,0:T(8,128)S(1)}, f32[192,128]{1,0:T(8,128)S(1)}, u32[]{:S(2)}, u32[]{:S(2)}) collective-permute-start(f32[192,128]{1,0:T(8,128)S(1)} %add_parts.6.refs_0_), channel_id=1, source_target_pairs={{0,4},{2,6},{4,0},{6,2},{8,12},{10,14},{12,8},{14,10},{16,20},{18,... | collective-permute-start | bytes 294920 | tf_op jit(solution)/shard_map/ppermute | solution.py:477
  44.6 1.4 %collective-permute-start.14 = (f32[192,128]{1,0:T(8,128)S(1)}, f32[192,128]{1,0:T(8,128)S(1)}, u32[]{:S(2)}, u32[]{:S(2)}) collective-permute-start(f32[192,128]{1,0:T(8,128)S(1)} %add_parts.7.refs_0_), channel_id=1, source_target_pairs={{0,2},{2,0},{4,6},{6,4},{8,10},{10,8},{12,14},{14,12},{16,18},{18,... | collective-permute-start | bytes 294920 | tf_op jit(solution)/shard_map/ppermute | solution.py:477
  55.8 1.9 %collective-permute-start.17 = (f32[4,16,256]{2,1,0:T(8,128)S(1)}, f32[4,16,256]{2,1,0:T(8,128)S(1)}, u32[]{:S(2)}, u32[]{:S(2)}) collective-permute-start(f32[4,16,256]{2,1,0:T(8,128)S(1)} %get-tuple-element.61), channel_id=1, source_target_pairs={{0,2},{2,0},{4,6},{6,4},{8,10},{10,8},{12,14},{14,12},{16,18},{18,... | collective-permute-start | bytes 196616 | tf_op jit(solution)/shard_map/ppermute | solution.py:477
  55.9 5.0 %collective-permute-start.18 = (f32[4,16,256]{2,1,0:T(8,128)S(1)}, f32[4,16,256]{2,1,0:T(8,128)S(1)}, u32[]{:S(2)}, u32[]{:S(2)}) collective-permute-start(f32[4,16,256]{2,1,0:T(8,128)S(1)} %get-tuple-element.62), channel_id=1, source_target_pairs={{0,4},{2,6},{4,0},{6,2},{8,12},{10,14},{12,8},{14,10},{16,20},{18,... | collective-permute-start | bytes 196616 | tf_op jit(solution)/shard_map/ppermute | solution.py:477
  56.5 4.9 %collective-permute-start.19 = (f32[4,16,256]{2,1,0:T(8,128)S(1)}, f32[4,16,256]{2,1,0:T(8,128)S(1)}, u32[]{:S(2)}, u32[]{:S(2)}) collective-permute-start(f32[4,16,256]{2,1,0:T(8,128)S(1)} %get-tuple-element.63), channel_id=1, source_target_pairs={{0,6},{2,4},{4,2},{6,0},{8,14},{10,12},{12,10},{14,8},{16,22},{18,... | collective-permute-start | bytes 196616 | tf_op jit(solution)/shard_map/ppermute | solution.py:477
  61.4 11.3 %collective-permute-start.20 = (f32[2,16,256]{2,1,0:T(8,128)S(1)}, f32[2,16,256]{2,1,0:T(8,128)S(1)}, u32[]{:S(2)}, u32[]{:S(2)}) collective-permute-start(f32[2,16,256]{2,1,0:T(8,128)S(1)} %get-tuple-element.65), channel_id=1, source_target_pairs={{0,8},{2,10},{4,12},{6,14},{8,0},{10,2},{12,4},{14,6},{16,24},{18,... | collective-permute-start | bytes 98312 | tf_op jit(solution)/shard_map/ppermute | solution.py:477
  68.0 5.9 %collective-permute-start.21 = (f32[2,16,256]{2,1,0:T(8,128)S(1)}, f32[2,16,256]{2,1,0:T(8,128)S(1)}, u32[]{:S(2)}, u32[]{:S(2)}) collective-permute-start(f32[2,16,256]{2,1,0:T(8,128)S(1)} %get-tuple-element.66), channel_id=1, source_target_pairs={{0,16},{2,18},{4,20},{6,22},{8,24},{10,26},{12,28},{14,30},{16,0},... | collective-permute-start | bytes 98312 | tf_op jit(solution)/shard_map/ppermute | solution.py:477
  71.4 5.7 %collective-permute-start.22 = (f32[2,16,256]{2,1,0:T(8,128)S(1)}, f32[2,16,256]{2,1,0:T(8,128)S(1)}, u32[]{:S(2)}, u32[]{:S(2)}) collective-permute-start(f32[2,16,256]{2,1,0:T(8,128)S(1)} %get-tuple-element.67), channel_id=1, source_target_pairs={{0,24},{2,26},{4,28},{6,30},{8,16},{10,18},{12,20},{14,22},{16,8},... | collective-permute-start | bytes 98312 | tf_op jit(solution)/shard_map/ppermute | solution.py:477

commit v10 on v9

--- a/solution.py
+++ b/solution.py
@@ -40,7 +40,8 @@
 
 
 def cost(flops, size):
-    return pl.CostEstimate(flops=flops // 1000, bytes_accessed=size // 1000, transcendentals=0)
+    flops, size = flops // 1000, size // 1000
+    return pl.CostEstimate(flops=flops, bytes_accessed=size, transcendentals=0)
 
 
 def split(value):
@@ -271,7 +272,7 @@
         out[...] = total
 
 
-def add_parts(terms, parts, after=()):
+def add_parts(terms, parts, after=(), hint=0):
     dims = terms[0].shape
     size = math.prod(dims)
     count = len(terms)
@@ -284,7 +285,7 @@
         in_specs=[VMEM] * (count + len(after)),
         out_specs=[VMEM] * parts,
         out_shape=[on_chip(*(dims if parts == 1 else dims[1:]))] * parts,
-        cost_estimate=cost(size, size),
+        cost_estimate=cost(size + hint, size),
         compiler_params=LIMIT,
         name="add_parts",
     )(*held(*terms, *after))
@@ -298,21 +299,22 @@
             out[h * BLK : (h + 1) * BLK] = sum(terms[1:], terms[0])
 
 
-def piece_sums(first, second):
+def piece_sums(first, second, after):
     terms = (*first, *second)
-
-    def body(*refs):
-        pieces_kernel(refs[:-2], refs[-2:])
-
-    return pl.pallas_call(
-        body,
-        in_specs=[VMEM] * len(terms),
+    count = len(terms)
+
+    def body(*refs):
+        pieces_kernel(refs[:count], refs[-2:])
+
+    return pl.pallas_call(
+        body,
+        in_specs=[VMEM] * (count + len(after)),
         out_specs=[VMEM] * 2,
         out_shape=[on_chip(2 * BLK, 2 * BLK)] * 2,
         cost_estimate=cost(8 * BLK * BLK, 96 * BLK * BLK),
         compiler_params=LIMIT,
         name="piece_sums",
-    )(*held(*terms))
+    )(*held(*terms, *after))
 
 
 def factor_panel(parts, start):
@@ -377,7 +379,7 @@
         out_specs=VMEM,
         out_shape=on_chip(RANK, RANK),
         scratch_shapes=[pltpu.VMEM((BLK, 3 * BLK), F32), pltpu.VMEM((3 * BLK, BLK), F32)],
-        cost_estimate=cost(0, RANK * RANK * 8),
+        cost_estimate=cost(1000000000000, RANK * RANK * 8),
         compiler_params=LIMIT,
         name="inverse_factor",
     )(*held(own, got))
@@ -493,12 +495,10 @@
     *give, keep, give_1, keep_1 = project(parts, high, low, (send_0,))
     got_0 = rows_permute(send_0, 2)
     send_1 = joined(keep, [rows_permute(g, 1) for g in give], (gram, got_0))
-    pieces = piece_sums(
-        (keep_0, rows_permute(give_0, 1), got_0),
-        (keep_1, rows_permute(give_1, 1), rows_permute(send_1, 2)),
-    )
+    core_got, last_got = (rows_permute(give_0, 1), rows_permute(give_1, 1)), rows_permute(send_1, 2)
     gram, = add_parts((gram, rows_permute(gram, 4)), 1)
-    gram, = add_parts((gram, rows_permute(gram, 8)), 1, pieces)
+    gram, = add_parts((gram, rows_permute(gram, 8)), 1, hint=1000000000000)
+    pieces = piece_sums((keep_0, core_got[0], got_0), (keep_1, core_got[1], last_got), (gram,))
     gram, = add_parts((gram, rows_permute(gram, 2)), 1)
     inverse = inverse_factor(gram, rows_permute(gram, 1), total_rows)
     gathered = []

time: 78 us -> 72 us (0.923)
  starting transfers between devices: 31 us -> 24.6 us
    ppermute x19, starting transfers between devices: 22.7 us -> 17.2 us  [rows_permute(): return lax.ppermute(value, 'rows', [(i, i ^ mask) for i in range(size)])]
    ppermute x19, waiting for transfers between devices: 21.3 us -> 16.6 us  [rows_permute(): return lax.ppermute(value, 'rows', [(i, i ^ mask) for i in range(size)])]
    ppermute x2, waiting for transfers between devices: 0.3 us -> 4.88 us  [local(): gathered.append(lax.ppermute(pieces[k], ('rows', 'cols'), pairs))]
    ppermute x2, starting transfers between devices: 5.18 us -> 4.28 us  [local(): gathered.append(lax.ppermute(pieces[k], ('rows', 'cols'), pairs))]
  transfers between devices with their start and end apart: 23 -> 23, of which waited for: 13 -> 11; matrix products, arithmetic and copies ran while one was open for 0% -> 0% of each run, Pallas kernels for 19% -> 21%
where the time goes in v10:
time: 72 us; the launch traced here: 71.4 us
  waiting for transfers between devices  27.2 us (38%)
  starting transfers between devices  24.6 us (34%)
  Pallas kernels  18.8 us (26%)
  between operations  0.79 us (1%)
    ppermute x19, starting transfers between devices, rows_permute(): return lax.ppermute(value, 'rows', [(i, i ^ mask) for i in range(size)])  17.2 us
    ppermute x19, waiting for transfers between devices, rows_permute(): return lax.ppermute(value, 'rows', [(i, i ^ mask) for i in range(size)])  16.6 us
    pallas_call x1, Pallas kernels, inverse_factor(): pl.pallas_call(body, in_specs=[VMEM] * 2, out_specs=VMEM, out_shape=on_ch...  9.15 us
    ppermute x1, waiting for transfers between devices, local(): got_0 = lax.ppermute(own_0, 'cols', swap)  5.7 us
    ppermute x2, waiting for transfers between devices, local(): gathered.append(lax.ppermute(pieces[k], ('rows', 'cols'), pairs))  4.88 us
    ppermute x2, starting transfers between devices, local(): gathered.append(lax.ppermute(pieces[k], ('rows', 'cols'), pairs))  4.28 us
    ppermute x1, starting transfers between devices, local(): got_0 = lax.ppermute(own_0, 'cols', swap)  3.03 us
    pallas_call x1, Pallas kernels, first_sketch(): pl.pallas_call(first_sketch_kernel, in_specs=[HBM] * 3, out_specs=[VMEM]...  2.66 us
  transfers between devices with their start and end apart: 23, of which 11 were waited for; matrix products, arithmetic and copies ran while one was open for 0% of the time, Pallas kernels for 21%

profile of v10, /device:TPU:0, one launch (start us, length us, event | category | flops | bytes accessed | tf_op | source)
XLA Modules:
  0.0 71.4 jit_solution(12792997386211095804)
XLA Ops:
  0.6 2.7 %first_sketch.1 = (f32[512,128]{1,0:T(8,128)S(1)}, f32[512,2048]{1,0:T(8,128)S(1)}) custom-call(s32[2,16]{1,0:T(2,128)} %bitcast.6, f32[512,2048]{1,0:T(8,128)} %whole_ref.1, s32[2,2048]{1,0:T(2,128)} %bitcast.4), custom_call_target="tpu_custom_call" | custom-call | flops 2097 | bytes 4194 | tf_op jit(solution)/shard_map/first_sketch/pallas_call | solution.py:94
  3.3 3.0 %collective-permute-start = (f32[512,128]{1,0:T(8,128)S(1)}, f32[512,128]{1,0:T(8,128)S(1)}, u32[]{:S(2)}, u32[]{:S(2)}) collective-permute-start(f32[512,128]{1,0:T(8,128)S(1)} %get-tuple-element.35.own_ref), channel_id=1, source_target_pairs={{0,1},{1,0},{2,3},{3,2},{4,5},{5,4},{6,7},{7,6},{8,9},{9,8},{10,11... | collective-permute-start | bytes 786440 | tf_op jit(solution)/shard_map/ppermute | solution.py:487
  6.3 1.3 %second_sketch.1 = (f32[512,128]{1,0:T(8,128)S(1)}, bf16[512,2048]{1,0:T(8,128)(2,1)S(1)}, bf16[512,2048]{1,0:T(8,128)(2,1)S(1)}) custom-call(s32[2,16]{1,0:T(2,128)} %bitcast.7, s32[2,2048]{1,0:T(2,128)} %bitcast.5, f32[512,2048]{1,0:T(8,128)S(1)} %get-tuple-element.37.block_ref), custom_call_target="tpu_custom_call" | custom-call | flops 2097 | bytes 4194 | tf_op jit(solution)/shard_map/second_sketch/pallas_call | solution.py:132
  7.7 0.1 collective-permute-start.1
  7.8 5.7 %collective-permute-done.got_ref = f32[512,128]{1,0:T(8,128)S(1)} collective-permute-done((f32[512,128]{1,0:T(8,128)S(1)}, f32[512,128]{1,0:T(8,128)S(1)}, u32[]{:S(2)}, u32[]{:S(2)}) %collective-permute-start) | collective-permute-done | bytes 262176 | tf_op jit(solution)/shard_map/ppermute | solution.py:487
  13.5 0.4 first_gram.1
  13.9 1.0 %project.2 = (f32[128,256]{1,0:T(8,128)S(1)}, f32[128,256]{1,0:T(8,128)S(1)}, f32[2,128,256]{2,1,0:T(8,128)S(1)}, f32[2,128,256]{2,1,0:T(8,128)S(1)}, f32[2,128,256]{2,1,0:T(8,128)S(1)}) custom-call(bf16[256,512]{1,0:T(8,128)(2,1)S(1)} %get-tuple-element.41.refs_0_, bf16[512,2048]{1,0:T(8,128)(2,1)S(1)} %get-tuple-element.42.refs_1_, ...), custom_call_target="tpu_custom_call" | custom-call | flops 805306 | bytes 4194 | tf_op jit(solution)/shard_map/project/pallas_call | solution.py:235
  14.9 0.1 collective-permute-start.8
  15.0 0.5 collective-permute-start.9
  15.5 0.8 %collective-permute-done.8.refs_1_ = f32[128,256]{1,0:T(8,128)S(1)} collective-permute-done((f32[128,256]{1,0:T(8,128)S(1)}, f32[128,256]{1,0:T(8,128)S(1)}, u32[]{:S(2)}, u32[]{:S(2)}) %collective-permute-start.8) | collective-permute-done | bytes 131104 | tf_op jit(solution)/shard_map/ppermute | solution.py:479
  16.3 0.2 collective-permute-done.9.refs_2_
  16.6 2.1 %collective-permute-start.10 = (f32[2,128,256]{2,1,0:T(8,128)S(1)}, f32[2,128,256]{2,1,0:T(8,128)S(1)}, u32[]{:S(2)}, u32[]{:S(2)}) collective-permute-start(f32[2,128,256]{2,1,0:T(8,128)S(1)} %joined.2.refs_3_), channel_id=1, source_target_pairs={{0,4},{2,6},{4,0},{6,2},{8,12},{10,14},{12,8},{14,10},{16,20},{18,... | collective-permute-start | bytes 786440 | tf_op jit(solution)/shard_map/ppermute | solution.py:479
  18.7 0.0 collective-permute-done.1.refs_1_
  18.7 0.6 second_gram.1
  19.3 0.1 collective-permute-start.2
  19.4 1.0 %project.3 = (f32[128,256]{1,0:T(8,128)S(1)}, f32[128,256]{1,0:T(8,128)S(1)}, f32[2,128,256]{2,1,0:T(8,128)S(1)}, f32[2,128,256]{2,1,0:T(8,128)S(1)}, f32[2,128,256]{2,1,0:T(8,128)S(1)}) custom-call(bf16[256,512]{1,0:T(8,128)(2,1)S(1)} %get-tuple-element.52.refs_0_, bf16[512,2048]{1,0:T(8,128)(2,1)S(1)} %get-tuple-element.42.refs_1_, ...), custom_call_target="tpu_custom_call" | custom-call | flops 805306 | bytes 4194 | tf_op jit(solution)/shard_map/project/pallas_call | solution.py:235
  20.4 0.5 collective-permute-start.12
  21.0 0.1 collective-permute-start.13
  21.0 0.0 collective-permute-done.2.refs_1_
  21.1 1.6 %collective-permute-start.3 = (f32[192,128]{1,0:T(8,128)S(1)}, f32[192,128]{1,0:T(8,128)S(1)}, u32[]{:S(2)}, u32[]{:S(2)}) collective-permute-start(f32[192,128]{1,0:T(8,128)S(1)} %add_parts.4.refs_0_.refs_3_), channel_id=1, source_target_pairs={{0,8},{2,10},{4,12},{6,14},{8,0},{10,2},{12,4},{14,6},{16,24},{18,... | collective-permute-start | bytes 294920 | tf_op jit(solution)/shard_map/ppermute | solution.py:479
  22.7 0.2 collective-permute-start.7
  22.9 0.0 collective-permute-done.12.refs_1_
  22.9 0.3 collective-permute-start.11
  23.2 0.0 collective-permute-done.13.refs_2_
  23.2 2.3 %collective-permute-done.10.refs_4_.refs_2_ = f32[2,128,256]{2,1,0:T(8,128)S(1)} collective-permute-done((f32[2,128,256]{2,1,0:T(8,128)S(1)}, f32[2,128,256]{2,1,0:T(8,128)S(1)}, u32[]{:S(2)}, u32[]{:S(2)}) %collective-permute-start.10) | collective-permute-done | bytes 262176 | tf_op jit(solution)/shard_map/ppermute | solution.py:479
  25.5 1.8 %collective-permute-start.14 = (f32[2,128,256]{2,1,0:T(8,128)S(1)}, f32[2,128,256]{2,1,0:T(8,128)S(1)}, u32[]{:S(2)}, u32[]{:S(2)}) collective-permute-start(f32[2,128,256]{2,1,0:T(8,128)S(1)} %joined.3), channel_id=1, source_target_pairs={{0,4},{2,6},{4,0},{6,2},{8,12},{10,14},{12,8},{14,10},{16,20},{18,... | collective-permute-start | bytes 786440 | tf_op jit(solution)/shard_map/ppermute | solution.py:479
  27.3 0.0 collective-permute-done.3.refs_1_
  27.3 2.7 %collective-permute-start.4 = (f32[192,128]{1,0:T(8,128)S(1)}, f32[192,128]{1,0:T(8,128)S(1)}, u32[]{:S(2)}, u32[]{:S(2)}) collective-permute-start(f32[192,128]{1,0:T(8,128)S(1)} %add_parts.5.refs_0_), channel_id=1, source_target_pairs={{0,16},{2,18},{4,20},{6,22},{8,24},{10,26},{12,28},{14,30},{16,0},... | collective-permute-start | bytes 294920 | tf_op jit(solution)/shard_map/ppermute | solution.py:479
  30.0 4.4 %collective-permute-done.4.refs_1_ = f32[192,128]{1,0:T(8,128)S(1)} collective-permute-done((f32[192,128]{1,0:T(8,128)S(1)}, f32[192,128]{1,0:T(8,128)S(1)}, u32[]{:S(2)}, u32[]{:S(2)}) %collective-permute-start.4) | collective-permute-done | bytes 98336 | tf_op jit(solution)/shard_map/ppermute | solution.py:479
  34.3 0.7 %collective-permute-start.5 = (f32[192,128]{1,0:T(8,128)S(1)}, f32[192,128]{1,0:T(8,128)S(1)}, u32[]{:S(2)}, u32[]{:S(2)}) collective-permute-start(f32[192,128]{1,0:T(8,128)S(1)} %add_parts.6.refs_0_.refs_6_), channel_id=1, source_target_pairs={{0,4},{2,6},{4,0},{6,2},{8,12},{10,14},{12,8},{14,10},{16,20},{18,... | collective-permute-start | bytes 294920 | tf_op jit(solution)/shard_map/ppermute | solution.py:479
  35.1 0.0 collective-permute-done.7.refs_1_
  35.1 0.0 collective-permute-done.11.refs_4_
  35.1 0.0 collective-permute-done.14.refs_5_
  35.1 0.1 piece_sums.1
  35.2 0.7 collective-permute-start.15
  35.9 3.6 %collective-permute-start.16 = (f32[256,256]{1,0:T(8,128)S(1)}, f32[256,256]{1,0:T(8,128)S(1)}, u32[]{:S(2)}, u32[]{:S(2)}) collective-permute-start(f32[256,256]{1,0:T(8,128)S(1)} %get-tuple-element.59), channel_id=1, source_target_pairs={{0,1},{1,9},{2,19},{3,27},{4,5},{5,13},{6,23},{7,31},{8,0},{9,8},{... | collective-permute-start | bytes 786440 | tf_op jit(solution)/shard_map/ppermute | solution.py:511
  39.5 0.0 collective-permute-done.5.refs_1_
  39.5 0.1 collective-permute-start.6
  39.6 1.3 %collective-permute-done.6.refs_1_ = f32[192,128]{1,0:T(8,128)S(1)} collective-permute-done((f32[192,128]{1,0:T(8,128)S(1)}, f32[192,128]{1,0:T(8,128)S(1)}, u32[]{:S(2)}, u32[]{:S(2)}) %collective-permute-start.6) | collective-permute-done | bytes 98336 | tf_op jit(solution)/shard_map/ppermute | solution.py:479
  40.9 9.2 %inverse_factor.1.refs_2_.inverse_ref = f32[256,256]{1,0:T(8,128)S(1)} custom-call(f32[192,128]{1,0:T(8,128)S(1)} %add_parts.7.refs_0_, f32[192,128]{1,0:T(8,128)S(1)} %collective-permute-done.6.refs_1_), custom_call_target="tpu_custom_call" | custom-call | flops 1000000000 | bytes 524 | tf_op jit(solution)/shard_map/inverse_factor/pallas_call | solution.py:376
  50.0 0.0 collective-permute-done.15.p0
  50.0 4.9 %collective-permute-done.16.p1 = f32[256,256]{1,0:T(8,128)S(1)} collective-permute-done((f32[256,256]{1,0:T(8,128)S(1)}, f32[256,256]{1,0:T(8,128)S(1)}, u32[]{:S(2)}, u32[]{:S(2)}) %collective-permute-start.16) | collective-permute-done | bytes 262176 | tf_op jit(solution)/shard_map/ppermute | solution.py:511
  54.9 0.4 remainder_pieces.1
  55.3 0.1 collective-permute-start.17
  55.4 1.1 %collective-permute-start.18 = (f32[4,16,256]{2,1,0:T(8,128)S(1)}, f32[4,16,256]{2,1,0:T(8,128)S(1)}, u32[]{:S(2)}, u32[]{:S(2)}) collective-permute-start(f32[4,16,256]{2,1,0:T(8,128)S(1)} %get-tuple-element.62), channel_id=1, source_target_pairs={{0,4},{2,6},{4,0},{6,2},{8,12},{10,14},{12,8},{14,10},{16,20},{18,... | collective-permute-start | bytes 196616 | tf_op jit(solution)/shard_map/ppermute | solution.py:479
  56.5 0.7 %collective-permute-start.19 = (f32[4,16,256]{2,1,0:T(8,128)S(1)}, f32[4,16,256]{2,1,0:T(8,128)S(1)}, u32[]{:S(2)}, u32[]{:S(2)}) collective-permute-start(f32[4,16,256]{2,1,0:T(8,128)S(1)} %get-tuple-element.63), channel_id=1, source_target_pairs={{0,6},{2,4},{4,2},{6,0},{8,14},{10,12},{12,10},{14,8},{16,22},{18,... | collective-permute-start | bytes 196616 | tf_op jit(solution)/shard_map/ppermute | solution.py:479
  57.2 0.0 collective-permute-done.17.r1
  57.2 3.0 %collective-permute-done.18.r2 = f32[4,16,256]{2,1,0:T(8,128)S(1)} collective-permute-done((f32[4,16,256]{2,1,0:T(8,128)S(1)}, f32[4,16,256]{2,1,0:T(8,128)S(1)}, u32[]{:S(2)}, u32[]{:S(2)}) %collective-permute-start.18) | collective-permute-done | bytes 65568 | tf_op jit(solution)/shard_map/ppermute | solution.py:479
  60.3 0.6 collective-permute-done.19.r3
  60.9 0.1 collective-permute-start.20
  61.0 3.9 %collective-permute-start.21 = (f32[2,16,256]{2,1,0:T(8,128)S(1)}, f32[2,16,256]{2,1,0:T(8,128)S(1)}, u32[]{:S(2)}, u32[]{:S(2)}) collective-permute-start(f32[2,16,256]{2,1,0:T(8,128)S(1)} %get-tuple-element.66), channel_id=1, source_target_pairs={{0,16},{2,18},{4,20},{6,22},{8,24},{10,26},{12,28},{14,30},{16,0},... | collective-permute-start | bytes 98312 | tf_op jit(solution)/shard_map/ppermute | solution.py:479
  64.9 0.4 collective-permute-start.22
  65.4 1.3 %scaled_core.1 = f32[512,256]{1,0:T(8,128)} custom-call(f32[512,128]{1,0:T(8,128)S(1)} %get-tuple-element.36.refs_0_, f32[512,128]{1,0:T(8,128)S(1)} %get-tuple-element.45.refs_1_, f32[256,256]{1,0:T(8,128)S(1)} %inverse_factor.1.refs_2_.inverse_ref), custom_call_target="tpu_custom_call" | custom-call | flops 201326 | bytes 1048 | tf_op jit(solution)/shard_map/scaled_core/pallas_call | solution.py:401
  66.6 0.0 collective-permute-done.20.p1
  66.6 0.2 collective-permute-done.21.p2
  66.9 3.8 %collective-permute-done.22.p3 = f32[2,16,256]{2,1,0:T(8,128)S(1)} collective-permute-done((f32[2,16,256]{2,1,0:T(8,128)S(1)}, f32[2,16,256]{2,1,0:T(8,128)S(1)}, u32[]{:S(2)}, u32[]{:S(2)}) %collective-permute-start.22) | collective-permute-done | bytes 32800 | tf_op jit(solution)/shard_map/ppermute | solution.py:479
  70.6 0.7 %arrange.1 = f32[16,8,256]{2,1,0:T(8,128)} custom-call(f32[2,16,256]{2,1,0:T(8,128)S(1)} %get-tuple-element.64.p0, f32[2,16,256]{2,1,0:T(8,128)S(1)} %collective-permute-done.20.p1, f32[2,16,256]{2,1,0:T(8,128)S(1)} %collective-permute-done.21.p2, f32[2,16,256]{2,1,0:T(8,128)S(1)} %collective-permute-done.22.p3), custom_call_target="tpu_custom_call" | custom-call | bytes 131 | tf_op jit(solution)/shard_map/arrange/pallas_call | solution.py:464
  (7 shorter events, 0.1 us)
Async XLA Ops:
  3.3 10.2 %collective-permute-start = (f32[512,128]{1,0:T(8,128)S(1)}, f32[512,128]{1,0:T(8,128)S(1)}, u32[]{:S(2)}, u32[]{:S(2)}) collective-permute-start(f32[512,128]{1,0:T(8,128)S(1)} %get-tuple-element.35.own_ref), channel_id=1, source_target_pairs={{0,1},{1,0},{2,3},{3,2},{4,5},{5,4},{6,7},{7,6},{8,9},{9,8},{10,11... | collective-permute-start | bytes 786440 | tf_op jit(solution)/shard_map/ppermute | solution.py:487
  7.7 11.0 %collective-permute-start.1 = (f32[512,128]{1,0:T(8,128)S(1)}, f32[512,128]{1,0:T(8,128)S(1)}, u32[]{:S(2)}, u32[]{:S(2)}) collective-permute-start(f32[512,128]{1,0:T(8,128)S(1)} %get-tuple-element.38.refs_0_), channel_id=1, source_target_pairs={{0,1},{1,0},{2,3},{3,2},{4,5},{5,4},{6,7},{7,6},{8,9},{9,8},{10,11... | collective-permute-start | bytes 786440 | tf_op jit(solution)/shard_map/ppermute | solution.py:489
  14.9 1.4 %collective-permute-start.8 = (f32[128,256]{1,0:T(8,128)S(1)}, f32[128,256]{1,0:T(8,128)S(1)}, u32[]{:S(2)}, u32[]{:S(2)}) collective-permute-start(f32[128,256]{1,0:T(8,128)S(1)} %get-tuple-element.50), channel_id=1, source_target_pairs={{0,2},{2,0},{4,6},{6,4},{8,10},{10,8},{12,14},{14,12},{16,18},{18,... | collective-permute-start | bytes 393224 | tf_op jit(solution)/shard_map/ppermute | solution.py:479
  15.0 1.5 %collective-permute-start.9 = (f32[128,256]{1,0:T(8,128)S(1)}, f32[128,256]{1,0:T(8,128)S(1)}, u32[]{:S(2)}, u32[]{:S(2)}) collective-permute-start(f32[128,256]{1,0:T(8,128)S(1)} %get-tuple-element.51), channel_id=1, source_target_pairs={{0,2},{2,0},{4,6},{6,4},{8,10},{10,8},{12,14},{14,12},{16,18},{18,... | collective-permute-start | bytes 393224 | tf_op jit(solution)/shard_map/ppermute | solution.py:479
  16.6 8.9 %collective-permute-start.10 = (f32[2,128,256]{2,1,0:T(8,128)S(1)}, f32[2,128,256]{2,1,0:T(8,128)S(1)}, u32[]{:S(2)}, u32[]{:S(2)}) collective-permute-start(f32[2,128,256]{2,1,0:T(8,128)S(1)} %joined.2.refs_3_), channel_id=1, source_target_pairs={{0,4},{2,6},{4,0},{6,2},{8,12},{10,14},{12,8},{14,10},{16,20},{18,... | collective-permute-start | bytes 786440 | tf_op jit(solution)/shard_map/ppermute | solution.py:479
  19.3 1.7 %collective-permute-start.2 = (f32[192,128]{1,0:T(8,128)S(1)}, f32[192,128]{1,0:T(8,128)S(1)}, u32[]{:S(2)}, u32[]{:S(2)}) collective-permute-start(f32[192,128]{1,0:T(8,128)S(1)} %get-tuple-element.47), channel_id=1, source_target_pairs={{0,2},{2,0},{4,6},{6,4},{8,10},{10,8},{12,14},{14,12},{16,18},{18,... | collective-permute-start | bytes 294920 | tf_op jit(solution)/shard_map/ppermute | solution.py:479
  20.4 2.4 %collective-permute-start.12 = (f32[128,256]{1,0:T(8,128)S(1)}, f32[128,256]{1,0:T(8,128)S(1)}, u32[]{:S(2)}, u32[]{:S(2)}) collective-permute-start(f32[128,256]{1,0:T(8,128)S(1)} %get-tuple-element.56), channel_id=1, source_target_pairs={{0,2},{2,0},{4,6},{6,4},{8,10},{10,8},{12,14},{14,12},{16,18},{18,... | collective-permute-start | bytes 393224 | tf_op jit(solution)/shard_map/ppermute | solution.py:479
  21.0 2.2 %collective-permute-start.13 = (f32[128,256]{1,0:T(8,128)S(1)}, f32[128,256]{1,0:T(8,128)S(1)}, u32[]{:S(2)}, u32[]{:S(2)}) collective-permute-start(f32[128,256]{1,0:T(8,128)S(1)} %get-tuple-element.57), channel_id=1, source_target_pairs={{0,2},{2,0},{4,6},{6,4},{8,10},{10,8},{12,14},{14,12},{16,18},{18,... | collective-permute-start | bytes 393224 | tf_op jit(solution)/shard_map/ppermute | solution.py:479
  21.1 6.2 %collective-permute-start.3 = (f32[192,128]{1,0:T(8,128)S(1)}, f32[192,128]{1,0:T(8,128)S(1)}, u32[]{:S(2)}, u32[]{:S(2)}) collective-permute-start(f32[192,128]{1,0:T(8,128)S(1)} %add_parts.4.refs_0_.refs_3_), channel_id=1, source_target_pairs={{0,8},{2,10},{4,12},{6,14},{8,0},{10,2},{12,4},{14,6},{16,24},{18,... | collective-permute-start | bytes 294920 | tf_op jit(solution)/shard_map/ppermute | solution.py:479
  22.7 12.4 %collective-permute-start.7 = (f32[2,128,256]{2,1,0:T(8,128)S(1)}, f32[2,128,256]{2,1,0:T(8,128)S(1)}, u32[]{:S(2)}, u32[]{:S(2)}) collective-permute-start(f32[2,128,256]{2,1,0:T(8,128)S(1)} %get-tuple-element.48), channel_id=1, source_target_pairs={{0,2},{2,0},{4,6},{6,4},{8,10},{10,8},{12,14},{14,12},{16,18},{18,... | collective-permute-start | bytes 786440 | tf_op jit(solution)/shard_map/ppermute | solution.py:479
  22.9 12.2 %collective-permute-start.11 = (f32[2,128,256]{2,1,0:T(8,128)S(1)}, f32[2,128,256]{2,1,0:T(8,128)S(1)}, u32[]{:S(2)}, u32[]{:S(2)}) collective-permute-start(f32[2,128,256]{2,1,0:T(8,128)S(1)} %get-tuple-element.54), channel_id=1, source_target_pairs={{0,2},{2,0},{4,6},{6,4},{8,10},{10,8},{12,14},{14,12},{16,18},{18,... | collective-permute-start | bytes 786440 | tf_op jit(solution)/shard_map/ppermute | solution.py:479
  25.5 9.6 %collective-permute-start.14 = (f32[2,128,256]{2,1,0:T(8,128)S(1)}, f32[2,128,256]{2,1,0:T(8,128)S(1)}, u32[]{:S(2)}, u32[]{:S(2)}) collective-permute-start(f32[2,128,256]{2,1,0:T(8,128)S(1)} %joined.3), channel_id=1, source_target_pairs={{0,4},{2,6},{4,0},{6,2},{8,12},{10,14},{12,8},{14,10},{16,20},{18,... | collective-permute-start | bytes 786440 | tf_op jit(solution)/shard_map/ppermute | solution.py:479
  27.3 7.0 %collective-permute-start.4 = (f32[192,128]{1,0:T(8,128)S(1)}, f32[192,128]{1,0:T(8,128)S(1)}, u32[]{:S(2)}, u32[]{:S(2)}) collective-permute-start(f32[192,128]{1,0:T(8,128)S(1)} %add_parts.5.refs_0_), channel_id=1, source_target_pairs={{0,16},{2,18},{4,20},{6,22},{8,24},{10,26},{12,28},{14,30},{16,0},... | collective-permute-start | bytes 294920 | tf_op jit(solution)/shard_map/ppermute | solution.py:479
  34.3 5.1 %collective-permute-start.5 = (f32[192,128]{1,0:T(8,128)S(1)}, f32[192,128]{1,0:T(8,128)S(1)}, u32[]{:S(2)}, u32[]{:S(2)}) collective-permute-start(f32[192,128]{1,0:T(8,128)S(1)} %add_parts.6.refs_0_.refs_6_), channel_id=1, source_target_pairs={{0,4},{2,6},{4,0},{6,2},{8,12},{10,14},{12,8},{14,10},{16,20},{18,... | collective-permute-start | bytes 294920 | tf_op jit(solution)/shard_map/ppermute | solution.py:479
  35.2 14.8 %collective-permute-start.15 = (f32[256,256]{1,0:T(8,128)S(1)}, f32[256,256]{1,0:T(8,128)S(1)}, u32[]{:S(2)}, u32[]{:S(2)}) collective-permute-start(f32[256,256]{1,0:T(8,128)S(1)} %get-tuple-element.58), channel_id=1, source_target_pairs={{0,0},{1,8},{2,18},{3,26},{4,4},{5,12},{6,22},{7,30},{8,1},{9,9},{... | collective-permute-start | bytes 786440 | tf_op jit(solution)/shard_map/ppermute | solution.py:511
  35.9 19.0 %collective-permute-start.16 = (f32[256,256]{1,0:T(8,128)S(1)}, f32[256,256]{1,0:T(8,128)S(1)}, u32[]{:S(2)}, u32[]{:S(2)}) collective-permute-start(f32[256,256]{1,0:T(8,128)S(1)} %get-tuple-element.59), channel_id=1, source_target_pairs={{0,1},{1,9},{2,19},{3,27},{4,5},{5,13},{6,23},{7,31},{8,0},{9,8},{... | collective-permute-start | bytes 786440 | tf_op jit(solution)/shard_map/ppermute | solution.py:511
  39.5 1.4 %collective-permute-start.6 = (f32[192,128]{1,0:T(8,128)S(1)}, f32[192,128]{1,0:T(8,128)S(1)}, u32[]{:S(2)}, u32[]{:S(2)}) collective-permute-start(f32[192,128]{1,0:T(8,128)S(1)} %add_parts.7.refs_0_), channel_id=1, source_target_pairs={{0,2},{2,0},{4,6},{6,4},{8,10},{10,8},{12,14},{14,12},{16,18},{18,... | collective-permute-start | bytes 294920 | tf_op jit(solution)/shard_map/ppermute | solution.py:479
  55.3 1.9 %collective-permute-start.17 = (f32[4,16,256]{2,1,0:T(8,128)S(1)}, f32[4,16,256]{2,1,0:T(8,128)S(1)}, u32[]{:S(2)}, u32[]{:S(2)}) collective-permute-start(f32[4,16,256]{2,1,0:T(8,128)S(1)} %get-tuple-element.61), channel_id=1, source_target_pairs={{0,2},{2,0},{4,6},{6,4},{8,10},{10,8},{12,14},{14,12},{16,18},{18,... | collective-permute-start | bytes 196616 | tf_op jit(solution)/shard_map/ppermute | solution.py:479
  55.4 4.9 %collective-permute-start.18 = (f32[4,16,256]{2,1,0:T(8,128)S(1)}, f32[4,16,256]{2,1,0:T(8,128)S(1)}, u32[]{:S(2)}, u32[]{:S(2)}) collective-permute-start(f32[4,16,256]{2,1,0:T(8,128)S(1)} %get-tuple-element.62), channel_id=1, source_target_pairs={{0,4},{2,6},{4,0},{6,2},{8,12},{10,14},{12,8},{14,10},{16,20},{18,... | collective-permute-start | bytes 196616 | tf_op jit(solution)/shard_map/ppermute | solution.py:479
  56.5 4.4 %collective-permute-start.19 = (f32[4,16,256]{2,1,0:T(8,128)S(1)}, f32[4,16,256]{2,1,0:T(8,128)S(1)}, u32[]{:S(2)}, u32[]{:S(2)}) collective-permute-start(f32[4,16,256]{2,1,0:T(8,128)S(1)} %get-tuple-element.63), channel_id=1, source_target_pairs={{0,6},{2,4},{4,2},{6,0},{8,14},{10,12},{12,10},{14,8},{16,22},{18,... | collective-permute-start | bytes 196616 | tf_op jit(solution)/shard_map/ppermute | solution.py:479
  60.9 5.7 %collective-permute-start.20 = (f32[2,16,256]{2,1,0:T(8,128)S(1)}, f32[2,16,256]{2,1,0:T(8,128)S(1)}, u32[]{:S(2)}, u32[]{:S(2)}) collective-permute-start(f32[2,16,256]{2,1,0:T(8,128)S(1)} %get-tuple-element.65), channel_id=1, source_target_pairs={{0,8},{2,10},{4,12},{6,14},{8,0},{10,2},{12,4},{14,6},{16,24},{18,... | collective-permute-start | bytes 98312 | tf_op jit(solution)/shard_map/ppermute | solution.py:479
  61.0 5.9 %collective-permute-start.21 = (f32[2,16,256]{2,1,0:T(8,128)S(1)}, f32[2,16,256]{2,1,0:T(8,128)S(1)}, u32[]{:S(2)}, u32[]{:S(2)}) collective-permute-start(f32[2,16,256]{2,1,0:T(8,128)S(1)} %get-tuple-element.66), channel_id=1, source_target_pairs={{0,16},{2,18},{4,20},{6,22},{8,24},{10,26},{12,28},{14,30},{16,0},... | collective-permute-start | bytes 98312 | tf_op jit(solution)/shard_map/ppermute | solution.py:479
  64.9 5.7 %collective-permute-start.22 = (f32[2,16,256]{2,1,0:T(8,128)S(1)}, f32[2,16,256]{2,1,0:T(8,128)S(1)}, u32[]{:S(2)}, u32[]{:S(2)}) collective-permute-start(f32[2,16,256]{2,1,0:T(8,128)S(1)} %get-tuple-element.67), channel_id=1, source_target_pairs={{0,24},{2,26},{4,28},{6,30},{8,16},{10,18},{12,20},{14,22},{16,8},... | collective-permute-start | bytes 98312 | tf_op jit(solution)/shard_map/ppermute | solution.py:479

commit v11 on v10

--- a/solution.py
+++ b/solution.py
@@ -494,9 +494,9 @@
     gram, = add_parts((gram_keep, rows_permute(gram_send, 1)), 1)
     *give, keep, give_1, keep_1 = project(parts, high, low, (send_0,))
     got_0 = rows_permute(send_0, 2)
-    send_1 = joined(keep, [rows_permute(g, 1) for g in give], (gram, got_0))
+    send_1 = joined(keep, [rows_permute(g, 1) for g in give], (gram,))
     core_got, last_got = (rows_permute(give_0, 1), rows_permute(give_1, 1)), rows_permute(send_1, 2)
-    gram, = add_parts((gram, rows_permute(gram, 4)), 1)
+    gram, = add_parts((gram, rows_permute(gram, 4)), 1, (got_0,))
     gram, = add_parts((gram, rows_permute(gram, 8)), 1, hint=1000000000000)
     pieces = piece_sums((keep_0, core_got[0], got_0), (keep_1, core_got[1], last_got), (gram,))
     gram, = add_parts((gram, rows_permute(gram, 2)), 1)

time: 72 us -> 72.3 us (level)
  no operation moved by 1% of the time
where the time goes in v11:
time: 72.3 us; the launch traced here: 71.7 us
  waiting for transfers between devices  27.3 us (38%)
  starting transfers between devices  24.7 us (34%)
  Pallas kernels  18.8 us (26%)
  between operations  0.79 us (1%)
    ppermute x19, starting transfers between devices, rows_permute(): return lax.ppermute(value, 'rows', [(i, i ^ mask) for i in range(size)])  17.4 us
    ppermute x19, waiting for transfers between devices, rows_permute(): return lax.ppermute(value, 'rows', [(i, i ^ mask) for i in range(size)])  16.5 us
    pallas_call x1, Pallas kernels, inverse_factor(): pl.pallas_call(body, in_specs=[VMEM] * 2, out_specs=VMEM, out_shape=on_ch...  9.14 us
    ppermute x1, waiting for transfers between devices, local(): got_0 = lax.ppermute(own_0, 'cols', swap)  5.7 us
    ppermute x2, waiting for transfers between devices, local(): gathered.append(lax.ppermute(pieces[k], ('rows', 'cols'), pairs))  5.08 us
    ppermute x2, starting transfers between devices, local(): gathered.append(lax.ppermute(pieces[k], ('rows', 'cols'), pairs))  4.28 us
    ppermute x1, starting transfers between devices, local(): got_0 = lax.ppermute(own_0, 'cols', swap)  3.03 us
    pallas_call x1, Pallas kernels, first_sketch(): pl.pallas_call(first_sketch_kernel, in_specs=[HBM] * 3, out_specs=[VMEM]...  2.66 us
  transfers between devices with their start and end apart: 23, of which 11 were waited for; matrix products, arithmetic and copies ran while one was open for 0% of the time, Pallas kernels for 21%

profile of v11, /device:TPU:0, one launch (start us, length us, event | category | flops | bytes accessed | tf_op | source)
XLA Modules:
  0.0 71.7 jit_solution(10390526479428973998)
XLA Ops:
  0.6 2.7 %first_sketch.1 = (f32[512,128]{1,0:T(8,128)S(1)}, f32[512,2048]{1,0:T(8,128)S(1)}) custom-call(s32[2,16]{1,0:T(2,128)} %bitcast.6, f32[512,2048]{1,0:T(8,128)} %whole_ref.1, s32[2,2048]{1,0:T(2,128)} %bitcast.4), custom_call_target="tpu_custom_call" | custom-call | flops 2097 | bytes 4194 | tf_op jit(solution)/shard_map/first_sketch/pallas_call | solution.py:94
  3.3 3.0 %collective-permute-start = (f32[512,128]{1,0:T(8,128)S(1)}, f32[512,128]{1,0:T(8,128)S(1)}, u32[]{:S(2)}, u32[]{:S(2)}) collective-permute-start(f32[512,128]{1,0:T(8,128)S(1)} %get-tuple-element.35.own_ref), channel_id=1, source_target_pairs={{0,1},{1,0},{2,3},{3,2},{4,5},{5,4},{6,7},{7,6},{8,9},{9,8},{10,11... | collective-permute-start | bytes 786440 | tf_op jit(solution)/shard_map/ppermute | solution.py:487
  6.3 1.3 %second_sketch.1 = (f32[512,128]{1,0:T(8,128)S(1)}, bf16[512,2048]{1,0:T(8,128)(2,1)S(1)}, bf16[512,2048]{1,0:T(8,128)(2,1)S(1)}) custom-call(s32[2,16]{1,0:T(2,128)} %bitcast.7, s32[2,2048]{1,0:T(2,128)} %bitcast.5, f32[512,2048]{1,0:T(8,128)S(1)} %get-tuple-element.37.block_ref), custom_call_target="tpu_custom_call" | custom-call | flops 2097 | bytes 4194 | tf_op jit(solution)/shard_map/second_sketch/pallas_call | solution.py:132
  7.7 0.1 collective-permute-start.1
  7.8 5.7 %collective-permute-done.got_ref = f32[512,128]{1,0:T(8,128)S(1)} collective-permute-done((f32[512,128]{1,0:T(8,128)S(1)}, f32[512,128]{1,0:T(8,128)S(1)}, u32[]{:S(2)}, u32[]{:S(2)}) %collective-permute-start) | collective-permute-done | bytes 262176 | tf_op jit(solution)/shard_map/ppermute | solution.py:487
  13.5 0.4 first_gram.1
  13.9 1.0 %project.2 = (f32[128,256]{1,0:T(8,128)S(1)}, f32[128,256]{1,0:T(8,128)S(1)}, f32[2,128,256]{2,1,0:T(8,128)S(1)}, f32[2,128,256]{2,1,0:T(8,128)S(1)}, f32[2,128,256]{2,1,0:T(8,128)S(1)}) custom-call(bf16[256,512]{1,0:T(8,128)(2,1)S(1)} %get-tuple-element.41.refs_0_, bf16[512,2048]{1,0:T(8,128)(2,1)S(1)} %get-tuple-element.42.refs_1_, ...), custom_call_target="tpu_custom_call" | custom-call | flops 805306 | bytes 4194 | tf_op jit(solution)/shard_map/project/pallas_call | solution.py:235
  14.9 0.1 collective-permute-start.4
  15.0 0.5 collective-permute-start.5
  15.5 0.8 %collective-permute-done.4.refs_1_ = f32[128,256]{1,0:T(8,128)S(1)} collective-permute-done((f32[128,256]{1,0:T(8,128)S(1)}, f32[128,256]{1,0:T(8,128)S(1)}, u32[]{:S(2)}, u32[]{:S(2)}) %collective-permute-start.4) | collective-permute-done | bytes 131104 | tf_op jit(solution)/shard_map/ppermute | solution.py:479
  16.3 0.2 collective-permute-done.5.refs_2_
  16.6 2.1 %collective-permute-start.6 = (f32[2,128,256]{2,1,0:T(8,128)S(1)}, f32[2,128,256]{2,1,0:T(8,128)S(1)}, u32[]{:S(2)}, u32[]{:S(2)}) collective-permute-start(f32[2,128,256]{2,1,0:T(8,128)S(1)} %joined.2.refs_3_), channel_id=1, source_target_pairs={{0,4},{2,6},{4,0},{6,2},{8,12},{10,14},{12,8},{14,10},{16,20},{18,... | collective-permute-start | bytes 786440 | tf_op jit(solution)/shard_map/ppermute | solution.py:479
  18.7 0.0 collective-permute-done.1.refs_1_
  18.7 0.6 second_gram.1
  19.3 0.1 collective-permute-start.2
  19.4 1.0 %project.3 = (f32[128,256]{1,0:T(8,128)S(1)}, f32[128,256]{1,0:T(8,128)S(1)}, f32[2,128,256]{2,1,0:T(8,128)S(1)}, f32[2,128,256]{2,1,0:T(8,128)S(1)}, f32[2,128,256]{2,1,0:T(8,128)S(1)}) custom-call(bf16[256,512]{1,0:T(8,128)(2,1)S(1)} %get-tuple-element.52.refs_0_, bf16[512,2048]{1,0:T(8,128)(2,1)S(1)} %get-tuple-element.42.refs_1_, ...), custom_call_target="tpu_custom_call" | custom-call | flops 805306 | bytes 4194 | tf_op jit(solution)/shard_map/project/pallas_call | solution.py:235
  20.4 0.5 collective-permute-start.12
  21.0 0.1 collective-permute-start.13
  21.0 0.0 collective-permute-done.2.refs_1_
  21.1 1.6 %collective-permute-start.3 = (f32[192,128]{1,0:T(8,128)S(1)}, f32[192,128]{1,0:T(8,128)S(1)}, u32[]{:S(2)}, u32[]{:S(2)}) collective-permute-start(f32[192,128]{1,0:T(8,128)S(1)} %add_parts.4.refs_0_.refs_3_), channel_id=1, source_target_pairs={{0,8},{2,10},{4,12},{6,14},{8,0},{10,2},{12,4},{14,6},{16,24},{18,... | collective-permute-start | bytes 294920 | tf_op jit(solution)/shard_map/ppermute | solution.py:479
  22.7 0.2 collective-permute-start.10
  22.9 0.0 collective-permute-done.12.refs_1_
  22.9 0.3 collective-permute-start.11
  23.2 0.0 collective-permute-done.13.refs_2_
  23.2 1.4 %collective-permute-start.14 = (f32[2,128,256]{2,1,0:T(8,128)S(1)}, f32[2,128,256]{2,1,0:T(8,128)S(1)}, u32[]{:S(2)}, u32[]{:S(2)}) collective-permute-start(f32[2,128,256]{2,1,0:T(8,128)S(1)} %joined.3), channel_id=1, source_target_pairs={{0,4},{2,6},{4,0},{6,2},{8,12},{10,14},{12,8},{14,10},{16,20},{18,... | collective-permute-start | bytes 786440 | tf_op jit(solution)/shard_map/ppermute | solution.py:479
  24.6 1.7 %collective-permute-done.3.refs_1_ = f32[192,128]{1,0:T(8,128)S(1)} collective-permute-done((f32[192,128]{1,0:T(8,128)S(1)}, f32[192,128]{1,0:T(8,128)S(1)}, u32[]{:S(2)}, u32[]{:S(2)}) %collective-permute-start.3) | collective-permute-done | bytes 98336 | tf_op jit(solution)/shard_map/ppermute | solution.py:479
  26.3 0.0 collective-permute-done.6.refs_2_
  26.3 2.7 %collective-permute-start.7 = (f32[192,128]{1,0:T(8,128)S(1)}, f32[192,128]{1,0:T(8,128)S(1)}, u32[]{:S(2)}, u32[]{:S(2)}) collective-permute-start(f32[192,128]{1,0:T(8,128)S(1)} %add_parts.5.refs_0_), channel_id=1, source_target_pairs={{0,16},{2,18},{4,20},{6,22},{8,24},{10,26},{12,28},{14,30},{16,0},... | collective-permute-start | bytes 294920 | tf_op jit(solution)/shard_map/ppermute | solution.py:479
  28.9 4.8 %collective-permute-done.7.refs_1_ = f32[192,128]{1,0:T(8,128)S(1)} collective-permute-done((f32[192,128]{1,0:T(8,128)S(1)}, f32[192,128]{1,0:T(8,128)S(1)}, u32[]{:S(2)}, u32[]{:S(2)}) %collective-permute-start.7) | collective-permute-done | bytes 98336 | tf_op jit(solution)/shard_map/ppermute | solution.py:479
  33.7 1.4 %collective-permute-start.8 = (f32[192,128]{1,0:T(8,128)S(1)}, f32[192,128]{1,0:T(8,128)S(1)}, u32[]{:S(2)}, u32[]{:S(2)}) collective-permute-start(f32[192,128]{1,0:T(8,128)S(1)} %add_parts.6.refs_0_.refs_6_), channel_id=1, source_target_pairs={{0,4},{2,6},{4,0},{6,2},{8,12},{10,14},{12,8},{14,10},{16,20},{18,... | collective-permute-start | bytes 294920 | tf_op jit(solution)/shard_map/ppermute | solution.py:479
  35.1 0.0 collective-permute-done.10.refs_1_
  35.1 0.0 collective-permute-done.11.refs_4_
  35.1 0.0 collective-permute-done.14.refs_5_
  35.1 0.1 piece_sums.1
  35.2 0.7 collective-permute-start.15
  35.9 3.6 %collective-permute-start.16 = (f32[256,256]{1,0:T(8,128)S(1)}, f32[256,256]{1,0:T(8,128)S(1)}, u32[]{:S(2)}, u32[]{:S(2)}) collective-permute-start(f32[256,256]{1,0:T(8,128)S(1)} %get-tuple-element.59), channel_id=1, source_target_pairs={{0,1},{1,9},{2,19},{3,27},{4,5},{5,13},{6,23},{7,31},{8,0},{9,8},{... | collective-permute-start | bytes 786440 | tf_op jit(solution)/shard_map/ppermute | solution.py:511
  39.5 0.0 collective-permute-done.8.refs_1_
  39.5 0.1 collective-permute-start.9
  39.6 1.3 %collective-permute-done.9.refs_1_ = f32[192,128]{1,0:T(8,128)S(1)} collective-permute-done((f32[192,128]{1,0:T(8,128)S(1)}, f32[192,128]{1,0:T(8,128)S(1)}, u32[]{:S(2)}, u32[]{:S(2)}) %collective-permute-start.9) | collective-permute-done | bytes 98336 | tf_op jit(solution)/shard_map/ppermute | solution.py:479
  40.9 9.1 %inverse_factor.1.refs_2_.inverse_ref = f32[256,256]{1,0:T(8,128)S(1)} custom-call(f32[192,128]{1,0:T(8,128)S(1)} %add_parts.7.refs_0_, f32[192,128]{1,0:T(8,128)S(1)} %collective-permute-done.9.refs_1_), custom_call_target="tpu_custom_call" | custom-call | flops 1000000000 | bytes 524 | tf_op jit(solution)/shard_map/inverse_factor/pallas_call | solution.py:376
  50.0 0.0 collective-permute-done.15.p0
  50.0 5.1 %collective-permute-done.16.p1 = f32[256,256]{1,0:T(8,128)S(1)} collective-permute-done((f32[256,256]{1,0:T(8,128)S(1)}, f32[256,256]{1,0:T(8,128)S(1)}, u32[]{:S(2)}, u32[]{:S(2)}) %collective-permute-start.16) | collective-permute-done | bytes 262176 | tf_op jit(solution)/shard_map/ppermute | solution.py:511
  55.1 0.4 remainder_pieces.1
  55.5 0.1 collective-permute-start.17
  55.6 0.8 %collective-permute-start.18 = (f32[4,16,256]{2,1,0:T(8,128)S(1)}, f32[4,16,256]{2,1,0:T(8,128)S(1)}, u32[]{:S(2)}, u32[]{:S(2)}) collective-permute-start(f32[4,16,256]{2,1,0:T(8,128)S(1)} %get-tuple-element.62), channel_id=1, source_target_pairs={{0,4},{2,6},{4,0},{6,2},{8,12},{10,14},{12,8},{14,10},{16,20},{18,... | collective-permute-start | bytes 196616 | tf_op jit(solution)/shard_map/ppermute | solution.py:479
  56.4 1.1 %collective-permute-start.19 = (f32[4,16,256]{2,1,0:T(8,128)S(1)}, f32[4,16,256]{2,1,0:T(8,128)S(1)}, u32[]{:S(2)}, u32[]{:S(2)}) collective-permute-start(f32[4,16,256]{2,1,0:T(8,128)S(1)} %get-tuple-element.63), channel_id=1, source_target_pairs={{0,6},{2,4},{4,2},{6,0},{8,14},{10,12},{12,10},{14,8},{16,22},{18,... | collective-permute-start | bytes 196616 | tf_op jit(solution)/shard_map/ppermute | solution.py:479
  57.4 0.0 collective-permute-done.17.r1
  57.4 3.1 %collective-permute-done.18.r2 = f32[4,16,256]{2,1,0:T(8,128)S(1)} collective-permute-done((f32[4,16,256]{2,1,0:T(8,128)S(1)}, f32[4,16,256]{2,1,0:T(8,128)S(1)}, u32[]{:S(2)}, u32[]{:S(2)}) %collective-permute-start.18) | collective-permute-done | bytes 65568 | tf_op jit(solution)/shard_map/ppermute | solution.py:479
  60.5 0.5 collective-permute-done.19.r3
  61.1 0.1 collective-permute-start.20
  61.1 4.1 %collective-permute-start.21 = (f32[2,16,256]{2,1,0:T(8,128)S(1)}, f32[2,16,256]{2,1,0:T(8,128)S(1)}, u32[]{:S(2)}, u32[]{:S(2)}) collective-permute-start(f32[2,16,256]{2,1,0:T(8,128)S(1)} %get-tuple-element.66), channel_id=1, source_target_pairs={{0,16},{2,18},{4,20},{6,22},{8,24},{10,26},{12,28},{14,30},{16,0},... | collective-permute-start | bytes 98312 | tf_op jit(solution)/shard_map/ppermute | solution.py:479
  65.2 0.3 collective-permute-start.22
  65.5 1.3 %scaled_core.1 = f32[512,256]{1,0:T(8,128)} custom-call(f32[512,128]{1,0:T(8,128)S(1)} %get-tuple-element.36.refs_0_, f32[512,128]{1,0:T(8,128)S(1)} %get-tuple-element.45.refs_1_, f32[256,256]{1,0:T(8,128)S(1)} %inverse_factor.1.refs_2_.inverse_ref), custom_call_target="tpu_custom_call" | custom-call | flops 201326 | bytes 1048 | tf_op jit(solution)/shard_map/scaled_core/pallas_call | solution.py:401
  66.8 0.0 collective-permute-done.20.p1
  66.8 0.9 %collective-permute-done.21.p2 = f32[2,16,256]{2,1,0:T(8,128)S(1)} collective-permute-done((f32[2,16,256]{2,1,0:T(8,128)S(1)}, f32[2,16,256]{2,1,0:T(8,128)S(1)}, u32[]{:S(2)}, u32[]{:S(2)}) %collective-permute-start.21) | collective-permute-done | bytes 32800 | tf_op jit(solution)/shard_map/ppermute | solution.py:479
  67.7 3.3 %collective-permute-done.22.p3 = f32[2,16,256]{2,1,0:T(8,128)S(1)} collective-permute-done((f32[2,16,256]{2,1,0:T(8,128)S(1)}, f32[2,16,256]{2,1,0:T(8,128)S(1)}, u32[]{:S(2)}, u32[]{:S(2)}) %collective-permute-start.22) | collective-permute-done | bytes 32800 | tf_op jit(solution)/shard_map/ppermute | solution.py:479
  70.9 0.7 arrange.1
  (7 shorter events, 0.1 us)
Async XLA Ops:
  3.3 10.2 %collective-permute-start = (f32[512,128]{1,0:T(8,128)S(1)}, f32[512,128]{1,0:T(8,128)S(1)}, u32[]{:S(2)}, u32[]{:S(2)}) collective-permute-start(f32[512,128]{1,0:T(8,128)S(1)} %get-tuple-element.35.own_ref), channel_id=1, source_target_pairs={{0,1},{1,0},{2,3},{3,2},{4,5},{5,4},{6,7},{7,6},{8,9},{9,8},{10,11... | collective-permute-start | bytes 786440 | tf_op jit(solution)/shard_map/ppermute | solution.py:487
  7.7 11.0 %collective-permute-start.1 = (f32[512,128]{1,0:T(8,128)S(1)}, f32[512,128]{1,0:T(8,128)S(1)}, u32[]{:S(2)}, u32[]{:S(2)}) collective-permute-start(f32[512,128]{1,0:T(8,128)S(1)} %get-tuple-element.38.refs_0_), channel_id=1, source_target_pairs={{0,1},{1,0},{2,3},{3,2},{4,5},{5,4},{6,7},{7,6},{8,9},{9,8},{10,11... | collective-permute-start | bytes 786440 | tf_op jit(solution)/shard_map/ppermute | solution.py:489
  14.9 1.4 %collective-permute-start.4 = (f32[128,256]{1,0:T(8,128)S(1)}, f32[128,256]{1,0:T(8,128)S(1)}, u32[]{:S(2)}, u32[]{:S(2)}) collective-permute-start(f32[128,256]{1,0:T(8,128)S(1)} %get-tuple-element.49), channel_id=1, source_target_pairs={{0,2},{2,0},{4,6},{6,4},{8,10},{10,8},{12,14},{14,12},{16,18},{18,... | collective-permute-start | bytes 393224 | tf_op jit(solution)/shard_map/ppermute | solution.py:479
  15.0 1.5 %collective-permute-start.5 = (f32[128,256]{1,0:T(8,128)S(1)}, f32[128,256]{1,0:T(8,128)S(1)}, u32[]{:S(2)}, u32[]{:S(2)}) collective-permute-start(f32[128,256]{1,0:T(8,128)S(1)} %get-tuple-element.50), channel_id=1, source_target_pairs={{0,2},{2,0},{4,6},{6,4},{8,10},{10,8},{12,14},{14,12},{16,18},{18,... | collective-permute-start | bytes 393224 | tf_op jit(solution)/shard_map/ppermute | solution.py:479
  16.6 9.7 %collective-permute-start.6 = (f32[2,128,256]{2,1,0:T(8,128)S(1)}, f32[2,128,256]{2,1,0:T(8,128)S(1)}, u32[]{:S(2)}, u32[]{:S(2)}) collective-permute-start(f32[2,128,256]{2,1,0:T(8,128)S(1)} %joined.2.refs_3_), channel_id=1, source_target_pairs={{0,4},{2,6},{4,0},{6,2},{8,12},{10,14},{12,8},{14,10},{16,20},{18,... | collective-permute-start | bytes 786440 | tf_op jit(solution)/shard_map/ppermute | solution.py:479
  19.3 1.7 %collective-permute-start.2 = (f32[192,128]{1,0:T(8,128)S(1)}, f32[192,128]{1,0:T(8,128)S(1)}, u32[]{:S(2)}, u32[]{:S(2)}) collective-permute-start(f32[192,128]{1,0:T(8,128)S(1)} %get-tuple-element.47), channel_id=1, source_target_pairs={{0,2},{2,0},{4,6},{6,4},{8,10},{10,8},{12,14},{14,12},{16,18},{18,... | collective-permute-start | bytes 294920 | tf_op jit(solution)/shard_map/ppermute | solution.py:479
  20.4 2.4 %collective-permute-start.12 = (f32[128,256]{1,0:T(8,128)S(1)}, f32[128,256]{1,0:T(8,128)S(1)}, u32[]{:S(2)}, u32[]{:S(2)}) collective-permute-start(f32[128,256]{1,0:T(8,128)S(1)} %get-tuple-element.56), channel_id=1, source_target_pairs={{0,2},{2,0},{4,6},{6,4},{8,10},{10,8},{12,14},{14,12},{16,18},{18,... | collective-permute-start | bytes 393224 | tf_op jit(solution)/shard_map/ppermute | solution.py:479
  21.0 2.2 %collective-permute-start.13 = (f32[128,256]{1,0:T(8,128)S(1)}, f32[128,256]{1,0:T(8,128)S(1)}, u32[]{:S(2)}, u32[]{:S(2)}) collective-permute-start(f32[128,256]{1,0:T(8,128)S(1)} %get-tuple-element.57), channel_id=1, source_target_pairs={{0,2},{2,0},{4,6},{6,4},{8,10},{10,8},{12,14},{14,12},{16,18},{18,... | collective-permute-start | bytes 393224 | tf_op jit(solution)/shard_map/ppermute | solution.py:479
  21.1 5.2 %collective-permute-start.3 = (f32[192,128]{1,0:T(8,128)S(1)}, f32[192,128]{1,0:T(8,128)S(1)}, u32[]{:S(2)}, u32[]{:S(2)}) collective-permute-start(f32[192,128]{1,0:T(8,128)S(1)} %add_parts.4.refs_0_.refs_3_), channel_id=1, source_target_pairs={{0,8},{2,10},{4,12},{6,14},{8,0},{10,2},{12,4},{14,6},{16,24},{18,... | collective-permute-start | bytes 294920 | tf_op jit(solution)/shard_map/ppermute | solution.py:479
  22.7 12.4 %collective-permute-start.10 = (f32[2,128,256]{2,1,0:T(8,128)S(1)}, f32[2,128,256]{2,1,0:T(8,128)S(1)}, u32[]{:S(2)}, u32[]{:S(2)}) collective-permute-start(f32[2,128,256]{2,1,0:T(8,128)S(1)} %get-tuple-element.51), channel_id=1, source_target_pairs={{0,2},{2,0},{4,6},{6,4},{8,10},{10,8},{12,14},{14,12},{16,18},{18,... | collective-permute-start | bytes 786440 | tf_op jit(solution)/shard_map/ppermute | solution.py:479
  22.9 12.2 %collective-permute-start.11 = (f32[2,128,256]{2,1,0:T(8,128)S(1)}, f32[2,128,256]{2,1,0:T(8,128)S(1)}, u32[]{:S(2)}, u32[]{:S(2)}) collective-permute-start(f32[2,128,256]{2,1,0:T(8,128)S(1)} %get-tuple-element.54), channel_id=1, source_target_pairs={{0,2},{2,0},{4,6},{6,4},{8,10},{10,8},{12,14},{14,12},{16,18},{18,... | collective-permute-start | bytes 786440 | tf_op jit(solution)/shard_map/ppermute | solution.py:479
  23.2 11.9 %collective-permute-start.14 = (f32[2,128,256]{2,1,0:T(8,128)S(1)}, f32[2,128,256]{2,1,0:T(8,128)S(1)}, u32[]{:S(2)}, u32[]{:S(2)}) collective-permute-start(f32[2,128,256]{2,1,0:T(8,128)S(1)} %joined.3), channel_id=1, source_target_pairs={{0,4},{2,6},{4,0},{6,2},{8,12},{10,14},{12,8},{14,10},{16,20},{18,... | collective-permute-start | bytes 786440 | tf_op jit(solution)/shard_map/ppermute | solution.py:479
  26.3 7.4 %collective-permute-start.7 = (f32[192,128]{1,0:T(8,128)S(1)}, f32[192,128]{1,0:T(8,128)S(1)}, u32[]{:S(2)}, u32[]{:S(2)}) collective-permute-start(f32[192,128]{1,0:T(8,128)S(1)} %add_parts.5.refs_0_), channel_id=1, source_target_pairs={{0,16},{2,18},{4,20},{6,22},{8,24},{10,26},{12,28},{14,30},{16,0},... | collective-permute-start | bytes 294920 | tf_op jit(solution)/shard_map/ppermute | solution.py:479
  33.7 5.7 %collective-permute-start.8 = (f32[192,128]{1,0:T(8,128)S(1)}, f32[192,128]{1,0:T(8,128)S(1)}, u32[]{:S(2)}, u32[]{:S(2)}) collective-permute-start(f32[192,128]{1,0:T(8,128)S(1)} %add_parts.6.refs_0_.refs_6_), channel_id=1, source_target_pairs={{0,4},{2,6},{4,0},{6,2},{8,12},{10,14},{12,8},{14,10},{16,20},{18,... | collective-permute-start | bytes 294920 | tf_op jit(solution)/shard_map/ppermute | solution.py:479
  35.2 14.8 %collective-permute-start.15 = (f32[256,256]{1,0:T(8,128)S(1)}, f32[256,256]{1,0:T(8,128)S(1)}, u32[]{:S(2)}, u32[]{:S(2)}) collective-permute-start(f32[256,256]{1,0:T(8,128)S(1)} %get-tuple-element.58), channel_id=1, source_target_pairs={{0,0},{1,8},{2,18},{3,26},{4,4},{5,12},{6,22},{7,30},{8,1},{9,9},{... | collective-permute-start | bytes 786440 | tf_op jit(solution)/shard_map/ppermute | solution.py:511
  35.9 19.2 %collective-permute-start.16 = (f32[256,256]{1,0:T(8,128)S(1)}, f32[256,256]{1,0:T(8,128)S(1)}, u32[]{:S(2)}, u32[]{:S(2)}) collective-permute-start(f32[256,256]{1,0:T(8,128)S(1)} %get-tuple-element.59), channel_id=1, source_target_pairs={{0,1},{1,9},{2,19},{3,27},{4,5},{5,13},{6,23},{7,31},{8,0},{9,8},{... | collective-permute-start | bytes 786440 | tf_op jit(solution)/shard_map/ppermute | solution.py:511
  39.5 1.4 %collective-permute-start.9 = (f32[192,128]{1,0:T(8,128)S(1)}, f32[192,128]{1,0:T(8,128)S(1)}, u32[]{:S(2)}, u32[]{:S(2)}) collective-permute-start(f32[192,128]{1,0:T(8,128)S(1)} %add_parts.7.refs_0_), channel_id=1, source_target_pairs={{0,2},{2,0},{4,6},{6,4},{8,10},{10,8},{12,14},{14,12},{16,18},{18,... | collective-permute-start | bytes 294920 | tf_op jit(solution)/shard_map/ppermute | solution.py:479
  55.5 1.9 %collective-permute-start.17 = (f32[4,16,256]{2,1,0:T(8,128)S(1)}, f32[4,16,256]{2,1,0:T(8,128)S(1)}, u32[]{:S(2)}, u32[]{:S(2)}) collective-permute-start(f32[4,16,256]{2,1,0:T(8,128)S(1)} %get-tuple-element.61), channel_id=1, source_target_pairs={{0,2},{2,0},{4,6},{6,4},{8,10},{10,8},{12,14},{14,12},{16,18},{18,... | collective-permute-start | bytes 196616 | tf_op jit(solution)/shard_map/ppermute | solution.py:479
  55.6 5.0 %collective-permute-start.18 = (f32[4,16,256]{2,1,0:T(8,128)S(1)}, f32[4,16,256]{2,1,0:T(8,128)S(1)}, u32[]{:S(2)}, u32[]{:S(2)}) collective-permute-start(f32[4,16,256]{2,1,0:T(8,128)S(1)} %get-tuple-element.62), channel_id=1, source_target_pairs={{0,4},{2,6},{4,0},{6,2},{8,12},{10,14},{12,8},{14,10},{16,20},{18,... | collective-permute-start | bytes 196616 | tf_op jit(solution)/shard_map/ppermute | solution.py:479
  56.4 4.7 %collective-permute-start.19 = (f32[4,16,256]{2,1,0:T(8,128)S(1)}, f32[4,16,256]{2,1,0:T(8,128)S(1)}, u32[]{:S(2)}, u32[]{:S(2)}) collective-permute-start(f32[4,16,256]{2,1,0:T(8,128)S(1)} %get-tuple-element.63), channel_id=1, source_target_pairs={{0,6},{2,4},{4,2},{6,0},{8,14},{10,12},{12,10},{14,8},{16,22},{18,... | collective-permute-start | bytes 196616 | tf_op jit(solution)/shard_map/ppermute | solution.py:479
  61.1 5.7 %collective-permute-start.20 = (f32[2,16,256]{2,1,0:T(8,128)S(1)}, f32[2,16,256]{2,1,0:T(8,128)S(1)}, u32[]{:S(2)}, u32[]{:S(2)}) collective-permute-start(f32[2,16,256]{2,1,0:T(8,128)S(1)} %get-tuple-element.65), channel_id=1, source_target_pairs={{0,8},{2,10},{4,12},{6,14},{8,0},{10,2},{12,4},{14,6},{16,24},{18,... | collective-permute-start | bytes 98312 | tf_op jit(solution)/shard_map/ppermute | solution.py:479
  61.1 6.5 %collective-permute-start.21 = (f32[2,16,256]{2,1,0:T(8,128)S(1)}, f32[2,16,256]{2,1,0:T(8,128)S(1)}, u32[]{:S(2)}, u32[]{:S(2)}) collective-permute-start(f32[2,16,256]{2,1,0:T(8,128)S(1)} %get-tuple-element.66), channel_id=1, source_target_pairs={{0,16},{2,18},{4,20},{6,22},{8,24},{10,26},{12,28},{14,30},{16,0},... | collective-permute-start | bytes 98312 | tf_op jit(solution)/shard_map/ppermute | solution.py:479
  65.2 5.7 %collective-permute-start.22 = (f32[2,16,256]{2,1,0:T(8,128)S(1)}, f32[2,16,256]{2,1,0:T(8,128)S(1)}, u32[]{:S(2)}, u32[]{:S(2)}) collective-permute-start(f32[2,16,256]{2,1,0:T(8,128)S(1)} %get-tuple-element.67), channel_id=1, source_target_pairs={{0,24},{2,26},{4,28},{6,30},{8,16},{10,18},{12,20},{14,22},{16,8},... | collective-permute-start | bytes 98312 | tf_op jit(solution)/shard_map/ppermute | solution.py:479

commit v12 on v11

--- a/solution.py
+++ b/solution.py
@@ -212,7 +212,8 @@
 
 def project_kernel(parts_ref, high_ref, low_ref, soon_0, soon_1, keep_1, give_0, keep_0):
     row = lax.axis_index("rows")
-    core, right, near, far = row & 1, (row >> 1) & 1, (row >> 2) & 1, row >> 3
+    core, right, far = row & 1, (row >> 1) & 1, row >> 3
+    near = ((row >> 2) & 1) ^ lax.axis_index("cols")
     for flip, give, keep in ((1, (soon_0, soon_1), keep_1), (0, (give_0.at[0], give_0.at[1]), keep_0)):
         for side in range(2):
             for t in range(2):
@@ -451,11 +452,11 @@
 
 def arrange_kernel(p0, p1, p2, p3, out_ref, work):
     row = lax.axis_index("rows")
-    right, deep = (row >> 1) & 1, row >> 2
+    right, deep, y = (row >> 1) & 1, row >> 2, lax.axis_index("cols")
     for t, piece in enumerate((p0, p1, p2, p3)):
         there = deep ^ t
         for m in range(2):
-            work[(there & 1) * 4 + (there >> 1) * 2 + (right ^ m)] = piece[m]
+            work[((there & 1) ^ y) * 4 + (there >> 1) * 2 + (right ^ m)] = piece[m]
     for mode in range(MODE):
         out_ref[:, mode, :] = work[mode]
 
@@ -506,8 +507,8 @@
         pairs = []
         for i in range(16):
             for y in range(2):
-                to = (i & 3) | (y << 2) | ((i & 8) ^ ((i & 1) << 3))
-                pairs.append((2 * i + y, 2 * to + (((i >> 2) & 1) ^ k)))
+                to = i ^ (k << 2) ^ ((i & 1) << 3)
+                pairs.append((2 * i + y, 2 * to + (y ^ ((to >> 2) & 1))))
         gathered.append(lax.ppermute(pieces[k], ("rows", "cols"), pairs))
     parts = remainder_pieces(inverse, gathered)
     core_scaled = scaled_core(first, second, inverse, math.sqrt(total_rows))

time: 72.3 us -> 68.6 us (0.949)
  waiting for transfers between devices: 27.3 us -> 22.2 us
  starting transfers between devices: 24.7 us -> 26.6 us
    ppermute x2, waiting for transfers between devices: 5.08 us -> 0.01 us  [local(): gathered.append(lax.ppermute(pieces[k], ('rows', 'cols'), pairs))]
    ppermute x19, starting transfers between devices: 17.4 us -> 19.2 us  [rows_permute(): return lax.ppermute(value, 'rows', [(i, i ^ mask) for i in range(size)])]
  transfers between devices with their start and end apart: 23 -> 23, of which waited for: 11 -> 10; matrix products, arithmetic and copies ran while one was open for 0% -> 0% of each run, Pallas kernels for 21% -> 22%
where the time goes in v12:
time: 68.6 us; the launch traced here: 68.4 us
  starting transfers between devices  26.6 us (39%)
  waiting for transfers between devices  22.2 us (32%)
  Pallas kernels  18.9 us (28%)
  between operations  0.77 us (1%)
    ppermute x19, starting transfers between devices, rows_permute(): return lax.ppermute(value, 'rows', [(i, i ^ mask) for i in range(size)])  19.2 us
    ppermute x19, waiting for transfers between devices, rows_permute(): return lax.ppermute(value, 'rows', [(i, i ^ mask) for i in range(size)])  16.5 us
    pallas_call x1, Pallas kernels, inverse_factor(): pl.pallas_call(body, in_specs=[VMEM] * 2, out_specs=VMEM, out_shape=on_ch...  9.16 us
    ppermute x1, waiting for transfers between devices, local(): got_0 = lax.ppermute(own_0, 'cols', swap)  5.7 us
    ppermute x2, starting transfers between devices, local(): gathered.append(lax.ppermute(pieces[k], ('rows', 'cols'), pairs))  4.27 us
    ppermute x1, starting transfers between devices, local(): got_0 = lax.ppermute(own_0, 'cols', swap)  3.03 us
    pallas_call x1, Pallas kernels, first_sketch(): pl.pallas_call(first_sketch_kernel, in_specs=[HBM] * 3, out_specs=[VMEM]...  2.66 us
    pallas_call x2, Pallas kernels, project(): pl.pallas_call(body, in_specs=[VMEM] * (3 + len(after)), out_specs=[VMEM]...  2.07 us
  transfers between devices with their start and end apart: 23, of which 10 were waited for; matrix products, arithmetic and copies ran while one was open for 0% of the time, Pallas kernels for 22%

profile of v12, /device:TPU:0, one launch (start us, length us, event | category | flops | bytes accessed | tf_op | source)
XLA Modules:
  0.0 68.4 jit_solution(7902205788330818659)
XLA Ops:
  0.6 2.7 %first_sketch.1 = (f32[512,128]{1,0:T(8,128)S(1)}, f32[512,2048]{1,0:T(8,128)S(1)}) custom-call(s32[2,16]{1,0:T(2,128)} %bitcast.6, f32[512,2048]{1,0:T(8,128)} %whole_ref.1, s32[2,2048]{1,0:T(2,128)} %bitcast.4), custom_call_target="tpu_custom_call" | custom-call | flops 2097 | bytes 4194 | tf_op jit(solution)/shard_map/first_sketch/pallas_call | solution.py:94
  3.3 3.0 %collective-permute-start = (f32[512,128]{1,0:T(8,128)S(1)}, f32[512,128]{1,0:T(8,128)S(1)}, u32[]{:S(2)}, u32[]{:S(2)}) collective-permute-start(f32[512,128]{1,0:T(8,128)S(1)} %get-tuple-element.35.own_ref), channel_id=1, source_target_pairs={{0,1},{1,0},{2,3},{3,2},{4,5},{5,4},{6,7},{7,6},{8,9},{9,8},{10,11... | collective-permute-start | bytes 786440 | tf_op jit(solution)/shard_map/ppermute | solution.py:488
  6.3 1.3 %second_sketch.1 = (f32[512,128]{1,0:T(8,128)S(1)}, bf16[512,2048]{1,0:T(8,128)(2,1)S(1)}, bf16[512,2048]{1,0:T(8,128)(2,1)S(1)}) custom-call(s32[2,16]{1,0:T(2,128)} %bitcast.7, s32[2,2048]{1,0:T(2,128)} %bitcast.5, f32[512,2048]{1,0:T(8,128)S(1)} %get-tuple-element.37.block_ref), custom_call_target="tpu_custom_call" | custom-call | flops 2097 | bytes 4194 | tf_op jit(solution)/shard_map/second_sketch/pallas_call | solution.py:132
  7.7 0.1 collective-permute-start.1
  7.8 5.7 %collective-permute-done.got_ref = f32[512,128]{1,0:T(8,128)S(1)} collective-permute-done((f32[512,128]{1,0:T(8,128)S(1)}, f32[512,128]{1,0:T(8,128)S(1)}, u32[]{:S(2)}, u32[]{:S(2)}) %collective-permute-start) | collective-permute-done | bytes 262176 | tf_op jit(solution)/shard_map/ppermute | solution.py:488
  13.5 0.4 first_gram.1
  13.9 1.0 %project.2 = (f32[128,256]{1,0:T(8,128)S(1)}, f32[128,256]{1,0:T(8,128)S(1)}, f32[2,128,256]{2,1,0:T(8,128)S(1)}, f32[2,128,256]{2,1,0:T(8,128)S(1)}, f32[2,128,256]{2,1,0:T(8,128)S(1)}) custom-call(bf16[256,512]{1,0:T(8,128)(2,1)S(1)} %get-tuple-element.41.refs_0_, bf16[512,2048]{1,0:T(8,128)(2,1)S(1)} %get-tuple-element.42.refs_1_, ...), custom_call_target="tpu_custom_call" | custom-call | flops 805306 | bytes 4194 | tf_op jit(solution)/shard_map/project/pallas_call | solution.py:236
  14.9 0.1 collective-permute-start.4
  15.0 0.5 collective-permute-start.5
  15.5 0.8 %collective-permute-done.4.refs_1_ = f32[128,256]{1,0:T(8,128)S(1)} collective-permute-done((f32[128,256]{1,0:T(8,128)S(1)}, f32[128,256]{1,0:T(8,128)S(1)}, u32[]{:S(2)}, u32[]{:S(2)}) %collective-permute-start.4) | collective-permute-done | bytes 131104 | tf_op jit(solution)/shard_map/ppermute | solution.py:480
  16.4 0.2 collective-permute-done.5.refs_2_
  16.6 2.1 %collective-permute-start.6 = (f32[2,128,256]{2,1,0:T(8,128)S(1)}, f32[2,128,256]{2,1,0:T(8,128)S(1)}, u32[]{:S(2)}, u32[]{:S(2)}) collective-permute-start(f32[2,128,256]{2,1,0:T(8,128)S(1)} %joined.2.refs_3_), channel_id=1, source_target_pairs={{0,4},{2,6},{4,0},{6,2},{8,12},{10,14},{12,8},{14,10},{16,20},{18,... | collective-permute-start | bytes 786440 | tf_op jit(solution)/shard_map/ppermute | solution.py:480
  18.7 0.0 collective-permute-done.1.refs_1_
  18.7 0.6 second_gram.1
  19.3 0.1 collective-permute-start.2
  19.4 1.0 %project.3 = (f32[128,256]{1,0:T(8,128)S(1)}, f32[128,256]{1,0:T(8,128)S(1)}, f32[2,128,256]{2,1,0:T(8,128)S(1)}, f32[2,128,256]{2,1,0:T(8,128)S(1)}, f32[2,128,256]{2,1,0:T(8,128)S(1)}) custom-call(bf16[256,512]{1,0:T(8,128)(2,1)S(1)} %get-tuple-element.52.refs_0_, bf16[512,2048]{1,0:T(8,128)(2,1)S(1)} %get-tuple-element.42.refs_1_, ...), custom_call_target="tpu_custom_call" | custom-call | flops 805306 | bytes 4194 | tf_op jit(solution)/shard_map/project/pallas_call | solution.py:236
  20.4 0.5 collective-permute-start.12
  21.0 0.1 collective-permute-start.13
  21.0 0.0 collective-permute-done.2.refs_1_
  21.1 1.6 %collective-permute-start.3 = (f32[192,128]{1,0:T(8,128)S(1)}, f32[192,128]{1,0:T(8,128)S(1)}, u32[]{:S(2)}, u32[]{:S(2)}) collective-permute-start(f32[192,128]{1,0:T(8,128)S(1)} %add_parts.4.refs_0_.refs_3_), channel_id=1, source_target_pairs={{0,8},{2,10},{4,12},{6,14},{8,0},{10,2},{12,4},{14,6},{16,24},{18,... | collective-permute-start | bytes 294920 | tf_op jit(solution)/shard_map/ppermute | solution.py:480
  22.7 0.2 collective-permute-start.10
  22.9 0.0 collective-permute-done.12.refs_1_
  22.9 0.3 collective-permute-start.11
  23.2 0.0 collective-permute-done.13.refs_2_
  23.2 1.4 %collective-permute-start.14 = (f32[2,128,256]{2,1,0:T(8,128)S(1)}, f32[2,128,256]{2,1,0:T(8,128)S(1)}, u32[]{:S(2)}, u32[]{:S(2)}) collective-permute-start(f32[2,128,256]{2,1,0:T(8,128)S(1)} %joined.3), channel_id=1, source_target_pairs={{0,4},{2,6},{4,0},{6,2},{8,12},{10,14},{12,8},{14,10},{16,20},{18,... | collective-permute-start | bytes 786440 | tf_op jit(solution)/shard_map/ppermute | solution.py:480
  24.6 1.7 %collective-permute-done.3.refs_1_ = f32[192,128]{1,0:T(8,128)S(1)} collective-permute-done((f32[192,128]{1,0:T(8,128)S(1)}, f32[192,128]{1,0:T(8,128)S(1)}, u32[]{:S(2)}, u32[]{:S(2)}) %collective-permute-start.3) | collective-permute-done | bytes 98336 | tf_op jit(solution)/shard_map/ppermute | solution.py:480
  26.3 0.0 collective-permute-done.6.refs_2_
  26.3 2.7 %collective-permute-start.7 = (f32[192,128]{1,0:T(8,128)S(1)}, f32[192,128]{1,0:T(8,128)S(1)}, u32[]{:S(2)}, u32[]{:S(2)}) collective-permute-start(f32[192,128]{1,0:T(8,128)S(1)} %add_parts.5.refs_0_), channel_id=1, source_target_pairs={{0,16},{2,18},{4,20},{6,22},{8,24},{10,26},{12,28},{14,30},{16,0},... | collective-permute-start | bytes 294920 | tf_op jit(solution)/shard_map/ppermute | solution.py:480
  28.9 4.8 %collective-permute-done.7.refs_1_ = f32[192,128]{1,0:T(8,128)S(1)} collective-permute-done((f32[192,128]{1,0:T(8,128)S(1)}, f32[192,128]{1,0:T(8,128)S(1)}, u32[]{:S(2)}, u32[]{:S(2)}) %collective-permute-start.7) | collective-permute-done | bytes 98336 | tf_op jit(solution)/shard_map/ppermute | solution.py:480
  33.7 1.4 %collective-permute-start.8 = (f32[192,128]{1,0:T(8,128)S(1)}, f32[192,128]{1,0:T(8,128)S(1)}, u32[]{:S(2)}, u32[]{:S(2)}) collective-permute-start(f32[192,128]{1,0:T(8,128)S(1)} %add_parts.6.refs_0_.refs_6_), channel_id=1, source_target_pairs={{0,4},{2,6},{4,0},{6,2},{8,12},{10,14},{12,8},{14,10},{16,20},{18,... | collective-permute-start | bytes 294920 | tf_op jit(solution)/shard_map/ppermute | solution.py:480
  35.1 0.0 collective-permute-done.10.refs_1_
  35.1 0.0 collective-permute-done.11.refs_4_
  35.1 0.0 collective-permute-done.14.refs_5_
  35.1 0.1 piece_sums.1
  35.2 0.7 collective-permute-start.15
  35.9 3.6 %collective-permute-start.16 = (f32[256,256]{1,0:T(8,128)S(1)}, f32[256,256]{1,0:T(8,128)S(1)}, u32[]{:S(2)}, u32[]{:S(2)}) collective-permute-start(f32[256,256]{1,0:T(8,128)S(1)} %get-tuple-element.59), channel_id=1, source_target_pairs={{0,9},{1,8},{2,27},{3,26},{4,13},{5,12},{6,31},{7,30},{8,0},{9,1},... | collective-permute-start | bytes 786440 | tf_op jit(solution)/shard_map/ppermute | solution.py:512
  39.5 0.0 collective-permute-done.8.refs_1_
  39.5 1.7 %collective-permute-start.9 = (f32[192,128]{1,0:T(8,128)S(1)}, f32[192,128]{1,0:T(8,128)S(1)}, u32[]{:S(2)}, u32[]{:S(2)}) collective-permute-start(f32[192,128]{1,0:T(8,128)S(1)} %add_parts.7.refs_0_), channel_id=1, source_target_pairs={{0,2},{2,0},{4,6},{6,4},{8,10},{10,8},{12,14},{14,12},{16,18},{18,... | collective-permute-start | bytes 294920 | tf_op jit(solution)/shard_map/ppermute | solution.py:480
  41.2 0.9 %collective-permute-done.9.refs_1_ = f32[192,128]{1,0:T(8,128)S(1)} collective-permute-done((f32[192,128]{1,0:T(8,128)S(1)}, f32[192,128]{1,0:T(8,128)S(1)}, u32[]{:S(2)}, u32[]{:S(2)}) %collective-permute-start.9) | collective-permute-done | bytes 98336 | tf_op jit(solution)/shard_map/ppermute | solution.py:480
  42.1 9.2 %inverse_factor.1.refs_2_.inverse_ref = f32[256,256]{1,0:T(8,128)S(1)} custom-call(f32[192,128]{1,0:T(8,128)S(1)} %add_parts.7.refs_0_, f32[192,128]{1,0:T(8,128)S(1)} %collective-permute-done.9.refs_1_), custom_call_target="tpu_custom_call" | custom-call | flops 1000000000 | bytes 524 | tf_op jit(solution)/shard_map/inverse_factor/pallas_call | solution.py:377
  51.3 0.0 collective-permute-done.15.p0
  51.3 0.0 collective-permute-done.16.p1
  51.3 0.4 remainder_pieces.1
  51.7 0.4 collective-permute-start.17
  52.1 0.7 %collective-permute-start.18 = (f32[4,16,256]{2,1,0:T(8,128)S(1)}, f32[4,16,256]{2,1,0:T(8,128)S(1)}, u32[]{:S(2)}, u32[]{:S(2)}) collective-permute-start(f32[4,16,256]{2,1,0:T(8,128)S(1)} %get-tuple-element.62), channel_id=1, source_target_pairs={{0,4},{2,6},{4,0},{6,2},{8,12},{10,14},{12,8},{14,10},{16,20},{18,... | collective-permute-start | bytes 196616 | tf_op jit(solution)/shard_map/ppermute | solution.py:480
  52.9 0.8 %collective-permute-start.19 = (f32[4,16,256]{2,1,0:T(8,128)S(1)}, f32[4,16,256]{2,1,0:T(8,128)S(1)}, u32[]{:S(2)}, u32[]{:S(2)}) collective-permute-start(f32[4,16,256]{2,1,0:T(8,128)S(1)} %get-tuple-element.63), channel_id=1, source_target_pairs={{0,6},{2,4},{4,2},{6,0},{8,14},{10,12},{12,10},{14,8},{16,22},{18,... | collective-permute-start | bytes 196616 | tf_op jit(solution)/shard_map/ppermute | solution.py:480
  53.6 0.0 collective-permute-done.17.r1
  53.6 3.3 %collective-permute-done.18.r2 = f32[4,16,256]{2,1,0:T(8,128)S(1)} collective-permute-done((f32[4,16,256]{2,1,0:T(8,128)S(1)}, f32[4,16,256]{2,1,0:T(8,128)S(1)}, u32[]{:S(2)}, u32[]{:S(2)}) %collective-permute-start.18) | collective-permute-done | bytes 65568 | tf_op jit(solution)/shard_map/ppermute | solution.py:480
  57.0 0.3 collective-permute-done.19.r3
  57.3 1.3 %collective-permute-start.20 = (f32[2,16,256]{2,1,0:T(8,128)S(1)}, f32[2,16,256]{2,1,0:T(8,128)S(1)}, u32[]{:S(2)}, u32[]{:S(2)}) collective-permute-start(f32[2,16,256]{2,1,0:T(8,128)S(1)} %get-tuple-element.65), channel_id=1, source_target_pairs={{0,8},{2,10},{4,12},{6,14},{8,0},{10,2},{12,4},{14,6},{16,24},{18,... | collective-permute-start | bytes 98312 | tf_op jit(solution)/shard_map/ppermute | solution.py:480
  58.6 3.4 %collective-permute-start.21 = (f32[2,16,256]{2,1,0:T(8,128)S(1)}, f32[2,16,256]{2,1,0:T(8,128)S(1)}, u32[]{:S(2)}, u32[]{:S(2)}) collective-permute-start(f32[2,16,256]{2,1,0:T(8,128)S(1)} %get-tuple-element.66), channel_id=1, source_target_pairs={{0,16},{2,18},{4,20},{6,22},{8,24},{10,26},{12,28},{14,30},{16,0},... | collective-permute-start | bytes 98312 | tf_op jit(solution)/shard_map/ppermute | solution.py:480
  62.0 0.0 collective-permute-start.22
  62.0 1.3 %scaled_core.1 = f32[512,256]{1,0:T(8,128)} custom-call(f32[512,128]{1,0:T(8,128)S(1)} %get-tuple-element.36.refs_0_, f32[512,128]{1,0:T(8,128)S(1)} %get-tuple-element.45.refs_1_, f32[256,256]{1,0:T(8,128)S(1)} %inverse_factor.1.refs_2_.inverse_ref), custom_call_target="tpu_custom_call" | custom-call | flops 201326 | bytes 1048 | tf_op jit(solution)/shard_map/scaled_core/pallas_call | solution.py:402
  63.3 0.0 collective-permute-done.20.p1
  63.3 1.2 %collective-permute-done.21.p2 = f32[2,16,256]{2,1,0:T(8,128)S(1)} collective-permute-done((f32[2,16,256]{2,1,0:T(8,128)S(1)}, f32[2,16,256]{2,1,0:T(8,128)S(1)}, u32[]{:S(2)}, u32[]{:S(2)}) %collective-permute-start.21) | collective-permute-done | bytes 32800 | tf_op jit(solution)/shard_map/ppermute | solution.py:480
  64.5 3.2 %collective-permute-done.22.p3 = f32[2,16,256]{2,1,0:T(8,128)S(1)} collective-permute-done((f32[2,16,256]{2,1,0:T(8,128)S(1)}, f32[2,16,256]{2,1,0:T(8,128)S(1)}, u32[]{:S(2)}, u32[]{:S(2)}) %collective-permute-start.22) | collective-permute-done | bytes 32800 | tf_op jit(solution)/shard_map/ppermute | solution.py:480
  67.7 0.7 %arrange.1 = f32[16,8,256]{2,1,0:T(8,128)} custom-call(f32[2,16,256]{2,1,0:T(8,128)S(1)} %get-tuple-element.64.p0, f32[2,16,256]{2,1,0:T(8,128)S(1)} %collective-permute-done.20.p1, f32[2,16,256]{2,1,0:T(8,128)S(1)} %collective-permute-done.21.p2, f32[2,16,256]{2,1,0:T(8,128)S(1)} %collective-permute-done.22.p3), custom_call_target="tpu_custom_call" | custom-call | bytes 131 | tf_op jit(solution)/shard_map/arrange/pallas_call | solution.py:465
  (7 shorter events, 0.1 us)
Async XLA Ops:
  3.3 10.2 %collective-permute-start = (f32[512,128]{1,0:T(8,128)S(1)}, f32[512,128]{1,0:T(8,128)S(1)}, u32[]{:S(2)}, u32[]{:S(2)}) collective-permute-start(f32[512,128]{1,0:T(8,128)S(1)} %get-tuple-element.35.own_ref), channel_id=1, source_target_pairs={{0,1},{1,0},{2,3},{3,2},{4,5},{5,4},{6,7},{7,6},{8,9},{9,8},{10,11... | collective-permute-start | bytes 786440 | tf_op jit(solution)/shard_map/ppermute | solution.py:488
  7.7 11.0 %collective-permute-start.1 = (f32[512,128]{1,0:T(8,128)S(1)}, f32[512,128]{1,0:T(8,128)S(1)}, u32[]{:S(2)}, u32[]{:S(2)}) collective-permute-start(f32[512,128]{1,0:T(8,128)S(1)} %get-tuple-element.38.refs_0_), channel_id=1, source_target_pairs={{0,1},{1,0},{2,3},{3,2},{4,5},{5,4},{6,7},{7,6},{8,9},{9,8},{10,11... | collective-permute-start | bytes 786440 | tf_op jit(solution)/shard_map/ppermute | solution.py:490
  14.9 1.4 %collective-permute-start.4 = (f32[128,256]{1,0:T(8,128)S(1)}, f32[128,256]{1,0:T(8,128)S(1)}, u32[]{:S(2)}, u32[]{:S(2)}) collective-permute-start(f32[128,256]{1,0:T(8,128)S(1)} %get-tuple-element.49), channel_id=1, source_target_pairs={{0,2},{2,0},{4,6},{6,4},{8,10},{10,8},{12,14},{14,12},{16,18},{18,... | collective-permute-start | bytes 393224 | tf_op jit(solution)/shard_map/ppermute | solution.py:480
  15.0 1.5 %collective-permute-start.5 = (f32[128,256]{1,0:T(8,128)S(1)}, f32[128,256]{1,0:T(8,128)S(1)}, u32[]{:S(2)}, u32[]{:S(2)}) collective-permute-start(f32[128,256]{1,0:T(8,128)S(1)} %get-tuple-element.50), channel_id=1, source_target_pairs={{0,2},{2,0},{4,6},{6,4},{8,10},{10,8},{12,14},{14,12},{16,18},{18,... | collective-permute-start | bytes 393224 | tf_op jit(solution)/shard_map/ppermute | solution.py:480
  16.6 9.7 %collective-permute-start.6 = (f32[2,128,256]{2,1,0:T(8,128)S(1)}, f32[2,128,256]{2,1,0:T(8,128)S(1)}, u32[]{:S(2)}, u32[]{:S(2)}) collective-permute-start(f32[2,128,256]{2,1,0:T(8,128)S(1)} %joined.2.refs_3_), channel_id=1, source_target_pairs={{0,4},{2,6},{4,0},{6,2},{8,12},{10,14},{12,8},{14,10},{16,20},{18,... | collective-permute-start | bytes 786440 | tf_op jit(solution)/shard_map/ppermute | solution.py:480
  19.3 1.8 %collective-permute-start.2 = (f32[192,128]{1,0:T(8,128)S(1)}, f32[192,128]{1,0:T(8,128)S(1)}, u32[]{:S(2)}, u32[]{:S(2)}) collective-permute-start(f32[192,128]{1,0:T(8,128)S(1)} %get-tuple-element.47), channel_id=1, source_target_pairs={{0,2},{2,0},{4,6},{6,4},{8,10},{10,8},{12,14},{14,12},{16,18},{18,... | collective-permute-start | bytes 294920 | tf_op jit(solution)/shard_map/ppermute | solution.py:480
  20.4 2.4 %collective-permute-start.12 = (f32[128,256]{1,0:T(8,128)S(1)}, f32[128,256]{1,0:T(8,128)S(1)}, u32[]{:S(2)}, u32[]{:S(2)}) collective-permute-start(f32[128,256]{1,0:T(8,128)S(1)} %get-tuple-element.56), channel_id=1, source_target_pairs={{0,2},{2,0},{4,6},{6,4},{8,10},{10,8},{12,14},{14,12},{16,18},{18,... | collective-permute-start | bytes 393224 | tf_op jit(solution)/shard_map/ppermute | solution.py:480
  21.0 2.2 %collective-permute-start.13 = (f32[128,256]{1,0:T(8,128)S(1)}, f32[128,256]{1,0:T(8,128)S(1)}, u32[]{:S(2)}, u32[]{:S(2)}) collective-permute-start(f32[128,256]{1,0:T(8,128)S(1)} %get-tuple-element.57), channel_id=1, source_target_pairs={{0,2},{2,0},{4,6},{6,4},{8,10},{10,8},{12,14},{14,12},{16,18},{18,... | collective-permute-start | bytes 393224 | tf_op jit(solution)/shard_map/ppermute | solution.py:480
  21.1 5.2 %collective-permute-start.3 = (f32[192,128]{1,0:T(8,128)S(1)}, f32[192,128]{1,0:T(8,128)S(1)}, u32[]{:S(2)}, u32[]{:S(2)}) collective-permute-start(f32[192,128]{1,0:T(8,128)S(1)} %add_parts.4.refs_0_.refs_3_), channel_id=1, source_target_pairs={{0,8},{2,10},{4,12},{6,14},{8,0},{10,2},{12,4},{14,6},{16,24},{18,... | collective-permute-start | bytes 294920 | tf_op jit(solution)/shard_map/ppermute | solution.py:480
  22.7 12.4 %collective-permute-start.10 = (f32[2,128,256]{2,1,0:T(8,128)S(1)}, f32[2,128,256]{2,1,0:T(8,128)S(1)}, u32[]{:S(2)}, u32[]{:S(2)}) collective-permute-start(f32[2,128,256]{2,1,0:T(8,128)S(1)} %get-tuple-element.51), channel_id=1, source_target_pairs={{0,2},{2,0},{4,6},{6,4},{8,10},{10,8},{12,14},{14,12},{16,18},{18,... | collective-permute-start | bytes 786440 | tf_op jit(solution)/shard_map/ppermute | solution.py:480
  22.9 12.2 %collective-permute-start.11 = (f32[2,128,256]{2,1,0:T(8,128)S(1)}, f32[2,128,256]{2,1,0:T(8,128)S(1)}, u32[]{:S(2)}, u32[]{:S(2)}) collective-permute-start(f32[2,128,256]{2,1,0:T(8,128)S(1)} %get-tuple-element.54), channel_id=1, source_target_pairs={{0,2},{2,0},{4,6},{6,4},{8,10},{10,8},{12,14},{14,12},{16,18},{18,... | collective-permute-start | bytes 786440 | tf_op jit(solution)/shard_map/ppermute | solution.py:480
  23.2 11.9 %collective-permute-start.14 = (f32[2,128,256]{2,1,0:T(8,128)S(1)}, f32[2,128,256]{2,1,0:T(8,128)S(1)}, u32[]{:S(2)}, u32[]{:S(2)}) collective-permute-start(f32[2,128,256]{2,1,0:T(8,128)S(1)} %joined.3), channel_id=1, source_target_pairs={{0,4},{2,6},{4,0},{6,2},{8,12},{10,14},{12,8},{14,10},{16,20},{18,... | collective-permute-start | bytes 786440 | tf_op jit(solution)/shard_map/ppermute | solution.py:480
  26.3 7.4 %collective-permute-start.7 = (f32[192,128]{1,0:T(8,128)S(1)}, f32[192,128]{1,0:T(8,128)S(1)}, u32[]{:S(2)}, u32[]{:S(2)}) collective-permute-start(f32[192,128]{1,0:T(8,128)S(1)} %add_parts.5.refs_0_), channel_id=1, source_target_pairs={{0,16},{2,18},{4,20},{6,22},{8,24},{10,26},{12,28},{14,30},{16,0},... | collective-permute-start | bytes 294920 | tf_op jit(solution)/shard_map/ppermute | solution.py:480
  33.7 5.7 %collective-permute-start.8 = (f32[192,128]{1,0:T(8,128)S(1)}, f32[192,128]{1,0:T(8,128)S(1)}, u32[]{:S(2)}, u32[]{:S(2)}) collective-permute-start(f32[192,128]{1,0:T(8,128)S(1)} %add_parts.6.refs_0_.refs_6_), channel_id=1, source_target_pairs={{0,4},{2,6},{4,0},{6,2},{8,12},{10,14},{12,8},{14,10},{16,20},{18,... | collective-permute-start | bytes 294920 | tf_op jit(solution)/shard_map/ppermute | solution.py:480
  35.2 16.1 %collective-permute-start.15 = (f32[256,256]{1,0:T(8,128)S(1)}, f32[256,256]{1,0:T(8,128)S(1)}, u32[]{:S(2)}, u32[]{:S(2)}) collective-permute-start(f32[256,256]{1,0:T(8,128)S(1)} %get-tuple-element.58), channel_id=1, source_target_pairs={{0,0},{1,1},{2,18},{3,19},{4,4},{5,5},{6,22},{7,23},{8,9},{9,8},{1... | collective-permute-start | bytes 786440 | tf_op jit(solution)/shard_map/ppermute | solution.py:512
  35.9 15.4 %collective-permute-start.16 = (f32[256,256]{1,0:T(8,128)S(1)}, f32[256,256]{1,0:T(8,128)S(1)}, u32[]{:S(2)}, u32[]{:S(2)}) collective-permute-start(f32[256,256]{1,0:T(8,128)S(1)} %get-tuple-element.59), channel_id=1, source_target_pairs={{0,9},{1,8},{2,27},{3,26},{4,13},{5,12},{6,31},{7,30},{8,0},{9,1},... | collective-permute-start | bytes 786440 | tf_op jit(solution)/shard_map/ppermute | solution.py:512
  39.5 2.6 %collective-permute-start.9 = (f32[192,128]{1,0:T(8,128)S(1)}, f32[192,128]{1,0:T(8,128)S(1)}, u32[]{:S(2)}, u32[]{:S(2)}) collective-permute-start(f32[192,128]{1,0:T(8,128)S(1)} %add_parts.7.refs_0_), channel_id=1, source_target_pairs={{0,2},{2,0},{4,6},{6,4},{8,10},{10,8},{12,14},{14,12},{16,18},{18,... | collective-permute-start | bytes 294920 | tf_op jit(solution)/shard_map/ppermute | solution.py:480
  51.7 1.9 %collective-permute-start.17 = (f32[4,16,256]{2,1,0:T(8,128)S(1)}, f32[4,16,256]{2,1,0:T(8,128)S(1)}, u32[]{:S(2)}, u32[]{:S(2)}) collective-permute-start(f32[4,16,256]{2,1,0:T(8,128)S(1)} %get-tuple-element.61), channel_id=1, source_target_pairs={{0,2},{2,0},{4,6},{6,4},{8,10},{10,8},{12,14},{14,12},{16,18},{18,... | collective-permute-start | bytes 196616 | tf_op jit(solution)/shard_map/ppermute | solution.py:480
  52.1 4.8 %collective-permute-start.18 = (f32[4,16,256]{2,1,0:T(8,128)S(1)}, f32[4,16,256]{2,1,0:T(8,128)S(1)}, u32[]{:S(2)}, u32[]{:S(2)}) collective-permute-start(f32[4,16,256]{2,1,0:T(8,128)S(1)} %get-tuple-element.62), channel_id=1, source_target_pairs={{0,4},{2,6},{4,0},{6,2},{8,12},{10,14},{12,8},{14,10},{16,20},{18,... | collective-permute-start | bytes 196616 | tf_op jit(solution)/shard_map/ppermute | solution.py:480
  52.9 4.4 %collective-permute-start.19 = (f32[4,16,256]{2,1,0:T(8,128)S(1)}, f32[4,16,256]{2,1,0:T(8,128)S(1)}, u32[]{:S(2)}, u32[]{:S(2)}) collective-permute-start(f32[4,16,256]{2,1,0:T(8,128)S(1)} %get-tuple-element.63), channel_id=1, source_target_pairs={{0,6},{2,4},{4,2},{6,0},{8,14},{10,12},{12,10},{14,8},{16,22},{18,... | collective-permute-start | bytes 196616 | tf_op jit(solution)/shard_map/ppermute | solution.py:480
  57.3 6.0 %collective-permute-start.20 = (f32[2,16,256]{2,1,0:T(8,128)S(1)}, f32[2,16,256]{2,1,0:T(8,128)S(1)}, u32[]{:S(2)}, u32[]{:S(2)}) collective-permute-start(f32[2,16,256]{2,1,0:T(8,128)S(1)} %get-tuple-element.65), channel_id=1, source_target_pairs={{0,8},{2,10},{4,12},{6,14},{8,0},{10,2},{12,4},{14,6},{16,24},{18,... | collective-permute-start | bytes 98312 | tf_op jit(solution)/shard_map/ppermute | solution.py:480
  58.6 5.9 %collective-permute-start.21 = (f32[2,16,256]{2,1,0:T(8,128)S(1)}, f32[2,16,256]{2,1,0:T(8,128)S(1)}, u32[]{:S(2)}, u32[]{:S(2)}) collective-permute-start(f32[2,16,256]{2,1,0:T(8,128)S(1)} %get-tuple-element.66), channel_id=1, source_target_pairs={{0,16},{2,18},{4,20},{6,22},{8,24},{10,26},{12,28},{14,30},{16,0},... | collective-permute-start | bytes 98312 | tf_op jit(solution)/shard_map/ppermute | solution.py:480
  62.0 5.7 %collective-permute-start.22 = (f32[2,16,256]{2,1,0:T(8,128)S(1)}, f32[2,16,256]{2,1,0:T(8,128)S(1)}, u32[]{:S(2)}, u32[]{:S(2)}) collective-permute-start(f32[2,16,256]{2,1,0:T(8,128)S(1)} %get-tuple-element.67), channel_id=1, source_target_pairs={{0,24},{2,26},{4,28},{6,30},{8,16},{10,18},{12,20},{14,22},{16,8},... | collective-permute-start | bytes 98312 | tf_op jit(solution)/shard_map/ppermute | solution.py:480

commit v13 on v12

--- a/solution.py
+++ b/solution.py
@@ -343,8 +343,11 @@
         for c in range(3):
             work[start:stop, c * BLK : (c + 1) * BLK] = parts[c]
         if stop < BLK:
-            left = parts[0].T[stop:]
-            work[stop:, :] = work[stop:, :] - jnp.dot(left, jnp.concatenate(parts, 1), precision=HIGHEST)
+            left, whole = parts[0].T, jnp.concatenate(parts, 1)
+            after = min(stop + PANEL, BLK)
+            work[stop:after, :] = work[stop:after, :] - jnp.dot(left[stop:after], whole, precision=HIGHEST)
+            if after < BLK:
+                work[after:, :] = work[after:, :] - jnp.dot(left[after:], whole, precision=HIGHEST)
 
 
 def factor_kernel(total_rows, own_ref, got_ref, out_ref, work, packed):

time: 68.6 us -> 68.6 us (level)
  Pallas kernels: 18.9 us -> 18.1 us
  starting transfers between devices: 26.6 us -> 27.3 us
    pallas_call x1, Pallas kernels: 9.16 us -> 8.4 us  [inverse_factor(): pl.pallas_call(body, in_specs=[VMEM] * 2, out_specs=VMEM, out_shape=on_ch...]
    ppermute x19, starting transfers between devices: 19.2 us -> 19.9 us  [rows_permute(): return lax.ppermute(value, 'rows', [(i, i ^ mask) for i in range(size)])]
  transfers between devices with their start and end apart: 23 -> 23, of which waited for: 10 -> 10; matrix products, arithmetic and copies ran while one was open for 0% -> 0% of each run, Pallas kernels for 22% -> 21%
where the time goes in v13:
time: 68.6 us; the launch traced here: 68.4 us
  starting transfers between devices  27.3 us (40%)
  waiting for transfers between devices  22.2 us (32%)
  Pallas kernels  18.1 us (26%)
  between operations  0.77 us (1%)
    ppermute x19, starting transfers between devices, rows_permute(): return lax.ppermute(value, 'rows', [(i, i ^ mask) for i in range(size)])  19.9 us
    ppermute x19, waiting for transfers between devices, rows_permute(): return lax.ppermute(value, 'rows', [(i, i ^ mask) for i in range(size)])  16.5 us
    pallas_call x1, Pallas kernels, inverse_factor(): pl.pallas_call(body, in_specs=[VMEM] * 2, out_specs=VMEM, out_shape=on_ch...  8.4 us
    ppermute x1, waiting for transfers between devices, local(): got_0 = lax.ppermute(own_0, 'cols', swap)  5.7 us
    ppermute x2, starting transfers between devices, local(): gathered.append(lax.ppermute(pieces[k], ('rows', 'cols'), pairs))  4.27 us
    ppermute x1, starting transfers between devices, local(): got_0 = lax.ppermute(own_0, 'cols', swap)  3.03 us
    pallas_call x1, Pallas kernels, first_sketch(): pl.pallas_call(first_sketch_kernel, in_specs=[HBM] * 3, out_specs=[VMEM]...  2.66 us
    pallas_call x2, Pallas kernels, project(): pl.pallas_call(body, in_specs=[VMEM] * (3 + len(after)), out_specs=[VMEM]...  2.07 us
  transfers between devices with their start and end apart: 23, of which 10 were waited for; matrix products, arithmetic and copies ran while one was open for 0% of the time, Pallas kernels for 21%

profile of v13, /device:TPU:0, one launch (start us, length us, event | category | flops | bytes accessed | tf_op | source)
XLA Modules:
  0.0 68.4 jit_solution(994834918985102405)
XLA Ops:
  0.6 2.7 %first_sketch.1 = (f32[512,128]{1,0:T(8,128)S(1)}, f32[512,2048]{1,0:T(8,128)S(1)}) custom-call(s32[2,16]{1,0:T(2,128)} %bitcast.6, f32[512,2048]{1,0:T(8,128)} %whole_ref.1, s32[2,2048]{1,0:T(2,128)} %bitcast.4), custom_call_target="tpu_custom_call" | custom-call | flops 2097 | bytes 4194 | tf_op jit(solution)/shard_map/first_sketch/pallas_call | solution.py:94
  3.3 3.0 %collective-permute-start = (f32[512,128]{1,0:T(8,128)S(1)}, f32[512,128]{1,0:T(8,128)S(1)}, u32[]{:S(2)}, u32[]{:S(2)}) collective-permute-start(f32[512,128]{1,0:T(8,128)S(1)} %get-tuple-element.35.own_ref), channel_id=1, source_target_pairs={{0,1},{1,0},{2,3},{3,2},{4,5},{5,4},{6,7},{7,6},{8,9},{9,8},{10,11... | collective-permute-start | bytes 786440 | tf_op jit(solution)/shard_map/ppermute | solution.py:491
  6.3 1.3 %second_sketch.1 = (f32[512,128]{1,0:T(8,128)S(1)}, bf16[512,2048]{1,0:T(8,128)(2,1)S(1)}, bf16[512,2048]{1,0:T(8,128)(2,1)S(1)}) custom-call(s32[2,16]{1,0:T(2,128)} %bitcast.7, s32[2,2048]{1,0:T(2,128)} %bitcast.5, f32[512,2048]{1,0:T(8,128)S(1)} %get-tuple-element.37.block_ref), custom_call_target="tpu_custom_call" | custom-call | flops 2097 | bytes 4194 | tf_op jit(solution)/shard_map/second_sketch/pallas_call | solution.py:132
  7.7 0.1 collective-permute-start.1
  7.8 5.7 %collective-permute-done.got_ref = f32[512,128]{1,0:T(8,128)S(1)} collective-permute-done((f32[512,128]{1,0:T(8,128)S(1)}, f32[512,128]{1,0:T(8,128)S(1)}, u32[]{:S(2)}, u32[]{:S(2)}) %collective-permute-start) | collective-permute-done | bytes 262176 | tf_op jit(solution)/shard_map/ppermute | solution.py:491
  13.5 0.4 first_gram.1
  13.9 1.0 %project.2 = (f32[128,256]{1,0:T(8,128)S(1)}, f32[128,256]{1,0:T(8,128)S(1)}, f32[2,128,256]{2,1,0:T(8,128)S(1)}, f32[2,128,256]{2,1,0:T(8,128)S(1)}, f32[2,128,256]{2,1,0:T(8,128)S(1)}) custom-call(bf16[256,512]{1,0:T(8,128)(2,1)S(1)} %get-tuple-element.41.refs_0_, bf16[512,2048]{1,0:T(8,128)(2,1)S(1)} %get-tuple-element.42.refs_1_, ...), custom_call_target="tpu_custom_call" | custom-call | flops 805306 | bytes 4194 | tf_op jit(solution)/shard_map/project/pallas_call | solution.py:236
  14.9 0.1 collective-permute-start.4
  15.0 0.5 collective-permute-start.5
  15.5 0.8 %collective-permute-done.4.refs_1_ = f32[128,256]{1,0:T(8,128)S(1)} collective-permute-done((f32[128,256]{1,0:T(8,128)S(1)}, f32[128,256]{1,0:T(8,128)S(1)}, u32[]{:S(2)}, u32[]{:S(2)}) %collective-permute-start.4) | collective-permute-done | bytes 131104 | tf_op jit(solution)/shard_map/ppermute | solution.py:483
  16.4 0.2 collective-permute-done.5.refs_2_
  16.6 2.1 %collective-permute-start.6 = (f32[2,128,256]{2,1,0:T(8,128)S(1)}, f32[2,128,256]{2,1,0:T(8,128)S(1)}, u32[]{:S(2)}, u32[]{:S(2)}) collective-permute-start(f32[2,128,256]{2,1,0:T(8,128)S(1)} %joined.2.refs_3_), channel_id=1, source_target_pairs={{0,4},{2,6},{4,0},{6,2},{8,12},{10,14},{12,8},{14,10},{16,20},{18,... | collective-permute-start | bytes 786440 | tf_op jit(solution)/shard_map/ppermute | solution.py:483
  18.7 0.0 collective-permute-done.1.refs_1_
  18.7 0.6 second_gram.1
  19.3 0.1 collective-permute-start.2
  19.4 1.0 %project.3 = (f32[128,256]{1,0:T(8,128)S(1)}, f32[128,256]{1,0:T(8,128)S(1)}, f32[2,128,256]{2,1,0:T(8,128)S(1)}, f32[2,128,256]{2,1,0:T(8,128)S(1)}, f32[2,128,256]{2,1,0:T(8,128)S(1)}) custom-call(bf16[256,512]{1,0:T(8,128)(2,1)S(1)} %get-tuple-element.52.refs_0_, bf16[512,2048]{1,0:T(8,128)(2,1)S(1)} %get-tuple-element.42.refs_1_, ...), custom_call_target="tpu_custom_call" | custom-call | flops 805306 | bytes 4194 | tf_op jit(solution)/shard_map/project/pallas_call | solution.py:236
  20.4 0.5 collective-permute-start.12
  21.0 0.1 collective-permute-start.13
  21.0 0.0 collective-permute-done.2.refs_1_
  21.1 1.6 %collective-permute-start.3 = (f32[192,128]{1,0:T(8,128)S(1)}, f32[192,128]{1,0:T(8,128)S(1)}, u32[]{:S(2)}, u32[]{:S(2)}) collective-permute-start(f32[192,128]{1,0:T(8,128)S(1)} %add_parts.4.refs_0_.refs_3_), channel_id=1, source_target_pairs={{0,8},{2,10},{4,12},{6,14},{8,0},{10,2},{12,4},{14,6},{16,24},{18,... | collective-permute-start | bytes 294920 | tf_op jit(solution)/shard_map/ppermute | solution.py:483
  22.7 0.2 collective-permute-start.10
  22.9 0.0 collective-permute-done.12.refs_1_
  22.9 0.3 collective-permute-start.11
  23.2 0.0 collective-permute-done.13.refs_2_
  23.2 1.4 %collective-permute-start.14 = (f32[2,128,256]{2,1,0:T(8,128)S(1)}, f32[2,128,256]{2,1,0:T(8,128)S(1)}, u32[]{:S(2)}, u32[]{:S(2)}) collective-permute-start(f32[2,128,256]{2,1,0:T(8,128)S(1)} %joined.3), channel_id=1, source_target_pairs={{0,4},{2,6},{4,0},{6,2},{8,12},{10,14},{12,8},{14,10},{16,20},{18,... | collective-permute-start | bytes 786440 | tf_op jit(solution)/shard_map/ppermute | solution.py:483
  24.6 1.7 %collective-permute-done.3.refs_1_ = f32[192,128]{1,0:T(8,128)S(1)} collective-permute-done((f32[192,128]{1,0:T(8,128)S(1)}, f32[192,128]{1,0:T(8,128)S(1)}, u32[]{:S(2)}, u32[]{:S(2)}) %collective-permute-start.3) | collective-permute-done | bytes 98336 | tf_op jit(solution)/shard_map/ppermute | solution.py:483
  26.3 0.0 collective-permute-done.6.refs_2_
  26.3 2.7 %collective-permute-start.7 = (f32[192,128]{1,0:T(8,128)S(1)}, f32[192,128]{1,0:T(8,128)S(1)}, u32[]{:S(2)}, u32[]{:S(2)}) collective-permute-start(f32[192,128]{1,0:T(8,128)S(1)} %add_parts.5.refs_0_), channel_id=1, source_target_pairs={{0,16},{2,18},{4,20},{6,22},{8,24},{10,26},{12,28},{14,30},{16,0},... | collective-permute-start | bytes 294920 | tf_op jit(solution)/shard_map/ppermute | solution.py:483
  28.9 4.8 %collective-permute-done.7.refs_1_ = f32[192,128]{1,0:T(8,128)S(1)} collective-permute-done((f32[192,128]{1,0:T(8,128)S(1)}, f32[192,128]{1,0:T(8,128)S(1)}, u32[]{:S(2)}, u32[]{:S(2)}) %collective-permute-start.7) | collective-permute-done | bytes 98336 | tf_op jit(solution)/shard_map/ppermute | solution.py:483
  33.7 1.4 %collective-permute-start.8 = (f32[192,128]{1,0:T(8,128)S(1)}, f32[192,128]{1,0:T(8,128)S(1)}, u32[]{:S(2)}, u32[]{:S(2)}) collective-permute-start(f32[192,128]{1,0:T(8,128)S(1)} %add_parts.6.refs_0_.refs_6_), channel_id=1, source_target_pairs={{0,4},{2,6},{4,0},{6,2},{8,12},{10,14},{12,8},{14,10},{16,20},{18,... | collective-permute-start | bytes 294920 | tf_op jit(solution)/shard_map/ppermute | solution.py:483
  35.1 0.0 collective-permute-done.10.refs_1_
  35.1 0.0 collective-permute-done.11.refs_4_
  35.1 0.0 collective-permute-done.14.refs_5_
  35.1 0.1 piece_sums.1
  35.2 0.7 collective-permute-start.15
  35.9 3.6 %collective-permute-start.16 = (f32[256,256]{1,0:T(8,128)S(1)}, f32[256,256]{1,0:T(8,128)S(1)}, u32[]{:S(2)}, u32[]{:S(2)}) collective-permute-start(f32[256,256]{1,0:T(8,128)S(1)} %get-tuple-element.59), channel_id=1, source_target_pairs={{0,9},{1,8},{2,27},{3,26},{4,13},{5,12},{6,31},{7,30},{8,0},{9,1},... | collective-permute-start | bytes 786440 | tf_op jit(solution)/shard_map/ppermute | solution.py:515
  39.5 0.0 collective-permute-done.8.refs_1_
  39.5 1.7 %collective-permute-start.9 = (f32[192,128]{1,0:T(8,128)S(1)}, f32[192,128]{1,0:T(8,128)S(1)}, u32[]{:S(2)}, u32[]{:S(2)}) collective-permute-start(f32[192,128]{1,0:T(8,128)S(1)} %add_parts.7.refs_0_), channel_id=1, source_target_pairs={{0,2},{2,0},{4,6},{6,4},{8,10},{10,8},{12,14},{14,12},{16,18},{18,... | collective-permute-start | bytes 294920 | tf_op jit(solution)/shard_map/ppermute | solution.py:483
  41.2 0.9 %collective-permute-done.9.refs_1_ = f32[192,128]{1,0:T(8,128)S(1)} collective-permute-done((f32[192,128]{1,0:T(8,128)S(1)}, f32[192,128]{1,0:T(8,128)S(1)}, u32[]{:S(2)}, u32[]{:S(2)}) %collective-permute-start.9) | collective-permute-done | bytes 98336 | tf_op jit(solution)/shard_map/ppermute | solution.py:483
  42.1 8.4 %inverse_factor.1.refs_2_.inverse_ref = f32[256,256]{1,0:T(8,128)S(1)} custom-call(f32[192,128]{1,0:T(8,128)S(1)} %add_parts.7.refs_0_, f32[192,128]{1,0:T(8,128)S(1)} %collective-permute-done.9.refs_1_), custom_call_target="tpu_custom_call" | custom-call | flops 1000000000 | bytes 524 | tf_op jit(solution)/shard_map/inverse_factor/pallas_call | solution.py:380
  50.5 0.0 collective-permute-done.15.p0
  50.6 0.0 collective-permute-done.16.p1
  50.6 0.4 remainder_pieces.1
  51.0 0.4 collective-permute-start.17
  51.4 0.7 %collective-permute-start.18 = (f32[4,16,256]{2,1,0:T(8,128)S(1)}, f32[4,16,256]{2,1,0:T(8,128)S(1)}, u32[]{:S(2)}, u32[]{:S(2)}) collective-permute-start(f32[4,16,256]{2,1,0:T(8,128)S(1)} %get-tuple-element.62), channel_id=1, source_target_pairs={{0,4},{2,6},{4,0},{6,2},{8,12},{10,14},{12,8},{14,10},{16,20},{18,... | collective-permute-start | bytes 196616 | tf_op jit(solution)/shard_map/ppermute | solution.py:483
  52.1 0.8 %collective-permute-start.19 = (f32[4,16,256]{2,1,0:T(8,128)S(1)}, f32[4,16,256]{2,1,0:T(8,128)S(1)}, u32[]{:S(2)}, u32[]{:S(2)}) collective-permute-start(f32[4,16,256]{2,1,0:T(8,128)S(1)} %get-tuple-element.63), channel_id=1, source_target_pairs={{0,6},{2,4},{4,2},{6,0},{8,14},{10,12},{12,10},{14,8},{16,22},{18,... | collective-permute-start | bytes 196616 | tf_op jit(solution)/shard_map/ppermute | solution.py:483
  52.9 0.0 collective-permute-done.17.r1
  52.9 3.3 %collective-permute-done.18.r2 = f32[4,16,256]{2,1,0:T(8,128)S(1)} collective-permute-done((f32[4,16,256]{2,1,0:T(8,128)S(1)}, f32[4,16,256]{2,1,0:T(8,128)S(1)}, u32[]{:S(2)}, u32[]{:S(2)}) %collective-permute-start.18) | collective-permute-done | bytes 65568 | tf_op jit(solution)/shard_map/ppermute | solution.py:483
  56.2 0.3 collective-permute-done.19.r3
  56.5 2.1 %collective-permute-start.20 = (f32[2,16,256]{2,1,0:T(8,128)S(1)}, f32[2,16,256]{2,1,0:T(8,128)S(1)}, u32[]{:S(2)}, u32[]{:S(2)}) collective-permute-start(f32[2,16,256]{2,1,0:T(8,128)S(1)} %get-tuple-element.65), channel_id=1, source_target_pairs={{0,8},{2,10},{4,12},{6,14},{8,0},{10,2},{12,4},{14,6},{16,24},{18,... | collective-permute-start | bytes 98312 | tf_op jit(solution)/shard_map/ppermute | solution.py:483
  58.6 3.4 %collective-permute-start.21 = (f32[2,16,256]{2,1,0:T(8,128)S(1)}, f32[2,16,256]{2,1,0:T(8,128)S(1)}, u32[]{:S(2)}, u32[]{:S(2)}) collective-permute-start(f32[2,16,256]{2,1,0:T(8,128)S(1)} %get-tuple-element.66), channel_id=1, source_target_pairs={{0,16},{2,18},{4,20},{6,22},{8,24},{10,26},{12,28},{14,30},{16,0},... | collective-permute-start | bytes 98312 | tf_op jit(solution)/shard_map/ppermute | solution.py:483
  62.0 0.0 collective-permute-start.22
  62.0 1.3 %scaled_core.1 = f32[512,256]{1,0:T(8,128)} custom-call(f32[512,128]{1,0:T(8,128)S(1)} %get-tuple-element.36.refs_0_, f32[512,128]{1,0:T(8,128)S(1)} %get-tuple-element.45.refs_1_, f32[256,256]{1,0:T(8,128)S(1)} %inverse_factor.1.refs_2_.inverse_ref), custom_call_target="tpu_custom_call" | custom-call | flops 201326 | bytes 1048 | tf_op jit(solution)/shard_map/scaled_core/pallas_call | solution.py:405
  63.3 0.0 collective-permute-done.20.p1
  63.3 1.2 %collective-permute-done.21.p2 = f32[2,16,256]{2,1,0:T(8,128)S(1)} collective-permute-done((f32[2,16,256]{2,1,0:T(8,128)S(1)}, f32[2,16,256]{2,1,0:T(8,128)S(1)}, u32[]{:S(2)}, u32[]{:S(2)}) %collective-permute-start.21) | collective-permute-done | bytes 32800 | tf_op jit(solution)/shard_map/ppermute | solution.py:483
  64.5 3.2 %collective-permute-done.22.p3 = f32[2,16,256]{2,1,0:T(8,128)S(1)} collective-permute-done((f32[2,16,256]{2,1,0:T(8,128)S(1)}, f32[2,16,256]{2,1,0:T(8,128)S(1)}, u32[]{:S(2)}, u32[]{:S(2)}) %collective-permute-start.22) | collective-permute-done | bytes 32800 | tf_op jit(solution)/shard_map/ppermute | solution.py:483
  67.7 0.7 %arrange.1 = f32[16,8,256]{2,1,0:T(8,128)} custom-call(f32[2,16,256]{2,1,0:T(8,128)S(1)} %get-tuple-element.64.p0, f32[2,16,256]{2,1,0:T(8,128)S(1)} %collective-permute-done.20.p1, f32[2,16,256]{2,1,0:T(8,128)S(1)} %collective-permute-done.21.p2, f32[2,16,256]{2,1,0:T(8,128)S(1)} %collective-permute-done.22.p3), custom_call_target="tpu_custom_call" | custom-call | bytes 131 | tf_op jit(solution)/shard_map/arrange/pallas_call | solution.py:468
  (7 shorter events, 0.1 us)
Async XLA Ops:
  3.3 10.2 %collective-permute-start = (f32[512,128]{1,0:T(8,128)S(1)}, f32[512,128]{1,0:T(8,128)S(1)}, u32[]{:S(2)}, u32[]{:S(2)}) collective-permute-start(f32[512,128]{1,0:T(8,128)S(1)} %get-tuple-element.35.own_ref), channel_id=1, source_target_pairs={{0,1},{1,0},{2,3},{3,2},{4,5},{5,4},{6,7},{7,6},{8,9},{9,8},{10,11... | collective-permute-start | bytes 786440 | tf_op jit(solution)/shard_map/ppermute | solution.py:491
  7.7 11.0 %collective-permute-start.1 = (f32[512,128]{1,0:T(8,128)S(1)}, f32[512,128]{1,0:T(8,128)S(1)}, u32[]{:S(2)}, u32[]{:S(2)}) collective-permute-start(f32[512,128]{1,0:T(8,128)S(1)} %get-tuple-element.38.refs_0_), channel_id=1, source_target_pairs={{0,1},{1,0},{2,3},{3,2},{4,5},{5,4},{6,7},{7,6},{8,9},{9,8},{10,11... | collective-permute-start | bytes 786440 | tf_op jit(solution)/shard_map/ppermute | solution.py:493
  14.9 1.4 %collective-permute-start.4 = (f32[128,256]{1,0:T(8,128)S(1)}, f32[128,256]{1,0:T(8,128)S(1)}, u32[]{:S(2)}, u32[]{:S(2)}) collective-permute-start(f32[128,256]{1,0:T(8,128)S(1)} %get-tuple-element.49), channel_id=1, source_target_pairs={{0,2},{2,0},{4,6},{6,4},{8,10},{10,8},{12,14},{14,12},{16,18},{18,... | collective-permute-start | bytes 393224 | tf_op jit(solution)/shard_map/ppermute | solution.py:483
  15.0 1.5 %collective-permute-start.5 = (f32[128,256]{1,0:T(8,128)S(1)}, f32[128,256]{1,0:T(8,128)S(1)}, u32[]{:S(2)}, u32[]{:S(2)}) collective-permute-start(f32[128,256]{1,0:T(8,128)S(1)} %get-tuple-element.50), channel_id=1, source_target_pairs={{0,2},{2,0},{4,6},{6,4},{8,10},{10,8},{12,14},{14,12},{16,18},{18,... | collective-permute-start | bytes 393224 | tf_op jit(solution)/shard_map/ppermute | solution.py:483
  16.6 9.7 %collective-permute-start.6 = (f32[2,128,256]{2,1,0:T(8,128)S(1)}, f32[2,128,256]{2,1,0:T(8,128)S(1)}, u32[]{:S(2)}, u32[]{:S(2)}) collective-permute-start(f32[2,128,256]{2,1,0:T(8,128)S(1)} %joined.2.refs_3_), channel_id=1, source_target_pairs={{0,4},{2,6},{4,0},{6,2},{8,12},{10,14},{12,8},{14,10},{16,20},{18,... | collective-permute-start | bytes 786440 | tf_op jit(solution)/shard_map/ppermute | solution.py:483
  19.3 1.8 %collective-permute-start.2 = (f32[192,128]{1,0:T(8,128)S(1)}, f32[192,128]{1,0:T(8,128)S(1)}, u32[]{:S(2)}, u32[]{:S(2)}) collective-permute-start(f32[192,128]{1,0:T(8,128)S(1)} %get-tuple-element.47), channel_id=1, source_target_pairs={{0,2},{2,0},{4,6},{6,4},{8,10},{10,8},{12,14},{14,12},{16,18},{18,... | collective-permute-start | bytes 294920 | tf_op jit(solution)/shard_map/ppermute | solution.py:483
  20.4 2.4 %collective-permute-start.12 = (f32[128,256]{1,0:T(8,128)S(1)}, f32[128,256]{1,0:T(8,128)S(1)}, u32[]{:S(2)}, u32[]{:S(2)}) collective-permute-start(f32[128,256]{1,0:T(8,128)S(1)} %get-tuple-element.56), channel_id=1, source_target_pairs={{0,2},{2,0},{4,6},{6,4},{8,10},{10,8},{12,14},{14,12},{16,18},{18,... | collective-permute-start | bytes 393224 | tf_op jit(solution)/shard_map/ppermute | solution.py:483
  21.0 2.2 %collective-permute-start.13 = (f32[128,256]{1,0:T(8,128)S(1)}, f32[128,256]{1,0:T(8,128)S(1)}, u32[]{:S(2)}, u32[]{:S(2)}) collective-permute-start(f32[128,256]{1,0:T(8,128)S(1)} %get-tuple-element.57), channel_id=1, source_target_pairs={{0,2},{2,0},{4,6},{6,4},{8,10},{10,8},{12,14},{14,12},{16,18},{18,... | collective-permute-start | bytes 393224 | tf_op jit(solution)/shard_map/ppermute | solution.py:483
  21.1 5.2 %collective-permute-start.3 = (f32[192,128]{1,0:T(8,128)S(1)}, f32[192,128]{1,0:T(8,128)S(1)}, u32[]{:S(2)}, u32[]{:S(2)}) collective-permute-start(f32[192,128]{1,0:T(8,128)S(1)} %add_parts.4.refs_0_.refs_3_), channel_id=1, source_target_pairs={{0,8},{2,10},{4,12},{6,14},{8,0},{10,2},{12,4},{14,6},{16,24},{18,... | collective-permute-start | bytes 294920 | tf_op jit(solution)/shard_map/ppermute | solution.py:483
  22.7 12.4 %collective-permute-start.10 = (f32[2,128,256]{2,1,0:T(8,128)S(1)}, f32[2,128,256]{2,1,0:T(8,128)S(1)}, u32[]{:S(2)}, u32[]{:S(2)}) collective-permute-start(f32[2,128,256]{2,1,0:T(8,128)S(1)} %get-tuple-element.51), channel_id=1, source_target_pairs={{0,2},{2,0},{4,6},{6,4},{8,10},{10,8},{12,14},{14,12},{16,18},{18,... | collective-permute-start | bytes 786440 | tf_op jit(solution)/shard_map/ppermute | solution.py:483
  22.9 12.2 %collective-permute-start.11 = (f32[2,128,256]{2,1,0:T(8,128)S(1)}, f32[2,128,256]{2,1,0:T(8,128)S(1)}, u32[]{:S(2)}, u32[]{:S(2)}) collective-permute-start(f32[2,128,256]{2,1,0:T(8,128)S(1)} %get-tuple-element.54), channel_id=1, source_target_pairs={{0,2},{2,0},{4,6},{6,4},{8,10},{10,8},{12,14},{14,12},{16,18},{18,... | collective-permute-start | bytes 786440 | tf_op jit(solution)/shard_map/ppermute | solution.py:483
  23.2 11.9 %collective-permute-start.14 = (f32[2,128,256]{2,1,0:T(8,128)S(1)}, f32[2,128,256]{2,1,0:T(8,128)S(1)}, u32[]{:S(2)}, u32[]{:S(2)}) collective-permute-start(f32[2,128,256]{2,1,0:T(8,128)S(1)} %joined.3), channel_id=1, source_target_pairs={{0,4},{2,6},{4,0},{6,2},{8,12},{10,14},{12,8},{14,10},{16,20},{18,... | collective-permute-start | bytes 786440 | tf_op jit(solution)/shard_map/ppermute | solution.py:483
  26.3 7.4 %collective-permute-start.7 = (f32[192,128]{1,0:T(8,128)S(1)}, f32[192,128]{1,0:T(8,128)S(1)}, u32[]{:S(2)}, u32[]{:S(2)}) collective-permute-start(f32[192,128]{1,0:T(8,128)S(1)} %add_parts.5.refs_0_), channel_id=1, source_target_pairs={{0,16},{2,18},{4,20},{6,22},{8,24},{10,26},{12,28},{14,30},{16,0},... | collective-permute-start | bytes 294920 | tf_op jit(solution)/shard_map/ppermute | solution.py:483
  33.7 5.7 %collective-permute-start.8 = (f32[192,128]{1,0:T(8,128)S(1)}, f32[192,128]{1,0:T(8,128)S(1)}, u32[]{:S(2)}, u32[]{:S(2)}) collective-permute-start(f32[192,128]{1,0:T(8,128)S(1)} %add_parts.6.refs_0_.refs_6_), channel_id=1, source_target_pairs={{0,4},{2,6},{4,0},{6,2},{8,12},{10,14},{12,8},{14,10},{16,20},{18,... | collective-permute-start | bytes 294920 | tf_op jit(solution)/shard_map/ppermute | solution.py:483
  35.2 15.3 %collective-permute-start.15 = (f32[256,256]{1,0:T(8,128)S(1)}, f32[256,256]{1,0:T(8,128)S(1)}, u32[]{:S(2)}, u32[]{:S(2)}) collective-permute-start(f32[256,256]{1,0:T(8,128)S(1)} %get-tuple-element.58), channel_id=1, source_target_pairs={{0,0},{1,1},{2,18},{3,19},{4,4},{5,5},{6,22},{7,23},{8,9},{9,8},{1... | collective-permute-start | bytes 786440 | tf_op jit(solution)/shard_map/ppermute | solution.py:515
  35.9 14.7 %collective-permute-start.16 = (f32[256,256]{1,0:T(8,128)S(1)}, f32[256,256]{1,0:T(8,128)S(1)}, u32[]{:S(2)}, u32[]{:S(2)}) collective-permute-start(f32[256,256]{1,0:T(8,128)S(1)} %get-tuple-element.59), channel_id=1, source_target_pairs={{0,9},{1,8},{2,27},{3,26},{4,13},{5,12},{6,31},{7,30},{8,0},{9,1},... | collective-permute-start | bytes 786440 | tf_op jit(solution)/shard_map/ppermute | solution.py:515
  39.5 2.6 %collective-permute-start.9 = (f32[192,128]{1,0:T(8,128)S(1)}, f32[192,128]{1,0:T(8,128)S(1)}, u32[]{:S(2)}, u32[]{:S(2)}) collective-permute-start(f32[192,128]{1,0:T(8,128)S(1)} %add_parts.7.refs_0_), channel_id=1, source_target_pairs={{0,2},{2,0},{4,6},{6,4},{8,10},{10,8},{12,14},{14,12},{16,18},{18,... | collective-permute-start | bytes 294920 | tf_op jit(solution)/shard_map/ppermute | solution.py:483
  51.0 1.9 %collective-permute-start.17 = (f32[4,16,256]{2,1,0:T(8,128)S(1)}, f32[4,16,256]{2,1,0:T(8,128)S(1)}, u32[]{:S(2)}, u32[]{:S(2)}) collective-permute-start(f32[4,16,256]{2,1,0:T(8,128)S(1)} %get-tuple-element.61), channel_id=1, source_target_pairs={{0,2},{2,0},{4,6},{6,4},{8,10},{10,8},{12,14},{14,12},{16,18},{18,... | collective-permute-start | bytes 196616 | tf_op jit(solution)/shard_map/ppermute | solution.py:483
  51.4 4.8 %collective-permute-start.18 = (f32[4,16,256]{2,1,0:T(8,128)S(1)}, f32[4,16,256]{2,1,0:T(8,128)S(1)}, u32[]{:S(2)}, u32[]{:S(2)}) collective-permute-start(f32[4,16,256]{2,1,0:T(8,128)S(1)} %get-tuple-element.62), channel_id=1, source_target_pairs={{0,4},{2,6},{4,0},{6,2},{8,12},{10,14},{12,8},{14,10},{16,20},{18,... | collective-permute-start | bytes 196616 | tf_op jit(solution)/shard_map/ppermute | solution.py:483
  52.1 4.4 %collective-permute-start.19 = (f32[4,16,256]{2,1,0:T(8,128)S(1)}, f32[4,16,256]{2,1,0:T(8,128)S(1)}, u32[]{:S(2)}, u32[]{:S(2)}) collective-permute-start(f32[4,16,256]{2,1,0:T(8,128)S(1)} %get-tuple-element.63), channel_id=1, source_target_pairs={{0,6},{2,4},{4,2},{6,0},{8,14},{10,12},{12,10},{14,8},{16,22},{18,... | collective-permute-start | bytes 196616 | tf_op jit(solution)/shard_map/ppermute | solution.py:483
  56.5 6.7 %collective-permute-start.20 = (f32[2,16,256]{2,1,0:T(8,128)S(1)}, f32[2,16,256]{2,1,0:T(8,128)S(1)}, u32[]{:S(2)}, u32[]{:S(2)}) collective-permute-start(f32[2,16,256]{2,1,0:T(8,128)S(1)} %get-tuple-element.65), channel_id=1, source_target_pairs={{0,8},{2,10},{4,12},{6,14},{8,0},{10,2},{12,4},{14,6},{16,24},{18,... | collective-permute-start | bytes 98312 | tf_op jit(solution)/shard_map/ppermute | solution.py:483
  58.6 5.9 %collective-permute-start.21 = (f32[2,16,256]{2,1,0:T(8,128)S(1)}, f32[2,16,256]{2,1,0:T(8,128)S(1)}, u32[]{:S(2)}, u32[]{:S(2)}) collective-permute-start(f32[2,16,256]{2,1,0:T(8,128)S(1)} %get-tuple-element.66), channel_id=1, source_target_pairs={{0,16},{2,18},{4,20},{6,22},{8,24},{10,26},{12,28},{14,30},{16,0},... | collective-permute-start | bytes 98312 | tf_op jit(solution)/shard_map/ppermute | solution.py:483
  62.0 5.7 %collective-permute-start.22 = (f32[2,16,256]{2,1,0:T(8,128)S(1)}, f32[2,16,256]{2,1,0:T(8,128)S(1)}, u32[]{:S(2)}, u32[]{:S(2)}) collective-permute-start(f32[2,16,256]{2,1,0:T(8,128)S(1)} %get-tuple-element.67), channel_id=1, source_target_pairs={{0,24},{2,26},{4,28},{6,30},{8,16},{10,18},{12,20},{14,22},{16,8},... | collective-permute-start | bytes 98312 | tf_op jit(solution)/shard_map/ppermute | solution.py:483

commit v14 on v13

--- a/solution.py
+++ b/solution.py
@@ -415,11 +415,13 @@
 
 def remainder_kernel(inverse_ref, p0, p1, o0, o1, o2, o3, work):
     work[...] = jnp.dot(inverse_ref[...], p0[...] + p1[...], precision=HIGHEST)
-    device = lax.axis_index("rows")
+    row = lax.axis_index("rows")
     for m, out in enumerate((o0, o1, o2, o3)):
-        for t in range(4):
-            rank_block = (4 * t + m) ^ device
-            out[t] = work[pl.ds(pl.multiple_of(rank_block * 16, 16), 16), :]
+        to = (row & 3) ^ m
+        for j in range(4):
+            deep = (row >> 2) ^ (((to & 1) << 1) | (j >> 1))
+            rank_block = (deep << 2) | (to ^ (j & 1))
+            out[j] = work[pl.ds(pl.multiple_of(rank_block * 16, 16), 16), :]
 
 
 def remainder_pieces(inverse, pieces):
@@ -435,31 +437,51 @@
     )(*held(inverse, *pieces))
 
 
-def collect_kernel(r0, r1, r2, r3, o0, o1, o2, o3):
-    for t, out in enumerate((o0, o1, o2, o3)):
-        out[0] = r0[t] + r1[t]
-        out[1] = r2[t] + r3[t]
+def collect_kernel(r0, r1, r2, r3, o0, o1):
+    for t, out in enumerate((o0, o1)):
+        for j in range(2):
+            out[j, 0] = r0[2 * t + j] + r1[2 * t + j]
+            out[j, 1] = r2[2 * t + j] + r3[2 * t + j]
 
 
 def collect(firsts):
     return pl.pallas_call(
         collect_kernel,
         in_specs=[VMEM] * 4,
-        out_specs=[VMEM] * 4,
-        out_shape=[on_chip(2, 16, 2 * BLK)] * 4,
+        out_specs=[VMEM] * 2,
+        out_shape=[on_chip(2, 2, 16, 2 * BLK)] * 2,
         cost_estimate=cost(0, 16 * BLK * 64),
         compiler_params=LIMIT,
         name="collect",
     )(*held(*firsts))
 
 
-def arrange_kernel(p0, p1, p2, p3, out_ref, work):
+def share_kernel(p0, p1, out):
+    out[0] = p0[1]
+    out[1] = p1[1]
+
+
+def share(pieces):
+    return pl.pallas_call(
+        share_kernel,
+        in_specs=[VMEM] * 2,
+        out_specs=VMEM,
+        out_shape=on_chip(2, 2, 16, 2 * BLK),
+        cost_estimate=cost(0, 16 * BLK * 64),
+        compiler_params=LIMIT,
+        name="share",
+    )(*held(*pieces))
+
+
+def arrange_kernel(p0, p1, shared, out_ref, work):
     row = lax.axis_index("rows")
-    right, deep, y = (row >> 1) & 1, row >> 2, lax.axis_index("cols")
-    for t, piece in enumerate((p0, p1, p2, p3)):
-        there = deep ^ t
-        for m in range(2):
-            work[((there & 1) ^ y) * 4 + (there >> 1) * 2 + (right ^ m)] = piece[m]
+    core, right, deep, y = row & 1, (row >> 1) & 1, row >> 2, lax.axis_index("cols")
+    for t, ours in enumerate((p0, p1)):
+        for other in range(2):
+            there = deep ^ (((core ^ other) << 1) | t)
+            piece = shared.at[t] if other else ours.at[0]
+            for m in range(2):
+                work[((there & 1) ^ y) * 4 + (there >> 1) * 2 + (right ^ m)] = piece[m]
     for mode in range(MODE):
         out_ref[:, mode, :] = work[mode]
 
@@ -467,7 +489,7 @@
 def arrange(pieces):
     out = pl.pallas_call(
         arrange_kernel,
-        in_specs=[VMEM] * 4,
+        in_specs=[VMEM] * 3,
         out_specs=VMEM,
         out_shape=jax.ShapeDtypeStruct((16, MODE, 2 * BLK), F32),
         scratch_shapes=[pltpu.VMEM((MODE, 16, 2 * BLK), F32)],
@@ -516,7 +538,11 @@
     parts = remainder_pieces(inverse, gathered)
     core_scaled = scaled_core(first, second, inverse, math.sqrt(total_rows))
     sums = collect([parts[0]] + [rows_permute(parts[m], m) for m in (1, 2, 3)])
-    return core_scaled, arrange([sums[0]] + [rows_permute(sums[t], 4 * t) for t in (1, 2, 3)])
+    passed = []
+    for t in range(2):
+        pairs = [(i, i ^ (t << 2) ^ ((i & 1) << 3)) for i in range(16)]
+        passed.append(lax.ppermute(sums[t], "rows", pairs))
+    return core_scaled, arrange([*passed, rows_permute(share(passed), 1)])
 
 
 def sketch_matrix(pattern, sign_bits, block_size):

time: 68.6 us -> 67.8 us (0.988)
  waiting for transfers between devices: 22.2 us -> 20 us
  starting transfers between devices: 27.3 us -> 28.7 us
    ppermute x19 -> x17, waiting for transfers between devices: 16.5 us -> 12 us  [rows_permute(): return lax.ppermute(value, 'rows', [(i, i ^ mask) for i in range(size)])]
    ppermute x0 -> x2, starting transfers between devices: none -> 2.91 us  [local(): passed.append(lax.ppermute(sums[t], 'rows', pairs))]
    ppermute x0 -> x2, waiting for transfers between devices: none -> 2.24 us  [local(): passed.append(lax.ppermute(sums[t], 'rows', pairs))]
    ppermute x19 -> x17, starting transfers between devices: 19.9 us -> 18.6 us  [rows_permute(): return lax.ppermute(value, 'rows', [(i, i ^ mask) for i in range(size)])]
  transfers between devices with their start and end apart: 23 -> 23, of which waited for: 10 -> 9; matrix products, arithmetic and copies ran while one was open for 0% -> 0% of each run, Pallas kernels for 21% -> 21%
where the time goes in v14:
time: 67.8 us; the launch traced here: 67.6 us
  starting transfers between devices  28.7 us (42%)
  waiting for transfers between devices  20 us (29%)
  Pallas kernels  18.1 us (27%)
  between operations  0.78 us (1%)
    ppermute x17, starting transfers between devices, rows_permute(): return lax.ppermute(value, 'rows', [(i, i ^ mask) for i in range(size)])  18.6 us
    ppermute x17, waiting for transfers between devices, rows_permute(): return lax.ppermute(value, 'rows', [(i, i ^ mask) for i in range(size)])  12 us
    pallas_call x1, Pallas kernels, inverse_factor(): pl.pallas_call(body, in_specs=[VMEM] * 2, out_specs=VMEM, out_shape=on_ch...  8.4 us
    ppermute x1, waiting for transfers between devices, local(): got_0 = lax.ppermute(own_0, 'cols', swap)  5.7 us
    ppermute x2, starting transfers between devices, local(): gathered.append(lax.ppermute(pieces[k], ('rows', 'cols'), pairs))  4.09 us
    ppermute x1, starting transfers between devices, local(): got_0 = lax.ppermute(own_0, 'cols', swap)  3.03 us
    ppermute x2, starting transfers between devices, local(): passed.append(lax.ppermute(sums[t], 'rows', pairs))  2.91 us
    pallas_call x1, Pallas kernels, first_sketch(): pl.pallas_call(first_sketch_kernel, in_specs=[HBM] * 3, out_specs=[VMEM]...  2.66 us
  transfers between devices with their start and end apart: 23, of which 9 were waited for; matrix products, arithmetic and copies ran while one was open for 0% of the time, Pallas kernels for 21%

profile of v14, /device:TPU:0, one launch (start us, length us, event | category | flops | bytes accessed | tf_op | source)
XLA Modules:
  0.0 67.6 jit_solution(18031523634058525550)
XLA Ops:
  0.6 2.7 %first_sketch.1 = (f32[512,128]{1,0:T(8,128)S(1)}, f32[512,2048]{1,0:T(8,128)S(1)}) custom-call(s32[2,16]{1,0:T(2,128)} %bitcast.6, f32[512,2048]{1,0:T(8,128)} %whole_ref.1, s32[2,2048]{1,0:T(2,128)} %bitcast.4), custom_call_target="tpu_custom_call" | custom-call | flops 2097 | bytes 4194 | tf_op jit(solution)/shard_map/first_sketch/pallas_call | solution.py:94
  3.3 3.0 %collective-permute-start = (f32[512,128]{1,0:T(8,128)S(1)}, f32[512,128]{1,0:T(8,128)S(1)}, u32[]{:S(2)}, u32[]{:S(2)}) collective-permute-start(f32[512,128]{1,0:T(8,128)S(1)} %get-tuple-element.33.own_ref), channel_id=1, source_target_pairs={{0,1},{1,0},{2,3},{3,2},{4,5},{5,4},{6,7},{7,6},{8,9},{9,8},{10,11... | collective-permute-start | bytes 786440 | tf_op jit(solution)/shard_map/ppermute | solution.py:513
  6.3 1.3 %second_sketch.1 = (f32[512,128]{1,0:T(8,128)S(1)}, bf16[512,2048]{1,0:T(8,128)(2,1)S(1)}, bf16[512,2048]{1,0:T(8,128)(2,1)S(1)}) custom-call(s32[2,16]{1,0:T(2,128)} %bitcast.7, s32[2,2048]{1,0:T(2,128)} %bitcast.5, f32[512,2048]{1,0:T(8,128)S(1)} %get-tuple-element.35.block_ref), custom_call_target="tpu_custom_call" | custom-call | flops 2097 | bytes 4194 | tf_op jit(solution)/shard_map/second_sketch/pallas_call | solution.py:132
  7.7 0.1 collective-permute-start.1
  7.8 5.7 %collective-permute-done.got_ref = f32[512,128]{1,0:T(8,128)S(1)} collective-permute-done((f32[512,128]{1,0:T(8,128)S(1)}, f32[512,128]{1,0:T(8,128)S(1)}, u32[]{:S(2)}, u32[]{:S(2)}) %collective-permute-start) | collective-permute-done | bytes 262176 | tf_op jit(solution)/shard_map/ppermute | solution.py:513
  13.5 0.4 first_gram.1
  13.9 1.0 %project.2 = (f32[128,256]{1,0:T(8,128)S(1)}, f32[128,256]{1,0:T(8,128)S(1)}, f32[2,128,256]{2,1,0:T(8,128)S(1)}, f32[2,128,256]{2,1,0:T(8,128)S(1)}, f32[2,128,256]{2,1,0:T(8,128)S(1)}) custom-call(bf16[256,512]{1,0:T(8,128)(2,1)S(1)} %get-tuple-element.39.refs_0_, bf16[512,2048]{1,0:T(8,128)(2,1)S(1)} %get-tuple-element.40.refs_1_, ...), custom_call_target="tpu_custom_call" | custom-call | flops 805306 | bytes 4194 | tf_op jit(solution)/shard_map/project/pallas_call | solution.py:236
  14.9 0.1 collective-permute-start.4
  15.0 0.5 collective-permute-start.5
  15.5 0.8 %collective-permute-done.4.refs_1_ = f32[128,256]{1,0:T(8,128)S(1)} collective-permute-done((f32[128,256]{1,0:T(8,128)S(1)}, f32[128,256]{1,0:T(8,128)S(1)}, u32[]{:S(2)}, u32[]{:S(2)}) %collective-permute-start.4) | collective-permute-done | bytes 131104 | tf_op jit(solution)/shard_map/ppermute | solution.py:505
  16.3 0.2 collective-permute-done.5.refs_2_
  16.6 2.1 %collective-permute-start.6 = (f32[2,128,256]{2,1,0:T(8,128)S(1)}, f32[2,128,256]{2,1,0:T(8,128)S(1)}, u32[]{:S(2)}, u32[]{:S(2)}) collective-permute-start(f32[2,128,256]{2,1,0:T(8,128)S(1)} %joined.2.refs_3_), channel_id=1, source_target_pairs={{0,4},{2,6},{4,0},{6,2},{8,12},{10,14},{12,8},{14,10},{16,20},{18,... | collective-permute-start | bytes 786440 | tf_op jit(solution)/shard_map/ppermute | solution.py:505
  18.7 0.0 collective-permute-done.1.refs_1_
  18.7 0.6 second_gram.1
  19.3 0.1 collective-permute-start.2
  19.4 1.0 %project.3 = (f32[128,256]{1,0:T(8,128)S(1)}, f32[128,256]{1,0:T(8,128)S(1)}, f32[2,128,256]{2,1,0:T(8,128)S(1)}, f32[2,128,256]{2,1,0:T(8,128)S(1)}, f32[2,128,256]{2,1,0:T(8,128)S(1)}) custom-call(bf16[256,512]{1,0:T(8,128)(2,1)S(1)} %get-tuple-element.50.refs_0_, bf16[512,2048]{1,0:T(8,128)(2,1)S(1)} %get-tuple-element.40.refs_1_, ...), custom_call_target="tpu_custom_call" | custom-call | flops 805306 | bytes 4194 | tf_op jit(solution)/shard_map/project/pallas_call | solution.py:236
  20.4 0.5 collective-permute-start.12
  21.0 0.1 collective-permute-start.13
  21.0 0.0 collective-permute-done.2.refs_1_
  21.1 1.6 %collective-permute-start.3 = (f32[192,128]{1,0:T(8,128)S(1)}, f32[192,128]{1,0:T(8,128)S(1)}, u32[]{:S(2)}, u32[]{:S(2)}) collective-permute-start(f32[192,128]{1,0:T(8,128)S(1)} %add_parts.4.refs_0_.refs_3_), channel_id=1, source_target_pairs={{0,8},{2,10},{4,12},{6,14},{8,0},{10,2},{12,4},{14,6},{16,24},{18,... | collective-permute-start | bytes 294920 | tf_op jit(solution)/shard_map/ppermute | solution.py:505
  22.7 0.2 collective-permute-start.10
  22.9 0.0 collective-permute-done.12.refs_1_
  22.9 0.3 collective-permute-start.11
  23.2 0.0 collective-permute-done.13.refs_2_
  23.2 1.4 %collective-permute-start.14 = (f32[2,128,256]{2,1,0:T(8,128)S(1)}, f32[2,128,256]{2,1,0:T(8,128)S(1)}, u32[]{:S(2)}, u32[]{:S(2)}) collective-permute-start(f32[2,128,256]{2,1,0:T(8,128)S(1)} %joined.3), channel_id=1, source_target_pairs={{0,4},{2,6},{4,0},{6,2},{8,12},{10,14},{12,8},{14,10},{16,20},{18,... | collective-permute-start | bytes 786440 | tf_op jit(solution)/shard_map/ppermute | solution.py:505
  24.6 1.7 %collective-permute-done.3.refs_1_ = f32[192,128]{1,0:T(8,128)S(1)} collective-permute-done((f32[192,128]{1,0:T(8,128)S(1)}, f32[192,128]{1,0:T(8,128)S(1)}, u32[]{:S(2)}, u32[]{:S(2)}) %collective-permute-start.3) | collective-permute-done | bytes 98336 | tf_op jit(solution)/shard_map/ppermute | solution.py:505
  26.3 0.0 collective-permute-done.6.refs_2_
  26.3 2.7 %collective-permute-start.7 = (f32[192,128]{1,0:T(8,128)S(1)}, f32[192,128]{1,0:T(8,128)S(1)}, u32[]{:S(2)}, u32[]{:S(2)}) collective-permute-start(f32[192,128]{1,0:T(8,128)S(1)} %add_parts.5.refs_0_), channel_id=1, source_target_pairs={{0,16},{2,18},{4,20},{6,22},{8,24},{10,26},{12,28},{14,30},{16,0},... | collective-permute-start | bytes 294920 | tf_op jit(solution)/shard_map/ppermute | solution.py:505
  28.9 4.8 %collective-permute-done.7.refs_1_ = f32[192,128]{1,0:T(8,128)S(1)} collective-permute-done((f32[192,128]{1,0:T(8,128)S(1)}, f32[192,128]{1,0:T(8,128)S(1)}, u32[]{:S(2)}, u32[]{:S(2)}) %collective-permute-start.7) | collective-permute-done | bytes 98336 | tf_op jit(solution)/shard_map/ppermute | solution.py:505
  33.7 1.4 %collective-permute-start.8 = (f32[192,128]{1,0:T(8,128)S(1)}, f32[192,128]{1,0:T(8,128)S(1)}, u32[]{:S(2)}, u32[]{:S(2)}) collective-permute-start(f32[192,128]{1,0:T(8,128)S(1)} %add_parts.6.refs_0_.refs_6_), channel_id=1, source_target_pairs={{0,4},{2,6},{4,0},{6,2},{8,12},{10,14},{12,8},{14,10},{16,20},{18,... | collective-permute-start | bytes 294920 | tf_op jit(solution)/shard_map/ppermute | solution.py:505
  35.1 0.0 collective-permute-done.10.refs_1_
  35.1 0.0 collective-permute-done.11.refs_4_
  35.1 0.0 collective-permute-done.14.refs_5_
  35.1 0.1 piece_sums.1
  35.2 0.7 %collective-permute-start.15 = (f32[256,256]{1,0:T(8,128)S(1)}, f32[256,256]{1,0:T(8,128)S(1)}, u32[]{:S(2)}, u32[]{:S(2)}) collective-permute-start(f32[256,256]{1,0:T(8,128)S(1)} %get-tuple-element.56), channel_id=1, source_target_pairs={{0,0},{1,1},{2,18},{3,19},{4,4},{5,5},{6,22},{7,23},{8,9},{9,8},{1... | collective-permute-start | bytes 786440 | tf_op jit(solution)/shard_map/ppermute | solution.py:537
  35.9 3.4 %collective-permute-start.16 = (f32[256,256]{1,0:T(8,128)S(1)}, f32[256,256]{1,0:T(8,128)S(1)}, u32[]{:S(2)}, u32[]{:S(2)}) collective-permute-start(f32[256,256]{1,0:T(8,128)S(1)} %get-tuple-element.57), channel_id=1, source_target_pairs={{0,9},{1,8},{2,27},{3,26},{4,13},{5,12},{6,31},{7,30},{8,0},{9,1},... | collective-permute-start | bytes 786440 | tf_op jit(solution)/shard_map/ppermute | solution.py:537
  39.3 0.0 collective-permute-done.8.refs_1_
  39.3 1.7 %collective-permute-start.9 = (f32[192,128]{1,0:T(8,128)S(1)}, f32[192,128]{1,0:T(8,128)S(1)}, u32[]{:S(2)}, u32[]{:S(2)}) collective-permute-start(f32[192,128]{1,0:T(8,128)S(1)} %add_parts.7.refs_0_), channel_id=1, source_target_pairs={{0,2},{2,0},{4,6},{6,4},{8,10},{10,8},{12,14},{14,12},{16,18},{18,... | collective-permute-start | bytes 294920 | tf_op jit(solution)/shard_map/ppermute | solution.py:505
  41.0 0.9 %collective-permute-done.9.refs_1_ = f32[192,128]{1,0:T(8,128)S(1)} collective-permute-done((f32[192,128]{1,0:T(8,128)S(1)}, f32[192,128]{1,0:T(8,128)S(1)}, u32[]{:S(2)}, u32[]{:S(2)}) %collective-permute-start.9) | collective-permute-done | bytes 98336 | tf_op jit(solution)/shard_map/ppermute | solution.py:505
  41.9 8.4 %inverse_factor.1.refs_2_.inverse_ref = f32[256,256]{1,0:T(8,128)S(1)} custom-call(f32[192,128]{1,0:T(8,128)S(1)} %add_parts.7.refs_0_, f32[192,128]{1,0:T(8,128)S(1)} %collective-permute-done.9.refs_1_), custom_call_target="tpu_custom_call" | custom-call | flops 1000000000 | bytes 524 | tf_op jit(solution)/shard_map/inverse_factor/pallas_call | solution.py:380
  50.4 0.0 collective-permute-done.15.p0
  50.4 0.0 collective-permute-done.16.p1
  50.4 0.4 remainder_pieces.1
  50.8 0.4 collective-permute-start.17
  51.2 0.7 %collective-permute-start.18 = (f32[4,16,256]{2,1,0:T(8,128)S(1)}, f32[4,16,256]{2,1,0:T(8,128)S(1)}, u32[]{:S(2)}, u32[]{:S(2)}) collective-permute-start(f32[4,16,256]{2,1,0:T(8,128)S(1)} %get-tuple-element.60), channel_id=1, source_target_pairs={{0,4},{2,6},{4,0},{6,2},{8,12},{10,14},{12,8},{14,10},{16,20},{18,... | collective-permute-start | bytes 196616 | tf_op jit(solution)/shard_map/ppermute | solution.py:505
  51.9 0.8 %collective-permute-start.19 = (f32[4,16,256]{2,1,0:T(8,128)S(1)}, f32[4,16,256]{2,1,0:T(8,128)S(1)}, u32[]{:S(2)}, u32[]{:S(2)}) collective-permute-start(f32[4,16,256]{2,1,0:T(8,128)S(1)} %get-tuple-element.61), channel_id=1, source_target_pairs={{0,6},{2,4},{4,2},{6,0},{8,14},{10,12},{12,10},{14,8},{16,22},{18,... | collective-permute-start | bytes 196616 | tf_op jit(solution)/shard_map/ppermute | solution.py:505
  52.7 0.0 collective-permute-done.17.r1
  52.7 3.3 %collective-permute-done.18.r2 = f32[4,16,256]{2,1,0:T(8,128)S(1)} collective-permute-done((f32[4,16,256]{2,1,0:T(8,128)S(1)}, f32[4,16,256]{2,1,0:T(8,128)S(1)}, u32[]{:S(2)}, u32[]{:S(2)}) %collective-permute-start.18) | collective-permute-done | bytes 65568 | tf_op jit(solution)/shard_map/ppermute | solution.py:505
  56.0 0.3 collective-permute-done.19.r3
  56.4 0.7 collective-permute-start.20
  57.0 2.2 %collective-permute-start.21 = (f32[2,2,16,256]{3,2,1,0:T(8,128)S(1)}, f32[2,2,16,256]{3,2,1,0:T(8,128)S(1)}, u32[]{:S(2)}, u32[]{:S(2)}) collective-permute-start(f32[2,2,16,256]{3,2,1,0:T(8,128)S(1)} %get-tuple-element.63), channel_id=1, source_target_pairs={{0,8},{2,26},{4,12},{6,30},{8,0},{10,18},{12,4},{14,22},{16,24},{1... | collective-permute-start | bytes 196616 | tf_op jit(solution)/shard_map/ppermute | solution.py:544
  59.3 0.0 collective-permute-done.20.p0
  59.3 2.2 %collective-permute-done.21.p1 = f32[2,2,16,256]{3,2,1,0:T(8,128)S(1)} collective-permute-done((f32[2,2,16,256]{3,2,1,0:T(8,128)S(1)}, f32[2,2,16,256]{3,2,1,0:T(8,128)S(1)}, u32[]{:S(2)}, u32[]{:S(2)}) %collective-permute-start.21) | collective-permute-done | bytes 65568 | tf_op jit(solution)/shard_map/ppermute | solution.py:544
  61.5 4.1 %collective-permute-start.22 = (f32[2,2,16,256]{3,2,1,0:T(8,128)S(1)}, f32[2,2,16,256]{3,2,1,0:T(8,128)S(1)}, u32[]{:S(2)}, u32[]{:S(2)}) collective-permute-start(f32[2,2,16,256]{3,2,1,0:T(8,128)S(1)} %share.1), channel_id=1, source_target_pairs={{0,2},{2,0},{4,6},{6,4},{8,10},{10,8},{12,14},{14,12},{16,18},{18,... | collective-permute-start | bytes 196616 | tf_op jit(solution)/shard_map/ppermute | solution.py:505
  65.6 1.3 %scaled_core.1 = f32[512,256]{1,0:T(8,128)} custom-call(f32[512,128]{1,0:T(8,128)S(1)} %get-tuple-element.34.refs_0_, f32[512,128]{1,0:T(8,128)S(1)} %get-tuple-element.43.refs_1_, f32[256,256]{1,0:T(8,128)S(1)} %inverse_factor.1.refs_2_.inverse_ref), custom_call_target="tpu_custom_call" | custom-call | flops 201326 | bytes 1048 | tf_op jit(solution)/shard_map/scaled_core/pallas_call | solution.py:405
  66.9 0.0 collective-permute-done.22.shared
  66.9 0.7 %arrange.1 = f32[16,8,256]{2,1,0:T(8,128)} custom-call(f32[2,2,16,256]{3,2,1,0:T(8,128)S(1)} %collective-permute-done.20.p0, f32[2,2,16,256]{3,2,1,0:T(8,128)S(1)} %collective-permute-done.21.p1, f32[2,2,16,256]{3,2,1,0:T(8,128)S(1)} %collective-permute-done.22.shared), custom_call_target="tpu_custom_call" | custom-call | bytes 131 | tf_op jit(solution)/shard_map/arrange/pallas_call | solution.py:490
  (8 shorter events, 0.1 us)
Async XLA Ops:
  3.3 10.2 %collective-permute-start = (f32[512,128]{1,0:T(8,128)S(1)}, f32[512,128]{1,0:T(8,128)S(1)}, u32[]{:S(2)}, u32[]{:S(2)}) collective-permute-start(f32[512,128]{1,0:T(8,128)S(1)} %get-tuple-element.33.own_ref), channel_id=1, source_target_pairs={{0,1},{1,0},{2,3},{3,2},{4,5},{5,4},{6,7},{7,6},{8,9},{9,8},{10,11... | collective-permute-start | bytes 786440 | tf_op jit(solution)/shard_map/ppermute | solution.py:513
  7.7 11.0 %collective-permute-start.1 = (f32[512,128]{1,0:T(8,128)S(1)}, f32[512,128]{1,0:T(8,128)S(1)}, u32[]{:S(2)}, u32[]{:S(2)}) collective-permute-start(f32[512,128]{1,0:T(8,128)S(1)} %get-tuple-element.36.refs_0_), channel_id=1, source_target_pairs={{0,1},{1,0},{2,3},{3,2},{4,5},{5,4},{6,7},{7,6},{8,9},{9,8},{10,11... | collective-permute-start | bytes 786440 | tf_op jit(solution)/shard_map/ppermute | solution.py:515
  14.9 1.4 %collective-permute-start.4 = (f32[128,256]{1,0:T(8,128)S(1)}, f32[128,256]{1,0:T(8,128)S(1)}, u32[]{:S(2)}, u32[]{:S(2)}) collective-permute-start(f32[128,256]{1,0:T(8,128)S(1)} %get-tuple-element.47), channel_id=1, source_target_pairs={{0,2},{2,0},{4,6},{6,4},{8,10},{10,8},{12,14},{14,12},{16,18},{18,... | collective-permute-start | bytes 393224 | tf_op jit(solution)/shard_map/ppermute | solution.py:505
  15.0 1.5 %collective-permute-start.5 = (f32[128,256]{1,0:T(8,128)S(1)}, f32[128,256]{1,0:T(8,128)S(1)}, u32[]{:S(2)}, u32[]{:S(2)}) collective-permute-start(f32[128,256]{1,0:T(8,128)S(1)} %get-tuple-element.48), channel_id=1, source_target_pairs={{0,2},{2,0},{4,6},{6,4},{8,10},{10,8},{12,14},{14,12},{16,18},{18,... | collective-permute-start | bytes 393224 | tf_op jit(solution)/shard_map/ppermute | solution.py:505
  16.6 9.7 %collective-permute-start.6 = (f32[2,128,256]{2,1,0:T(8,128)S(1)}, f32[2,128,256]{2,1,0:T(8,128)S(1)}, u32[]{:S(2)}, u32[]{:S(2)}) collective-permute-start(f32[2,128,256]{2,1,0:T(8,128)S(1)} %joined.2.refs_3_), channel_id=1, source_target_pairs={{0,4},{2,6},{4,0},{6,2},{8,12},{10,14},{12,8},{14,10},{16,20},{18,... | collective-permute-start | bytes 786440 | tf_op jit(solution)/shard_map/ppermute | solution.py:505
  19.3 1.8 %collective-permute-start.2 = (f32[192,128]{1,0:T(8,128)S(1)}, f32[192,128]{1,0:T(8,128)S(1)}, u32[]{:S(2)}, u32[]{:S(2)}) collective-permute-start(f32[192,128]{1,0:T(8,128)S(1)} %get-tuple-element.45), channel_id=1, source_target_pairs={{0,2},{2,0},{4,6},{6,4},{8,10},{10,8},{12,14},{14,12},{16,18},{18,... | collective-permute-start | bytes 294920 | tf_op jit(solution)/shard_map/ppermute | solution.py:505
  20.4 2.4 %collective-permute-start.12 = (f32[128,256]{1,0:T(8,128)S(1)}, f32[128,256]{1,0:T(8,128)S(1)}, u32[]{:S(2)}, u32[]{:S(2)}) collective-permute-start(f32[128,256]{1,0:T(8,128)S(1)} %get-tuple-element.54), channel_id=1, source_target_pairs={{0,2},{2,0},{4,6},{6,4},{8,10},{10,8},{12,14},{14,12},{16,18},{18,... | collective-permute-start | bytes 393224 | tf_op jit(solution)/shard_map/ppermute | solution.py:505
  21.0 2.3 %collective-permute-start.13 = (f32[128,256]{1,0:T(8,128)S(1)}, f32[128,256]{1,0:T(8,128)S(1)}, u32[]{:S(2)}, u32[]{:S(2)}) collective-permute-start(f32[128,256]{1,0:T(8,128)S(1)} %get-tuple-element.55), channel_id=1, source_target_pairs={{0,2},{2,0},{4,6},{6,4},{8,10},{10,8},{12,14},{14,12},{16,18},{18,... | collective-permute-start | bytes 393224 | tf_op jit(solution)/shard_map/ppermute | solution.py:505
  21.1 5.2 %collective-permute-start.3 = (f32[192,128]{1,0:T(8,128)S(1)}, f32[192,128]{1,0:T(8,128)S(1)}, u32[]{:S(2)}, u32[]{:S(2)}) collective-permute-start(f32[192,128]{1,0:T(8,128)S(1)} %add_parts.4.refs_0_.refs_3_), channel_id=1, source_target_pairs={{0,8},{2,10},{4,12},{6,14},{8,0},{10,2},{12,4},{14,6},{16,24},{18,... | collective-permute-start | bytes 294920 | tf_op jit(solution)/shard_map/ppermute | solution.py:505
  22.7 12.4 %collective-permute-start.10 = (f32[2,128,256]{2,1,0:T(8,128)S(1)}, f32[2,128,256]{2,1,0:T(8,128)S(1)}, u32[]{:S(2)}, u32[]{:S(2)}) collective-permute-start(f32[2,128,256]{2,1,0:T(8,128)S(1)} %get-tuple-element.49), channel_id=1, source_target_pairs={{0,2},{2,0},{4,6},{6,4},{8,10},{10,8},{12,14},{14,12},{16,18},{18,... | collective-permute-start | bytes 786440 | tf_op jit(solution)/shard_map/ppermute | solution.py:505
  22.9 12.2 %collective-permute-start.11 = (f32[2,128,256]{2,1,0:T(8,128)S(1)}, f32[2,128,256]{2,1,0:T(8,128)S(1)}, u32[]{:S(2)}, u32[]{:S(2)}) collective-permute-start(f32[2,128,256]{2,1,0:T(8,128)S(1)} %get-tuple-element.52), channel_id=1, source_target_pairs={{0,2},{2,0},{4,6},{6,4},{8,10},{10,8},{12,14},{14,12},{16,18},{18,... | collective-permute-start | bytes 786440 | tf_op jit(solution)/shard_map/ppermute | solution.py:505
  23.2 11.9 %collective-permute-start.14 = (f32[2,128,256]{2,1,0:T(8,128)S(1)}, f32[2,128,256]{2,1,0:T(8,128)S(1)}, u32[]{:S(2)}, u32[]{:S(2)}) collective-permute-start(f32[2,128,256]{2,1,0:T(8,128)S(1)} %joined.3), channel_id=1, source_target_pairs={{0,4},{2,6},{4,0},{6,2},{8,12},{10,14},{12,8},{14,10},{16,20},{18,... | collective-permute-start | bytes 786440 | tf_op jit(solution)/shard_map/ppermute | solution.py:505
  26.3 7.4 %collective-permute-start.7 = (f32[192,128]{1,0:T(8,128)S(1)}, f32[192,128]{1,0:T(8,128)S(1)}, u32[]{:S(2)}, u32[]{:S(2)}) collective-permute-start(f32[192,128]{1,0:T(8,128)S(1)} %add_parts.5.refs_0_), channel_id=1, source_target_pairs={{0,16},{2,18},{4,20},{6,22},{8,24},{10,26},{12,28},{14,30},{16,0},... | collective-permute-start | bytes 294920 | tf_op jit(solution)/shard_map/ppermute | solution.py:505
  33.7 5.6 %collective-permute-start.8 = (f32[192,128]{1,0:T(8,128)S(1)}, f32[192,128]{1,0:T(8,128)S(1)}, u32[]{:S(2)}, u32[]{:S(2)}) collective-permute-start(f32[192,128]{1,0:T(8,128)S(1)} %add_parts.6.refs_0_.refs_6_), channel_id=1, source_target_pairs={{0,4},{2,6},{4,0},{6,2},{8,12},{10,14},{12,8},{14,10},{16,20},{18,... | collective-permute-start | bytes 294920 | tf_op jit(solution)/shard_map/ppermute | solution.py:505
  35.2 15.2 %collective-permute-start.15 = (f32[256,256]{1,0:T(8,128)S(1)}, f32[256,256]{1,0:T(8,128)S(1)}, u32[]{:S(2)}, u32[]{:S(2)}) collective-permute-start(f32[256,256]{1,0:T(8,128)S(1)} %get-tuple-element.56), channel_id=1, source_target_pairs={{0,0},{1,1},{2,18},{3,19},{4,4},{5,5},{6,22},{7,23},{8,9},{9,8},{1... | collective-permute-start | bytes 786440 | tf_op jit(solution)/shard_map/ppermute | solution.py:537
  35.9 14.5 %collective-permute-start.16 = (f32[256,256]{1,0:T(8,128)S(1)}, f32[256,256]{1,0:T(8,128)S(1)}, u32[]{:S(2)}, u32[]{:S(2)}) collective-permute-start(f32[256,256]{1,0:T(8,128)S(1)} %get-tuple-element.57), channel_id=1, source_target_pairs={{0,9},{1,8},{2,27},{3,26},{4,13},{5,12},{6,31},{7,30},{8,0},{9,1},... | collective-permute-start | bytes 786440 | tf_op jit(solution)/shard_map/ppermute | solution.py:537
  39.3 2.6 %collective-permute-start.9 = (f32[192,128]{1,0:T(8,128)S(1)}, f32[192,128]{1,0:T(8,128)S(1)}, u32[]{:S(2)}, u32[]{:S(2)}) collective-permute-start(f32[192,128]{1,0:T(8,128)S(1)} %add_parts.7.refs_0_), channel_id=1, source_target_pairs={{0,2},{2,0},{4,6},{6,4},{8,10},{10,8},{12,14},{14,12},{16,18},{18,... | collective-permute-start | bytes 294920 | tf_op jit(solution)/shard_map/ppermute | solution.py:505
  50.8 1.9 %collective-permute-start.17 = (f32[4,16,256]{2,1,0:T(8,128)S(1)}, f32[4,16,256]{2,1,0:T(8,128)S(1)}, u32[]{:S(2)}, u32[]{:S(2)}) collective-permute-start(f32[4,16,256]{2,1,0:T(8,128)S(1)} %get-tuple-element.59), channel_id=1, source_target_pairs={{0,2},{2,0},{4,6},{6,4},{8,10},{10,8},{12,14},{14,12},{16,18},{18,... | collective-permute-start | bytes 196616 | tf_op jit(solution)/shard_map/ppermute | solution.py:505
  51.2 4.8 %collective-permute-start.18 = (f32[4,16,256]{2,1,0:T(8,128)S(1)}, f32[4,16,256]{2,1,0:T(8,128)S(1)}, u32[]{:S(2)}, u32[]{:S(2)}) collective-permute-start(f32[4,16,256]{2,1,0:T(8,128)S(1)} %get-tuple-element.60), channel_id=1, source_target_pairs={{0,4},{2,6},{4,0},{6,2},{8,12},{10,14},{12,8},{14,10},{16,20},{18,... | collective-permute-start | bytes 196616 | tf_op jit(solution)/shard_map/ppermute | solution.py:505
  51.9 4.4 %collective-permute-start.19 = (f32[4,16,256]{2,1,0:T(8,128)S(1)}, f32[4,16,256]{2,1,0:T(8,128)S(1)}, u32[]{:S(2)}, u32[]{:S(2)}) collective-permute-start(f32[4,16,256]{2,1,0:T(8,128)S(1)} %get-tuple-element.61), channel_id=1, source_target_pairs={{0,6},{2,4},{4,2},{6,0},{8,14},{10,12},{12,10},{14,8},{16,22},{18,... | collective-permute-start | bytes 196616 | tf_op jit(solution)/shard_map/ppermute | solution.py:505
  56.4 2.9 %collective-permute-start.20 = (f32[2,2,16,256]{3,2,1,0:T(8,128)S(1)}, f32[2,2,16,256]{3,2,1,0:T(8,128)S(1)}, u32[]{:S(2)}, u32[]{:S(2)}) collective-permute-start(f32[2,2,16,256]{3,2,1,0:T(8,128)S(1)} %get-tuple-element.62), channel_id=1, source_target_pairs={{0,0},{2,18},{4,4},{6,22},{8,8},{10,26},{12,12},{14,30},{16,16},{1... | collective-permute-start | bytes 196616 | tf_op jit(solution)/shard_map/ppermute | solution.py:544
  57.0 4.5 %collective-permute-start.21 = (f32[2,2,16,256]{3,2,1,0:T(8,128)S(1)}, f32[2,2,16,256]{3,2,1,0:T(8,128)S(1)}, u32[]{:S(2)}, u32[]{:S(2)}) collective-permute-start(f32[2,2,16,256]{3,2,1,0:T(8,128)S(1)} %get-tuple-element.63), channel_id=1, source_target_pairs={{0,8},{2,26},{4,12},{6,30},{8,0},{10,18},{12,4},{14,22},{16,24},{1... | collective-permute-start | bytes 196616 | tf_op jit(solution)/shard_map/ppermute | solution.py:544
  61.5 5.4 %collective-permute-start.22 = (f32[2,2,16,256]{3,2,1,0:T(8,128)S(1)}, f32[2,2,16,256]{3,2,1,0:T(8,128)S(1)}, u32[]{:S(2)}, u32[]{:S(2)}) collective-permute-start(f32[2,2,16,256]{3,2,1,0:T(8,128)S(1)} %share.1), channel_id=1, source_target_pairs={{0,2},{2,0},{4,6},{6,4},{8,10},{10,8},{12,14},{14,12},{16,18},{18,... | collective-permute-start | bytes 196616 | tf_op jit(solution)/shard_map/ppermute | solution.py:505

commit v15 on v14

--- a/solution.py
+++ b/solution.py
@@ -389,11 +389,12 @@
     )(*held(own, got))
 
 
-def core_kernel(scale, first_ref, second_ref, inverse_ref, out_ref):
+def core_kernel(scale, first_ref, second_ref, inverse_ref, out_ref, done_ref):
     t_high, t_low = split(inverse_ref[...].T)
     s_high, s_low = split(jnp.concatenate([first_ref[...], second_ref[...]], 1))
     total = dot(s_high, t_high) + dot(s_high, t_low) + dot(s_low, t_high)
     out_ref[...] = total * scale
+    done_ref[...] = total[:8, :BLK]
 
 
 def scaled_core(first, second, inverse, scale):
@@ -405,8 +406,8 @@
     return pl.pallas_call(
         body,
         in_specs=[VMEM] * 3,
-        out_specs=VMEM,
-        out_shape=jax.ShapeDtypeStruct((rows, RANK), F32),
+        out_specs=[VMEM] * 2,
+        out_shape=[jax.ShapeDtypeStruct((rows, RANK), F32), on_chip(8, BLK)],
         cost_estimate=cost(rows * RANK * RANK * 6, rows * RANK * 8),
         compiler_params=LIMIT,
         name="scaled_core",
@@ -456,21 +457,21 @@
     )(*held(*firsts))
 
 
-def share_kernel(p0, p1, out):
+def share_kernel(p0, p1, after, out):
     out[0] = p0[1]
     out[1] = p1[1]
 
 
-def share(pieces):
+def share(pieces, after):
     return pl.pallas_call(
         share_kernel,
-        in_specs=[VMEM] * 2,
+        in_specs=[VMEM] * 3,
         out_specs=VMEM,
         out_shape=on_chip(2, 2, 16, 2 * BLK),
         cost_estimate=cost(0, 16 * BLK * 64),
         compiler_params=LIMIT,
         name="share",
-    )(*held(*pieces))
+    )(*held(*pieces, after))
 
 
 def arrange_kernel(p0, p1, shared, out_ref, work):
@@ -536,13 +537,13 @@
                 pairs.append((2 * i + y, 2 * to + (y ^ ((to >> 2) & 1))))
         gathered.append(lax.ppermute(pieces[k], ("rows", "cols"), pairs))
     parts = remainder_pieces(inverse, gathered)
-    core_scaled = scaled_core(first, second, inverse, math.sqrt(total_rows))
+    core_scaled, scaled = scaled_core(first, second, inverse, math.sqrt(total_rows))
     sums = collect([parts[0]] + [rows_permute(parts[m], m) for m in (1, 2, 3)])
     passed = []
     for t in range(2):
         pairs = [(i, i ^ (t << 2) ^ ((i & 1) << 3)) for i in range(16)]
         passed.append(lax.ppermute(sums[t], "rows", pairs))
-    return core_scaled, arrange([*passed, rows_permute(share(passed), 1)])
+    return core_scaled, arrange([*passed, rows_permute(share(passed, scaled), 1)])
 
 
 def sketch_matrix(pattern, sign_bits, block_size):

time: 67.8 us -> 67.4 us (level)
    ppermute x2, waiting for transfers between devices: 2.24 us -> 0.97 us  [local(): passed.append(lax.ppermute(sums[t], 'rows', pairs))]
    ppermute x17, waiting for transfers between devices: 12 us -> 12.9 us  [rows_permute(): return lax.ppermute(value, 'rows', [(i, i ^ mask) for i in range(size)])]
  transfers between devices with their start and end apart: 23 -> 23, of which waited for: 9 -> 10; matrix products, arithmetic and copies ran while one was open for 0% -> 0% of each run, Pallas kernels for 21% -> 21%
where the time goes in v15:
time: 67.4 us; the launch traced here: 67.2 us
  starting transfers between devices  28.7 us (43%)
  waiting for transfers between devices  19.6 us (29%)
  Pallas kernels  18.1 us (27%)
  between operations  0.78 us (1%)
    ppermute x17, starting transfers between devices, rows_permute(): return lax.ppermute(value, 'rows', [(i, i ^ mask) for i in range(size)])  18.6 us
    ppermute x17, waiting for transfers between devices, rows_permute(): return lax.ppermute(value, 'rows', [(i, i ^ mask) for i in range(size)])  12.9 us
    pallas_call x1, Pallas kernels, inverse_factor(): pl.pallas_call(body, in_specs=[VMEM] * 2, out_specs=VMEM, out_shape=on_ch...  8.4 us
    ppermute x1, waiting for transfers between devices, local(): got_0 = lax.ppermute(own_0, 'cols', swap)  5.7 us
    ppermute x2, starting transfers between devices, local(): gathered.append(lax.ppermute(pieces[k], ('rows', 'cols'), pairs))  4.09 us
    ppermute x1, starting transfers between devices, local(): got_0 = lax.ppermute(own_0, 'cols', swap)  3.03 us
    ppermute x2, starting transfers between devices, local(): passed.append(lax.ppermute(sums[t], 'rows', pairs))  2.91 us
    pallas_call x1, Pallas kernels, first_sketch(): pl.pallas_call(first_sketch_kernel, in_specs=[HBM] * 3, out_specs=[VMEM]...  2.66 us
  transfers between devices with their start and end apart: 23, of which 10 were waited for; matrix products, arithmetic and copies ran while one was open for 0% of the time, Pallas kernels for 21%

profile of v15, /device:TPU:0, one launch (start us, length us, event | category | flops | bytes accessed | tf_op | source)
XLA Modules:
  0.0 67.2 jit_solution(15295924899507316127)
XLA Ops:
  0.6 2.7 %first_sketch.1 = (f32[512,128]{1,0:T(8,128)S(1)}, f32[512,2048]{1,0:T(8,128)S(1)}) custom-call(s32[2,16]{1,0:T(2,128)} %bitcast.6, f32[512,2048]{1,0:T(8,128)} %whole_ref.1, s32[2,2048]{1,0:T(2,128)} %bitcast.4), custom_call_target="tpu_custom_call" | custom-call | flops 2097 | bytes 4194 | tf_op jit(solution)/shard_map/first_sketch/pallas_call | solution.py:94
  3.3 3.0 %collective-permute-start = (f32[512,128]{1,0:T(8,128)S(1)}, f32[512,128]{1,0:T(8,128)S(1)}, u32[]{:S(2)}, u32[]{:S(2)}) collective-permute-start(f32[512,128]{1,0:T(8,128)S(1)} %get-tuple-element.35.own_ref), channel_id=1, source_target_pairs={{0,1},{1,0},{2,3},{3,2},{4,5},{5,4},{6,7},{7,6},{8,9},{9,8},{10,11... | collective-permute-start | bytes 786440 | tf_op jit(solution)/shard_map/ppermute | solution.py:514
  6.3 1.3 %second_sketch.1 = (f32[512,128]{1,0:T(8,128)S(1)}, bf16[512,2048]{1,0:T(8,128)(2,1)S(1)}, bf16[512,2048]{1,0:T(8,128)(2,1)S(1)}) custom-call(s32[2,16]{1,0:T(2,128)} %bitcast.7, s32[2,2048]{1,0:T(2,128)} %bitcast.5, f32[512,2048]{1,0:T(8,128)S(1)} %get-tuple-element.37.block_ref), custom_call_target="tpu_custom_call" | custom-call | flops 2097 | bytes 4194 | tf_op jit(solution)/shard_map/second_sketch/pallas_call | solution.py:132
  7.7 0.1 collective-permute-start.1
  7.8 5.7 %collective-permute-done.got_ref = f32[512,128]{1,0:T(8,128)S(1)} collective-permute-done((f32[512,128]{1,0:T(8,128)S(1)}, f32[512,128]{1,0:T(8,128)S(1)}, u32[]{:S(2)}, u32[]{:S(2)}) %collective-permute-start) | collective-permute-done | bytes 262176 | tf_op jit(solution)/shard_map/ppermute | solution.py:514
  13.5 0.4 first_gram.1
  13.9 1.0 %project.2 = (f32[128,256]{1,0:T(8,128)S(1)}, f32[128,256]{1,0:T(8,128)S(1)}, f32[2,128,256]{2,1,0:T(8,128)S(1)}, f32[2,128,256]{2,1,0:T(8,128)S(1)}, f32[2,128,256]{2,1,0:T(8,128)S(1)}) custom-call(bf16[256,512]{1,0:T(8,128)(2,1)S(1)} %get-tuple-element.41.refs_0_, bf16[512,2048]{1,0:T(8,128)(2,1)S(1)} %get-tuple-element.42.refs_1_, ...), custom_call_target="tpu_custom_call" | custom-call | flops 805306 | bytes 4194 | tf_op jit(solution)/shard_map/project/pallas_call | solution.py:236
  14.9 0.1 collective-permute-start.4
  15.0 0.5 collective-permute-start.5
  15.5 0.8 %collective-permute-done.4.refs_1_ = f32[128,256]{1,0:T(8,128)S(1)} collective-permute-done((f32[128,256]{1,0:T(8,128)S(1)}, f32[128,256]{1,0:T(8,128)S(1)}, u32[]{:S(2)}, u32[]{:S(2)}) %collective-permute-start.4) | collective-permute-done | bytes 131104 | tf_op jit(solution)/shard_map/ppermute | solution.py:506
  16.3 0.2 collective-permute-done.5.refs_2_
  16.6 2.1 %collective-permute-start.6 = (f32[2,128,256]{2,1,0:T(8,128)S(1)}, f32[2,128,256]{2,1,0:T(8,128)S(1)}, u32[]{:S(2)}, u32[]{:S(2)}) collective-permute-start(f32[2,128,256]{2,1,0:T(8,128)S(1)} %joined.2.refs_3_), channel_id=1, source_target_pairs={{0,4},{2,6},{4,0},{6,2},{8,12},{10,14},{12,8},{14,10},{16,20},{18,... | collective-permute-start | bytes 786440 | tf_op jit(solution)/shard_map/ppermute | solution.py:506
  18.7 0.0 collective-permute-done.1.refs_1_
  18.7 0.6 second_gram.1
  19.3 0.1 collective-permute-start.2
  19.4 1.0 %project.3 = (f32[128,256]{1,0:T(8,128)S(1)}, f32[128,256]{1,0:T(8,128)S(1)}, f32[2,128,256]{2,1,0:T(8,128)S(1)}, f32[2,128,256]{2,1,0:T(8,128)S(1)}, f32[2,128,256]{2,1,0:T(8,128)S(1)}) custom-call(bf16[256,512]{1,0:T(8,128)(2,1)S(1)} %get-tuple-element.53.refs_0_, bf16[512,2048]{1,0:T(8,128)(2,1)S(1)} %get-tuple-element.42.refs_1_, ...), custom_call_target="tpu_custom_call" | custom-call | flops 805306 | bytes 4194 | tf_op jit(solution)/shard_map/project/pallas_call | solution.py:236
  20.4 0.5 collective-permute-start.12
  21.0 0.1 collective-permute-start.13
  21.0 0.0 collective-permute-done.2.refs_1_
  21.1 1.6 %collective-permute-start.3 = (f32[192,128]{1,0:T(8,128)S(1)}, f32[192,128]{1,0:T(8,128)S(1)}, u32[]{:S(2)}, u32[]{:S(2)}) collective-permute-start(f32[192,128]{1,0:T(8,128)S(1)} %add_parts.4.refs_0_.refs_3_), channel_id=1, source_target_pairs={{0,8},{2,10},{4,12},{6,14},{8,0},{10,2},{12,4},{14,6},{16,24},{18,... | collective-permute-start | bytes 294920 | tf_op jit(solution)/shard_map/ppermute | solution.py:506
  22.7 0.2 collective-permute-start.10
  22.9 0.0 collective-permute-done.12.refs_1_
  22.9 0.3 collective-permute-start.11
  23.2 0.0 collective-permute-done.13.refs_2_
  23.2 1.4 %collective-permute-start.14 = (f32[2,128,256]{2,1,0:T(8,128)S(1)}, f32[2,128,256]{2,1,0:T(8,128)S(1)}, u32[]{:S(2)}, u32[]{:S(2)}) collective-permute-start(f32[2,128,256]{2,1,0:T(8,128)S(1)} %joined.3), channel_id=1, source_target_pairs={{0,4},{2,6},{4,0},{6,2},{8,12},{10,14},{12,8},{14,10},{16,20},{18,... | collective-permute-start | bytes 786440 | tf_op jit(solution)/shard_map/ppermute | solution.py:506
  24.6 1.7 %collective-permute-done.3.refs_1_ = f32[192,128]{1,0:T(8,128)S(1)} collective-permute-done((f32[192,128]{1,0:T(8,128)S(1)}, f32[192,128]{1,0:T(8,128)S(1)}, u32[]{:S(2)}, u32[]{:S(2)}) %collective-permute-start.3) | collective-permute-done | bytes 98336 | tf_op jit(solution)/shard_map/ppermute | solution.py:506
  26.3 0.0 collective-permute-done.6.refs_2_
  26.3 2.7 %collective-permute-start.7 = (f32[192,128]{1,0:T(8,128)S(1)}, f32[192,128]{1,0:T(8,128)S(1)}, u32[]{:S(2)}, u32[]{:S(2)}) collective-permute-start(f32[192,128]{1,0:T(8,128)S(1)} %add_parts.5.refs_0_), channel_id=1, source_target_pairs={{0,16},{2,18},{4,20},{6,22},{8,24},{10,26},{12,28},{14,30},{16,0},... | collective-permute-start | bytes 294920 | tf_op jit(solution)/shard_map/ppermute | solution.py:506
  28.9 4.8 %collective-permute-done.7.refs_1_ = f32[192,128]{1,0:T(8,128)S(1)} collective-permute-done((f32[192,128]{1,0:T(8,128)S(1)}, f32[192,128]{1,0:T(8,128)S(1)}, u32[]{:S(2)}, u32[]{:S(2)}) %collective-permute-start.7) | collective-permute-done | bytes 98336 | tf_op jit(solution)/shard_map/ppermute | solution.py:506
  33.7 1.4 %collective-permute-start.8 = (f32[192,128]{1,0:T(8,128)S(1)}, f32[192,128]{1,0:T(8,128)S(1)}, u32[]{:S(2)}, u32[]{:S(2)}) collective-permute-start(f32[192,128]{1,0:T(8,128)S(1)} %add_parts.6.refs_0_.refs_6_), channel_id=1, source_target_pairs={{0,4},{2,6},{4,0},{6,2},{8,12},{10,14},{12,8},{14,10},{16,20},{18,... | collective-permute-start | bytes 294920 | tf_op jit(solution)/shard_map/ppermute | solution.py:506
  35.1 0.0 collective-permute-done.10.refs_1_
  35.1 0.0 collective-permute-done.11.refs_4_
  35.1 0.0 collective-permute-done.14.refs_5_
  35.1 0.1 piece_sums.1
  35.2 0.7 %collective-permute-start.15 = (f32[256,256]{1,0:T(8,128)S(1)}, f32[256,256]{1,0:T(8,128)S(1)}, u32[]{:S(2)}, u32[]{:S(2)}) collective-permute-start(f32[256,256]{1,0:T(8,128)S(1)} %get-tuple-element.59), channel_id=1, source_target_pairs={{0,0},{1,1},{2,18},{3,19},{4,4},{5,5},{6,22},{7,23},{8,9},{9,8},{1... | collective-permute-start | bytes 786440 | tf_op jit(solution)/shard_map/ppermute | solution.py:538
  35.9 3.4 %collective-permute-start.16 = (f32[256,256]{1,0:T(8,128)S(1)}, f32[256,256]{1,0:T(8,128)S(1)}, u32[]{:S(2)}, u32[]{:S(2)}) collective-permute-start(f32[256,256]{1,0:T(8,128)S(1)} %get-tuple-element.60), channel_id=1, source_target_pairs={{0,9},{1,8},{2,27},{3,26},{4,13},{5,12},{6,31},{7,30},{8,0},{9,1},... | collective-permute-start | bytes 786440 | tf_op jit(solution)/shard_map/ppermute | solution.py:538
  39.3 0.0 collective-permute-done.8.refs_1_
  39.3 1.7 %collective-permute-start.9 = (f32[192,128]{1,0:T(8,128)S(1)}, f32[192,128]{1,0:T(8,128)S(1)}, u32[]{:S(2)}, u32[]{:S(2)}) collective-permute-start(f32[192,128]{1,0:T(8,128)S(1)} %add_parts.7.refs_0_), channel_id=1, source_target_pairs={{0,2},{2,0},{4,6},{6,4},{8,10},{10,8},{12,14},{14,12},{16,18},{18,... | collective-permute-start | bytes 294920 | tf_op jit(solution)/shard_map/ppermute | solution.py:506
  41.0 0.9 %collective-permute-done.9.refs_1_ = f32[192,128]{1,0:T(8,128)S(1)} collective-permute-done((f32[192,128]{1,0:T(8,128)S(1)}, f32[192,128]{1,0:T(8,128)S(1)}, u32[]{:S(2)}, u32[]{:S(2)}) %collective-permute-start.9) | collective-permute-done | bytes 98336 | tf_op jit(solution)/shard_map/ppermute | solution.py:506
  41.9 8.4 %inverse_factor.1.refs_2_.inverse_ref = f32[256,256]{1,0:T(8,128)S(1)} custom-call(f32[192,128]{1,0:T(8,128)S(1)} %add_parts.7.refs_0_, f32[192,128]{1,0:T(8,128)S(1)} %collective-permute-done.9.refs_1_), custom_call_target="tpu_custom_call" | custom-call | flops 1000000000 | bytes 524 | tf_op jit(solution)/shard_map/inverse_factor/pallas_call | solution.py:380
  50.4 0.0 collective-permute-done.15.p0
  50.4 0.0 collective-permute-done.16.p1
  50.4 0.4 remainder_pieces.1
  50.8 0.4 collective-permute-start.17
  51.2 0.7 %collective-permute-start.18 = (f32[4,16,256]{2,1,0:T(8,128)S(1)}, f32[4,16,256]{2,1,0:T(8,128)S(1)}, u32[]{:S(2)}, u32[]{:S(2)}) collective-permute-start(f32[4,16,256]{2,1,0:T(8,128)S(1)} %get-tuple-element.63), channel_id=1, source_target_pairs={{0,4},{2,6},{4,0},{6,2},{8,12},{10,14},{12,8},{14,10},{16,20},{18,... | collective-permute-start | bytes 196616 | tf_op jit(solution)/shard_map/ppermute | solution.py:506
  51.9 0.8 %collective-permute-start.19 = (f32[4,16,256]{2,1,0:T(8,128)S(1)}, f32[4,16,256]{2,1,0:T(8,128)S(1)}, u32[]{:S(2)}, u32[]{:S(2)}) collective-permute-start(f32[4,16,256]{2,1,0:T(8,128)S(1)} %get-tuple-element.64), channel_id=1, source_target_pairs={{0,6},{2,4},{4,2},{6,0},{8,14},{10,12},{12,10},{14,8},{16,22},{18,... | collective-permute-start | bytes 196616 | tf_op jit(solution)/shard_map/ppermute | solution.py:506
  52.7 0.0 collective-permute-done.17.r1
  52.7 3.3 %collective-permute-done.18.r2 = f32[4,16,256]{2,1,0:T(8,128)S(1)} collective-permute-done((f32[4,16,256]{2,1,0:T(8,128)S(1)}, f32[4,16,256]{2,1,0:T(8,128)S(1)}, u32[]{:S(2)}, u32[]{:S(2)}) %collective-permute-start.18) | collective-permute-done | bytes 65568 | tf_op jit(solution)/shard_map/ppermute | solution.py:506
  56.0 0.3 collective-permute-done.19.r3
  56.4 0.7 collective-permute-start.20
  57.0 2.2 %collective-permute-start.21 = (f32[2,2,16,256]{3,2,1,0:T(8,128)S(1)}, f32[2,2,16,256]{3,2,1,0:T(8,128)S(1)}, u32[]{:S(2)}, u32[]{:S(2)}) collective-permute-start(f32[2,2,16,256]{3,2,1,0:T(8,128)S(1)} %get-tuple-element.66), channel_id=1, source_target_pairs={{0,8},{2,26},{4,12},{6,30},{8,0},{10,18},{12,4},{14,22},{16,24},{1... | collective-permute-start | bytes 196616 | tf_op jit(solution)/shard_map/ppermute | solution.py:545
  59.3 1.3 %scaled_core.1 = (f32[512,256]{1,0:T(8,128)}, f32[8,128]{1,0:T(8,128)S(1)}) custom-call(f32[512,128]{1,0:T(8,128)S(1)} %get-tuple-element.36.refs_0_, f32[512,128]{1,0:T(8,128)S(1)} %get-tuple-element.45.refs_1_, f32[256,256]{1,0:T(8,128)S(1)} %inverse_factor.1.refs_2_.inverse_ref), custom_call_target="tpu_custom_call" | custom-call | flops 201326 | bytes 1048 | tf_op jit(solution)/shard_map/scaled_core/pallas_call | solution.py:406
  60.5 0.0 collective-permute-done.20.p0
  60.6 1.0 %collective-permute-done.21.p1 = f32[2,2,16,256]{3,2,1,0:T(8,128)S(1)} collective-permute-done((f32[2,2,16,256]{3,2,1,0:T(8,128)S(1)}, f32[2,2,16,256]{3,2,1,0:T(8,128)S(1)}, u32[]{:S(2)}, u32[]{:S(2)}) %collective-permute-start.21) | collective-permute-done | bytes 65568 | tf_op jit(solution)/shard_map/ppermute | solution.py:545
  61.5 4.1 %collective-permute-start.22 = (f32[2,2,16,256]{3,2,1,0:T(8,128)S(1)}, f32[2,2,16,256]{3,2,1,0:T(8,128)S(1)}, u32[]{:S(2)}, u32[]{:S(2)}) collective-permute-start(f32[2,2,16,256]{3,2,1,0:T(8,128)S(1)} %share.1), channel_id=1, source_target_pairs={{0,2},{2,0},{4,6},{6,4},{8,10},{10,8},{12,14},{14,12},{16,18},{18,... | collective-permute-start | bytes 196616 | tf_op jit(solution)/shard_map/ppermute | solution.py:506
  65.6 0.9 %collective-permute-done.22.shared = f32[2,2,16,256]{3,2,1,0:T(8,128)S(1)} collective-permute-done((f32[2,2,16,256]{3,2,1,0:T(8,128)S(1)}, f32[2,2,16,256]{3,2,1,0:T(8,128)S(1)}, u32[]{:S(2)}, u32[]{:S(2)}) %collective-permute-start.22) | collective-permute-done | bytes 65568 | tf_op jit(solution)/shard_map/ppermute | solution.py:506
  66.5 0.7 %arrange.1 = f32[16,8,256]{2,1,0:T(8,128)} custom-call(f32[2,2,16,256]{3,2,1,0:T(8,128)S(1)} %collective-permute-done.20.p0, f32[2,2,16,256]{3,2,1,0:T(8,128)S(1)} %collective-permute-done.21.p1, f32[2,2,16,256]{3,2,1,0:T(8,128)S(1)} %collective-permute-done.22.shared), custom_call_target="tpu_custom_call" | custom-call | bytes 131 | tf_op jit(solution)/shard_map/arrange/pallas_call | solution.py:491
  (8 shorter events, 0.1 us)
Async XLA Ops:
  3.3 10.2 %collective-permute-start = (f32[512,128]{1,0:T(8,128)S(1)}, f32[512,128]{1,0:T(8,128)S(1)}, u32[]{:S(2)}, u32[]{:S(2)}) collective-permute-start(f32[512,128]{1,0:T(8,128)S(1)} %get-tuple-element.35.own_ref), channel_id=1, source_target_pairs={{0,1},{1,0},{2,3},{3,2},{4,5},{5,4},{6,7},{7,6},{8,9},{9,8},{10,11... | collective-permute-start | bytes 786440 | tf_op jit(solution)/shard_map/ppermute | solution.py:514
  7.7 11.0 %collective-permute-start.1 = (f32[512,128]{1,0:T(8,128)S(1)}, f32[512,128]{1,0:T(8,128)S(1)}, u32[]{:S(2)}, u32[]{:S(2)}) collective-permute-start(f32[512,128]{1,0:T(8,128)S(1)} %get-tuple-element.38.refs_0_), channel_id=1, source_target_pairs={{0,1},{1,0},{2,3},{3,2},{4,5},{5,4},{6,7},{7,6},{8,9},{9,8},{10,11... | collective-permute-start | bytes 786440 | tf_op jit(solution)/shard_map/ppermute | solution.py:516
  14.9 1.4 %collective-permute-start.4 = (f32[128,256]{1,0:T(8,128)S(1)}, f32[128,256]{1,0:T(8,128)S(1)}, u32[]{:S(2)}, u32[]{:S(2)}) collective-permute-start(f32[128,256]{1,0:T(8,128)S(1)} %get-tuple-element.49), channel_id=1, source_target_pairs={{0,2},{2,0},{4,6},{6,4},{8,10},{10,8},{12,14},{14,12},{16,18},{18,... | collective-permute-start | bytes 393224 | tf_op jit(solution)/shard_map/ppermute | solution.py:506
  15.0 1.5 %collective-permute-start.5 = (f32[128,256]{1,0:T(8,128)S(1)}, f32[128,256]{1,0:T(8,128)S(1)}, u32[]{:S(2)}, u32[]{:S(2)}) collective-permute-start(f32[128,256]{1,0:T(8,128)S(1)} %get-tuple-element.50), channel_id=1, source_target_pairs={{0,2},{2,0},{4,6},{6,4},{8,10},{10,8},{12,14},{14,12},{16,18},{18,... | collective-permute-start | bytes 393224 | tf_op jit(solution)/shard_map/ppermute | solution.py:506
  16.6 9.7 %collective-permute-start.6 = (f32[2,128,256]{2,1,0:T(8,128)S(1)}, f32[2,128,256]{2,1,0:T(8,128)S(1)}, u32[]{:S(2)}, u32[]{:S(2)}) collective-permute-start(f32[2,128,256]{2,1,0:T(8,128)S(1)} %joined.2.refs_3_), channel_id=1, source_target_pairs={{0,4},{2,6},{4,0},{6,2},{8,12},{10,14},{12,8},{14,10},{16,20},{18,... | collective-permute-start | bytes 786440 | tf_op jit(solution)/shard_map/ppermute | solution.py:506
  19.3 1.8 %collective-permute-start.2 = (f32[192,128]{1,0:T(8,128)S(1)}, f32[192,128]{1,0:T(8,128)S(1)}, u32[]{:S(2)}, u32[]{:S(2)}) collective-permute-start(f32[192,128]{1,0:T(8,128)S(1)} %get-tuple-element.47), channel_id=1, source_target_pairs={{0,2},{2,0},{4,6},{6,4},{8,10},{10,8},{12,14},{14,12},{16,18},{18,... | collective-permute-start | bytes 294920 | tf_op jit(solution)/shard_map/ppermute | solution.py:506
  20.4 2.4 %collective-permute-start.12 = (f32[128,256]{1,0:T(8,128)S(1)}, f32[128,256]{1,0:T(8,128)S(1)}, u32[]{:S(2)}, u32[]{:S(2)}) collective-permute-start(f32[128,256]{1,0:T(8,128)S(1)} %get-tuple-element.57), channel_id=1, source_target_pairs={{0,2},{2,0},{4,6},{6,4},{8,10},{10,8},{12,14},{14,12},{16,18},{18,... | collective-permute-start | bytes 393224 | tf_op jit(solution)/shard_map/ppermute | solution.py:506
  21.0 2.3 %collective-permute-start.13 = (f32[128,256]{1,0:T(8,128)S(1)}, f32[128,256]{1,0:T(8,128)S(1)}, u32[]{:S(2)}, u32[]{:S(2)}) collective-permute-start(f32[128,256]{1,0:T(8,128)S(1)} %get-tuple-element.58), channel_id=1, source_target_pairs={{0,2},{2,0},{4,6},{6,4},{8,10},{10,8},{12,14},{14,12},{16,18},{18,... | collective-permute-start | bytes 393224 | tf_op jit(solution)/shard_map/ppermute | solution.py:506
  21.1 5.2 %collective-permute-start.3 = (f32[192,128]{1,0:T(8,128)S(1)}, f32[192,128]{1,0:T(8,128)S(1)}, u32[]{:S(2)}, u32[]{:S(2)}) collective-permute-start(f32[192,128]{1,0:T(8,128)S(1)} %add_parts.4.refs_0_.refs_3_), channel_id=1, source_target_pairs={{0,8},{2,10},{4,12},{6,14},{8,0},{10,2},{12,4},{14,6},{16,24},{18,... | collective-permute-start | bytes 294920 | tf_op jit(solution)/shard_map/ppermute | solution.py:506
  22.7 12.4 %collective-permute-start.10 = (f32[2,128,256]{2,1,0:T(8,128)S(1)}, f32[2,128,256]{2,1,0:T(8,128)S(1)}, u32[]{:S(2)}, u32[]{:S(2)}) collective-permute-start(f32[2,128,256]{2,1,0:T(8,128)S(1)} %get-tuple-element.52), channel_id=1, source_target_pairs={{0,2},{2,0},{4,6},{6,4},{8,10},{10,8},{12,14},{14,12},{16,18},{18,... | collective-permute-start | bytes 786440 | tf_op jit(solution)/shard_map/ppermute | solution.py:506
  22.9 12.2 %collective-permute-start.11 = (f32[2,128,256]{2,1,0:T(8,128)S(1)}, f32[2,128,256]{2,1,0:T(8,128)S(1)}, u32[]{:S(2)}, u32[]{:S(2)}) collective-permute-start(f32[2,128,256]{2,1,0:T(8,128)S(1)} %get-tuple-element.55), channel_id=1, source_target_pairs={{0,2},{2,0},{4,6},{6,4},{8,10},{10,8},{12,14},{14,12},{16,18},{18,... | collective-permute-start | bytes 786440 | tf_op jit(solution)/shard_map/ppermute | solution.py:506
  23.2 11.9 %collective-permute-start.14 = (f32[2,128,256]{2,1,0:T(8,128)S(1)}, f32[2,128,256]{2,1,0:T(8,128)S(1)}, u32[]{:S(2)}, u32[]{:S(2)}) collective-permute-start(f32[2,128,256]{2,1,0:T(8,128)S(1)} %joined.3), channel_id=1, source_target_pairs={{0,4},{2,6},{4,0},{6,2},{8,12},{10,14},{12,8},{14,10},{16,20},{18,... | collective-permute-start | bytes 786440 | tf_op jit(solution)/shard_map/ppermute | solution.py:506
  26.3 7.4 %collective-permute-start.7 = (f32[192,128]{1,0:T(8,128)S(1)}, f32[192,128]{1,0:T(8,128)S(1)}, u32[]{:S(2)}, u32[]{:S(2)}) collective-permute-start(f32[192,128]{1,0:T(8,128)S(1)} %add_parts.5.refs_0_), channel_id=1, source_target_pairs={{0,16},{2,18},{4,20},{6,22},{8,24},{10,26},{12,28},{14,30},{16,0},... | collective-permute-start | bytes 294920 | tf_op jit(solution)/shard_map/ppermute | solution.py:506
  33.7 5.6 %collective-permute-start.8 = (f32[192,128]{1,0:T(8,128)S(1)}, f32[192,128]{1,0:T(8,128)S(1)}, u32[]{:S(2)}, u32[]{:S(2)}) collective-permute-start(f32[192,128]{1,0:T(8,128)S(1)} %add_parts.6.refs_0_.refs_6_), channel_id=1, source_target_pairs={{0,4},{2,6},{4,0},{6,2},{8,12},{10,14},{12,8},{14,10},{16,20},{18,... | collective-permute-start | bytes 294920 | tf_op jit(solution)/shard_map/ppermute | solution.py:506
  35.2 15.2 %collective-permute-start.15 = (f32[256,256]{1,0:T(8,128)S(1)}, f32[256,256]{1,0:T(8,128)S(1)}, u32[]{:S(2)}, u32[]{:S(2)}) collective-permute-start(f32[256,256]{1,0:T(8,128)S(1)} %get-tuple-element.59), channel_id=1, source_target_pairs={{0,0},{1,1},{2,18},{3,19},{4,4},{5,5},{6,22},{7,23},{8,9},{9,8},{1... | collective-permute-start | bytes 786440 | tf_op jit(solution)/shard_map/ppermute | solution.py:538
  35.9 14.5 %collective-permute-start.16 = (f32[256,256]{1,0:T(8,128)S(1)}, f32[256,256]{1,0:T(8,128)S(1)}, u32[]{:S(2)}, u32[]{:S(2)}) collective-permute-start(f32[256,256]{1,0:T(8,128)S(1)} %get-tuple-element.60), channel_id=1, source_target_pairs={{0,9},{1,8},{2,27},{3,26},{4,13},{5,12},{6,31},{7,30},{8,0},{9,1},... | collective-permute-start | bytes 786440 | tf_op jit(solution)/shard_map/ppermute | solution.py:538
  39.3 2.6 %collective-permute-start.9 = (f32[192,128]{1,0:T(8,128)S(1)}, f32[192,128]{1,0:T(8,128)S(1)}, u32[]{:S(2)}, u32[]{:S(2)}) collective-permute-start(f32[192,128]{1,0:T(8,128)S(1)} %add_parts.7.refs_0_), channel_id=1, source_target_pairs={{0,2},{2,0},{4,6},{6,4},{8,10},{10,8},{12,14},{14,12},{16,18},{18,... | collective-permute-start | bytes 294920 | tf_op jit(solution)/shard_map/ppermute | solution.py:506
  50.8 1.9 %collective-permute-start.17 = (f32[4,16,256]{2,1,0:T(8,128)S(1)}, f32[4,16,256]{2,1,0:T(8,128)S(1)}, u32[]{:S(2)}, u32[]{:S(2)}) collective-permute-start(f32[4,16,256]{2,1,0:T(8,128)S(1)} %get-tuple-element.62), channel_id=1, source_target_pairs={{0,2},{2,0},{4,6},{6,4},{8,10},{10,8},{12,14},{14,12},{16,18},{18,... | collective-permute-start | bytes 196616 | tf_op jit(solution)/shard_map/ppermute | solution.py:506
  51.2 4.8 %collective-permute-start.18 = (f32[4,16,256]{2,1,0:T(8,128)S(1)}, f32[4,16,256]{2,1,0:T(8,128)S(1)}, u32[]{:S(2)}, u32[]{:S(2)}) collective-permute-start(f32[4,16,256]{2,1,0:T(8,128)S(1)} %get-tuple-element.63), channel_id=1, source_target_pairs={{0,4},{2,6},{4,0},{6,2},{8,12},{10,14},{12,8},{14,10},{16,20},{18,... | collective-permute-start | bytes 196616 | tf_op jit(solution)/shard_map/ppermute | solution.py:506
  51.9 4.4 %collective-permute-start.19 = (f32[4,16,256]{2,1,0:T(8,128)S(1)}, f32[4,16,256]{2,1,0:T(8,128)S(1)}, u32[]{:S(2)}, u32[]{:S(2)}) collective-permute-start(f32[4,16,256]{2,1,0:T(8,128)S(1)} %get-tuple-element.64), channel_id=1, source_target_pairs={{0,6},{2,4},{4,2},{6,0},{8,14},{10,12},{12,10},{14,8},{16,22},{18,... | collective-permute-start | bytes 196616 | tf_op jit(solution)/shard_map/ppermute | solution.py:506
  56.4 4.2 %collective-permute-start.20 = (f32[2,2,16,256]{3,2,1,0:T(8,128)S(1)}, f32[2,2,16,256]{3,2,1,0:T(8,128)S(1)}, u32[]{:S(2)}, u32[]{:S(2)}) collective-permute-start(f32[2,2,16,256]{3,2,1,0:T(8,128)S(1)} %get-tuple-element.65), channel_id=1, source_target_pairs={{0,0},{2,18},{4,4},{6,22},{8,8},{10,26},{12,12},{14,30},{16,16},{1... | collective-permute-start | bytes 196616 | tf_op jit(solution)/shard_map/ppermute | solution.py:545
  57.0 4.5 %collective-permute-start.21 = (f32[2,2,16,256]{3,2,1,0:T(8,128)S(1)}, f32[2,2,16,256]{3,2,1,0:T(8,128)S(1)}, u32[]{:S(2)}, u32[]{:S(2)}) collective-permute-start(f32[2,2,16,256]{3,2,1,0:T(8,128)S(1)} %get-tuple-element.66), channel_id=1, source_target_pairs={{0,8},{2,26},{4,12},{6,30},{8,0},{10,18},{12,4},{14,22},{16,24},{1... | collective-permute-start | bytes 196616 | tf_op jit(solution)/shard_map/ppermute | solution.py:545
  61.5 5.0 %collective-permute-start.22 = (f32[2,2,16,256]{3,2,1,0:T(8,128)S(1)}, f32[2,2,16,256]{3,2,1,0:T(8,128)S(1)}, u32[]{:S(2)}, u32[]{:S(2)}) collective-permute-start(f32[2,2,16,256]{3,2,1,0:T(8,128)S(1)} %share.1), channel_id=1, source_target_pairs={{0,2},{2,0},{4,6},{6,4},{8,10},{10,8},{12,14},{14,12},{16,18},{18,... | collective-permute-start | bytes 196616 | tf_op jit(solution)/shard_map/ppermute | solution.py:506

commit v16 on v15

--- a/solution.py
+++ b/solution.py
@@ -97,7 +97,7 @@
         out_specs=[VMEM] * 2,
         out_shape=[on_chip(rows, BLK), on_chip(rows, cols)],
         scratch_shapes=[
-            pltpu.SemaphoreType.DMA((10,)),
+            pltpu.SemaphoreType.DMA((18,)),
             pltpu.VMEM(sign_rows.shape, jnp.int32),
             pltpu.SMEM(pattern_rows.shape, jnp.int32),
         ],

time: 67.4 us -> 68.7 us (1.019)
  Pallas kernels: 18.1 us -> 19.4 us
    pallas_call x1, Pallas kernels: 2.66 us -> 3.96 us  [first_sketch(): pl.pallas_call(first_sketch_kernel, in_specs=[HBM] * 3, out_specs=[VMEM]...]
where the time goes in v16:
time: 68.7 us; the launch traced here: 68.5 us
  starting transfers between devices  28.7 us (42%)
  waiting for transfers between devices  19.6 us (29%)
  Pallas kernels  19.4 us (28%)
  between operations  0.78 us (1%)
    ppermute x17, starting transfers between devices, rows_permute(): return lax.ppermute(value, 'rows', [(i, i ^ mask) for i in range(size)])  18.6 us
    ppermute x17, waiting for transfers between devices, rows_permute(): return lax.ppermute(value, 'rows', [(i, i ^ mask) for i in range(size)])  12.9 us
    pallas_call x1, Pallas kernels, inverse_factor(): pl.pallas_call(body, in_specs=[VMEM] * 2, out_specs=VMEM, out_shape=on_ch...  8.41 us
    ppermute x1, waiting for transfers between devices, local(): got_0 = lax.ppermute(own_0, 'cols', swap)  5.7 us
    ppermute x2, starting transfers between devices, local(): gathered.append(lax.ppermute(pieces[k], ('rows', 'cols'), pairs))  4.27 us
    pallas_call x1, Pallas kernels, first_sketch(): pl.pallas_call(first_sketch_kernel, in_specs=[HBM] * 3, out_specs=[VMEM]...  3.96 us
    ppermute x1, starting transfers between devices, local(): got_0 = lax.ppermute(own_0, 'cols', swap)  3.03 us
    ppermute x2, starting transfers between devices, local(): passed.append(lax.ppermute(sums[t], 'rows', pairs))  2.73 us
  transfers between devices with their start and end apart: 23, of which 10 were waited for; matrix products, arithmetic and copies ran while one was open for 0% of the time, Pallas kernels for 21%

profile of v16, /device:TPU:0, one launch (start us, length us, event | category | flops | bytes accessed | tf_op | source)
XLA Modules:
  0.0 68.5 jit_solution(16317434623368378710)
XLA Ops:
  0.6 4.0 %first_sketch.1 = (f32[512,128]{1,0:T(8,128)S(1)}, f32[512,2048]{1,0:T(8,128)S(1)}) custom-call(s32[2,16]{1,0:T(2,128)} %bitcast.6, f32[512,2048]{1,0:T(8,128)} %whole_ref.1, s32[2,2048]{1,0:T(2,128)} %bitcast.4), custom_call_target="tpu_custom_call" | custom-call | flops 2097 | bytes 4194 | tf_op jit(solution)/shard_map/first_sketch/pallas_call | solution.py:94
  4.6 3.0 %collective-permute-start = (f32[512,128]{1,0:T(8,128)S(1)}, f32[512,128]{1,0:T(8,128)S(1)}, u32[]{:S(2)}, u32[]{:S(2)}) collective-permute-start(f32[512,128]{1,0:T(8,128)S(1)} %get-tuple-element.35.own_ref), channel_id=1, source_target_pairs={{0,1},{1,0},{2,3},{3,2},{4,5},{5,4},{6,7},{7,6},{8,9},{9,8},{10,11... | collective-permute-start | bytes 786440 | tf_op jit(solution)/shard_map/ppermute | solution.py:514
  7.6 1.3 %second_sketch.1 = (f32[512,128]{1,0:T(8,128)S(1)}, bf16[512,2048]{1,0:T(8,128)(2,1)S(1)}, bf16[512,2048]{1,0:T(8,128)(2,1)S(1)}) custom-call(s32[2,16]{1,0:T(2,128)} %bitcast.7, s32[2,2048]{1,0:T(2,128)} %bitcast.5, f32[512,2048]{1,0:T(8,128)S(1)} %get-tuple-element.37.block_ref), custom_call_target="tpu_custom_call" | custom-call | flops 2097 | bytes 4194 | tf_op jit(solution)/shard_map/second_sketch/pallas_call | solution.py:132
  9.0 0.1 collective-permute-start.1
  9.1 5.7 %collective-permute-done.got_ref = f32[512,128]{1,0:T(8,128)S(1)} collective-permute-done((f32[512,128]{1,0:T(8,128)S(1)}, f32[512,128]{1,0:T(8,128)S(1)}, u32[]{:S(2)}, u32[]{:S(2)}) %collective-permute-start) | collective-permute-done | bytes 262176 | tf_op jit(solution)/shard_map/ppermute | solution.py:514
  14.8 0.4 first_gram.1
  15.2 1.0 %project.2 = (f32[128,256]{1,0:T(8,128)S(1)}, f32[128,256]{1,0:T(8,128)S(1)}, f32[2,128,256]{2,1,0:T(8,128)S(1)}, f32[2,128,256]{2,1,0:T(8,128)S(1)}, f32[2,128,256]{2,1,0:T(8,128)S(1)}) custom-call(bf16[256,512]{1,0:T(8,128)(2,1)S(1)} %get-tuple-element.41.refs_0_, bf16[512,2048]{1,0:T(8,128)(2,1)S(1)} %get-tuple-element.42.refs_1_, ...), custom_call_target="tpu_custom_call" | custom-call | flops 805306 | bytes 4194 | tf_op jit(solution)/shard_map/project/pallas_call | solution.py:236
  16.2 0.1 collective-permute-start.4
  16.3 0.5 collective-permute-start.5
  16.8 0.8 %collective-permute-done.4.refs_1_ = f32[128,256]{1,0:T(8,128)S(1)} collective-permute-done((f32[128,256]{1,0:T(8,128)S(1)}, f32[128,256]{1,0:T(8,128)S(1)}, u32[]{:S(2)}, u32[]{:S(2)}) %collective-permute-start.4) | collective-permute-done | bytes 131104 | tf_op jit(solution)/shard_map/ppermute | solution.py:506
  17.7 0.2 collective-permute-done.5.refs_2_
  17.9 2.1 %collective-permute-start.6 = (f32[2,128,256]{2,1,0:T(8,128)S(1)}, f32[2,128,256]{2,1,0:T(8,128)S(1)}, u32[]{:S(2)}, u32[]{:S(2)}) collective-permute-start(f32[2,128,256]{2,1,0:T(8,128)S(1)} %joined.2.refs_3_), channel_id=1, source_target_pairs={{0,4},{2,6},{4,0},{6,2},{8,12},{10,14},{12,8},{14,10},{16,20},{18,... | collective-permute-start | bytes 786440 | tf_op jit(solution)/shard_map/ppermute | solution.py:506
  20.0 0.0 collective-permute-done.1.refs_1_
  20.0 0.6 second_gram.1
  20.6 0.1 collective-permute-start.2
  20.7 1.0 %project.3 = (f32[128,256]{1,0:T(8,128)S(1)}, f32[128,256]{1,0:T(8,128)S(1)}, f32[2,128,256]{2,1,0:T(8,128)S(1)}, f32[2,128,256]{2,1,0:T(8,128)S(1)}, f32[2,128,256]{2,1,0:T(8,128)S(1)}) custom-call(bf16[256,512]{1,0:T(8,128)(2,1)S(1)} %get-tuple-element.53.refs_0_, bf16[512,2048]{1,0:T(8,128)(2,1)S(1)} %get-tuple-element.42.refs_1_, ...), custom_call_target="tpu_custom_call" | custom-call | flops 805306 | bytes 4194 | tf_op jit(solution)/shard_map/project/pallas_call | solution.py:236
  21.7 0.5 collective-permute-start.12
  22.3 0.1 collective-permute-start.13
  22.3 0.0 collective-permute-done.2.refs_1_
  22.4 1.6 %collective-permute-start.3 = (f32[192,128]{1,0:T(8,128)S(1)}, f32[192,128]{1,0:T(8,128)S(1)}, u32[]{:S(2)}, u32[]{:S(2)}) collective-permute-start(f32[192,128]{1,0:T(8,128)S(1)} %add_parts.4.refs_0_.refs_3_), channel_id=1, source_target_pairs={{0,8},{2,10},{4,12},{6,14},{8,0},{10,2},{12,4},{14,6},{16,24},{18,... | collective-permute-start | bytes 294920 | tf_op jit(solution)/shard_map/ppermute | solution.py:506
  24.0 0.2 collective-permute-start.10
  24.2 0.0 collective-permute-done.12.refs_1_
  24.2 0.3 collective-permute-start.11
  24.5 0.0 collective-permute-done.13.refs_2_
  24.5 1.4 %collective-permute-start.14 = (f32[2,128,256]{2,1,0:T(8,128)S(1)}, f32[2,128,256]{2,1,0:T(8,128)S(1)}, u32[]{:S(2)}, u32[]{:S(2)}) collective-permute-start(f32[2,128,256]{2,1,0:T(8,128)S(1)} %joined.3), channel_id=1, source_target_pairs={{0,4},{2,6},{4,0},{6,2},{8,12},{10,14},{12,8},{14,10},{16,20},{18,... | collective-permute-start | bytes 786440 | tf_op jit(solution)/shard_map/ppermute | solution.py:506
  25.9 1.7 %collective-permute-done.3.refs_1_ = f32[192,128]{1,0:T(8,128)S(1)} collective-permute-done((f32[192,128]{1,0:T(8,128)S(1)}, f32[192,128]{1,0:T(8,128)S(1)}, u32[]{:S(2)}, u32[]{:S(2)}) %collective-permute-start.3) | collective-permute-done | bytes 98336 | tf_op jit(solution)/shard_map/ppermute | solution.py:506
  27.6 0.0 collective-permute-done.6.refs_2_
  27.6 2.7 %collective-permute-start.7 = (f32[192,128]{1,0:T(8,128)S(1)}, f32[192,128]{1,0:T(8,128)S(1)}, u32[]{:S(2)}, u32[]{:S(2)}) collective-permute-start(f32[192,128]{1,0:T(8,128)S(1)} %add_parts.5.refs_0_), channel_id=1, source_target_pairs={{0,16},{2,18},{4,20},{6,22},{8,24},{10,26},{12,28},{14,30},{16,0},... | collective-permute-start | bytes 294920 | tf_op jit(solution)/shard_map/ppermute | solution.py:506
  30.2 4.8 %collective-permute-done.7.refs_1_ = f32[192,128]{1,0:T(8,128)S(1)} collective-permute-done((f32[192,128]{1,0:T(8,128)S(1)}, f32[192,128]{1,0:T(8,128)S(1)}, u32[]{:S(2)}, u32[]{:S(2)}) %collective-permute-start.7) | collective-permute-done | bytes 98336 | tf_op jit(solution)/shard_map/ppermute | solution.py:506
  35.0 1.4 %collective-permute-start.8 = (f32[192,128]{1,0:T(8,128)S(1)}, f32[192,128]{1,0:T(8,128)S(1)}, u32[]{:S(2)}, u32[]{:S(2)}) collective-permute-start(f32[192,128]{1,0:T(8,128)S(1)} %add_parts.6.refs_0_.refs_6_), channel_id=1, source_target_pairs={{0,4},{2,6},{4,0},{6,2},{8,12},{10,14},{12,8},{14,10},{16,20},{18,... | collective-permute-start | bytes 294920 | tf_op jit(solution)/shard_map/ppermute | solution.py:506
  36.4 0.0 collective-permute-done.10.refs_1_
  36.4 0.0 collective-permute-done.11.refs_4_
  36.4 0.0 collective-permute-done.14.refs_5_
  36.4 0.1 piece_sums.1
  36.5 0.7 collective-permute-start.15
  37.2 3.6 %collective-permute-start.16 = (f32[256,256]{1,0:T(8,128)S(1)}, f32[256,256]{1,0:T(8,128)S(1)}, u32[]{:S(2)}, u32[]{:S(2)}) collective-permute-start(f32[256,256]{1,0:T(8,128)S(1)} %get-tuple-element.60), channel_id=1, source_target_pairs={{0,9},{1,8},{2,27},{3,26},{4,13},{5,12},{6,31},{7,30},{8,0},{9,1},... | collective-permute-start | bytes 786440 | tf_op jit(solution)/shard_map/ppermute | solution.py:538
  40.8 0.0 collective-permute-done.8.refs_1_
  40.8 1.7 %collective-permute-start.9 = (f32[192,128]{1,0:T(8,128)S(1)}, f32[192,128]{1,0:T(8,128)S(1)}, u32[]{:S(2)}, u32[]{:S(2)}) collective-permute-start(f32[192,128]{1,0:T(8,128)S(1)} %add_parts.7.refs_0_), channel_id=1, source_target_pairs={{0,2},{2,0},{4,6},{6,4},{8,10},{10,8},{12,14},{14,12},{16,18},{18,... | collective-permute-start | bytes 294920 | tf_op jit(solution)/shard_map/ppermute | solution.py:506
  42.5 0.9 %collective-permute-done.9.refs_1_ = f32[192,128]{1,0:T(8,128)S(1)} collective-permute-done((f32[192,128]{1,0:T(8,128)S(1)}, f32[192,128]{1,0:T(8,128)S(1)}, u32[]{:S(2)}, u32[]{:S(2)}) %collective-permute-start.9) | collective-permute-done | bytes 98336 | tf_op jit(solution)/shard_map/ppermute | solution.py:506
  43.4 8.4 %inverse_factor.1.refs_2_.inverse_ref = f32[256,256]{1,0:T(8,128)S(1)} custom-call(f32[192,128]{1,0:T(8,128)S(1)} %add_parts.7.refs_0_, f32[192,128]{1,0:T(8,128)S(1)} %collective-permute-done.9.refs_1_), custom_call_target="tpu_custom_call" | custom-call | flops 1000000000 | bytes 524 | tf_op jit(solution)/shard_map/inverse_factor/pallas_call | solution.py:380
  51.8 0.0 collective-permute-done.15.p0
  51.9 0.0 collective-permute-done.16.p1
  51.9 0.4 remainder_pieces.1
  52.3 0.4 collective-permute-start.17
  52.7 0.7 %collective-permute-start.18 = (f32[4,16,256]{2,1,0:T(8,128)S(1)}, f32[4,16,256]{2,1,0:T(8,128)S(1)}, u32[]{:S(2)}, u32[]{:S(2)}) collective-permute-start(f32[4,16,256]{2,1,0:T(8,128)S(1)} %get-tuple-element.63), channel_id=1, source_target_pairs={{0,4},{2,6},{4,0},{6,2},{8,12},{10,14},{12,8},{14,10},{16,20},{18,... | collective-permute-start | bytes 196616 | tf_op jit(solution)/shard_map/ppermute | solution.py:506
  53.4 0.8 %collective-permute-start.19 = (f32[4,16,256]{2,1,0:T(8,128)S(1)}, f32[4,16,256]{2,1,0:T(8,128)S(1)}, u32[]{:S(2)}, u32[]{:S(2)}) collective-permute-start(f32[4,16,256]{2,1,0:T(8,128)S(1)} %get-tuple-element.64), channel_id=1, source_target_pairs={{0,6},{2,4},{4,2},{6,0},{8,14},{10,12},{12,10},{14,8},{16,22},{18,... | collective-permute-start | bytes 196616 | tf_op jit(solution)/shard_map/ppermute | solution.py:506
  54.2 0.0 collective-permute-done.17.r1
  54.2 3.3 %collective-permute-done.18.r2 = f32[4,16,256]{2,1,0:T(8,128)S(1)} collective-permute-done((f32[4,16,256]{2,1,0:T(8,128)S(1)}, f32[4,16,256]{2,1,0:T(8,128)S(1)}, u32[]{:S(2)}, u32[]{:S(2)}) %collective-permute-start.18) | collective-permute-done | bytes 65568 | tf_op jit(solution)/shard_map/ppermute | solution.py:506
  57.5 0.3 collective-permute-done.19.r3
  57.8 0.7 collective-permute-start.20
  58.5 2.1 %collective-permute-start.21 = (f32[2,2,16,256]{3,2,1,0:T(8,128)S(1)}, f32[2,2,16,256]{3,2,1,0:T(8,128)S(1)}, u32[]{:S(2)}, u32[]{:S(2)}) collective-permute-start(f32[2,2,16,256]{3,2,1,0:T(8,128)S(1)} %get-tuple-element.66), channel_id=1, source_target_pairs={{0,8},{2,26},{4,12},{6,30},{8,0},{10,18},{12,4},{14,22},{16,24},{1... | collective-permute-start | bytes 196616 | tf_op jit(solution)/shard_map/ppermute | solution.py:545
  60.6 1.3 %scaled_core.1 = (f32[512,256]{1,0:T(8,128)}, f32[8,128]{1,0:T(8,128)S(1)}) custom-call(f32[512,128]{1,0:T(8,128)S(1)} %get-tuple-element.36.refs_0_, f32[512,128]{1,0:T(8,128)S(1)} %get-tuple-element.45.refs_1_, f32[256,256]{1,0:T(8,128)S(1)} %inverse_factor.1.refs_2_.inverse_ref), custom_call_target="tpu_custom_call" | custom-call | flops 201326 | bytes 1048 | tf_op jit(solution)/shard_map/scaled_core/pallas_call | solution.py:406
  61.8 0.0 collective-permute-done.20.p0
  61.8 1.0 %collective-permute-done.21.p1 = f32[2,2,16,256]{3,2,1,0:T(8,128)S(1)} collective-permute-done((f32[2,2,16,256]{3,2,1,0:T(8,128)S(1)}, f32[2,2,16,256]{3,2,1,0:T(8,128)S(1)}, u32[]{:S(2)}, u32[]{:S(2)}) %collective-permute-start.21) | collective-permute-done | bytes 65568 | tf_op jit(solution)/shard_map/ppermute | solution.py:545
  62.8 4.1 %collective-permute-start.22 = (f32[2,2,16,256]{3,2,1,0:T(8,128)S(1)}, f32[2,2,16,256]{3,2,1,0:T(8,128)S(1)}, u32[]{:S(2)}, u32[]{:S(2)}) collective-permute-start(f32[2,2,16,256]{3,2,1,0:T(8,128)S(1)} %share.1), channel_id=1, source_target_pairs={{0,2},{2,0},{4,6},{6,4},{8,10},{10,8},{12,14},{14,12},{16,18},{18,... | collective-permute-start | bytes 196616 | tf_op jit(solution)/shard_map/ppermute | solution.py:506
  66.9 0.9 %collective-permute-done.22.shared = f32[2,2,16,256]{3,2,1,0:T(8,128)S(1)} collective-permute-done((f32[2,2,16,256]{3,2,1,0:T(8,128)S(1)}, f32[2,2,16,256]{3,2,1,0:T(8,128)S(1)}, u32[]{:S(2)}, u32[]{:S(2)}) %collective-permute-start.22) | collective-permute-done | bytes 65568 | tf_op jit(solution)/shard_map/ppermute | solution.py:506
  67.8 0.7 %arrange.1 = f32[16,8,256]{2,1,0:T(8,128)} custom-call(f32[2,2,16,256]{3,2,1,0:T(8,128)S(1)} %collective-permute-done.20.p0, f32[2,2,16,256]{3,2,1,0:T(8,128)S(1)} %collective-permute-done.21.p1, f32[2,2,16,256]{3,2,1,0:T(8,128)S(1)} %collective-permute-done.22.shared), custom_call_target="tpu_custom_call" | custom-call | bytes 131 | tf_op jit(solution)/shard_map/arrange/pallas_call | solution.py:491
  (8 shorter events, 0.1 us)
Async XLA Ops:
  4.6 10.2 %collective-permute-start = (f32[512,128]{1,0:T(8,128)S(1)}, f32[512,128]{1,0:T(8,128)S(1)}, u32[]{:S(2)}, u32[]{:S(2)}) collective-permute-start(f32[512,128]{1,0:T(8,128)S(1)} %get-tuple-element.35.own_ref), channel_id=1, source_target_pairs={{0,1},{1,0},{2,3},{3,2},{4,5},{5,4},{6,7},{7,6},{8,9},{9,8},{10,11... | collective-permute-start | bytes 786440 | tf_op jit(solution)/shard_map/ppermute | solution.py:514
  9.0 11.0 %collective-permute-start.1 = (f32[512,128]{1,0:T(8,128)S(1)}, f32[512,128]{1,0:T(8,128)S(1)}, u32[]{:S(2)}, u32[]{:S(2)}) collective-permute-start(f32[512,128]{1,0:T(8,128)S(1)} %get-tuple-element.38.refs_0_), channel_id=1, source_target_pairs={{0,1},{1,0},{2,3},{3,2},{4,5},{5,4},{6,7},{7,6},{8,9},{9,8},{10,11... | collective-permute-start | bytes 786440 | tf_op jit(solution)/shard_map/ppermute | solution.py:516
  16.2 1.4 %collective-permute-start.4 = (f32[128,256]{1,0:T(8,128)S(1)}, f32[128,256]{1,0:T(8,128)S(1)}, u32[]{:S(2)}, u32[]{:S(2)}) collective-permute-start(f32[128,256]{1,0:T(8,128)S(1)} %get-tuple-element.49), channel_id=1, source_target_pairs={{0,2},{2,0},{4,6},{6,4},{8,10},{10,8},{12,14},{14,12},{16,18},{18,... | collective-permute-start | bytes 393224 | tf_op jit(solution)/shard_map/ppermute | solution.py:506
  16.3 1.5 %collective-permute-start.5 = (f32[128,256]{1,0:T(8,128)S(1)}, f32[128,256]{1,0:T(8,128)S(1)}, u32[]{:S(2)}, u32[]{:S(2)}) collective-permute-start(f32[128,256]{1,0:T(8,128)S(1)} %get-tuple-element.50), channel_id=1, source_target_pairs={{0,2},{2,0},{4,6},{6,4},{8,10},{10,8},{12,14},{14,12},{16,18},{18,... | collective-permute-start | bytes 393224 | tf_op jit(solution)/shard_map/ppermute | solution.py:506
  17.9 9.7 %collective-permute-start.6 = (f32[2,128,256]{2,1,0:T(8,128)S(1)}, f32[2,128,256]{2,1,0:T(8,128)S(1)}, u32[]{:S(2)}, u32[]{:S(2)}) collective-permute-start(f32[2,128,256]{2,1,0:T(8,128)S(1)} %joined.2.refs_3_), channel_id=1, source_target_pairs={{0,4},{2,6},{4,0},{6,2},{8,12},{10,14},{12,8},{14,10},{16,20},{18,... | collective-permute-start | bytes 786440 | tf_op jit(solution)/shard_map/ppermute | solution.py:506
  20.6 1.8 %collective-permute-start.2 = (f32[192,128]{1,0:T(8,128)S(1)}, f32[192,128]{1,0:T(8,128)S(1)}, u32[]{:S(2)}, u32[]{:S(2)}) collective-permute-start(f32[192,128]{1,0:T(8,128)S(1)} %get-tuple-element.47), channel_id=1, source_target_pairs={{0,2},{2,0},{4,6},{6,4},{8,10},{10,8},{12,14},{14,12},{16,18},{18,... | collective-permute-start | bytes 294920 | tf_op jit(solution)/shard_map/ppermute | solution.py:506
  21.7 2.4 %collective-permute-start.12 = (f32[128,256]{1,0:T(8,128)S(1)}, f32[128,256]{1,0:T(8,128)S(1)}, u32[]{:S(2)}, u32[]{:S(2)}) collective-permute-start(f32[128,256]{1,0:T(8,128)S(1)} %get-tuple-element.57), channel_id=1, source_target_pairs={{0,2},{2,0},{4,6},{6,4},{8,10},{10,8},{12,14},{14,12},{16,18},{18,... | collective-permute-start | bytes 393224 | tf_op jit(solution)/shard_map/ppermute | solution.py:506
  22.3 2.2 %collective-permute-start.13 = (f32[128,256]{1,0:T(8,128)S(1)}, f32[128,256]{1,0:T(8,128)S(1)}, u32[]{:S(2)}, u32[]{:S(2)}) collective-permute-start(f32[128,256]{1,0:T(8,128)S(1)} %get-tuple-element.58), channel_id=1, source_target_pairs={{0,2},{2,0},{4,6},{6,4},{8,10},{10,8},{12,14},{14,12},{16,18},{18,... | collective-permute-start | bytes 393224 | tf_op jit(solution)/shard_map/ppermute | solution.py:506
  22.4 5.2 %collective-permute-start.3 = (f32[192,128]{1,0:T(8,128)S(1)}, f32[192,128]{1,0:T(8,128)S(1)}, u32[]{:S(2)}, u32[]{:S(2)}) collective-permute-start(f32[192,128]{1,0:T(8,128)S(1)} %add_parts.4.refs_0_.refs_3_), channel_id=1, source_target_pairs={{0,8},{2,10},{4,12},{6,14},{8,0},{10,2},{12,4},{14,6},{16,24},{18,... | collective-permute-start | bytes 294920 | tf_op jit(solution)/shard_map/ppermute | solution.py:506
  24.0 12.4 %collective-permute-start.10 = (f32[2,128,256]{2,1,0:T(8,128)S(1)}, f32[2,128,256]{2,1,0:T(8,128)S(1)}, u32[]{:S(2)}, u32[]{:S(2)}) collective-permute-start(f32[2,128,256]{2,1,0:T(8,128)S(1)} %get-tuple-element.52), channel_id=1, source_target_pairs={{0,2},{2,0},{4,6},{6,4},{8,10},{10,8},{12,14},{14,12},{16,18},{18,... | collective-permute-start | bytes 786440 | tf_op jit(solution)/shard_map/ppermute | solution.py:506
  24.2 12.2 %collective-permute-start.11 = (f32[2,128,256]{2,1,0:T(8,128)S(1)}, f32[2,128,256]{2,1,0:T(8,128)S(1)}, u32[]{:S(2)}, u32[]{:S(2)}) collective-permute-start(f32[2,128,256]{2,1,0:T(8,128)S(1)} %get-tuple-element.55), channel_id=1, source_target_pairs={{0,2},{2,0},{4,6},{6,4},{8,10},{10,8},{12,14},{14,12},{16,18},{18,... | collective-permute-start | bytes 786440 | tf_op jit(solution)/shard_map/ppermute | solution.py:506
  24.5 11.9 %collective-permute-start.14 = (f32[2,128,256]{2,1,0:T(8,128)S(1)}, f32[2,128,256]{2,1,0:T(8,128)S(1)}, u32[]{:S(2)}, u32[]{:S(2)}) collective-permute-start(f32[2,128,256]{2,1,0:T(8,128)S(1)} %joined.3), channel_id=1, source_target_pairs={{0,4},{2,6},{4,0},{6,2},{8,12},{10,14},{12,8},{14,10},{16,20},{18,... | collective-permute-start | bytes 786440 | tf_op jit(solution)/shard_map/ppermute | solution.py:506
  27.6 7.4 %collective-permute-start.7 = (f32[192,128]{1,0:T(8,128)S(1)}, f32[192,128]{1,0:T(8,128)S(1)}, u32[]{:S(2)}, u32[]{:S(2)}) collective-permute-start(f32[192,128]{1,0:T(8,128)S(1)} %add_parts.5.refs_0_), channel_id=1, source_target_pairs={{0,16},{2,18},{4,20},{6,22},{8,24},{10,26},{12,28},{14,30},{16,0},... | collective-permute-start | bytes 294920 | tf_op jit(solution)/shard_map/ppermute | solution.py:506
  35.0 5.7 %collective-permute-start.8 = (f32[192,128]{1,0:T(8,128)S(1)}, f32[192,128]{1,0:T(8,128)S(1)}, u32[]{:S(2)}, u32[]{:S(2)}) collective-permute-start(f32[192,128]{1,0:T(8,128)S(1)} %add_parts.6.refs_0_.refs_6_), channel_id=1, source_target_pairs={{0,4},{2,6},{4,0},{6,2},{8,12},{10,14},{12,8},{14,10},{16,20},{18,... | collective-permute-start | bytes 294920 | tf_op jit(solution)/shard_map/ppermute | solution.py:506
  36.5 15.3 %collective-permute-start.15 = (f32[256,256]{1,0:T(8,128)S(1)}, f32[256,256]{1,0:T(8,128)S(1)}, u32[]{:S(2)}, u32[]{:S(2)}) collective-permute-start(f32[256,256]{1,0:T(8,128)S(1)} %get-tuple-element.59), channel_id=1, source_target_pairs={{0,0},{1,1},{2,18},{3,19},{4,4},{5,5},{6,22},{7,23},{8,9},{9,8},{1... | collective-permute-start | bytes 786440 | tf_op jit(solution)/shard_map/ppermute | solution.py:538
  37.2 14.7 %collective-permute-start.16 = (f32[256,256]{1,0:T(8,128)S(1)}, f32[256,256]{1,0:T(8,128)S(1)}, u32[]{:S(2)}, u32[]{:S(2)}) collective-permute-start(f32[256,256]{1,0:T(8,128)S(1)} %get-tuple-element.60), channel_id=1, source_target_pairs={{0,9},{1,8},{2,27},{3,26},{4,13},{5,12},{6,31},{7,30},{8,0},{9,1},... | collective-permute-start | bytes 786440 | tf_op jit(solution)/shard_map/ppermute | solution.py:538
  40.8 2.6 %collective-permute-start.9 = (f32[192,128]{1,0:T(8,128)S(1)}, f32[192,128]{1,0:T(8,128)S(1)}, u32[]{:S(2)}, u32[]{:S(2)}) collective-permute-start(f32[192,128]{1,0:T(8,128)S(1)} %add_parts.7.refs_0_), channel_id=1, source_target_pairs={{0,2},{2,0},{4,6},{6,4},{8,10},{10,8},{12,14},{14,12},{16,18},{18,... | collective-permute-start | bytes 294920 | tf_op jit(solution)/shard_map/ppermute | solution.py:506
  52.3 1.9 %collective-permute-start.17 = (f32[4,16,256]{2,1,0:T(8,128)S(1)}, f32[4,16,256]{2,1,0:T(8,128)S(1)}, u32[]{:S(2)}, u32[]{:S(2)}) collective-permute-start(f32[4,16,256]{2,1,0:T(8,128)S(1)} %get-tuple-element.62), channel_id=1, source_target_pairs={{0,2},{2,0},{4,6},{6,4},{8,10},{10,8},{12,14},{14,12},{16,18},{18,... | collective-permute-start | bytes 196616 | tf_op jit(solution)/shard_map/ppermute | solution.py:506
  52.7 4.8 %collective-permute-start.18 = (f32[4,16,256]{2,1,0:T(8,128)S(1)}, f32[4,16,256]{2,1,0:T(8,128)S(1)}, u32[]{:S(2)}, u32[]{:S(2)}) collective-permute-start(f32[4,16,256]{2,1,0:T(8,128)S(1)} %get-tuple-element.63), channel_id=1, source_target_pairs={{0,4},{2,6},{4,0},{6,2},{8,12},{10,14},{12,8},{14,10},{16,20},{18,... | collective-permute-start | bytes 196616 | tf_op jit(solution)/shard_map/ppermute | solution.py:506
  53.4 4.4 %collective-permute-start.19 = (f32[4,16,256]{2,1,0:T(8,128)S(1)}, f32[4,16,256]{2,1,0:T(8,128)S(1)}, u32[]{:S(2)}, u32[]{:S(2)}) collective-permute-start(f32[4,16,256]{2,1,0:T(8,128)S(1)} %get-tuple-element.64), channel_id=1, source_target_pairs={{0,6},{2,4},{4,2},{6,0},{8,14},{10,12},{12,10},{14,8},{16,22},{18,... | collective-permute-start | bytes 196616 | tf_op jit(solution)/shard_map/ppermute | solution.py:506
  57.8 4.0 %collective-permute-start.20 = (f32[2,2,16,256]{3,2,1,0:T(8,128)S(1)}, f32[2,2,16,256]{3,2,1,0:T(8,128)S(1)}, u32[]{:S(2)}, u32[]{:S(2)}) collective-permute-start(f32[2,2,16,256]{3,2,1,0:T(8,128)S(1)} %get-tuple-element.65), channel_id=1, source_target_pairs={{0,0},{2,18},{4,4},{6,22},{8,8},{10,26},{12,12},{14,30},{16,16},{1... | collective-permute-start | bytes 196616 | tf_op jit(solution)/shard_map/ppermute | solution.py:545
  58.5 4.3 %collective-permute-start.21 = (f32[2,2,16,256]{3,2,1,0:T(8,128)S(1)}, f32[2,2,16,256]{3,2,1,0:T(8,128)S(1)}, u32[]{:S(2)}, u32[]{:S(2)}) collective-permute-start(f32[2,2,16,256]{3,2,1,0:T(8,128)S(1)} %get-tuple-element.66), channel_id=1, source_target_pairs={{0,8},{2,26},{4,12},{6,30},{8,0},{10,18},{12,4},{14,22},{16,24},{1... | collective-permute-start | bytes 196616 | tf_op jit(solution)/shard_map/ppermute | solution.py:545
  62.8 5.0 %collective-permute-start.22 = (f32[2,2,16,256]{3,2,1,0:T(8,128)S(1)}, f32[2,2,16,256]{3,2,1,0:T(8,128)S(1)}, u32[]{:S(2)}, u32[]{:S(2)}) collective-permute-start(f32[2,2,16,256]{3,2,1,0:T(8,128)S(1)} %share.1), channel_id=1, source_target_pairs={{0,2},{2,0},{4,6},{6,4},{8,10},{10,8},{12,14},{14,12},{16,18},{18,... | collective-permute-start | bytes 196616 | tf_op jit(solution)/shard_map/ppermute | solution.py:506
